TPU v7x, 32 devices: a whole 2x2x4 slice. The times are simulated.
32 devices in a mesh: probe: 4 (over y, core), store: 8 (over z, x).
Axes of the slice: x: 2, y: 2, z: 4, core: 2. Of those that a mesh axis runs over, the one named last changes fastest.
Arguments:
- probe_field: bfloat16 [96, 128, 8, 128], P('probe', 'store'), may hold values from -6 to 6
- bounds: int32 [96, 2], P('probe'), may hold values from 0 to 128, as said below
- courant: float32 [128, 8, 128], P('store'), may hold values from 0.1 to 0.2
- snapshots: bfloat16 [8, 128, 8, 128], P(None, 'store', 'probe'), may hold values from -0.5 to 0.5
- snap_times: int32 [8], replicated, may hold values from 0 to 7, each once
- basis_panels: bfloat16 [96, 128, 8, 128], P('probe', 'store'), may hold values from -0.015625 to 0.015625
Outputs:
- response: float32 [96, 128, 8, 128], P('probe', 'store')
- projection: float32 [96, 96], P(None, 'probe')
Inputs may be any that keep to these rules, and one draw needn't show every extreme that they name: 0 <= bounds[k, 0] < bounds[k, 1] <= 128 for every probe k, and each region holds at least 32 rows.
All inputs are finite; a program needn't handle non-finite values.
Results may differ from a plain program's by a relative error of at most 0.0031.
Values may be sent and summed in bfloat16 or wider, within the bound.
No kernel may reach another device: no remote copies, remote signals or barrier semaphores. Data moves between devices by JAX's collectives and lax.ppermute only.
A program may use at most 64 MiB of HBM per device.

v0:
```python
import jax
import jax.numpy as jnp
from jax import lax
from jax.sharding import PartitionSpec as P

stencil_taps = (-205.0 / 72.0, 8.0 / 5.0, -1.0 / 5.0, 8.0 / 315.0, -1.0 / 560.0)


def extended(x, sides, width):
    for axis, dim in sides:
        devices, length = (lax.axis_size(axis), x.shape[dim])
        up = [(i, (i + 1) % devices) for i in range(devices - 1)]
        down = [(j, i) for i, j in up]
        last = lax.slice_in_dim(x, length - width, length, axis=dim)
        leading = lax.slice_in_dim(x, 0, width, axis=dim)
        before = lax.ppermute(last, axis, up)
        after = lax.ppermute(leading, axis, down)
        x = jnp.concatenate([before, x, after], axis=dim)
    return x


def laplace(full):
    extent_x = full.shape[-3] - 8
    extent_y = full.shape[-2] - 8
    extent_z = full.shape[-1] - 8
    centre = full[..., 4 : 4 + extent_x, 4 : 4 + extent_y, 4 : 4 + extent_z]
    totals = 3.0 * stencil_taps[0] * centre
    for distance in range(1, 5):
        along = full[
            ..., 4 + distance : 4 + distance + extent_x, 4 : 4 + extent_y, 4 : 4 + extent_z
        ]
        along = (
            along
            + full[..., 4 - distance : 4 - distance + extent_x, 4 : 4 + extent_y, 4 : 4 + extent_z]
        )
        along = (
            along
            + full[..., 4 : 4 + extent_x, 4 + distance : 4 + distance + extent_y, 4 : 4 + extent_z]
        )
        along = (
            along
            + full[..., 4 : 4 + extent_x, 4 - distance : 4 - distance + extent_y, 4 : 4 + extent_z]
        )
        along = (
            along
            + full[..., 4 : 4 + extent_x, 4 : 4 + extent_y, 4 + distance : 4 + distance + extent_z]
        )
        along = (
            along
            + full[..., 4 : 4 + extent_x, 4 : 4 + extent_y, 4 - distance : 4 - distance + extent_z]
        )
        totals = totals + stencil_taps[distance] * along
    return totals


def slab_mask(row_index, bounds):
    return ((row_index[None, :] >= bounds[:, 0:1]) & (row_index[None, :] < bounds[:, 1:2])).astype(
        jnp.float32
    )


def side_frame(field):
    return jnp.pad(field, ((0, 0), (0, 0), (4, 4), (4, 4)))


def local(probe_field, bounds, courant, snapshots, snap_times, basis_panels):
    probes_here, depth_rows, cells_y, cells_z = probe_field.shape
    steps_total = snap_times.shape[0]
    all_snaps = lax.all_gather(snapshots, "probe", axis=2, tiled=True)
    row_start = lax.axis_index("store") * depth_rows
    inside = slab_mask(row_start + jnp.arange(depth_rows, dtype=jnp.int32), bounds)
    perturb = probe_field.astype(jnp.float32) * inside[:, :, None, None]
    earlier = jnp.zeros((probes_here, depth_rows, cells_y, cells_z), jnp.float32)
    current = earlier
    for turn_index in range(steps_total):
        picked = lax.dynamic_index_in_dim(all_snaps, snap_times[turn_index], 0, keepdims=False)
        padded = extended(current, (("store", 1),), 4)
        advanced = (
            2.0 * current
            - earlier
            + courant * laplace(side_frame(padded))
            + perturb * picked.astype(jnp.float32)
        )
        earlier = current
        current = advanced
    response_low = current.astype(jnp.bfloat16)
    flat_fields = response_low.reshape(probes_here, -1)
    portion = lax.all_gather(basis_panels, "probe", axis=0, tiled=True)
    product = lax.dot_general(
        portion.reshape(portion.shape[0], -1),
        flat_fields,
        (((1,), (1,)), ((), ())),
        preferred_element_type=jnp.float32,
    )
    projection = lax.psum(product, "store")
    return (current, projection)


def solution(mesh):
    placed = (
        P("probe", "store", None, None),
        P("probe", None),
        P("store", None, None),
        P(None, "store", "probe", None),
        P(),
        P("probe", "store", None, None),
    )
    return jax.shard_map(
        local,
        mesh=mesh,
        in_specs=placed,
        out_specs=(P("probe", "store", None, None), P(None, "probe")),
        check_vma=False,
    )
```

profile of v0, /device:TPU:0, one launch (start us, length us, event | category | flops | bytes accessed | tf_op | source)
XLA Modules:
  0.0 564.6 jit_solution(12925683046278286328)
XLA Ops:
  26.5 6.3 %all_gather.6 = bf16[8,16,8,128]{3,1,0,2:T(8,128)(2,1)S(1)} all-gather(bf16[8,16,2,128]{3,1,0,2:T(8,128)(2,1)S(1)} %copy.10), channel_id=1, replica_groups=mesh['probe'=4,'store'=8] {'probe'}, dimensions={2}, use_global_device_ids=true | all-gather | bytes 327680 | tf_op jit(solution)/shard_map/all_gather | solution.py:69
  50.1 7.6 %collective-permute-done.2 = f32[24,4,8,128]{3,2,1,0:T(8,128)S(1)} collective-permute-done((f32[24,4,8,128]{3,2,1,0:T(8,128)S(1)}, f32[24,4,8,128]{3,2,1,0:T(8,128)S(1)}, u32[]{:S(2)}, u32[]{:S(2)}) %collective-permute-start.2) | collective-permute-done | bytes 393248 | tf_op jit(solution)/shard_map/ppermute | solution.py:17
  57.7 8.6 %collective-permute-done.3 = f32[24,4,8,128]{3,2,1,0:T(8,128)S(1)} collective-permute-done((f32[24,4,8,128]{3,2,1,0:T(8,128)S(1)}, f32[24,4,8,128]{3,2,1,0:T(8,128)S(1)}, u32[]{:S(2)}, u32[]{:S(2)}) %collective-permute-start.3) | collective-permute-done | bytes 393248 | tf_op jit(solution)/shard_map/ppermute | solution.py:16
  66.3 6.0 %select_maximum_fusion.12 = f32[24,24,16,136]{3,2,1,0:T(8,128)} fusion(f32[24,4,8,128]{3,2,1,0:T(8,128)S(1)} %collective-permute-done.2, f32[24,16,8,128]{3,2,1,0:T(8,128)S(1)} %fusion.231, f32[24,4,8,128]{3,2,1,0:T(8,128)S(1)} %collective-permute-done.3), kind=kLoop, calls=%fused_computation.32 | loop fusion | flops 18800640 | bytes 7372800 | tf_op jit(solution)/shard_map/concatenate | solution.py:18
  72.3 39.5 %fusion.200 = f32[24,16,8,128]{3,2,1,0:T(8,128)S(1)} fusion(f32[24,16,8,128]{3,2,1,0:T(8,128)} %copy-done.5, f32[24,4,8,128]{3,2,1,0:T(8,128)S(1)} %collective-permute-done.3, f32[24,4,8,128]{3,2,1,0:T(8,128)S(1)} %collective-permute-done.2, f32[24,24,16,136]{3,2,1,0:T(8,128)} %select_maximum_fusion.12, bf16[24,16,8,128]{3,2,1,0:T(8,128)(2,1)S(1)} %copy-done, ...), kind=kLoop, calls=%fused_computation.327 | loop fusion | flops 17301504 | bytes 30017024 | tf_op jit(solution)/shard_map/add | solution.py:79
  118.4 7.3 %collective-permute-done.4 = f32[24,4,8,128]{3,2,1,0:T(8,128)S(1)} collective-permute-done((f32[24,4,8,128]{3,2,1,0:T(8,128)S(1)}, f32[24,4,8,128]{3,2,1,0:T(8,128)S(1)}, u32[]{:S(2)}, u32[]{:S(2)}) %collective-permute-start.4) | collective-permute-done | bytes 393248 | tf_op jit(solution)/shard_map/ppermute | solution.py:17
  125.8 8.6 %collective-permute-done.5 = f32[24,4,8,128]{3,2,1,0:T(8,128)S(1)} collective-permute-done((f32[24,4,8,128]{3,2,1,0:T(8,128)S(1)}, f32[24,4,8,128]{3,2,1,0:T(8,128)S(1)}, u32[]{:S(2)}, u32[]{:S(2)}) %collective-permute-start.5) | collective-permute-done | bytes 393248 | tf_op jit(solution)/shard_map/ppermute | solution.py:16
  134.4 6.0 %select_maximum_fusion.10 = f32[24,24,16,136]{3,2,1,0:T(8,128)} fusion(f32[24,4,8,128]{3,2,1,0:T(8,128)S(1)} %collective-permute-done.4, f32[24,16,8,128]{3,2,1,0:T(8,128)S(1)} %fusion.200, f32[24,4,8,128]{3,2,1,0:T(8,128)S(1)} %collective-permute-done.5), kind=kLoop, calls=%fused_computation.30 | loop fusion | flops 18800640 | bytes 7372800 | tf_op jit(solution)/shard_map/concatenate | solution.py:18
  140.3 40.2 %fusion.169 = f32[24,16,8,128]{3,2,1,0:T(8,128)S(1)} fusion(f32[24,16,8,128]{3,2,1,0:T(8,128)} %copy-done.4, f32[24,4,8,128]{3,2,1,0:T(8,128)S(1)} %collective-permute-done.5, f32[24,4,8,128]{3,2,1,0:T(8,128)S(1)} %collective-permute-done.4, f32[24,24,16,136]{3,2,1,0:T(8,128)} %select_maximum_fusion.10, f32[24,16,8,128]{3,2,1,0:T(8,128)} %copy-done.5, ...), kind=kLoop, calls=%fused_computation.296 | loop fusion | flops 17694720 | bytes 31589888 | tf_op jit(solution)/shard_map/add | solution.py:79
  187.3 7.1 %collective-permute-done.6 = f32[24,4,8,128]{3,2,1,0:T(8,128)S(1)} collective-permute-done((f32[24,4,8,128]{3,2,1,0:T(8,128)S(1)}, f32[24,4,8,128]{3,2,1,0:T(8,128)S(1)}, u32[]{:S(2)}, u32[]{:S(2)}) %collective-permute-start.6) | collective-permute-done | bytes 393248 | tf_op jit(solution)/shard_map/ppermute | solution.py:17
  194.4 8.6 %collective-permute-done.7 = f32[24,4,8,128]{3,2,1,0:T(8,128)S(1)} collective-permute-done((f32[24,4,8,128]{3,2,1,0:T(8,128)S(1)}, f32[24,4,8,128]{3,2,1,0:T(8,128)S(1)}, u32[]{:S(2)}, u32[]{:S(2)}) %collective-permute-start.7) | collective-permute-done | bytes 393248 | tf_op jit(solution)/shard_map/ppermute | solution.py:16
  208.9 36.7 %fusion.138 = f32[24,16,8,128]{3,2,1,0:T(8,128)} fusion(f32[24,16,8,128]{3,2,1,0:T(8,128)S(1)} %fusion.169, f32[24,4,8,128]{3,2,1,0:T(8,128)S(1)} %collective-permute-done.7, f32[24,4,8,128]{3,2,1,0:T(8,128)S(1)} %collective-permute-done.6, f32[24,24,16,136]{3,2,1,0:T(8,128)} %select_maximum_fusion.8, f32[24,16,8,128]{3,2,1,0:T(8,128)} %copy-done.4, ...), kind=kLoop, calls=%fused_computation.265 | loop fusion | flops 17694720 | bytes 31589888 | tf_op jit(solution)/shard_map/add | solution.py:79
  253.3 7.3 %collective-permute-done.8 = f32[24,4,8,128]{3,2,1,0:T(8,128)S(1)} collective-permute-done((f32[24,4,8,128]{3,2,1,0:T(8,128)S(1)}, f32[24,4,8,128]{3,2,1,0:T(8,128)S(1)}, u32[]{:S(2)}, u32[]{:S(2)}) %collective-permute-start.8) | collective-permute-done | bytes 393248 | tf_op jit(solution)/shard_map/ppermute | solution.py:17
  260.6 8.6 %collective-permute-done.9 = f32[24,4,8,128]{3,2,1,0:T(8,128)S(1)} collective-permute-done((f32[24,4,8,128]{3,2,1,0:T(8,128)S(1)}, f32[24,4,8,128]{3,2,1,0:T(8,128)S(1)}, u32[]{:S(2)}, u32[]{:S(2)}) %collective-permute-start.9) | collective-permute-done | bytes 393248 | tf_op jit(solution)/shard_map/ppermute | solution.py:16
  275.2 39.8 %fusion.107 = f32[24,16,8,128]{3,2,1,0:T(8,128)S(1)} fusion(f32[24,16,8,128]{3,2,1,0:T(8,128)} %fusion.138, f32[24,4,8,128]{3,2,1,0:T(8,128)S(1)} %collective-permute-done.9, f32[24,4,8,128]{3,2,1,0:T(8,128)S(1)} %collective-permute-done.8, f32[24,24,16,136]{3,2,1,0:T(8,128)} %select_maximum_fusion.6, f32[24,16,8,128]{3,2,1,0:T(8,128)} %copy-done.2, ...), kind=kLoop, calls=%fused_computation.234 | loop fusion | flops 17694720 | bytes 31589888 | tf_op jit(solution)/shard_map/add | solution.py:79
  321.5 7.3 %collective-permute-done.10 = f32[24,4,8,128]{3,2,1,0:T(8,128)S(1)} collective-permute-done((f32[24,4,8,128]{3,2,1,0:T(8,128)S(1)}, f32[24,4,8,128]{3,2,1,0:T(8,128)S(1)}, u32[]{:S(2)}, u32[]{:S(2)}) %collective-permute-start.10) | collective-permute-done | bytes 393248 | tf_op jit(solution)/shard_map/ppermute | solution.py:17
  328.8 8.6 %collective-permute-done.11 = f32[24,4,8,128]{3,2,1,0:T(8,128)S(1)} collective-permute-done((f32[24,4,8,128]{3,2,1,0:T(8,128)S(1)}, f32[24,4,8,128]{3,2,1,0:T(8,128)S(1)}, u32[]{:S(2)}, u32[]{:S(2)}) %collective-permute-start.11) | collective-permute-done | bytes 393248 | tf_op jit(solution)/shard_map/ppermute | solution.py:16
  343.3 39.2 %fusion.76 = f32[24,16,8,128]{3,2,1,0:T(8,128)S(1)} fusion(f32[24,16,8,128]{3,2,1,0:T(8,128)} %copy-done.1, f32[24,4,8,128]{3,2,1,0:T(8,128)S(1)} %collective-permute-done.11, f32[24,4,8,128]{3,2,1,0:T(8,128)S(1)} %collective-permute-done.10, f32[24,24,16,136]{3,2,1,0:T(8,128)} %select_maximum_fusion.4, f32[24,16,8,128]{3,2,1,0:T(8,128)} %fusion.138, ...), kind=kLoop, calls=%fused_computation.203 | loop fusion | flops 17694720 | bytes 31589888 | tf_op jit(solution)/shard_map/add | solution.py:79
  397.4 8.7 %collective-permute-done.13 = f32[24,4,8,128]{3,2,1,0:T(8,128)S(1)} collective-permute-done((f32[24,4,8,128]{3,2,1,0:T(8,128)}, f32[24,4,8,128]{3,2,1,0:T(8,128)S(1)}, u32[]{:S(2)}, u32[]{:S(2)}) %collective-permute-start.13) | collective-permute-done | bytes 393248 | tf_op jit(solution)/shard_map/ppermute | solution.py:16
  412.0 36.5 %fusion.45 = f32[24,16,8,128]{3,2,1,0:T(8,128)} fusion(f32[24,16,8,128]{3,2,1,0:T(8,128)S(1)} %fusion.76, f32[24,4,8,128]{3,2,1,0:T(8,128)S(1)} %collective-permute-done.13, f32[24,4,8,128]{3,2,1,0:T(8,128)S(1)} %collective-permute-done.12, f32[24,24,16,136]{3,2,1,0:T(8,128)} %select_maximum_fusion.2, f32[24,16,8,128]{3,2,1,0:T(8,128)} %copy-done.1, ...), kind=kLoop, calls=%fused_computation.172 | loop fusion | flops 17694720 | bytes 31589888 | tf_op jit(solution)/shard_map/add | solution.py:79
  456.1 7.4 %collective-permute-done.14 = f32[24,4,8,128]{3,2,1,0:T(8,128)S(1)} collective-permute-done((f32[24,4,8,128]{3,2,1,0:T(8,128)S(1)}, f32[24,4,8,128]{3,2,1,0:T(8,128)S(1)}, u32[]{:S(2)}, u32[]{:S(2)}) %collective-permute-start.14) | collective-permute-done | bytes 393248 | tf_op jit(solution)/shard_map/ppermute | solution.py:17
  463.5 8.6 %collective-permute-done.15 = f32[24,4,8,128]{3,2,1,0:T(8,128)S(1)} collective-permute-done((f32[24,4,8,128]{3,2,1,0:T(8,128)S(1)}, f32[24,4,8,128]{3,2,1,0:T(8,128)S(1)}, u32[]{:S(2)}, u32[]{:S(2)}) %collective-permute-start.15) | collective-permute-done | bytes 393248 | tf_op jit(solution)/shard_map/ppermute | solution.py:16
  478.8 40.4 %fusion.265 = (bf16[24,16,8,128]{3,2,1,0:T(8,128)(2,1)S(1)}, f32[24,16,8,128]{3,2,1,0:T(8,128)}) fusion(f32[16,8,128]{2,1,0:T(8,128)S(1)} %copy.18, f32[24,16]{1,0:T(8,128)S(1)} %and_convert_fusion, bf16[24,16,8,128]{3,2,1,0:T(8,128)(2,1)S(1)} %copy-done, f32[24,24,16,136]{3,2,1,0:T(8,128)} %select_maximum_fusion, f32[24,16,8,128]{3,2,1,0:T(8,128)} %fusion.45, ...), kind=kLoop, calls=%fused_computation.448 | loop fusion | flops 18087936 | bytes 32376320 | tf_op jit(solution)/shard_map/convert_element_type | solution.py:86
  522.2 35.5 %psum.7 = f32[96,24]{0,1:T(8,128)} all-reduce(f32[96,24]{0,1:T(8,128)S(1)} %convolution_bitcast_fusion), channel_id=1, replica_groups=mesh['probe'=4,'store'=8] {'store'}, use_global_device_ids=true, to_apply=%region_0.1 | all-reduce | flops 2304 | bytes 18432 | tf_op jit(solution)/shard_map/psum | solution.py:95
  (83 shorter events, 104.8 us)
Async XLA Ops:
  7.2 31.4 %copy-start.13 = (s32[24,2]{0,1:T(2,128)S(1)}, s32[24,2]{0,1:T(2,128)}, u32[]{:S(2)}) copy-start(s32[24,2]{0,1:T(2,128)} %param.7) | copy-start | bytes 580
  7.2 512.0 %all-gather.2.cloned.1.call-start = ((), (), s32[]{:S(2)}) async-start(), calls=%async_computation | async-start | bytes 3932160 | tf_op jit(solution)/shard_map/all_gather | solution.py:88
  7.3 31.4 %collective-permute-start = (f32[24,4,8,128]{3,2,1,0:T(8,128)S(1)}, f32[24,4,8,128]{3,2,1,0:T(8,128)S(1)}, u32[]{:S(2)}, u32[]{:S(2)}) collective-permute-start(f32[24,4,8,128]{3,2,1,0:T(8,128)S(1)} %broadcast.90), channel_id=1, source_target_pairs={{1,0},{2,1},{3,2},{4,3},{5,4},{6,5},{7,6},{9,8},{10,9},{11,10},{12... | collective-permute-start | bytes 1179656 | tf_op jit(solution)/shard_map/ppermute | solution.py:17
  8.6 30.1 %collective-permute-start.1 = (f32[24,4,8,128]{3,2,1,0:T(8,128)S(1)}, f32[24,4,8,128]{3,2,1,0:T(8,128)S(1)}, u32[]{:S(2)}, u32[]{:S(2)}) collective-permute-start(f32[24,4,8,128]{3,2,1,0:T(8,128)S(1)} %broadcast.90), channel_id=1, source_target_pairs={{0,1},{1,2},{2,3},{3,4},{4,5},{5,6},{6,7},{8,9},{9,10},{10,11},{11... | collective-permute-start | bytes 1179656 | tf_op jit(solution)/shard_map/ppermute | solution.py:16
  43.8 22.6 %copy-start.5 = (f32[24,16,8,128]{3,2,1,0:T(8,128)}, f32[24,16,8,128]{3,2,1,0:T(8,128)S(1)}, u32[]{:S(2)}) copy-start(f32[24,16,8,128]{3,2,1,0:T(8,128)S(1)} %fusion.231) | copy-start | bytes 4718596
  43.8 13.9 %collective-permute-start.2 = (f32[24,4,8,128]{3,2,1,0:T(8,128)S(1)}, f32[24,4,8,128]{3,2,1,0:T(8,128)S(1)}, u32[]{:S(2)}, u32[]{:S(2)}) collective-permute-start(f32[24,4,8,128]{3,2,1,0:T(8,128)S(1)} %get-tuple-element.16), channel_id=1, source_target_pairs={{1,0},{2,1},{3,2},{4,3},{5,4},{6,5},{7,6},{9,8},{10,9},{11,10},{12... | collective-permute-start | bytes 1179656 | tf_op jit(solution)/shard_map/ppermute | solution.py:17
  45.1 21.2 %collective-permute-start.3 = (f32[24,4,8,128]{3,2,1,0:T(8,128)S(1)}, f32[24,4,8,128]{3,2,1,0:T(8,128)S(1)}, u32[]{:S(2)}, u32[]{:S(2)}) collective-permute-start(f32[24,4,8,128]{3,2,1,0:T(8,128)S(1)} %get-tuple-element.17), channel_id=1, source_target_pairs={{0,1},{1,2},{2,3},{3,4},{4,5},{5,6},{6,7},{8,9},{9,10},{10,11},{11... | collective-permute-start | bytes 1179656 | tf_op jit(solution)/shard_map/ppermute | solution.py:16
  111.9 22.5 %copy-start.4 = (f32[24,16,8,128]{3,2,1,0:T(8,128)}, f32[24,16,8,128]{3,2,1,0:T(8,128)S(1)}, u32[]{:S(2)}) copy-start(f32[24,16,8,128]{3,2,1,0:T(8,128)S(1)} %fusion.200) | copy-start | bytes 4718596
  112.0 13.8 %collective-permute-start.4 = (f32[24,4,8,128]{3,2,1,0:T(8,128)S(1)}, f32[24,4,8,128]{3,2,1,0:T(8,128)S(1)}, u32[]{:S(2)}, u32[]{:S(2)}) collective-permute-start(f32[24,4,8,128]{3,2,1,0:T(8,128)S(1)} %get-tuple-element.14), channel_id=1, source_target_pairs={{1,0},{2,1},{3,2},{4,3},{5,4},{6,5},{7,6},{9,8},{10,9},{11,10},{12... | collective-permute-start | bytes 1179656 | tf_op jit(solution)/shard_map/ppermute | solution.py:17
  113.4 21.0 %collective-permute-start.5 = (f32[24,4,8,128]{3,2,1,0:T(8,128)S(1)}, f32[24,4,8,128]{3,2,1,0:T(8,128)S(1)}, u32[]{:S(2)}, u32[]{:S(2)}) collective-permute-start(f32[24,4,8,128]{3,2,1,0:T(8,128)S(1)} %get-tuple-element.15), channel_id=1, source_target_pairs={{0,1},{1,2},{2,3},{3,4},{4,5},{5,6},{6,7},{8,9},{9,10},{10,11},{11... | collective-permute-start | bytes 1179656 | tf_op jit(solution)/shard_map/ppermute | solution.py:16
  180.5 28.5 %copy-start.2 = (f32[24,16,8,128]{3,2,1,0:T(8,128)}, f32[24,16,8,128]{3,2,1,0:T(8,128)S(1)}, u32[]{:S(2)}) copy-start(f32[24,16,8,128]{3,2,1,0:T(8,128)S(1)} %fusion.169) | copy-start | bytes 4718596
  180.6 13.8 %collective-permute-start.6 = (f32[24,4,8,128]{3,2,1,0:T(8,128)S(1)}, f32[24,4,8,128]{3,2,1,0:T(8,128)S(1)}, u32[]{:S(2)}, u32[]{:S(2)}) collective-permute-start(f32[24,4,8,128]{3,2,1,0:T(8,128)S(1)} %get-tuple-element.12), channel_id=1, source_target_pairs={{1,0},{2,1},{3,2},{4,3},{5,4},{6,5},{7,6},{9,8},{10,9},{11,10},{12... | collective-permute-start | bytes 1179656 | tf_op jit(solution)/shard_map/ppermute | solution.py:17
  182.0 21.0 %collective-permute-start.7 = (f32[24,4,8,128]{3,2,1,0:T(8,128)S(1)}, f32[24,4,8,128]{3,2,1,0:T(8,128)S(1)}, u32[]{:S(2)}, u32[]{:S(2)}) collective-permute-start(f32[24,4,8,128]{3,2,1,0:T(8,128)S(1)} %get-tuple-element.13), channel_id=1, source_target_pairs={{0,1},{1,2},{2,3},{3,4},{4,5},{5,6},{6,7},{8,9},{9,10},{10,11},{11... | collective-permute-start | bytes 1179656 | tf_op jit(solution)/shard_map/ppermute | solution.py:16
  245.6 23.6 %copy-start.3 = (f32[24,16,8,128]{3,2,1,0:T(8,128)S(1)}, f32[24,16,8,128]{3,2,1,0:T(8,128)}, u32[]{:S(2)}) copy-start(f32[24,16,8,128]{3,2,1,0:T(8,128)} %fusion.138) | copy-start | bytes 4718596
  246.9 13.7 %collective-permute-start.8 = (f32[24,4,8,128]{3,2,1,0:T(8,128)S(1)}, f32[24,4,8,128]{3,2,1,0:T(8,128)S(1)}, u32[]{:S(2)}, u32[]{:S(2)}) collective-permute-start(f32[24,4,8,128]{3,2,1,0:T(8,128)S(1)} %get-tuple-element.10), channel_id=1, source_target_pairs={{1,0},{2,1},{3,2},{4,3},{5,4},{6,5},{7,6},{9,8},{10,9},{11,10},{12... | collective-permute-start | bytes 1179656 | tf_op jit(solution)/shard_map/ppermute | solution.py:17
  248.2 21.0 %collective-permute-start.9 = (f32[24,4,8,128]{3,2,1,0:T(8,128)S(1)}, f32[24,4,8,128]{3,2,1,0:T(8,128)S(1)}, u32[]{:S(2)}, u32[]{:S(2)}) collective-permute-start(f32[24,4,8,128]{3,2,1,0:T(8,128)S(1)} %get-tuple-element.11), channel_id=1, source_target_pairs={{0,1},{1,2},{2,3},{3,4},{4,5},{5,6},{6,7},{8,9},{9,10},{10,11},{11... | collective-permute-start | bytes 1179656 | tf_op jit(solution)/shard_map/ppermute | solution.py:16
  315.0 22.3 %copy-start.1 = (f32[24,16,8,128]{3,2,1,0:T(8,128)}, f32[24,16,8,128]{3,2,1,0:T(8,128)S(1)}, u32[]{:S(2)}) copy-start(f32[24,16,8,128]{3,2,1,0:T(8,128)S(1)} %fusion.107) | copy-start | bytes 4718596
  315.1 13.7 %collective-permute-start.10 = (f32[24,4,8,128]{3,2,1,0:T(8,128)S(1)}, f32[24,4,8,128]{3,2,1,0:T(8,128)S(1)}, u32[]{:S(2)}, u32[]{:S(2)}) collective-permute-start(f32[24,4,8,128]{3,2,1,0:T(8,128)S(1)} %get-tuple-element.8), channel_id=1, source_target_pairs={{1,0},{2,1},{3,2},{4,3},{5,4},{6,5},{7,6},{9,8},{10,9},{11,10},{12... | collective-permute-start | bytes 1179656 | tf_op jit(solution)/shard_map/ppermute | solution.py:17
  316.4 21.0 %collective-permute-start.11 = (f32[24,4,8,128]{3,2,1,0:T(8,128)S(1)}, f32[24,4,8,128]{3,2,1,0:T(8,128)S(1)}, u32[]{:S(2)}, u32[]{:S(2)}) collective-permute-start(f32[24,4,8,128]{3,2,1,0:T(8,128)S(1)} %get-tuple-element.9), channel_id=1, source_target_pairs={{0,1},{1,2},{2,3},{3,4},{4,5},{5,6},{6,7},{8,9},{9,10},{10,11},{11... | collective-permute-start | bytes 1179656 | tf_op jit(solution)/shard_map/ppermute | solution.py:16
  383.5 13.9 %collective-permute-start.12 = (f32[24,4,8,128]{3,2,1,0:T(8,128)}, f32[24,4,8,128]{3,2,1,0:T(8,128)S(1)}, u32[]{:S(2)}, u32[]{:S(2)}) collective-permute-start(f32[24,4,8,128]{3,2,1,0:T(8,128)} %get-tuple-element.6), channel_id=1, source_target_pairs={{1,0},{2,1},{3,2},{4,3},{5,4},{6,5},{7,6},{9,8},{10,9},{11,10},{12... | collective-permute-start | bytes 1179656 | tf_op jit(solution)/shard_map/ppermute | solution.py:17
  384.8 21.3 %collective-permute-start.13 = (f32[24,4,8,128]{3,2,1,0:T(8,128)}, f32[24,4,8,128]{3,2,1,0:T(8,128)S(1)}, u32[]{:S(2)}, u32[]{:S(2)}) collective-permute-start(f32[24,4,8,128]{3,2,1,0:T(8,128)} %get-tuple-element.7), channel_id=1, source_target_pairs={{0,1},{1,2},{2,3},{3,4},{4,5},{5,6},{6,7},{8,9},{9,10},{10,11},{11... | collective-permute-start | bytes 1179656 | tf_op jit(solution)/shard_map/ppermute | solution.py:16
  448.5 24.3 %copy-start.6 = (f32[24,16,8,128]{3,2,1,0:T(8,128)S(1)}, f32[24,16,8,128]{3,2,1,0:T(8,128)}, u32[]{:S(2)}) copy-start(f32[24,16,8,128]{3,2,1,0:T(8,128)} %fusion.45) | copy-start | bytes 4718596
  449.8 13.7 %collective-permute-start.14 = (f32[24,4,8,128]{3,2,1,0:T(8,128)S(1)}, f32[24,4,8,128]{3,2,1,0:T(8,128)S(1)}, u32[]{:S(2)}, u32[]{:S(2)}) collective-permute-start(f32[24,4,8,128]{3,2,1,0:T(8,128)S(1)} %get-tuple-element.5), channel_id=1, source_target_pairs={{1,0},{2,1},{3,2},{4,3},{5,4},{6,5},{7,6},{9,8},{10,9},{11,10},{12... | collective-permute-start | bytes 1179656 | tf_op jit(solution)/shard_map/ppermute | solution.py:17
  451.1 21.0 %collective-permute-start.15 = (f32[24,4,8,128]{3,2,1,0:T(8,128)S(1)}, f32[24,4,8,128]{3,2,1,0:T(8,128)S(1)}, u32[]{:S(2)}, u32[]{:S(2)}) collective-permute-start(f32[24,4,8,128]{3,2,1,0:T(8,128)S(1)} %get-tuple-element.4), channel_id=1, source_target_pairs={{0,1},{1,2},{2,3},{3,4},{4,5},{5,6},{6,7},{8,9},{9,10},{10,11},{11... | collective-permute-start | bytes 1179656 | tf_op jit(solution)/shard_map/ppermute | solution.py:16
  (7 other events, 32.4 us)
Sparse Core Ops, SparseCore 0:
  391.6 30.1 all-gather.1
where the time goes:
time: 566 us; the launch traced here: 565 us
  other arithmetic  319 us (56%)
  waiting for transfers between devices  110 us (19%)
  starting transfers between devices  51.6 us (9%)
  blocking collectives  41.8 us (7%)
  between operations  29.4 us (5%)
  local copies, waits for them, and re-layouts  9.52 us (2%)
    add x7, other arithmetic, local(): 2.0 * current - earlier + courant * laplace(side_frame(padded))  236 us
    ppermute x8, waiting for transfers between devices, extended(): before = lax.ppermute(last, axis, up)  60.2 us
    ppermute x8, waiting for transfers between devices, extended(): after = lax.ppermute(leading, axis, down)  50 us
    concatenate x8, other arithmetic, extended(): x = jnp.concatenate([before, x, after], axis=dim)  42.1 us
    ppermute x8, starting transfers between devices, extended(): before = lax.ppermute(last, axis, up)  40.9 us
    convert_element_type x1, other arithmetic, local(): response_low = current.astype(jnp.bfloat16)  40.4 us
    psum x1, blocking collectives, local(): projection = lax.psum(product, 'store')  35.5 us
  transfers between devices with their start and end apart: 17, of which 14 were waited for; matrix products, arithmetic and copies ran while one was open for 17% of the time, Pallas kernels for 0%

commit v1 on v0

v1 whole, which is shorter than its diff:
```python
import functools

import jax
import jax.numpy as jnp
import numpy as np
from jax import lax
from jax.experimental import pallas as pl
from jax.experimental.pallas import tpu as pltpu
from jax.sharding import PartitionSpec as P

taps = (-205.0 / 72.0, 8.0 / 5.0, -1.0 / 5.0, 8.0 / 315.0, -1.0 / 560.0)
SPAN = 24


def tables(cells_y, cells_z):
    ratio = [0.0] + [t / taps[1] for t in taps[1:]]
    left = np.zeros((SPAN, cells_y, SPAN + 8, cells_y), np.float32)
    for i in range(SPAN):
        for d in range(1, 5):
            for y in range(cells_y):
                left[i, y, i + 4 + d, y] = ratio[d]
                left[i, y, i + 4 - d, y] = ratio[d]
                if y + d < cells_y:
                    left[i, y, i + 4, y + d] = ratio[d]
                if y - d >= 0:
                    left[i, y, i + 4, y - d] = ratio[d]
    right = np.zeros((cells_z, cells_z), np.float32)
    for z in range(cells_z):
        for d in range(1, 5):
            if z + d < cells_z:
                right[z, z + d] = ratio[d]
            if z - d >= 0:
                right[z, z - d] = ratio[d]
    left = left.reshape(SPAN * cells_y, (SPAN + 8) * cells_y)
    return left, np.concatenate([right, right], axis=0)


def spans(rows):
    out = []
    while rows > 0:
        out.append(min(SPAN, rows))
        rows -= out[-1]
    return out


def march(steps, rows, halo, wide, par_ref, *refs):
    pieces = refs[0:6]
    extras = refs[6:12]
    left_ref, right_ref, own_ref, send_ref = refs[12:16]
    pert, snap, scale, gain, fields, split = refs[16:22]
    total = 2 * rows + 2 * halo
    cy = 8
    par = par_ref[0]
    even = (halo, halo + rows, halo + 2 * rows, 0, halo - rows, halo + 3 * rows)
    odd = (halo + rows, halo, halo - rows, halo + 3 * rows, halo + 2 * rows, 0)
    counts = (rows, rows, rows, halo - rows, rows, halo - rows)
    starts = [e + par * (o - e) for e, o in zip(even, odd)]

    def put(piece, value):
        at = pl.multiple_of(starts[piece] * cy, 32)
        return pl.ds(at, counts[piece] * cy), value

    @pl.when(pl.program_id(0) == 0)
    def _():
        for j in range(6):
            where = pl.ds(pl.multiple_of(starts[j] * cy, 32), counts[j] * cy)
            flat = (counts[j] * cy, 128)
            for t in range(steps):
                snap[t, where, :] = extras[j][t].reshape(flat).astype(jnp.float32)
            c = extras[j][steps].astype(jnp.float32) + extras[j][steps + 1].astype(jnp.float32)
            c = c.reshape(flat)
            scale[where, :] = 2.0 + (3.0 * taps[0]) * c
            gain[where, :] = taps[1] * c

    for j in range(6):
        where = pl.ds(pl.multiple_of(starts[j] * cy, 32), counts[j] * cy)
        pert[where, :] = pieces[j][0].reshape(counts[j] * cy, 128).astype(jnp.float32)

    def keep(slot, where, value):
        high = value.astype(jnp.bfloat16)
        low = (value - high.astype(jnp.float32)).astype(jnp.bfloat16)
        split[slot, where, 0:128] = high
        split[slot, where, 128:256] = low

    at = 0
    for m in spans(total):
        where = pl.ds(at * cy, m * cy)
        first = pert[where, :] * snap[0, where, :]
        fields[0, where, :] = first
        keep(0, where, first)
        at += m

    def advanced(n, row, m):
        now, before = (n + 1) % 2, n % 2
        where = pl.ds(row * cy, m * cy) if isinstance(row, int) else pl.ds(pl.multiple_of(row * cy, 32), m * cy)
        low = (row - 4) * cy
        around = pl.ds(low, (m + 8) * cy) if isinstance(row, int) else pl.ds(pl.multiple_of(low, 32), (m + 8) * cy)
        both = jnp.dot(
            left_ref[0 : m * cy, 0 : (m + 8) * cy],
            split[now, around, :],
            preferred_element_type=jnp.float32,
        )
        along = jnp.dot(split[now, where, :], right_ref[...], preferred_element_type=jnp.float32)
        total_taps = both[:, 0:128] + both[:, 128:256] + along
        value = scale[where, :] * fields[now, where, :] + gain[where, :] * total_taps
        value = value + pert[where, :] * snap[n, where, :]
        if n > 1:
            value = value - fields[before, where, :]
        return where, value

    for n in range(1, steps - 1):
        at = 4 * n
        for m in spans(total - 8 * n):
            where, value = advanced(n, at, m)
            fields[n % 2, where, :] = value
            keep(n % 2, where, value)
            at += m
    _, value = advanced(steps - 1, starts[0], rows)
    own_ref[0] = value.reshape(rows, cy, 128)
    _, value = advanced(steps - 1, starts[1], rows)
    send_ref[0] = value.reshape(rows, cy, 128).astype(jnp.bfloat16)


def propagate(par, pieces, extras, steps, rows, halo):
    half, _, cy, cz = pieces[0].shape
    left, right = tables(cy, cz)
    left, right = jnp.asarray(left, jnp.bfloat16), jnp.asarray(right, jnp.bfloat16)
    counts = (rows, rows, rows, halo - rows, rows, halo - rows)
    total = 2 * rows + 2 * halo
    fixed = lambda *shape: pl.BlockSpec(shape, lambda k, p: (0,) * len(shape), pipeline_mode=pl.Buffered(1))
    block = lambda count: pl.BlockSpec((1, count, cy, cz), lambda k, p: (k, 0, 0, 0))
    grid_spec = pltpu.PrefetchScalarGridSpec(
        num_scalar_prefetch=1,
        grid=(half,),
        in_specs=[block(c) for c in counts]
        + [fixed(steps + 2, c, cy, cz) for c in counts]
        + [fixed(*left.shape), fixed(*right.shape)],
        out_specs=[block(rows), block(rows)],
        scratch_shapes=[
            pltpu.VMEM((total * cy, cz), jnp.float32),
            pltpu.VMEM((steps, total * cy, cz), jnp.float32),
            pltpu.VMEM((total * cy, cz), jnp.float32),
            pltpu.VMEM((total * cy, cz), jnp.float32),
            pltpu.VMEM((2, total * cy, cz), jnp.float32),
            pltpu.VMEM((2, total * cy, 2 * cz), jnp.bfloat16),
        ],
    )
    return pl.pallas_call(
        functools.partial(march, steps, rows, halo, half),
        grid_spec=grid_spec,
        out_shape=[
            jax.ShapeDtypeStruct((half, rows, cy, cz), jnp.float32),
            jax.ShapeDtypeStruct((half, rows, cy, cz), jnp.bfloat16),
        ],
        compiler_params=pltpu.CompilerParams(vmem_limit_bytes=40 << 20),
        name="march",
    )(par[None], *pieces, *extras, left, right)


def local(probe_field, bounds, courant, snapshots, snap_times, basis_panels):
    probes_here, rows, cy, cz = probe_field.shape
    steps = snap_times.shape[0]
    half = probes_here // 2
    halo = 4 * (steps - 1)
    far = halo - rows
    devices = lax.axis_size("store")
    place = lax.axis_index("store")
    par = (place % 2).astype(jnp.int32)
    swap = [(i, i ^ 1) for i in range(devices)]
    perm_a = [(i, i - 2) for i in range(2, devices, 2)] + [(i, i + 2) for i in range(1, devices - 2, 2)]
    perm_b = [(i, i + 2) for i in range(0, devices - 2, 2)] + [(i, i - 2) for i in range(3, devices, 2)]
    hop = lambda x, pairs: lax.ppermute(x, "store", pairs)
    cut = lambda x, start: lax.dynamic_slice_in_dim(x, start, far, axis=1)
    near = rows - far

    def around(own, other):
        partner = hop(other, swap)
        return (
            own,
            partner,
            hop(own, perm_a),
            hop(cut(own, near * (1 - par)), perm_b),
            hop(partner, perm_b),
            hop(cut(partner, near * par), perm_a),
        )

    row = place * rows + jnp.arange(rows, dtype=jnp.int32)
    inside = (row[None, :] >= bounds[:, 0:1]) & (row[None, :] < bounds[:, 1:2])
    perturb = jnp.where(inside[:, :, None, None], probe_field, jnp.zeros_like(probe_field))
    mine = lax.dynamic_slice_in_dim(perturb, half * par, half, axis=0)
    theirs = lax.dynamic_slice_in_dim(perturb, half * (1 - par), half, axis=0)

    all_snaps = lax.all_gather(snapshots, "probe", axis=2, tiled=True)
    all_snaps = jnp.take(all_snaps, snap_times, axis=0)
    high = lax.reduce_precision(courant, 8, 7)
    extra = jnp.concatenate(
        [all_snaps, high.astype(jnp.bfloat16)[None], (courant - high).astype(jnp.bfloat16)[None]], axis=0
    )
    extras = around(extra, extra)
    pieces = around(mine, theirs)
    own, send = propagate(par, pieces, extras, steps, rows, halo)
    back = hop(send, swap).astype(jnp.float32)
    first = par == 0
    response = jnp.concatenate([jnp.where(first, own, back), jnp.where(first, back, own)], axis=0)
    low = response.astype(jnp.bfloat16).reshape(probes_here, -1)

    member = lax.axis_index("probe")
    members = lax.axis_size("probe")
    panels = [basis_panels]
    span = 1
    while span < members:
        pairs = [(i, i ^ span) for i in range(members)]
        panels = panels + [lax.ppermute(x, "probe", pairs) for x in panels]
        span *= 2
    parts = [
        lax.dot_general(
            x.reshape(x.shape[0], -1), low, (((1,), (1,)), ((), ())), preferred_element_type=jnp.float32
        )
        for x in panels
    ]
    parts = jnp.stack(parts)
    order = jnp.arange(members) ^ member
    product = jnp.take(parts, order, axis=0).reshape(-1, probes_here)
    span = 1
    while span < devices:
        product = product + hop(product, [(i, i ^ span) for i in range(devices)])
        span *= 2
    return response, product


def solution(mesh):
    placed = (
        P("probe", "store", None, None),
        P("probe", None),
        P("store", None, None),
        P(None, "store", "probe", None),
        P(),
        P("probe", "store", None, None),
    )
    return jax.shard_map(
        local,
        mesh=mesh,
        in_specs=placed,
        out_specs=(P("probe", "store", None, None), P(None, "probe")),
        check_vma=False,
    )
```

time: 566 us -> 127 us (0.22)
  other arithmetic: 319 us -> 4.14 us
  waiting for transfers between devices: 110 us -> 50.6 us
  blocking collectives: 41.8 us -> 5.79 us
  between operations: 29.4 us -> 0.99 us
  Pallas kernels: 0 us -> 22.1 us
  starting transfers between devices: 51.6 us -> 31.6 us
    add x8 -> x4, other arithmetic: 236 us -> 0.62 us  [the longest x3 0.61 us: local(): product = product + hop(product, [(i, i ^ span) for i in range(devices)])]
    ppermute x16 -> x17, waiting for transfers between devices: 110 us -> 50.6 us  [the longest x14 30.8 us: local(): hop = lambda x, pairs: lax.ppermute(x, 'store', pairs)]
    concatenate x8 -> x1, other arithmetic: 42.1 us -> 0.04 us  [local(): jnp.concatenate([all_snaps, high.astype(jnp.bfloat16)[None], (courant - h...]
    convert_element_type x2 -> x1, other arithmetic: 40.5 us -> 1.44 us  [local(): low = response.astype(jnp.bfloat16).reshape(probes_here, -1)]
    psum x1 -> x0, blocking collectives: 35.5 us -> none  [local(): projection = lax.psum(product, 'store')]
    pallas_call x0 -> x1, Pallas kernels: none -> 22.1 us  [propagate(): pl.pallas_call(functools.partial(march, steps, rows, halo, half), grid_sp...]
    ppermute x16 -> x17, starting transfers between devices: 51.5 us -> 31.6 us  [the longest x14 29.5 us: local(): hop = lambda x, pairs: lax.ppermute(x, 'store', pairs)]
  transfers between devices with their start and end apart: 17 -> 17, of which waited for: 14 -> 10; matrix products, arithmetic and copies ran while one was open for 17% -> 7% of each run, Pallas kernels for 0% -> 18%
where the time goes in v1:
time: 127 us; the launch traced here: 126 us
  waiting for transfers between devices  50.6 us (40%)
  starting transfers between devices  31.6 us (25%)
  Pallas kernels  22.1 us (17%)
  local copies, waits for them, and re-layouts  6.34 us (5%)
  blocking collectives  5.79 us (5%)
  matrix products  4.67 us (4%)
  other arithmetic  4.14 us (3%)
    ppermute x14, waiting for transfers between devices, local(): hop = lambda x, pairs: lax.ppermute(x, 'store', pairs)  30.8 us
    ppermute x14, starting transfers between devices, local(): hop = lambda x, pairs: lax.ppermute(x, 'store', pairs)  29.5 us
    pallas_call x1, Pallas kernels, propagate(): pl.pallas_call(functools.partial(march, steps, rows, halo, half), grid_sp...  22.1 us
    ppermute x3, waiting for transfers between devices, local(): panels = panels + [lax.ppermute(x, 'probe', pairs) for x in panels]  19.7 us
    all_gather x1, blocking collectives, local(): all_snaps = lax.all_gather(snapshots, 'probe', axis=2, tiled=True)  5.79 us
    dot_general x4, matrix products, local(): lax.dot_general(x.reshape(x.shape[0], -1), low, (((1,), (1,)), ((), ())),...  4.67 us
  transfers between devices with their start and end apart: 17, of which 10 were waited for; matrix products, arithmetic and copies ran while one was open for 7% of the time, Pallas kernels for 18%

profile of v1, /device:TPU:0, one launch (start us, length us, event | category | flops | bytes accessed | tf_op | source)
XLA Modules:
  0.0 126.2 jit_solution(1469471002920256564)
XLA Ops:
  1.5 1.6 %broadcast_select_fusion = bf16[24,16,8,128]{3,2,1,0:T(8,128)(2,1)S(1)} fusion(bf16[24,16,8,128]{3,2,1,0:T(8,128)(2,1)} %param.8, pred[24,16]{1,0:T(8,128)(4,1)S(1)} %compare_and_fusion), kind=kLoop, calls=%fused_computation.9 | loop fusion | flops 393216 | bytes 1573248 | tf_op jit(solution)/shard_map/jit(_where)/select_n | solution.py:189
  4.0 2.9 %collective-permute-start = (bf16[12,16,8,128]{3,2,1,0:T(8,128)(2,1)}, bf16[12,16,8,128]{3,2,1,0:T(8,128)(2,1)S(1)}, u32[]{:S(2)}, u32[]{:S(2)}) collective-permute-start(bf16[12,16,8,128]{3,2,1,0:T(8,128)(2,1)} %get-tuple-element.10), channel_id=1, source_target_pairs={{0,1},{1,0},{2,3},{3,2},{4,5},{5,4},{6,7},{7,6},{8,9},{9,8},{10,11... | collective-permute-start | bytes 1179656 | tf_op jit(solution)/shard_map/ppermute | solution.py:172
  7.0 5.8 %all_gather.3 = bf16[8,16,8,128]{3,1,0,2:T(8,128)(2,1)S(1)} all-gather(bf16[8,16,2,128]{3,1,0,2:T(8,128)(2,1)S(1)} %copy.34), channel_id=1, replica_groups=mesh['probe'=4,'store'=8] {'probe'}, dimensions={2}, use_global_device_ids=true | all-gather | bytes 327680 | tf_op jit(solution)/shard_map/all_gather | solution.py:193
  13.8 3.5 %collective-permute-start.7 = (bf16[10,12,8,128]{3,2,1,0:T(8,128)(2,1)S(1)}, bf16[10,12,8,128]{3,2,1,0:T(8,128)(2,1)S(1)}, u32[]{:S(2)}, u32[]{:S(2)}) collective-permute-start(bf16[10,12,8,128]{3,2,1,0:T(8,128)(2,1)S(1)} %constant_dynamic-slice_fusion.1), channel_id=1, source_target_pairs={{0,2},{2,4},{4,6},{3,1},{5,3},{7,5},{8,10},{10,12},{12,14},{11,9},... | collective-permute-start | bytes 737288 | tf_op jit(solution)/shard_map/ppermute | solution.py:172
  18.1 3.5 %collective-permute-start.2 = (bf16[12,12,8,128]{3,2,1,0:T(8,128)(2,1)}, bf16[12,12,8,128]{3,2,1,0:T(8,128)(2,1)S(1)}, u32[]{:S(2)}, u32[]{:S(2)}) collective-permute-start(bf16[12,12,8,128]{3,2,1,0:T(8,128)(2,1)} %constant_dynamic-slice_fusion.3), channel_id=1, source_target_pairs={{0,2},{2,4},{4,6},{3,1},{5,3},{7,5},{8,10},{10,12},{12,14},{11,9},... | collective-permute-start | bytes 884744 | tf_op jit(solution)/shard_map/ppermute | solution.py:172
  24.8 1.4 %copy.37 = bf16[24,16,8,128]{3,0,2,1:T(8,128)(2,1)} copy(bf16[24,16,8,128]{3,2,1,0:T(8,128)(2,1)S(1)} %copy-done.2) | data formatting | bytes 1572864 | tf_op args[5]
  26.2 3.2 %collective-permute-done.2.refs_3_ = bf16[12,12,8,128]{3,2,1,0:T(8,128)(2,1)S(1)} collective-permute-done((bf16[12,12,8,128]{3,2,1,0:T(8,128)(2,1)}, bf16[12,12,8,128]{3,2,1,0:T(8,128)(2,1)S(1)}, u32[]{:S(2)}, u32[]{:S(2)}) %collective-permute-start.2) | collective-permute-done | bytes 294944 | tf_op jit(solution)/shard_map/ppermute | solution.py:172
  29.4 4.3 %collective-permute-start.3 = (bf16[12,16,8,128]{3,2,1,0:T(8,128)(2,1)S(1)}, bf16[12,16,8,128]{3,2,1,0:T(8,128)(2,1)S(1)}, u32[]{:S(2)}, u32[]{:S(2)}) collective-permute-start(bf16[12,16,8,128]{3,2,1,0:T(8,128)(2,1)S(1)} %collective-permute-done.refs_1_), channel_id=1, source_target_pairs={{0,2},{2,4},{4,6},{3,1},{5,3},{7,5},{8,10},{10,12},{12,14},{11,9},... | collective-permute-start | bytes 1179656 | tf_op jit(solution)/shard_map/ppermute | solution.py:172
  33.8 3.5 %collective-permute-start.8 = (bf16[10,16,8,128]{3,2,1,0:T(8,128)(2,1)S(1)}, bf16[10,16,8,128]{3,2,1,0:T(8,128)(2,1)S(1)}, u32[]{:S(2)}, u32[]{:S(2)}) collective-permute-start(bf16[10,16,8,128]{3,2,1,0:T(8,128)(2,1)S(1)} %collective-permute-done.5.refs_7_), channel_id=1, source_target_pairs={{0,2},{2,4},{4,6},{3,1},{5,3},{7,5},{8,10},{10,12},{12,14},{11,9},... | collective-permute-start | bytes 983048 | tf_op jit(solution)/shard_map/ppermute | solution.py:172
  38.6 2.8 %collective-permute-done.1.refs_2_ = bf16[12,16,8,128]{3,2,1,0:T(8,128)(2,1)S(1)} collective-permute-done((bf16[12,16,8,128]{3,2,1,0:T(8,128)(2,1)S(1)}, bf16[12,16,8,128]{3,2,1,0:T(8,128)(2,1)S(1)}, u32[]{:S(2)}, u32[]{:S(2)}) %collective-permute-start.1) | collective-permute-done | bytes 393248 | tf_op jit(solution)/shard_map/ppermute | solution.py:172
  42.6 10.6 %collective-permute-done.9.refs_11_ = bf16[10,12,8,128]{3,2,1,0:T(8,128)(2,1)S(1)} collective-permute-done((bf16[10,12,8,128]{3,2,1,0:T(8,128)(2,1)S(1)}, bf16[10,12,8,128]{3,2,1,0:T(8,128)(2,1)S(1)}, u32[]{:S(2)}, u32[]{:S(2)}) %collective-permute-start.9) | collective-permute-done | bytes 245792 | tf_op jit(solution)/shard_map/ppermute | solution.py:172
  54.2 22.1 %march.1 = (f32[12,16,8,128]{3,2,1,0:T(8,128)S(1)}, bf16[12,16,8,128]{3,2,1,0:T(8,128)(2,1)}) custom-call(s32[1]{0:T(128)} %bitcast.par_ref, bf16[12,16,8,128]{3,2,1,0:T(8,128)(2,1)S(1)} %get-tuple-element.11.refs_0_, bf16[12,16,8,128]{3,2,1,0:T(8,128)(2,1)S(1)} %collective-permute-done.refs_1_, bf16[12,16,8,128]{3,2,1,0:T(8,128)(2,1)S(1)} %collective-permute-done.1.refs_2_, ...), custom_call_target="tpu_custom_call" | custom-call | tf_op jit(solution)/shard_map/march/pallas_call | solution.py:148
  76.8 1.5 %collective-permute-start.12 = (bf16[24,16,8,128]{3,0,2,1:T(8,128)(2,1)}, bf16[24,16,8,128]{3,0,2,1:T(8,128)(2,1)S(1)}, u32[]{:S(2)}, u32[]{:S(2)}) collective-permute-start(bf16[24,16,8,128]{3,0,2,1:T(8,128)(2,1)} %copy.37), channel_id=1, source_target_pairs={{0,16},{8,24},{16,0},{24,8},{1,17},{9,25},{17,1},{25,9},{2,18},{10... | collective-permute-start | bytes 2359304 | tf_op jit(solution)/shard_map/ppermute | solution.py:213
  79.1 7.5 %collective-permute-done.10 = bf16[12,16,8,128]{3,2,1,0:T(8,128)(2,1)S(1)} collective-permute-done((bf16[12,16,8,128]{3,2,1,0:T(8,128)(2,1)}, bf16[12,16,8,128]{3,2,1,0:T(8,128)(2,1)S(1)}, u32[]{:S(2)}, u32[]{:S(2)}) %collective-permute-start.10) | collective-permute-done | bytes 393248 | tf_op jit(solution)/shard_map/ppermute | solution.py:172
  86.8 1.4 %fusion.9 = (bf16[24,16,8,128]{3,2,1,0:T(8,128)(2,1)S(1)}, f32[24,16,8,128]{3,2,1,0:T(8,128)}) fusion(f32[12,16,8,128]{3,2,1,0:T(8,128)S(1)} %get-tuple-element.9, f32[12,16,8,128]{3,2,1,0:T(8,128)S(1)} %get-tuple-element.8), kind=kLoop, calls=%fused_computation.42 | loop fusion | flops 786432 | bytes 3932160 | tf_op jit(solution)/shard_map/convert_element_type | solution.py:205
  88.2 2.0 %convolution_bitcast_fusion.2 = f32[1,24,24]{1,2,0:T(8,128)S(1)} fusion(bf16[24,16,8,128]{3,0,2,1:T(8,128)(2,1)} %collective-permute-done.11, bf16[24,16,8,128]{3,2,1,0:T(8,128)(2,1)S(1)} %get-tuple-element.6), kind=kOutput, calls=%fused_computation.5 | convolution fusion | flops 18874368 | bytes 1575168 | tf_op jit(solution)/shard_map/dot_general | solution.py:216
  90.2 7.3 %collective-permute-done.12 = bf16[24,16,8,128]{3,0,2,1:T(8,128)(2,1)S(1)} collective-permute-done((bf16[24,16,8,128]{3,0,2,1:T(8,128)(2,1)}, bf16[24,16,8,128]{3,0,2,1:T(8,128)(2,1)S(1)}, u32[]{:S(2)}, u32[]{:S(2)}) %collective-permute-start.12) | collective-permute-done | bytes 786464 | tf_op jit(solution)/shard_map/ppermute | solution.py:213
  99.5 12.5 %collective-permute-done.13 = bf16[24,16,8,128]{3,0,2,1:T(8,128)(2,1)S(1)} collective-permute-done((bf16[24,16,8,128]{3,0,2,1:T(8,128)(2,1)}, bf16[24,16,8,128]{3,0,2,1:T(8,128)(2,1)S(1)}, u32[]{:S(2)}, u32[]{:S(2)}) %collective-permute-start.13) | collective-permute-done | bytes 786464 | tf_op jit(solution)/shard_map/ppermute | solution.py:213
  113.4 1.8 %collective-permute-start.14 = (f32[96,24]{0,1:T(8,128)S(1)}, f32[96,24]{0,1:T(8,128)S(1)}, u32[]{:S(2)}, u32[]{:S(2)}) collective-permute-start(f32[96,24]{0,1:T(8,128)S(1)} %broadcast_select_fusion.2), channel_id=1, source_target_pairs={{0,1},{1,0},{2,3},{3,2},{4,5},{5,4},{6,7},{7,6},{8,9},{9,8},{10,11... | collective-permute-start | bytes 27656 | tf_op jit(solution)/shard_map/ppermute | solution.py:172
  115.2 2.0 %collective-permute-done.14 = f32[96,24]{0,1:T(8,128)S(1)} collective-permute-done((f32[96,24]{0,1:T(8,128)S(1)}, f32[96,24]{0,1:T(8,128)S(1)}, u32[]{:S(2)}, u32[]{:S(2)}) %collective-permute-start.14) | collective-permute-done | bytes 9248 | tf_op jit(solution)/shard_map/ppermute | solution.py:172
  117.1 2.2 %collective-permute-start.15 = (f32[96,24]{0,1:T(8,128)S(1)}, f32[96,24]{0,1:T(8,128)S(1)}, u32[]{:S(2)}, u32[]{:S(2)}) collective-permute-start(f32[96,24]{0,1:T(8,128)S(1)} %fusion.13), channel_id=1, source_target_pairs={{0,2},{1,3},{2,0},{3,1},{4,6},{5,7},{6,4},{7,5},{8,10},{9,11},{10,... | collective-permute-start | bytes 27656 | tf_op jit(solution)/shard_map/ppermute | solution.py:172
  119.3 1.7 %collective-permute-done.15 = f32[96,24]{0,1:T(8,128)S(1)} collective-permute-done((f32[96,24]{0,1:T(8,128)S(1)}, f32[96,24]{0,1:T(8,128)S(1)}, u32[]{:S(2)}, u32[]{:S(2)}) %collective-permute-start.15) | collective-permute-done | bytes 9248 | tf_op jit(solution)/shard_map/ppermute | solution.py:172
  121.0 2.1 %collective-permute-start.16 = (f32[96,24]{0,1:T(8,128)S(1)}, f32[96,24]{0,1:T(8,128)S(1)}, u32[]{:S(2)}, u32[]{:S(2)}) collective-permute-start(f32[96,24]{0,1:T(8,128)S(1)} %add.71), channel_id=1, source_target_pairs={{0,4},{1,5},{2,6},{3,7},{4,0},{5,1},{6,2},{7,3},{8,12},{9,13},{10,... | collective-permute-start | bytes 27656 | tf_op jit(solution)/shard_map/ppermute | solution.py:172
  123.1 2.5 %collective-permute-done.16 = f32[96,24]{0,1:T(8,128)S(1)} collective-permute-done((f32[96,24]{0,1:T(8,128)S(1)}, f32[96,24]{0,1:T(8,128)S(1)}, u32[]{:S(2)}, u32[]{:S(2)}) %collective-permute-start.16) | collective-permute-done | bytes 9248 | tf_op jit(solution)/shard_map/ppermute | solution.py:172
  (64 shorter events, 15.6 us)
Async XLA Ops:
  1.5 5.4 %copy-start.6 = (s32[8]{0:T(128)S(1)}, s32[8]{0:T(128)}, u32[]{:S(2)}) copy-start(s32[8]{0:T(128)} %param.12) | copy-start | bytes 100
  1.5 5.4 %copy-start.4 = (f32[16,8,128]{2,1,0:T(8,128)S(1)}, f32[16,8,128]{2,1,0:T(8,128)}, u32[]{:S(2)}) copy-start(f32[16,8,128]{2,1,0:T(8,128)} %param.10) | copy-start | bytes 196612
  1.5 5.5 %copy-start.5 = (bf16[8,16,2,128]{3,2,1,0:T(2,128)(2,1)S(1)}, bf16[8,16,2,128]{3,2,1,0:T(2,128)(2,1)}, u32[]{:S(2)}) copy-start(bf16[8,16,2,128]{3,2,1,0:T(2,128)(2,1)} %param.11) | copy-start | bytes 196612
  4.0 25.4 %collective-permute-start = (bf16[12,16,8,128]{3,2,1,0:T(8,128)(2,1)}, bf16[12,16,8,128]{3,2,1,0:T(8,128)(2,1)S(1)}, u32[]{:S(2)}, u32[]{:S(2)}) collective-permute-start(bf16[12,16,8,128]{3,2,1,0:T(8,128)(2,1)} %get-tuple-element.10), channel_id=1, source_target_pairs={{0,1},{1,0},{2,3},{3,2},{4,5},{5,4},{6,7},{7,6},{8,9},{9,8},{10,11... | collective-permute-start | bytes 1179656 | tf_op jit(solution)/shard_map/ppermute | solution.py:172
  12.8 12.0 %copy-start.2 = (bf16[24,16,8,128]{3,2,1,0:T(8,128)(2,1)S(1)}, bf16[24,16,8,128]{3,2,1,0:T(8,128)(2,1)}, u32[]{:S(2)}) copy-start(bf16[24,16,8,128]{3,2,1,0:T(8,128)(2,1)} %param.13) | copy-start | bytes 2359300
  13.8 9.8 %collective-permute-start.7 = (bf16[10,12,8,128]{3,2,1,0:T(8,128)(2,1)S(1)}, bf16[10,12,8,128]{3,2,1,0:T(8,128)(2,1)S(1)}, u32[]{:S(2)}, u32[]{:S(2)}) collective-permute-start(bf16[10,12,8,128]{3,2,1,0:T(8,128)(2,1)S(1)} %constant_dynamic-slice_fusion.1), channel_id=1, source_target_pairs={{0,2},{2,4},{4,6},{3,1},{5,3},{7,5},{8,10},{10,12},{12,14},{11,9},... | collective-permute-start | bytes 737288 | tf_op jit(solution)/shard_map/ppermute | solution.py:172
  17.3 36.0 %copy-start.1 = (bf16[256,128]{1,0:T(8,128)(2,1)S(1)}, bf16[256,128]{1,0:T(8,128)(2,1)}, u32[]{:S(2)}) copy-start(bf16[256,128]{1,0:T(8,128)(2,1)} %constant.86.clone.refs_13_) | copy-start | bytes 196612
  18.1 11.3 %collective-permute-start.2 = (bf16[12,12,8,128]{3,2,1,0:T(8,128)(2,1)}, bf16[12,12,8,128]{3,2,1,0:T(8,128)(2,1)S(1)}, u32[]{:S(2)}, u32[]{:S(2)}) collective-permute-start(bf16[12,12,8,128]{3,2,1,0:T(8,128)(2,1)} %constant_dynamic-slice_fusion.3), channel_id=1, source_target_pairs={{0,2},{2,4},{4,6},{3,1},{5,3},{7,5},{8,10},{10,12},{12,14},{11,9},... | collective-permute-start | bytes 884744 | tf_op jit(solution)/shard_map/ppermute | solution.py:172
  21.6 12.2 %collective-permute-start.5 = (bf16[10,16,8,128]{3,2,1,0:T(8,128)(2,1)S(1)}, bf16[10,16,8,128]{3,2,1,0:T(8,128)(2,1)S(1)}, u32[]{:S(2)}, u32[]{:S(2)}) collective-permute-start(bf16[10,16,8,128]{3,2,1,0:T(8,128)(2,1)S(1)} %pad_maximum_fusion.1.refs_6_), channel_id=1, source_target_pairs={{0,1},{1,0},{2,3},{3,2},{4,5},{5,4},{6,7},{7,6},{8,9},{9,8},{10,11... | collective-permute-start | bytes 983048 | tf_op jit(solution)/shard_map/ppermute | solution.py:172
  21.6 15.6 %collective-permute-start.6 = (bf16[10,16,8,128]{3,2,1,0:T(8,128)(2,1)S(1)}, bf16[10,16,8,128]{3,2,1,0:T(8,128)(2,1)S(1)}, u32[]{:S(2)}, u32[]{:S(2)}) collective-permute-start(bf16[10,16,8,128]{3,2,1,0:T(8,128)(2,1)S(1)} %pad_maximum_fusion.1.refs_6_), channel_id=1, source_target_pairs={{2,0},{4,2},{6,4},{1,3},{3,5},{5,7},{10,8},{12,10},{14,12},{9,11},... | collective-permute-start | bytes 983048 | tf_op jit(solution)/shard_map/ppermute | solution.py:172
  23.5 17.8 %collective-permute-start.1 = (bf16[12,16,8,128]{3,2,1,0:T(8,128)(2,1)S(1)}, bf16[12,16,8,128]{3,2,1,0:T(8,128)(2,1)S(1)}, u32[]{:S(2)}, u32[]{:S(2)}) collective-permute-start(bf16[12,16,8,128]{3,2,1,0:T(8,128)(2,1)S(1)} %get-tuple-element.11.refs_0_), channel_id=1, source_target_pairs={{2,0},{4,2},{6,4},{1,3},{3,5},{5,7},{10,8},{12,10},{14,12},{9,11},... | collective-permute-start | bytes 1179656 | tf_op jit(solution)/shard_map/ppermute | solution.py:172
  29.4 49.1 %collective-permute-start.11 = (bf16[24,16,8,128]{3,0,2,1:T(8,128)(2,1)}, bf16[24,16,8,128]{3,0,2,1:T(8,128)(2,1)}, u32[]{:S(2)}, u32[]{:S(2)}) collective-permute-start(bf16[24,16,8,128]{3,0,2,1:T(8,128)(2,1)} %copy.37), channel_id=1, source_target_pairs={{0,8},{8,0},{16,24},{24,16},{1,9},{9,1},{17,25},{25,17},{2,10},{10... | collective-permute-start | bytes 2359304 | tf_op jit(solution)/shard_map/ppermute | solution.py:213
  29.4 23.9 %collective-permute-start.3 = (bf16[12,16,8,128]{3,2,1,0:T(8,128)(2,1)S(1)}, bf16[12,16,8,128]{3,2,1,0:T(8,128)(2,1)S(1)}, u32[]{:S(2)}, u32[]{:S(2)}) collective-permute-start(bf16[12,16,8,128]{3,2,1,0:T(8,128)(2,1)S(1)} %collective-permute-done.refs_1_), channel_id=1, source_target_pairs={{0,2},{2,4},{4,6},{3,1},{5,3},{7,5},{8,10},{10,12},{12,14},{11,9},... | collective-permute-start | bytes 1179656 | tf_op jit(solution)/shard_map/ppermute | solution.py:172
  33.8 19.5 %collective-permute-start.8 = (bf16[10,16,8,128]{3,2,1,0:T(8,128)(2,1)S(1)}, bf16[10,16,8,128]{3,2,1,0:T(8,128)(2,1)S(1)}, u32[]{:S(2)}, u32[]{:S(2)}) collective-permute-start(bf16[10,16,8,128]{3,2,1,0:T(8,128)(2,1)S(1)} %collective-permute-done.5.refs_7_), channel_id=1, source_target_pairs={{0,2},{2,4},{4,6},{3,1},{5,3},{7,5},{8,10},{10,12},{12,14},{11,9},... | collective-permute-start | bytes 983048 | tf_op jit(solution)/shard_map/ppermute | solution.py:172
  37.3 16.0 %collective-permute-start.4 = (bf16[12,12,8,128]{3,2,1,0:T(8,128)(2,1)S(1)}, bf16[12,12,8,128]{3,2,1,0:T(8,128)(2,1)S(1)}, u32[]{:S(2)}, u32[]{:S(2)}) collective-permute-start(bf16[12,12,8,128]{3,2,1,0:T(8,128)(2,1)S(1)} %constant_dynamic-slice_fusion.2), channel_id=1, source_target_pairs={{2,0},{4,2},{6,4},{1,3},{3,5},{5,7},{10,8},{12,10},{14,12},{9,11},... | collective-permute-start | bytes 884744 | tf_op jit(solution)/shard_map/ppermute | solution.py:172
  41.4 11.9 %collective-permute-start.9 = (bf16[10,12,8,128]{3,2,1,0:T(8,128)(2,1)S(1)}, bf16[10,12,8,128]{3,2,1,0:T(8,128)(2,1)S(1)}, u32[]{:S(2)}, u32[]{:S(2)}) collective-permute-start(bf16[10,12,8,128]{3,2,1,0:T(8,128)(2,1)S(1)} %constant_dynamic-slice_fusion), channel_id=1, source_target_pairs={{2,0},{4,2},{6,4},{1,3},{3,5},{5,7},{10,8},{12,10},{14,12},{9,11},... | collective-permute-start | bytes 737288 | tf_op jit(solution)/shard_map/ppermute | solution.py:172
  53.3 0.9 copy-start
  76.3 10.3 %collective-permute-start.10 = (bf16[12,16,8,128]{3,2,1,0:T(8,128)(2,1)}, bf16[12,16,8,128]{3,2,1,0:T(8,128)(2,1)S(1)}, u32[]{:S(2)}, u32[]{:S(2)}) collective-permute-start(bf16[12,16,8,128]{3,2,1,0:T(8,128)(2,1)} %get-tuple-element.5), channel_id=1, source_target_pairs={{0,1},{1,0},{2,3},{3,2},{4,5},{5,4},{6,7},{7,6},{8,9},{9,8},{10,11... | collective-permute-start | bytes 1179656 | tf_op jit(solution)/shard_map/ppermute | solution.py:172
  76.8 20.7 %collective-permute-start.12 = (bf16[24,16,8,128]{3,0,2,1:T(8,128)(2,1)}, bf16[24,16,8,128]{3,0,2,1:T(8,128)(2,1)S(1)}, u32[]{:S(2)}, u32[]{:S(2)}) collective-permute-start(bf16[24,16,8,128]{3,0,2,1:T(8,128)(2,1)} %copy.37), channel_id=1, source_target_pairs={{0,16},{8,24},{16,0},{24,8},{1,17},{9,25},{17,1},{25,9},{2,18},{10... | collective-permute-start | bytes 2359304 | tf_op jit(solution)/shard_map/ppermute | solution.py:213
  78.5 33.4 %collective-permute-start.13 = (bf16[24,16,8,128]{3,0,2,1:T(8,128)(2,1)}, bf16[24,16,8,128]{3,0,2,1:T(8,128)(2,1)S(1)}, u32[]{:S(2)}, u32[]{:S(2)}) collective-permute-start(bf16[24,16,8,128]{3,0,2,1:T(8,128)(2,1)} %collective-permute-done.11), channel_id=1, source_target_pairs={{0,16},{8,24},{16,0},{24,8},{1,17},{9,25},{17,1},{25,9},{2,18},{10... | collective-permute-start | bytes 2359304 | tf_op jit(solution)/shard_map/ppermute | solution.py:213
  88.2 10.0 %copy-start.3 = (bf16[24,16,8,128]{3,2,1,0:T(8,128)(2,1)S(1)}, bf16[24,16,8,128]{3,2,1,0:T(8,128)(2,1)}, u32[]{:S(2)}) copy-start(bf16[24,16,8,128]{3,2,1,0:T(8,128)(2,1)} %param.13) | copy-start | bytes 2359300
  113.4 3.8 %collective-permute-start.14 = (f32[96,24]{0,1:T(8,128)S(1)}, f32[96,24]{0,1:T(8,128)S(1)}, u32[]{:S(2)}, u32[]{:S(2)}) collective-permute-start(f32[96,24]{0,1:T(8,128)S(1)} %broadcast_select_fusion.2), channel_id=1, source_target_pairs={{0,1},{1,0},{2,3},{3,2},{4,5},{5,4},{6,7},{7,6},{8,9},{9,8},{10,11... | collective-permute-start | bytes 27656 | tf_op jit(solution)/shard_map/ppermute | solution.py:172
  117.1 3.9 %collective-permute-start.15 = (f32[96,24]{0,1:T(8,128)S(1)}, f32[96,24]{0,1:T(8,128)S(1)}, u32[]{:S(2)}, u32[]{:S(2)}) collective-permute-start(f32[96,24]{0,1:T(8,128)S(1)} %fusion.13), channel_id=1, source_target_pairs={{0,2},{1,3},{2,0},{3,1},{4,6},{5,7},{6,4},{7,5},{8,10},{9,11},{10,... | collective-permute-start | bytes 27656 | tf_op jit(solution)/shard_map/ppermute | solution.py:172
  121.0 4.6 %collective-permute-start.16 = (f32[96,24]{0,1:T(8,128)S(1)}, f32[96,24]{0,1:T(8,128)S(1)}, u32[]{:S(2)}, u32[]{:S(2)}) collective-permute-start(f32[96,24]{0,1:T(8,128)S(1)} %add.71), channel_id=1, source_target_pairs={{0,4},{1,5},{2,6},{3,7},{4,0},{5,1},{6,2},{7,3},{8,12},{9,13},{10,... | collective-permute-start | bytes 27656 | tf_op jit(solution)/shard_map/ppermute | solution.py:172

commit v2 on v1

v2 whole, which is shorter than its diff:
```python
import functools

import jax
import jax.numpy as jnp
import numpy as np
from jax import lax
from jax.experimental import pallas as pl
from jax.experimental.pallas import tpu as pltpu
from jax.sharding import PartitionSpec as P

taps = (-205.0 / 72.0, 8.0 / 5.0, -1.0 / 5.0, 8.0 / 315.0, -1.0 / 560.0)
SPAN = 24
PACK = 2
AHEAD = 1


def tables(cells_y, cells_z):
    ratio = [0.0] + [t / taps[1] for t in taps[1:]]
    left = np.zeros((SPAN, cells_y, SPAN + 8, cells_y), np.float32)
    for i in range(SPAN):
        for d in range(1, 5):
            for y in range(cells_y):
                left[i, y, i + 4 + d, y] = ratio[d]
                left[i, y, i + 4 - d, y] = ratio[d]
                if y + d < cells_y:
                    left[i, y, i + 4, y + d] = ratio[d]
                if y - d >= 0:
                    left[i, y, i + 4, y - d] = ratio[d]
    right = np.zeros((cells_z, cells_z), np.float32)
    for z in range(cells_z):
        for d in range(1, 5):
            if z + d < cells_z:
                right[z, z + d] = ratio[d]
            if z - d >= 0:
                right[z, z - d] = ratio[d]
    left = left.reshape(SPAN * cells_y, (SPAN + 8) * cells_y)
    return left, np.concatenate([right, right], axis=0)


def spans(rows):
    out = []
    while rows > 0:
        out.append(min(SPAN, rows))
        rows -= out[-1]
    return out


def shares(steps, rows, halo):
    return (steps + 1) // 2, (-(-(halo - rows) // 4) + 1) // 2


def march(steps, rows, halo, scalars, *refs):
    pieces = refs[0:6]
    extras = refs[6:10]
    left_ref, right_ref, own_ref, send_ref = refs[10:14]
    pert, snap, scale, gain, fields, split = refs[14:20]
    total = 2 * rows + 2 * halo
    cy = 8
    far = halo - rows
    par, core = scalars[0], scalars[1]
    even = (halo, halo + rows, halo + 2 * rows, 0, halo - rows, halo + 3 * rows)
    odd = (halo + rows, halo, halo - rows, halo + 3 * rows, halo + 2 * rows, 0)
    counts = (rows, rows, rows, far, rows, far)
    starts = [e + par * (o - e) for e, o in zip(even, odd)]
    near_half, far_half = shares(steps, rows, halo)

    @pl.when(pl.program_id(0) == 0)
    def _():
        for side, order in ((0, (0, 2, 3)), (1, (1, 4, 5))):
            at = 0
            for j, kept in zip(order, (near_half, near_half, far_half)):
                where = pl.ds(pl.multiple_of(starts[j] * cy, 32), counts[j] * cy)
                flat = (counts[j] * cy, 128)
                for t in range(kept + 1):
                    mine = extras[side][at : at + counts[j]].reshape(flat).astype(jnp.float32)
                    other = extras[side + 2][at : at + counts[j]].reshape(flat).astype(jnp.float32)
                    at += counts[j]
                    if t < kept:
                        snap[2 * t + core, where, :] = mine
                        snap[2 * t + 1 - core, where, :] = other
                    else:
                        scale[where, :] = 2.0 + (3.0 * taps[0]) * (mine + other)
                        gain[where, :] = taps[1] * (mine + other)

    for q in range(PACK):
        probe = pl.program_id(0) * PACK + q
        low = scalars[2 + 2 * probe]
        high = scalars[3 + 2 * probe]
        for j in range(6):
            where = pl.ds(pl.multiple_of(starts[j] * cy, 32), counts[j] * cy)
            value = pieces[j][q].astype(jnp.float32)
            plane = lax.broadcasted_iota(jnp.int32, value.shape, 0) + starts[j]
            value = jnp.where((plane >= low) & (plane < high), value, 0.0)
            pert[q, where, :] = value.reshape(counts[j] * cy, 128)

    def keep(q, slot, where, value):
        high = value.astype(jnp.bfloat16)
        low = (value - high.astype(jnp.float32)).astype(jnp.bfloat16)
        split[q, slot, where, 0:128] = high
        split[q, slot, where, 128:256] = low

    at = 0
    for m in spans(total):
        where = pl.ds(at * cy, m * cy)
        for q in range(PACK):
            first = pert[q, where, :] * snap[0, where, :]
            fields[q, 0, where, :] = first
            keep(q, 0, where, first)
        at += m

    def slab(row, count):
        if isinstance(row, int):
            return pl.ds(row * cy, count * cy)
        return pl.ds(pl.multiple_of(row * cy, 32), count * cy)

    def products(q, n, row, m):
        now = (n + 1) % 2
        both = jnp.dot(
            left_ref[0 : m * cy, 0 : (m + 8) * cy],
            split[q, now, slab(row - 4, m + 8), :],
            preferred_element_type=jnp.float32,
        )
        along = jnp.dot(split[q, now, slab(row, m), :], right_ref[...], preferred_element_type=jnp.float32)
        return both, along

    def advanced(q, n, row, m, both, along):
        now, before = (n + 1) % 2, n % 2
        where = slab(row, m)
        total_taps = both[:, 0:128] + both[:, 128:256] + along
        value = scale[where, :] * fields[q, now, where, :] + gain[where, :] * total_taps
        value = value + pert[q, where, :] * snap[n, where, :]
        if n > 1:
            value = value - fields[q, before, where, :]
        if n < steps - 1:
            fields[q, before, where, :] = value
            keep(q, before, where, value)
        elif row is starts[0]:
            own_ref[q] = value.reshape(rows, cy, 128)
        else:
            send_ref[q] = value.reshape(rows, cy, 128).astype(jnp.bfloat16)

    items = []
    for n in range(1, steps - 1):
        at = 4 * n
        for m in spans(total - 8 * n):
            items += [(q, n, at, m) for q in range(PACK)]
            at += m
    for row in starts[0:2]:
        items += [(q, steps - 1, row, rows) for q in range(PACK)]
    queue = []
    for item in items:
        queue.append((item, products(*item)))
        if len(queue) > AHEAD:
            first, made = queue.pop(0)
            advanced(*first, *made)
    for first, made in queue:
        advanced(*first, *made)


def propagate(scalars, pieces, extras, steps, rows, halo):
    half, _, cy, cz = pieces[0].shape
    left, right = tables(cy, cz)
    left, right = jnp.asarray(left, jnp.bfloat16), jnp.asarray(right, jnp.bfloat16)
    counts = (rows, rows, rows, halo - rows, rows, halo - rows)
    total = 2 * rows + 2 * halo
    fixed = lambda *shape: pl.BlockSpec(shape, lambda k, p: (0,) * len(shape), pipeline_mode=pl.Buffered(1))
    block = lambda count: pl.BlockSpec((PACK, count, cy, cz), lambda k, p: (k, 0, 0, 0))
    grid_spec = pltpu.PrefetchScalarGridSpec(
        num_scalar_prefetch=1,
        grid=(half // PACK,),
        in_specs=[block(c) for c in counts]
        + [fixed(*x.shape) for x in extras]
        + [fixed(*left.shape), fixed(*right.shape)],
        out_specs=[block(rows), block(rows)],
        scratch_shapes=[
            pltpu.VMEM((PACK, total * cy, cz), jnp.float32),
            pltpu.VMEM((steps + steps % 2, total * cy, cz), jnp.float32),
            pltpu.VMEM((total * cy, cz), jnp.float32),
            pltpu.VMEM((total * cy, cz), jnp.float32),
            pltpu.VMEM((PACK, 2, total * cy, cz), jnp.float32),
            pltpu.VMEM((PACK, 2, total * cy, 2 * cz), jnp.bfloat16),
        ],
    )
    cells = half * total * cy * cz
    return pl.pallas_call(
        functools.partial(march, steps, rows, halo),
        grid_spec=grid_spec,
        out_shape=[
            jax.ShapeDtypeStruct((half, rows, cy, cz), jnp.float32),
            jax.ShapeDtypeStruct((half, rows, cy, cz), jnp.bfloat16),
        ],
        compiler_params=pltpu.CompilerParams(vmem_limit_bytes=40 << 20),
        cost_estimate=pl.CostEstimate(flops=cells * 4000, bytes_accessed=cells * 4, transcendentals=0),
        name="march",
    )(scalars, *pieces, *extras, left, right)


def local(probe_field, bounds, courant, snapshots, snap_times, basis_panels):
    probes_here, rows, cy, cz = probe_field.shape
    steps = snap_times.shape[0]
    half = probes_here // 2
    halo = 4 * (steps - 1)
    far = halo - rows
    devices = lax.axis_size("store")
    place = lax.axis_index("store")
    member = lax.axis_index("probe")
    members = lax.axis_size("probe")
    par = (place % 2).astype(jnp.int32)
    core = (member % 2).astype(jnp.int32)
    swap = [(i, i ^ 1) for i in range(devices)]
    perm_a = [(i, i - 2) for i in range(2, devices, 2)] + [(i, i + 2) for i in range(1, devices - 2, 2)]
    perm_b = [(i, i + 2) for i in range(0, devices - 2, 2)] + [(i, i - 2) for i in range(3, devices, 2)]
    hop = lambda x, pairs: lax.ppermute(x, "store", pairs)
    cores = lambda x: lax.ppermute(x, "probe", [(i, i ^ 1) for i in range(members)])
    cut = lambda x, start: lax.dynamic_slice_in_dim(x, start, far, axis=1)
    near = rows - far

    all_snaps = lax.all_gather(snapshots, "probe", axis=2, tiled=True)
    near_half, far_half = shares(steps, rows, halo)
    chosen = jnp.minimum(2 * jnp.arange(near_half) + core, steps - 1)
    picked = jnp.take(all_snaps, jnp.take(snap_times, chosen, mode="clip"), axis=0, mode="clip")
    high = lax.reduce_precision(courant, 8, 7)
    rate = jnp.where(core == 0, high, courant - high).astype(jnp.bfloat16)[None]
    extra = jnp.concatenate([picked, rate], axis=0)
    extra_a = hop(extra, perm_a)
    extra_b = hop(cut(jnp.concatenate([picked[:far_half], rate], axis=0), near * (1 - par)), perm_b)
    planes = lambda x: x.reshape(-1, cy, cz)
    bundle = jnp.concatenate([planes(extra), planes(extra_a), planes(extra_b)], axis=0)
    bundle_x = hop(bundle, swap)
    extras = (bundle, bundle_x, cores(bundle), cores(bundle_x))

    mine = lax.dynamic_slice_in_dim(probe_field, half * par, half, axis=0)
    theirs = lax.dynamic_slice_in_dim(probe_field, half * (1 - par), half, axis=0)
    partner = hop(theirs, swap)
    pieces = (
        mine,
        partner,
        hop(mine, perm_a),
        hop(cut(mine, near * (1 - par)), perm_b),
        hop(partner, perm_b),
        hop(cut(partner, near * par), perm_a),
    )
    base = (place // 2) * 2 * rows - halo
    mine_bounds = lax.dynamic_slice_in_dim(bounds, half * par, half, axis=0) - base
    scalars = jnp.concatenate([jnp.stack([par, core]), mine_bounds.reshape(-1)]).astype(jnp.int32)
    own, send = propagate(scalars, pieces, extras, steps, rows, halo)
    back = hop(send, swap).astype(jnp.float32)
    first = par == 0
    response = jnp.concatenate([jnp.where(first, own, back), jnp.where(first, back, own)], axis=0)
    low = response.astype(jnp.bfloat16).reshape(probes_here, -1)

    panels = [basis_panels]
    span = members // 2
    while span:
        pairs = [(i, i ^ span) for i in range(members)]
        panels = [y for x in panels for y in (x, lax.ppermute(x, "probe", pairs))]
        span //= 2
    parts = [
        lax.dot_general(
            x.reshape(x.shape[0], -1), low, (((1,), (1,)), ((), ())), preferred_element_type=jnp.float32
        )
        for x in panels
    ]
    parts = jnp.stack(parts)
    order = jnp.arange(members) ^ member
    product = jnp.take(parts, order, axis=0, mode="clip").reshape(-1, probes_here)
    span = 1
    while span < devices:
        product = product + hop(product, [(i, i ^ span) for i in range(devices)])
        span *= 2
    return response, product


def solution(mesh):
    placed = (
        P("probe", "store", None, None),
        P("probe", None),
        P("store", None, None),
        P(None, "store", "probe", None),
        P(),
        P("probe", "store", None, None),
    )
    return jax.shard_map(
        local,
        mesh=mesh,
        in_specs=placed,
        out_specs=(P("probe", "store", None, None), P(None, "probe")),
        check_vma=False,
    )
```

time: 127 us -> 109 us (0.86)
  waiting for transfers between devices: 50.6 us -> 37.4 us
  starting transfers between devices: 31.6 us -> 24.9 us
  local copies, waits for them, and re-layouts: 6.34 us -> 11.4 us
  Pallas kernels: 22.1 us -> 18 us
  blocking collectives: 5.79 us -> 7.22 us
    ppermute x3 -> x5, waiting for transfers between devices: 19.7 us -> 0.01 us  [the longest x3 0.01 us: local(): panels = [y for x in panels for y in (x, lax.ppermute(x, 'probe', pairs))]]
    ppermute x14 -> x12, starting transfers between devices: 29.5 us -> 22.7 us  [local(): hop = lambda x, pairs: lax.ppermute(x, 'store', pairs)]
    ppermute x14 -> x12, waiting for transfers between devices: 30.8 us -> 37.4 us  [local(): hop = lambda x, pairs: lax.ppermute(x, 'store', pairs)]
    unnamed x16 -> x22, local copies, waits for them, and re-layouts: 2.33 us -> 7.65 us
    pallas_call x1, Pallas kernels: 22.1 us -> 18 us  [propagate(): pl.pallas_call(functools.partial(march, steps, rows, halo), grid_spec=gri...]
    select_n x5 -> x0, other arithmetic: 1.74 us -> none  [the longest x1 1.63 us: local(): jnp.where(inside[:, :, None, None], probe_field, jnp.zeros_like(probe_fie...]
    all_gather x1, blocking collectives: 5.79 us -> 7.22 us  [local(): all_snaps = lax.all_gather(snapshots, 'probe', axis=2, tiled=True)]
  transfers between devices with their start and end apart: 17 -> 17, of which waited for: 10 -> 8; matrix products, arithmetic and copies ran while one was open for 7% -> 9% of each run, Pallas kernels for 18% -> 17%
where the time goes in v2:
time: 109 us; the launch traced here: 108 us
  waiting for transfers between devices  37.4 us (34%)
  starting transfers between devices  24.9 us (23%)
  Pallas kernels  18 us (17%)
  local copies, waits for them, and re-layouts  11.4 us (10%)
  blocking collectives  7.22 us (7%)
  matrix products  4.69 us (4%)
  other arithmetic  3.37 us (3%)
    ppermute x12, waiting for transfers between devices, local(): hop = lambda x, pairs: lax.ppermute(x, 'store', pairs)  37.4 us
    ppermute x12, starting transfers between devices, local(): hop = lambda x, pairs: lax.ppermute(x, 'store', pairs)  22.7 us
    pallas_call x1, Pallas kernels, propagate(): pl.pallas_call(functools.partial(march, steps, rows, halo), grid_spec=gri...  18 us
    unnamed x22, local copies, waits for them, and re-layouts  7.65 us
    all_gather x1, blocking collectives, local(): all_snaps = lax.all_gather(snapshots, 'probe', axis=2, tiled=True)  7.22 us
    dot_general x4, matrix products, local(): lax.dot_general(x.reshape(x.shape[0], -1), low, (((1,), (1,)), ((), ())),...  4.69 us
  transfers between devices with their start and end apart: 17, of which 8 were waited for; matrix products, arithmetic and copies ran while one was open for 9% of the time, Pallas kernels for 17%

profile of v2, /device:TPU:0, one launch (start us, length us, event | category | flops | bytes accessed | tf_op | source)
XLA Modules:
  0.0 108.0 jit_solution(16325443889043303514)
XLA Ops:
  2.9 7.2 %all_gather.3 = bf16[8,16,8,128]{3,1,0,2:T(8,128)(2,1)S(1)} all-gather(bf16[8,16,2,128]{3,1,0,2:T(8,128)(2,1)S(1)} %copy.28), channel_id=1, replica_groups=mesh['probe'=4,'store'=8] {'probe'}, dimensions={2}, use_global_device_ids=true | all-gather | bytes 327680 | tf_op jit(solution)/shard_map/all_gather | solution.py:218
  11.6 1.3 %collective-permute-start.5 = (bf16[5,16,8,128]{3,1,2,0:T(8,128)(2,1)S(1)}, bf16[5,16,8,128]{3,1,2,0:T(8,128)(2,1)S(1)}, u32[]{:S(2)}, u32[]{:S(2)}) collective-permute-start(bf16[5,16,8,128]{3,1,2,0:T(8,128)(2,1)S(1)} %pad_maximum_fusion.2), channel_id=1, source_target_pairs={{2,0},{4,2},{6,4},{1,3},{3,5},{5,7},{10,8},{12,10},{14,12},{9,11},... | collective-permute-start | bytes 491528 | tf_op jit(solution)/shard_map/ppermute | solution.py:213
  12.9 4.6 %collective-permute-start.6 = (bf16[3,12,8,128]{3,1,2,0:T(8,128)(2,1)S(1)}, bf16[3,12,8,128]{3,1,2,0:T(8,128)(2,1)S(1)}, u32[]{:S(2)}, u32[]{:S(2)}) collective-permute-start(bf16[3,12,8,128]{3,1,2,0:T(8,128)(2,1)S(1)} %dynamic-slice_maximum_fusion), channel_id=1, source_target_pairs={{0,2},{2,4},{4,6},{3,1},{5,3},{7,5},{8,10},{10,12},{12,14},{11,9},... | collective-permute-start | bytes 221192 | tf_op jit(solution)/shard_map/ppermute | solution.py:213
  17.6 2.2 %collective-permute-done.6 = bf16[3,12,8,128]{3,1,2,0:T(8,128)(2,1)S(1)} collective-permute-done((bf16[3,12,8,128]{3,1,2,0:T(8,128)(2,1)S(1)}, bf16[3,12,8,128]{3,1,2,0:T(8,128)(2,1)S(1)}, u32[]{:S(2)}, u32[]{:S(2)}) %collective-permute-start.6) | collective-permute-done | bytes 73760 | tf_op jit(solution)/shard_map/ppermute | solution.py:213
  20.0 3.5 %collective-permute-start.7 = (bf16[196,8,128]{2,1,0:T(8,128)(2,1)S(1)}, bf16[196,8,128]{2,1,0:T(8,128)(2,1)S(1)}, u32[]{:S(2)}, u32[]{:S(2)}) collective-permute-start(bf16[196,8,128]{2,1,0:T(8,128)(2,1)S(1)} %pad_maximum_fusion.1.refs_6_), channel_id=1, source_target_pairs={{0,1},{1,0},{2,3},{3,2},{4,5},{5,4},{6,7},{7,6},{8,9},{9,8},{10,11... | collective-permute-start | bytes 1204232 | tf_op jit(solution)/shard_map/ppermute | solution.py:213
  24.4 3.5 %collective-permute-start.2 = (bf16[12,12,8,128]{3,2,1,0:T(8,128)(2,1)}, bf16[12,12,8,128]{3,2,1,0:T(8,128)(2,1)S(1)}, u32[]{:S(2)}, u32[]{:S(2)}) collective-permute-start(bf16[12,12,8,128]{3,2,1,0:T(8,128)(2,1)} %constant_dynamic-slice_fusion.1), channel_id=1, source_target_pairs={{0,2},{2,4},{4,6},{3,1},{5,3},{7,5},{8,10},{10,12},{12,14},{11,9},... | collective-permute-start | bytes 884744 | tf_op jit(solution)/shard_map/ppermute | solution.py:213
  27.9 1.3 %collective-permute-start.1 = (bf16[12,16,8,128]{3,2,1,0:T(8,128)(2,1)S(1)}, bf16[12,16,8,128]{3,2,1,0:T(8,128)(2,1)S(1)}, u32[]{:S(2)}, u32[]{:S(2)}) collective-permute-start(bf16[12,16,8,128]{3,2,1,0:T(8,128)(2,1)S(1)} %get-tuple-element.11.refs_0_), channel_id=1, source_target_pairs={{2,0},{4,2},{6,4},{1,3},{3,5},{5,7},{10,8},{12,10},{14,12},{9,11},... | collective-permute-start | bytes 1179656 | tf_op jit(solution)/shard_map/ppermute | solution.py:213
  29.3 11.3 %collective-permute-done.refs_1_ = bf16[12,16,8,128]{3,2,1,0:T(8,128)(2,1)S(1)} collective-permute-done((bf16[12,16,8,128]{3,2,1,0:T(8,128)(2,1)S(1)}, bf16[12,16,8,128]{3,2,1,0:T(8,128)(2,1)S(1)}, u32[]{:S(2)}, u32[]{:S(2)}) %collective-permute-start) | collective-permute-done | bytes 393248 | tf_op jit(solution)/shard_map/ppermute | solution.py:213
  40.6 3.5 %collective-permute-start.3 = (bf16[12,16,8,128]{3,2,1,0:T(8,128)(2,1)S(1)}, bf16[12,16,8,128]{3,2,1,0:T(8,128)(2,1)S(1)}, u32[]{:S(2)}, u32[]{:S(2)}) collective-permute-start(bf16[12,16,8,128]{3,2,1,0:T(8,128)(2,1)S(1)} %collective-permute-done.refs_1_), channel_id=1, source_target_pairs={{0,2},{2,4},{4,6},{3,1},{5,3},{7,5},{8,10},{10,12},{12,14},{11,9},... | collective-permute-start | bytes 1179656 | tf_op jit(solution)/shard_map/ppermute | solution.py:213
  45.0 1.3 %collective-permute-start.4 = (bf16[12,12,8,128]{3,2,1,0:T(8,128)(2,1)}, bf16[12,12,8,128]{3,2,1,0:T(8,128)(2,1)}, u32[]{:S(2)}, u32[]{:S(2)}) collective-permute-start(bf16[12,12,8,128]{3,2,1,0:T(8,128)(2,1)} %constant_dynamic-slice_fusion), channel_id=1, source_target_pairs={{2,0},{4,2},{6,4},{1,3},{3,5},{5,7},{10,8},{12,10},{14,12},{9,11},... | collective-permute-start | bytes 884744 | tf_op jit(solution)/shard_map/ppermute | solution.py:213
  46.6 2.6 %copy.35 = bf16[24,16,8,128]{3,0,2,1:T(8,128)(2,1)} copy(bf16[24,16,8,128]{3,2,1,0:T(8,128)(2,1)} %param.13) | data formatting | bytes 1572864 | tf_op args[5]
  50.0 1.5 %collective-permute-start.12 = (bf16[24,16,8,128]{3,0,2,1:T(8,128)(2,1)}, bf16[24,16,8,128]{3,0,2,1:T(8,128)(2,1)}, u32[]{:S(2)}, u32[]{:S(2)}) collective-permute-start(bf16[24,16,8,128]{3,0,2,1:T(8,128)(2,1)} %copy.35), channel_id=1, source_target_pairs={{0,16},{8,24},{16,0},{24,8},{1,17},{9,25},{17,1},{25,9},{2,18},{10... | collective-permute-start | bytes 2359304 | tf_op jit(solution)/shard_map/ppermute | solution.py:256
  51.5 5.1 %collective-permute-done.4.refs_5_ = bf16[12,12,8,128]{3,2,1,0:T(8,128)(2,1)} collective-permute-done((bf16[12,12,8,128]{3,2,1,0:T(8,128)(2,1)}, bf16[12,12,8,128]{3,2,1,0:T(8,128)(2,1)}, u32[]{:S(2)}, u32[]{:S(2)}) %collective-permute-start.4) | collective-permute-done | bytes 294944 | tf_op jit(solution)/shard_map/ppermute | solution.py:213
  58.4 1.0 copy-done.4
  59.4 18.0 %march.1 = (f32[12,16,8,128]{3,2,1,0:T(8,128)S(1)}, bf16[12,16,8,128]{3,2,1,0:T(8,128)(2,1)}) custom-call(s32[26]{0:T(128)S(1)} %pad_add_fusion.scalars, bf16[12,16,8,128]{3,2,1,0:T(8,128)(2,1)S(1)} %get-tuple-element.11.refs_0_, bf16[12,16,8,128]{3,2,1,0:T(8,128)(2,1)S(1)} %collective-permute-done.refs_1_, bf16[12,16,8,128]{3,2,1,0:T(8,128)(2,1)S(1)} %copy-done.2, ...), custom_call_target="tpu_custom_call" | custom-call | flops 4325376000 | bytes 4325376 | tf_op jit(solution)/shard_map/march/pallas_call | solution.py:185
  78.0 10.3 %collective-permute-done.10 = bf16[12,16,8,128]{3,2,1,0:T(8,128)(2,1)S(1)} collective-permute-done((bf16[12,16,8,128]{3,2,1,0:T(8,128)(2,1)}, bf16[12,16,8,128]{3,2,1,0:T(8,128)(2,1)S(1)}, u32[]{:S(2)}, u32[]{:S(2)}) %collective-permute-start.10) | collective-permute-done | bytes 393248 | tf_op jit(solution)/shard_map/ppermute | solution.py:213
  88.5 1.4 %fusion.8 = (bf16[24,16,8,128]{3,2,1,0:T(8,128)(2,1)S(1)}, f32[24,16,8,128]{3,2,1,0:T(8,128)}) fusion(f32[12,16,8,128]{3,2,1,0:T(8,128)S(1)} %get-tuple-element.9, f32[12,16,8,128]{3,2,1,0:T(8,128)S(1)} %get-tuple-element.8), kind=kLoop, calls=%fused_computation.34 | loop fusion | flops 786432 | bytes 3932160 | tf_op jit(solution)/shard_map/convert_element_type | solution.py:250
  89.9 2.0 %convolution_bitcast_fusion.1 = f32[1,24,24]{1,2,0:T(8,128)S(1)} fusion(bf16[24,16,8,128]{3,0,2,1:T(8,128)(2,1)} %collective-permute-done.12, bf16[24,16,8,128]{3,2,1,0:T(8,128)(2,1)S(1)} %get-tuple-element.6), kind=kOutput, calls=%fused_computation.5 | convolution fusion | flops 18874368 | bytes 1575168 | tf_op jit(solution)/shard_map/dot_general | solution.py:259
  92.7 1.2 %convolution_bitcast_fusion.3 = f32[1,24,24]{1,2,0:T(8,128)S(1)} fusion(bf16[24,16,8,128]{3,2,1,0:T(8,128)(2,1)S(1)} %get-tuple-element.6, bf16[24,16,8,128]{3,2,1,0:T(8,128)(2,1)S(1)} %copy-done.8), kind=kOutput, calls=%fused_computation.7 | convolution fusion | flops 18874368 | bytes 1575168 | tf_op jit(solution)/shard_map/dot_general | solution.py:259
  95.7 3.4 %collective-permute-done.14 = f32[96,24]{0,1:T(8,128)S(1)} collective-permute-done((f32[96,24]{0,1:T(8,128)S(1)}, f32[96,24]{0,1:T(8,128)S(1)}, u32[]{:S(2)}, u32[]{:S(2)}) %collective-permute-start.14) | collective-permute-done | bytes 9248 | tf_op jit(solution)/shard_map/ppermute | solution.py:213
  99.1 1.6 %collective-permute-start.15 = (f32[96,24]{0,1:T(8,128)S(1)}, f32[96,24]{0,1:T(8,128)S(1)}, u32[]{:S(2)}, u32[]{:S(2)}) collective-permute-start(f32[96,24]{0,1:T(8,128)S(1)} %add.57), channel_id=1, source_target_pairs={{0,2},{1,3},{2,0},{3,1},{4,6},{5,7},{6,4},{7,5},{8,10},{9,11},{10,... | collective-permute-start | bytes 27656 | tf_op jit(solution)/shard_map/ppermute | solution.py:213
  100.7 2.1 %collective-permute-done.15 = f32[96,24]{0,1:T(8,128)S(1)} collective-permute-done((f32[96,24]{0,1:T(8,128)S(1)}, f32[96,24]{0,1:T(8,128)S(1)}, u32[]{:S(2)}, u32[]{:S(2)}) %collective-permute-start.15) | collective-permute-done | bytes 9248 | tf_op jit(solution)/shard_map/ppermute | solution.py:213
  102.8 1.8 %collective-permute-start.16 = (f32[96,24]{0,1:T(8,128)S(1)}, f32[96,24]{0,1:T(8,128)S(1)}, u32[]{:S(2)}, u32[]{:S(2)}) collective-permute-start(f32[96,24]{0,1:T(8,128)S(1)} %add.58), channel_id=1, source_target_pairs={{0,4},{1,5},{2,6},{3,7},{4,0},{5,1},{6,2},{7,3},{8,12},{9,13},{10,... | collective-permute-start | bytes 27656 | tf_op jit(solution)/shard_map/ppermute | solution.py:213
  104.6 2.8 %collective-permute-done.16 = f32[96,24]{0,1:T(8,128)S(1)} collective-permute-done((f32[96,24]{0,1:T(8,128)S(1)}, f32[96,24]{0,1:T(8,128)S(1)}, u32[]{:S(2)}, u32[]{:S(2)}) %collective-permute-start.16) | collective-permute-done | bytes 9248 | tf_op jit(solution)/shard_map/ppermute | solution.py:213
  (69 shorter events, 12.6 us)
Async XLA Ops:
  1.9 21.6 %copy-start.7 = (bf16[24,16,8,128]{3,2,1,0:T(8,128)(2,1)S(1)}, bf16[24,16,8,128]{3,2,1,0:T(8,128)(2,1)}, u32[]{:S(2)}) copy-start(bf16[24,16,8,128]{3,2,1,0:T(8,128)(2,1)} %param.8) | copy-start | bytes 2359300
  11.6 8.3 %collective-permute-start.5 = (bf16[5,16,8,128]{3,1,2,0:T(8,128)(2,1)S(1)}, bf16[5,16,8,128]{3,1,2,0:T(8,128)(2,1)S(1)}, u32[]{:S(2)}, u32[]{:S(2)}) collective-permute-start(bf16[5,16,8,128]{3,1,2,0:T(8,128)(2,1)S(1)} %pad_maximum_fusion.2), channel_id=1, source_target_pairs={{2,0},{4,2},{6,4},{1,3},{3,5},{5,7},{10,8},{12,10},{14,12},{9,11},... | collective-permute-start | bytes 491528 | tf_op jit(solution)/shard_map/ppermute | solution.py:213
  12.9 6.8 %collective-permute-start.6 = (bf16[3,12,8,128]{3,1,2,0:T(8,128)(2,1)S(1)}, bf16[3,12,8,128]{3,1,2,0:T(8,128)(2,1)S(1)}, u32[]{:S(2)}, u32[]{:S(2)}) collective-permute-start(bf16[3,12,8,128]{3,1,2,0:T(8,128)(2,1)S(1)} %dynamic-slice_maximum_fusion), channel_id=1, source_target_pairs={{0,2},{2,4},{4,6},{3,1},{5,3},{7,5},{8,10},{10,12},{12,14},{11,9},... | collective-permute-start | bytes 221192 | tf_op jit(solution)/shard_map/ppermute | solution.py:213
  20.0 26.3 %copy-start.9 = (s32[24,2]{0,1:T(2,128)S(1)}, s32[24,2]{0,1:T(2,128)}, u32[]{:S(2)}) copy-start(s32[24,2]{0,1:T(2,128)} %param.9) | copy-start | bytes 580
  20.0 24.1 %collective-permute-start.7 = (bf16[196,8,128]{2,1,0:T(8,128)(2,1)S(1)}, bf16[196,8,128]{2,1,0:T(8,128)(2,1)S(1)}, u32[]{:S(2)}, u32[]{:S(2)}) collective-permute-start(bf16[196,8,128]{2,1,0:T(8,128)(2,1)S(1)} %pad_maximum_fusion.1.refs_6_), channel_id=1, source_target_pairs={{0,1},{1,0},{2,3},{3,2},{4,5},{5,4},{6,7},{7,6},{8,9},{9,8},{10,11... | collective-permute-start | bytes 1204232 | tf_op jit(solution)/shard_map/ppermute | solution.py:213
  23.6 33.8 %copy-start.6 = (bf16[256,128]{1,0:T(8,128)(2,1)S(1)}, bf16[256,128]{1,0:T(8,128)(2,1)}, u32[]{:S(2)}) copy-start(bf16[256,128]{1,0:T(8,128)(2,1)} %constant.78.clone.refs_11_) | copy-start | bytes 196612
  23.6 17.0 %collective-permute-start = (bf16[12,16,8,128]{3,2,1,0:T(8,128)(2,1)S(1)}, bf16[12,16,8,128]{3,2,1,0:T(8,128)(2,1)S(1)}, u32[]{:S(2)}, u32[]{:S(2)}) collective-permute-start(bf16[12,16,8,128]{3,2,1,0:T(8,128)(2,1)S(1)} %get-tuple-element.10), channel_id=1, source_target_pairs={{0,1},{1,0},{2,3},{3,2},{4,5},{5,4},{6,7},{7,6},{8,9},{9,8},{10,11... | collective-permute-start | bytes 1179656 | tf_op jit(solution)/shard_map/ppermute | solution.py:213
  24.4 20.6 %collective-permute-start.2 = (bf16[12,12,8,128]{3,2,1,0:T(8,128)(2,1)}, bf16[12,12,8,128]{3,2,1,0:T(8,128)(2,1)S(1)}, u32[]{:S(2)}, u32[]{:S(2)}) collective-permute-start(bf16[12,12,8,128]{3,2,1,0:T(8,128)(2,1)} %constant_dynamic-slice_fusion.1), channel_id=1, source_target_pairs={{0,2},{2,4},{4,6},{3,1},{5,3},{7,5},{8,10},{10,12},{12,14},{11,9},... | collective-permute-start | bytes 884744 | tf_op jit(solution)/shard_map/ppermute | solution.py:213
  27.9 21.3 %collective-permute-start.1 = (bf16[12,16,8,128]{3,2,1,0:T(8,128)(2,1)S(1)}, bf16[12,16,8,128]{3,2,1,0:T(8,128)(2,1)S(1)}, u32[]{:S(2)}, u32[]{:S(2)}) collective-permute-start(bf16[12,16,8,128]{3,2,1,0:T(8,128)(2,1)S(1)} %get-tuple-element.11.refs_0_), channel_id=1, source_target_pairs={{2,0},{4,2},{6,4},{1,3},{3,5},{5,7},{10,8},{12,10},{14,12},{9,11},... | collective-permute-start | bytes 1179656 | tf_op jit(solution)/shard_map/ppermute | solution.py:213
  29.2 22.3 %collective-permute-start.8 = (bf16[196,8,128]{2,1,0:T(8,128)(2,1)S(1)}, bf16[196,8,128]{2,1,0:T(8,128)(2,1)S(1)}, u32[]{:S(2)}, u32[]{:S(2)}) collective-permute-start(bf16[196,8,128]{2,1,0:T(8,128)(2,1)S(1)} %pad_maximum_fusion.1.refs_6_), channel_id=1, source_target_pairs={{0,8},{8,0},{16,24},{24,16},{1,9},{9,1},{17,25},{25,17},{2,10},{10... | collective-permute-start | bytes 1204232 | tf_op jit(solution)/shard_map/ppermute | solution.py:214
  40.6 16.0 %collective-permute-start.3 = (bf16[12,16,8,128]{3,2,1,0:T(8,128)(2,1)S(1)}, bf16[12,16,8,128]{3,2,1,0:T(8,128)(2,1)S(1)}, u32[]{:S(2)}, u32[]{:S(2)}) collective-permute-start(bf16[12,16,8,128]{3,2,1,0:T(8,128)(2,1)S(1)} %collective-permute-done.refs_1_), channel_id=1, source_target_pairs={{0,2},{2,4},{4,6},{3,1},{5,3},{7,5},{8,10},{10,12},{12,14},{11,9},... | collective-permute-start | bytes 1179656 | tf_op jit(solution)/shard_map/ppermute | solution.py:213
  44.1 13.3 %collective-permute-start.9 = (bf16[196,8,128]{2,1,0:T(8,128)(2,1)S(1)}, bf16[196,8,128]{2,1,0:T(8,128)(2,1)S(1)}, u32[]{:S(2)}, u32[]{:S(2)}) collective-permute-start(bf16[196,8,128]{2,1,0:T(8,128)(2,1)S(1)} %collective-permute-done.7.refs_7_), channel_id=1, source_target_pairs={{0,8},{8,0},{16,24},{24,16},{1,9},{9,1},{17,25},{25,17},{2,10},{10... | collective-permute-start | bytes 1204232 | tf_op jit(solution)/shard_map/ppermute | solution.py:214
  45.0 11.6 %collective-permute-start.4 = (bf16[12,12,8,128]{3,2,1,0:T(8,128)(2,1)}, bf16[12,12,8,128]{3,2,1,0:T(8,128)(2,1)}, u32[]{:S(2)}, u32[]{:S(2)}) collective-permute-start(bf16[12,12,8,128]{3,2,1,0:T(8,128)(2,1)} %constant_dynamic-slice_fusion), channel_id=1, source_target_pairs={{2,0},{4,2},{6,4},{1,3},{3,5},{5,7},{10,8},{12,10},{14,12},{9,11},... | collective-permute-start | bytes 884744 | tf_op jit(solution)/shard_map/ppermute | solution.py:213
  46.6 10.8 %copy-start.5 = (bf16[192,256]{1,0:T(8,128)(2,1)S(1)}, bf16[192,256]{1,0:T(8,128)(2,1)}, u32[]{:S(2)}) copy-start(bf16[192,256]{1,0:T(8,128)(2,1)} %constant.77.clone.refs_10_) | copy-start | bytes 294916
  50.0 27.4 %collective-permute-start.12 = (bf16[24,16,8,128]{3,0,2,1:T(8,128)(2,1)}, bf16[24,16,8,128]{3,0,2,1:T(8,128)(2,1)}, u32[]{:S(2)}, u32[]{:S(2)}) collective-permute-start(bf16[24,16,8,128]{3,0,2,1:T(8,128)(2,1)} %copy.35), channel_id=1, source_target_pairs={{0,16},{8,24},{16,0},{24,8},{1,17},{9,25},{17,1},{25,9},{2,18},{10... | collective-permute-start | bytes 2359304 | tf_op jit(solution)/shard_map/ppermute | solution.py:256
  57.4 1.0 copy-start.2
  58.4 1.0 copy-start.4
  77.4 10.9 %collective-permute-start.10 = (bf16[12,16,8,128]{3,2,1,0:T(8,128)(2,1)}, bf16[12,16,8,128]{3,2,1,0:T(8,128)(2,1)S(1)}, u32[]{:S(2)}, u32[]{:S(2)}) collective-permute-start(bf16[12,16,8,128]{3,2,1,0:T(8,128)(2,1)} %get-tuple-element.5), channel_id=1, source_target_pairs={{0,1},{1,0},{2,3},{3,2},{4,5},{5,4},{6,7},{7,6},{8,9},{9,8},{10,11... | collective-permute-start | bytes 1179656 | tf_op jit(solution)/shard_map/ppermute | solution.py:213
  77.4 14.5 %collective-permute-start.11 = (bf16[24,16,8,128]{3,0,2,1:T(8,128)(2,1)}, bf16[24,16,8,128]{3,0,2,1:T(8,128)(2,1)S(1)}, u32[]{:S(2)}, u32[]{:S(2)}) collective-permute-start(bf16[24,16,8,128]{3,0,2,1:T(8,128)(2,1)} %copy.35), channel_id=1, source_target_pairs={{0,8},{8,0},{16,24},{24,16},{1,9},{9,1},{17,25},{25,17},{2,10},{10... | collective-permute-start | bytes 2359304 | tf_op jit(solution)/shard_map/ppermute | solution.py:256
  77.4 16.4 %collective-permute-start.13 = (bf16[24,16,8,128]{3,0,2,1:T(8,128)(2,1)}, bf16[24,16,8,128]{3,0,2,1:T(8,128)(2,1)S(1)}, u32[]{:S(2)}, u32[]{:S(2)}) collective-permute-start(bf16[24,16,8,128]{3,0,2,1:T(8,128)(2,1)} %collective-permute-done.12), channel_id=1, source_target_pairs={{0,8},{8,0},{16,24},{24,16},{1,9},{9,1},{17,25},{25,17},{2,10},{10... | collective-permute-start | bytes 2359304 | tf_op jit(solution)/shard_map/ppermute | solution.py:256
  89.9 2.7 %copy-start.8 = (bf16[24,16,8,128]{3,2,1,0:T(8,128)(2,1)S(1)}, bf16[24,16,8,128]{3,2,1,0:T(8,128)(2,1)}, u32[]{:S(2)}) copy-start(bf16[24,16,8,128]{3,2,1,0:T(8,128)(2,1)} %param.13) | copy-start | bytes 2359300
  95.3 3.8 %collective-permute-start.14 = (f32[96,24]{0,1:T(8,128)S(1)}, f32[96,24]{0,1:T(8,128)S(1)}, u32[]{:S(2)}, u32[]{:S(2)}) collective-permute-start(f32[96,24]{0,1:T(8,128)S(1)} %reshape.48), channel_id=1, source_target_pairs={{0,1},{1,0},{2,3},{3,2},{4,5},{5,4},{6,7},{7,6},{8,9},{9,8},{10,11... | collective-permute-start | bytes 27656 | tf_op jit(solution)/shard_map/ppermute | solution.py:213
  99.1 3.7 %collective-permute-start.15 = (f32[96,24]{0,1:T(8,128)S(1)}, f32[96,24]{0,1:T(8,128)S(1)}, u32[]{:S(2)}, u32[]{:S(2)}) collective-permute-start(f32[96,24]{0,1:T(8,128)S(1)} %add.57), channel_id=1, source_target_pairs={{0,2},{1,3},{2,0},{3,1},{4,6},{5,7},{6,4},{7,5},{8,10},{9,11},{10,... | collective-permute-start | bytes 27656 | tf_op jit(solution)/shard_map/ppermute | solution.py:213
  102.8 4.6 %collective-permute-start.16 = (f32[96,24]{0,1:T(8,128)S(1)}, f32[96,24]{0,1:T(8,128)S(1)}, u32[]{:S(2)}, u32[]{:S(2)}) collective-permute-start(f32[96,24]{0,1:T(8,128)S(1)} %add.58), channel_id=1, source_target_pairs={{0,4},{1,5},{2,6},{3,7},{4,0},{5,1},{6,2},{7,3},{8,12},{9,13},{10,... | collective-permute-start | bytes 27656 | tf_op jit(solution)/shard_map/ppermute | solution.py:213
  (3 other events, 2.2 us)

commit v3 on v2

--- a/solution.py
+++ b/solution.py
@@ -49,7 +49,7 @@
     return (steps + 1) // 2, (-(-(halo - rows) // 4) + 1) // 2
 
 
-def march(steps, rows, halo, scalars, *refs):
+def march(steps, rows, halo, begin, scalars, *refs):
     pieces = refs[0:6]
     extras = refs[6:10]
     left_ref, right_ref, own_ref, send_ref = refs[10:14]
@@ -83,12 +83,12 @@
                         gain[where, :] = taps[1] * (mine + other)
 
     for q in range(PACK):
-        probe = pl.program_id(0) * PACK + q
+        probe = begin + pl.program_id(0) * PACK + q
         low = scalars[2 + 2 * probe]
         high = scalars[3 + 2 * probe]
         for j in range(6):
             where = pl.ds(pl.multiple_of(starts[j] * cy, 32), counts[j] * cy)
-            value = pieces[j][q].astype(jnp.float32)
+            value = pieces[j][probe].astype(jnp.float32)
             plane = lax.broadcasted_iota(jnp.int32, value.shape, 0) + starts[j]
             value = jnp.where((plane >= low) & (plane < high), value, 0.0)
             pert[q, where, :] = value.reshape(counts[j] * cy, 128)
@@ -135,9 +135,9 @@
             fields[q, before, where, :] = value
             keep(q, before, where, value)
         elif row is starts[0]:
-            own_ref[q] = value.reshape(rows, cy, 128)
+            own_ref[pl.program_id(0) * PACK + q] = value.reshape(rows, cy, 128)
         else:
-            send_ref[q] = value.reshape(rows, cy, 128).astype(jnp.bfloat16)
+            send_ref[pl.program_id(0) * PACK + q] = value.reshape(rows, cy, 128).astype(jnp.bfloat16)
 
     items = []
     for n in range(1, steps - 1):
@@ -157,21 +157,17 @@
         advanced(*first, *made)
 
 
-def propagate(scalars, pieces, extras, steps, rows, halo):
-    half, _, cy, cz = pieces[0].shape
+def propagate(scalars, pieces, extras, begin, count, steps, rows, halo):
+    _, _, cy, cz = pieces[0].shape
     left, right = tables(cy, cz)
     left, right = jnp.asarray(left, jnp.bfloat16), jnp.asarray(right, jnp.bfloat16)
-    counts = (rows, rows, rows, halo - rows, rows, halo - rows)
     total = 2 * rows + 2 * halo
-    fixed = lambda *shape: pl.BlockSpec(shape, lambda k, p: (0,) * len(shape), pipeline_mode=pl.Buffered(1))
-    block = lambda count: pl.BlockSpec((PACK, count, cy, cz), lambda k, p: (k, 0, 0, 0))
+    whole = pl.BlockSpec(memory_space=pltpu.VMEM)
     grid_spec = pltpu.PrefetchScalarGridSpec(
         num_scalar_prefetch=1,
-        grid=(half // PACK,),
-        in_specs=[block(c) for c in counts]
-        + [fixed(*x.shape) for x in extras]
-        + [fixed(*left.shape), fixed(*right.shape)],
-        out_specs=[block(rows), block(rows)],
+        grid=(count // PACK,),
+        in_specs=[whole] * (len(pieces) + len(extras) + 2),
+        out_specs=[whole, whole],
         scratch_shapes=[
             pltpu.VMEM((PACK, total * cy, cz), jnp.float32),
             pltpu.VMEM((steps + steps % 2, total * cy, cz), jnp.float32),
@@ -181,16 +177,16 @@
             pltpu.VMEM((PACK, 2, total * cy, 2 * cz), jnp.bfloat16),
         ],
     )
-    cells = half * total * cy * cz
+    cells = count * total * cy * cz
     return pl.pallas_call(
-        functools.partial(march, steps, rows, halo),
+        functools.partial(march, steps, rows, halo, begin),
         grid_spec=grid_spec,
         out_shape=[
-            jax.ShapeDtypeStruct((half, rows, cy, cz), jnp.float32),
-            jax.ShapeDtypeStruct((half, rows, cy, cz), jnp.bfloat16),
+            jax.ShapeDtypeStruct((count, rows, cy, cz), jnp.float32),
+            jax.ShapeDtypeStruct((count, rows, cy, cz), jnp.bfloat16),
         ],
         compiler_params=pltpu.CompilerParams(vmem_limit_bytes=40 << 20),
-        cost_estimate=pl.CostEstimate(flops=cells * 4000, bytes_accessed=cells * 4, transcendentals=0),
+        cost_estimate=pl.CostEstimate(flops=cells * 8000, bytes_accessed=cells * 4, transcendentals=0),
         name="march",
     )(scalars, *pieces, *extras, left, right)
 
@@ -222,48 +218,62 @@
     high = lax.reduce_precision(courant, 8, 7)
     rate = jnp.where(core == 0, high, courant - high).astype(jnp.bfloat16)[None]
     extra = jnp.concatenate([picked, rate], axis=0)
+    mine = lax.dynamic_slice_in_dim(probe_field, half * par, half, axis=0)
+    theirs = lax.dynamic_slice_in_dim(probe_field, half * (1 - par), half, axis=0)
+    partner = hop(theirs, swap)
+    side_a = hop(mine, perm_a)
+    side_b = hop(cut(mine, near * (1 - par)), perm_b)
+    extra, side_a, side_b = lax.optimization_barrier((extra, side_a, side_b))
     extra_a = hop(extra, perm_a)
-    extra_b = hop(cut(jnp.concatenate([picked[:far_half], rate], axis=0), near * (1 - par)), perm_b)
+    tail = jnp.concatenate([extra[:far_half], extra[near_half:]], axis=0)
+    extra_b = hop(cut(tail, near * (1 - par)), perm_b)
     planes = lambda x: x.reshape(-1, cy, cz)
     bundle = jnp.concatenate([planes(extra), planes(extra_a), planes(extra_b)], axis=0)
     bundle_x = hop(bundle, swap)
     extras = (bundle, bundle_x, cores(bundle), cores(bundle_x))
-
-    mine = lax.dynamic_slice_in_dim(probe_field, half * par, half, axis=0)
-    theirs = lax.dynamic_slice_in_dim(probe_field, half * (1 - par), half, axis=0)
-    partner = hop(theirs, swap)
     pieces = (
         mine,
         partner,
-        hop(mine, perm_a),
-        hop(cut(mine, near * (1 - par)), perm_b),
+        side_a,
+        side_b,
         hop(partner, perm_b),
         hop(cut(partner, near * par), perm_a),
     )
     base = (place // 2) * 2 * rows - halo
     mine_bounds = lax.dynamic_slice_in_dim(bounds, half * par, half, axis=0) - base
     scalars = jnp.concatenate([jnp.stack([par, core]), mine_bounds.reshape(-1)]).astype(jnp.int32)
-    own, send = propagate(scalars, pieces, extras, steps, rows, halo)
-    back = hop(send, swap).astype(jnp.float32)
     first = par == 0
-    response = jnp.concatenate([jnp.where(first, own, back), jnp.where(first, back, own)], axis=0)
-    low = response.astype(jnp.bfloat16).reshape(probes_here, -1)
-
+    own, back = [], []
+    for begin, count in ((0, half // 2), (half // 2, half - half // 2)):
+        kept, sent = propagate(scalars, pieces, extras, begin, count, steps, rows, halo)
+        own.append(kept)
+        back.append(hop(sent, swap))
     panels = [basis_panels]
     span = members // 2
     while span:
         pairs = [(i, i ^ span) for i in range(members)]
         panels = [y for x in panels for y in (x, lax.ppermute(x, "probe", pairs))]
         span //= 2
-    parts = [
-        lax.dot_general(
-            x.reshape(x.shape[0], -1), low, (((1,), (1,)), ((), ())), preferred_element_type=jnp.float32
-        )
-        for x in panels
-    ]
-    parts = jnp.stack(parts)
-    order = jnp.arange(members) ^ member
-    product = jnp.take(parts, order, axis=0, mode="clip").reshape(-1, probes_here)
+    panels = jnp.concatenate(panels, axis=0)
+    dots = lambda x: lax.dot_general(
+        panels, x, (((1, 2, 3), (1, 2, 3)), ((), ())), preferred_element_type=jnp.float32
+    )
+    own = jnp.concatenate(own, axis=0)
+    mine_part = dots(own.astype(jnp.bfloat16))
+    back = jnp.concatenate(back, axis=0)
+    back_part = dots(back)
+    back = back.astype(jnp.float32)
+    response = jnp.concatenate([jnp.where(first, own, back), jnp.where(first, back, own)], axis=0)
+    product = jnp.concatenate(
+        [jnp.where(first, mine_part, back_part), jnp.where(first, back_part, mine_part)], axis=1
+    )
+    product = product.reshape(members, -1, probes_here)
+    span = 1
+    while span < members:
+        swapped = product.reshape(-1, 2, span, *product.shape[1:])[:, ::-1].reshape(product.shape)
+        product = jnp.where((member // span) % 2 == 1, swapped, product)
+        span *= 2
+    product = product.reshape(-1, probes_here)
     span = 1
     while span < devices:
         product = product + hop(product, [(i, i ^ span) for i in range(devices)])

time: 109 us -> 108 us (level)
  starting transfers between devices: 24.9 us -> 32.3 us
  waiting for transfers between devices: 37.4 us -> 31 us
  matrix products: 4.69 us -> 1.83 us
  Pallas kernels: 18 us -> 19.5 us
  local copies, waits for them, and re-layouts: 11.4 us -> 12.7 us
    ppermute x12 -> x13, starting transfers between devices: 22.7 us -> 29.8 us  [local(): hop = lambda x, pairs: lax.ppermute(x, 'store', pairs)]
    ppermute x12 -> x13, waiting for transfers between devices: 37.4 us -> 31 us  [local(): hop = lambda x, pairs: lax.ppermute(x, 'store', pairs)]
    dot_general x4 -> x2, matrix products: 4.69 us -> 1.83 us  [local(): lax.dot_general(panels, x, (((1, 2, 3), (1, 2, 3)), ((), ())), preferred_...]
    pallas_call x1 -> x2, Pallas kernels: 18 us -> 19.5 us  [propagate(): pl.pallas_call(functools.partial(march, steps, rows, halo, begin), grid_s...]
    convert_element_type x1 -> x0, other arithmetic: 1.44 us -> none  [local(): low = response.astype(jnp.bfloat16).reshape(probes_here, -1)]
    concatenate x1 -> x3, other arithmetic: 0.04 us -> 1.31 us  [the longest x1 1.25 us: local(): jnp.concatenate([jnp.where(first, own, back), jnp.where(first, back, own)...]
    dynamic_slice x1, local copies, waits for them, and re-layouts: 0.05 us -> 1.22 us  [local(): lax.dynamic_slice_in_dim(probe_field, half * (1 - par), half, axis=0)]
    unnamed x22 -> x20, local copies, waits for them, and re-layouts: 7.65 us -> 7.45 us
  transfers between devices with their start and end apart: 17 -> 18, of which waited for: 8 -> 8; matrix products, arithmetic and copies ran while one was open for 9% -> 12% of each run, Pallas kernels for 17% -> 18%
where the time goes in v3:
time: 108 us; the launch traced here: 107 us
  starting transfers between devices  32.3 us (30%)
  waiting for transfers between devices  31 us (29%)
  Pallas kernels  19.5 us (18%)
  local copies, waits for them, and re-layouts  12.7 us (12%)
  blocking collectives  6.23 us (6%)
  other arithmetic  2.43 us (2%)
  matrix products  1.83 us (2%)
  between operations  1.08 us (1%)
    ppermute x13, waiting for transfers between devices, local(): hop = lambda x, pairs: lax.ppermute(x, 'store', pairs)  31 us
    ppermute x13, starting transfers between devices, local(): hop = lambda x, pairs: lax.ppermute(x, 'store', pairs)  29.8 us
    pallas_call x2, Pallas kernels, propagate(): pl.pallas_call(functools.partial(march, steps, rows, halo, begin), grid_s...  19.5 us
    unnamed x20, local copies, waits for them, and re-layouts  7.45 us
    all_gather x1, blocking collectives, local(): all_snaps = lax.all_gather(snapshots, 'probe', axis=2, tiled=True)  6.23 us
  transfers between devices with their start and end apart: 18, of which 8 were waited for; matrix products, arithmetic and copies ran while one was open for 12% of the time, Pallas kernels for 18%

profile of v3, /device:TPU:0, one launch (start us, length us, event | category | flops | bytes accessed | tf_op | source)
XLA Modules:
  0.0 107.1 jit_solution(3730764629877844235)
XLA Ops:
  1.9 1.3 %collective-permute-start.1 = (bf16[12,16,8,128]{3,2,1,0:T(8,128)(2,1)S(1)}, bf16[12,16,8,128]{3,2,1,0:T(8,128)(2,1)S(1)}, u32[]{:S(2)}, u32[]{:S(2)}) collective-permute-start(bf16[12,16,8,128]{3,2,1,0:T(8,128)(2,1)S(1)} %get-tuple-element.22.refs_0_), channel_id=1, source_target_pairs={{2,0},{4,2},{6,4},{1,3},{3,5},{5,7},{10,8},{12,10},{14,12},{9,11},... | collective-permute-start | bytes 1179656 | tf_op jit(solution)/shard_map/ppermute | solution.py:209
  4.2 5.6 %collective-permute-start.2 = (bf16[12,12,8,128]{3,2,1,0:T(8,128)(2,1)S(1)}, bf16[12,12,8,128]{3,2,1,0:T(8,128)(2,1)S(1)}, u32[]{:S(2)}, u32[]{:S(2)}) collective-permute-start(bf16[12,12,8,128]{3,2,1,0:T(8,128)(2,1)S(1)} %constant_dynamic-slice_fusion.1), channel_id=1, source_target_pairs={{0,2},{2,4},{4,6},{3,1},{5,3},{7,5},{8,10},{10,12},{12,14},{11,9},... | collective-permute-start | bytes 884744 | tf_op jit(solution)/shard_map/ppermute | solution.py:209
  9.8 2.9 %fusion.5 = (bf16[24,16,8,128]{3,0,2,1:T(8,128)(2,1)}, bf16[96,16,8,128]{3,0,2,1:T(8,128)(2,1)}) fusion(bf16[24,16,8,128]{3,2,1,0:T(8,128)(2,1)} %param.15), kind=kLoop, calls=%fused_computation.38 | loop fusion | bytes 2359296 | tf_op args[5]
  13.5 6.2 %all_gather.3 = bf16[8,16,8,128]{3,1,0,2:T(8,128)(2,1)S(1)} all-gather(bf16[8,16,2,128]{3,1,0,2:T(8,128)(2,1)S(1)} %copy.25), channel_id=1, replica_groups=mesh['probe'=4,'store'=8] {'probe'}, dimensions={2}, use_global_device_ids=true | all-gather | bytes 327680 | tf_op jit(solution)/shard_map/all_gather | solution.py:214
  20.4 1.3 %collective-permute-start.5 = (bf16[5,16,8,128]{3,1,2,0:T(8,128)(2,1)S(1)}, bf16[5,16,8,128]{3,1,2,0:T(8,128)(2,1)S(1)}, u32[]{:S(2)}, u32[]{:S(2)}) collective-permute-start(bf16[5,16,8,128]{3,1,2,0:T(8,128)(2,1)S(1)} %pad_maximum_fusion.2), channel_id=1, source_target_pairs={{2,0},{4,2},{6,4},{1,3},{3,5},{5,7},{10,8},{12,10},{14,12},{9,11},... | collective-permute-start | bytes 491528 | tf_op jit(solution)/shard_map/ppermute | solution.py:209
  21.8 4.6 %collective-permute-start.6 = (bf16[3,12,8,128]{3,1,2,0:T(8,128)(2,1)S(1)}, bf16[3,12,8,128]{3,1,2,0:T(8,128)(2,1)S(1)}, u32[]{:S(2)}, u32[]{:S(2)}) collective-permute-start(bf16[3,12,8,128]{3,1,2,0:T(8,128)(2,1)S(1)} %dynamic-slice_maximum_fusion), channel_id=1, source_target_pairs={{0,2},{2,4},{4,6},{3,1},{5,3},{7,5},{8,10},{10,12},{12,14},{11,9},... | collective-permute-start | bytes 221192 | tf_op jit(solution)/shard_map/ppermute | solution.py:209
  26.3 1.8 %collective-permute-start.13 = (bf16[24,16,8,128]{3,0,2,1:T(8,128)(2,1)}, bf16[24,16,8,128]{3,0,2,1:T(8,128)(2,1)}, u32[]{:S(2)}, u32[]{:S(2)}) collective-permute-start(bf16[24,16,8,128]{3,0,2,1:T(8,128)(2,1)} %get-tuple-element.19), channel_id=1, source_target_pairs={{0,16},{8,24},{16,0},{24,8},{1,17},{9,25},{17,1},{25,9},{2,18},{10... | collective-permute-start | bytes 2359304 | tf_op jit(solution)/shard_map/ppermute | solution.py:255
  28.9 3.6 %collective-permute-start.7 = (bf16[196,8,128]{2,1,0:T(8,128)(2,1)S(1)}, bf16[196,8,128]{2,1,0:T(8,128)(2,1)S(1)}, u32[]{:S(2)}, u32[]{:S(2)}) collective-permute-start(bf16[196,8,128]{2,1,0:T(8,128)(2,1)S(1)} %pad_maximum_fusion.1.refs_6_), channel_id=1, source_target_pairs={{0,1},{1,0},{2,3},{3,2},{4,5},{5,4},{6,7},{7,6},{8,9},{9,8},{10,11... | collective-permute-start | bytes 1204232 | tf_op jit(solution)/shard_map/ppermute | solution.py:209
  32.9 16.9 %collective-permute-done.refs_1_ = bf16[12,16,8,128]{3,2,1,0:T(8,128)(2,1)S(1)} collective-permute-done((bf16[12,16,8,128]{3,2,1,0:T(8,128)(2,1)S(1)}, bf16[12,16,8,128]{3,2,1,0:T(8,128)(2,1)S(1)}, u32[]{:S(2)}, u32[]{:S(2)}) %collective-permute-start) | collective-permute-done | bytes 393248 | tf_op jit(solution)/shard_map/ppermute | solution.py:209
  49.8 3.4 %collective-permute-start.3 = (bf16[12,16,8,128]{3,2,1,0:T(8,128)(2,1)S(1)}, bf16[12,16,8,128]{3,2,1,0:T(8,128)(2,1)S(1)}, u32[]{:S(2)}, u32[]{:S(2)}) collective-permute-start(bf16[12,16,8,128]{3,2,1,0:T(8,128)(2,1)S(1)} %collective-permute-done.refs_1_), channel_id=1, source_target_pairs={{0,2},{2,4},{4,6},{3,1},{5,3},{7,5},{8,10},{10,12},{12,14},{11,9},... | collective-permute-start | bytes 1179656 | tf_op jit(solution)/shard_map/ppermute | solution.py:209
  54.5 1.3 %collective-permute-start.4 = (bf16[12,12,8,128]{3,2,1,0:T(8,128)(2,1)}, bf16[12,12,8,128]{3,2,1,0:T(8,128)(2,1)}, u32[]{:S(2)}, u32[]{:S(2)}) collective-permute-start(bf16[12,12,8,128]{3,2,1,0:T(8,128)(2,1)} %constant_dynamic-slice_fusion), channel_id=1, source_target_pairs={{2,0},{4,2},{6,4},{1,3},{3,5},{5,7},{10,8},{12,10},{14,12},{9,11},... | collective-permute-start | bytes 884744 | tf_op jit(solution)/shard_map/ppermute | solution.py:209
  56.0 2.2 %constant_dynamic-update-slice_fusion.6 = bf16[96,16,8,128]{3,0,2,1:T(8,128)(2,1)} fusion(bf16[96,16,8,128]{3,0,2,1:T(8,128)(2,1)} %get-tuple-element.20, bf16[24,16,8,128]{3,0,2,1:T(8,128)(2,1)} %collective-permute-done.12), kind=kLoop, calls=%fused_computation.22 | loop fusion | bytes 1572864
  58.2 2.2 %constant_dynamic-update-slice_fusion.5 = bf16[96,16,8,128]{3,0,2,1:T(8,128)(2,1)} fusion(bf16[96,16,8,128]{3,0,2,1:T(8,128)(2,1)} %constant_dynamic-update-slice_fusion.6, bf16[24,16,8,128]{3,0,2,1:T(8,128)(2,1)} %collective-permute-done.13), kind=kLoop, calls=%fused_computation.21 | loop fusion | bytes 1572864
  60.4 5.3 %collective-permute-done.4.refs_5_ = bf16[12,12,8,128]{3,2,1,0:T(8,128)(2,1)} collective-permute-done((bf16[12,12,8,128]{3,2,1,0:T(8,128)(2,1)}, bf16[12,12,8,128]{3,2,1,0:T(8,128)(2,1)}, u32[]{:S(2)}, u32[]{:S(2)}) %collective-permute-start.4) | collective-permute-done | bytes 294944 | tf_op jit(solution)/shard_map/ppermute | solution.py:209
  65.7 9.7 %march.3 = (f32[6,16,8,128]{3,2,1,0:T(8,128)S(1)}, bf16[6,16,8,128]{3,2,1,0:T(8,128)(2,1)S(1)}) custom-call(s32[26]{0:T(128)S(1)} %pad_add_fusion.scalars, bf16[12,16,8,128]{3,2,1,0:T(8,128)(2,1)S(1)} %get-tuple-element.22.refs_0_, bf16[12,16,8,128]{3,2,1,0:T(8,128)(2,1)S(1)} %collective-permute-done.refs_1_, ...), custom_call_target="tpu_custom_call" | custom-call | flops 4325376000 | bytes 2162688 | tf_op jit(solution)/shard_map/march/pallas_call | solution.py:181
  75.5 9.8 %march.2 = (f32[6,16,8,128]{3,2,1,0:T(8,128)S(1)}, bf16[6,16,8,128]{3,2,1,0:T(8,128)(2,1)S(1)}) custom-call(s32[26]{0:T(128)S(1)} %pad_add_fusion.scalars, bf16[12,16,8,128]{3,2,1,0:T(8,128)(2,1)S(1)} %get-tuple-element.22.refs_0_, bf16[12,16,8,128]{3,2,1,0:T(8,128)(2,1)S(1)} %collective-permute-done.refs_1_, ...), custom_call_target="tpu_custom_call" | custom-call | flops 4325376000 | bytes 2162688 | tf_op jit(solution)/shard_map/march/pallas_call | solution.py:181
  85.3 2.1 %collective-permute-start.10 = (bf16[6,16,8,128]{3,2,1,0:T(8,128)(2,1)S(1)}, bf16[6,16,8,128]{3,2,1,0:T(8,128)(2,1)S(1)}, u32[]{:S(2)}, u32[]{:S(2)}) collective-permute-start(bf16[6,16,8,128]{3,2,1,0:T(8,128)(2,1)S(1)} %get-tuple-element.14), channel_id=1, source_target_pairs={{0,1},{1,0},{2,3},{3,2},{4,5},{5,4},{6,7},{7,6},{8,9},{9,8},{10,11... | collective-permute-start | bytes 589832 | tf_op jit(solution)/shard_map/ppermute | solution.py:209
  87.4 4.0 %collective-permute-done.10 = bf16[6,16,8,128]{3,2,1,0:T(8,128)(2,1)S(1)} collective-permute-done((bf16[6,16,8,128]{3,2,1,0:T(8,128)(2,1)S(1)}, bf16[6,16,8,128]{3,2,1,0:T(8,128)(2,1)S(1)}, u32[]{:S(2)}, u32[]{:S(2)}) %collective-permute-start.10) | collective-permute-done | bytes 196640 | tf_op jit(solution)/shard_map/ppermute | solution.py:209
  94.3 1.8 %collective-permute-start.15 = (f32[96,24]{0,1:T(8,128)S(1)}, f32[96,24]{0,1:T(8,128)S(1)}, u32[]{:S(2)}, u32[]{:S(2)}) collective-permute-start(f32[96,24]{0,1:T(8,128)S(1)} %select_select_fusion), channel_id=1, source_target_pairs={{0,1},{1,0},{2,3},{3,2},{4,5},{5,4},{6,7},{7,6},{8,9},{9,8},{10,11... | collective-permute-start | bytes 27656 | tf_op jit(solution)/shard_map/ppermute | solution.py:209
  96.1 2.0 %collective-permute-done.15 = f32[96,24]{0,1:T(8,128)S(1)} collective-permute-done((f32[96,24]{0,1:T(8,128)S(1)}, f32[96,24]{0,1:T(8,128)S(1)}, u32[]{:S(2)}, u32[]{:S(2)}) %collective-permute-start.15) | collective-permute-done | bytes 9248 | tf_op jit(solution)/shard_map/ppermute | solution.py:209
  98.1 2.0 %collective-permute-start.16 = (f32[96,24]{0,1:T(8,128)S(1)}, f32[96,24]{0,1:T(8,128)S(1)}, u32[]{:S(2)}, u32[]{:S(2)}) collective-permute-start(f32[96,24]{0,1:T(8,128)S(1)} %add.64), channel_id=1, source_target_pairs={{0,2},{1,3},{2,0},{3,1},{4,6},{5,7},{6,4},{7,5},{8,10},{9,11},{10,... | collective-permute-start | bytes 27656 | tf_op jit(solution)/shard_map/ppermute | solution.py:209
  100.1 1.8 %collective-permute-done.16 = f32[96,24]{0,1:T(8,128)S(1)} collective-permute-done((f32[96,24]{0,1:T(8,128)S(1)}, f32[96,24]{0,1:T(8,128)S(1)}, u32[]{:S(2)}, u32[]{:S(2)}) %collective-permute-start.16) | collective-permute-done | bytes 9248 | tf_op jit(solution)/shard_map/ppermute | solution.py:209
  101.9 2.8 %collective-permute-start.17 = (f32[96,24]{0,1:T(8,128)S(1)}, f32[96,24]{0,1:T(8,128)S(1)}, u32[]{:S(2)}, u32[]{:S(2)}) collective-permute-start(f32[96,24]{0,1:T(8,128)S(1)} %add.65), channel_id=1, source_target_pairs={{0,4},{1,5},{2,6},{3,7},{4,0},{5,1},{6,2},{7,3},{8,12},{9,13},{10,... | collective-permute-start | bytes 27656 | tf_op jit(solution)/shard_map/ppermute | solution.py:209
  104.7 1.2 %pad_maximum_fusion = f32[24,16,8,128]{3,2,1,0:T(8,128)} fusion(f32[12,16,8,128]{3,2,1,0:T(8,128)S(1)} %get-tuple-element.17, f32[12,16,8,128]{3,2,1,0:T(8,128)S(1)} %get-tuple-element.16), kind=kLoop, calls=%fused_computation.2 | loop fusion | flops 393216 | bytes 3145728 | tf_op jit(solution)/shard_map/concatenate | solution.py:266
  (75 shorter events, 10.4 us)
Async XLA Ops:
  0.6 12.2 %copy-start = (s32[8]{0:T(128)S(1)}, s32[8]{0:T(128)}, u32[]{:S(2)}) copy-start(s32[8]{0:T(128)} %param.14) | copy-start | bytes 100
  0.6 12.8 %copy-start.5 = (bf16[8,16,2,128]{3,2,1,0:T(2,128)(2,1)S(1)}, bf16[8,16,2,128]{3,2,1,0:T(2,128)(2,1)}, u32[]{:S(2)}) copy-start(bf16[8,16,2,128]{3,2,1,0:T(2,128)(2,1)} %param.13) | copy-start | bytes 196612
  0.7 19.6 %copy-start.4 = (f32[16,8,128]{2,1,0:T(8,128)S(1)}, f32[16,8,128]{2,1,0:T(8,128)}, u32[]{:S(2)}) copy-start(f32[16,8,128]{2,1,0:T(8,128)} %param.12) | copy-start | bytes 196612
  1.9 18.5 %collective-permute-start.1 = (bf16[12,16,8,128]{3,2,1,0:T(8,128)(2,1)S(1)}, bf16[12,16,8,128]{3,2,1,0:T(8,128)(2,1)S(1)}, u32[]{:S(2)}, u32[]{:S(2)}) collective-permute-start(bf16[12,16,8,128]{3,2,1,0:T(8,128)(2,1)S(1)} %get-tuple-element.22.refs_0_), channel_id=1, source_target_pairs={{2,0},{4,2},{6,4},{1,3},{3,5},{5,7},{10,8},{12,10},{14,12},{9,11},... | collective-permute-start | bytes 1179656 | tf_op jit(solution)/shard_map/ppermute | solution.py:209
  4.2 28.4 %copy-start.6 = (s32[24,2]{0,1:T(2,128)S(1)}, s32[24,2]{0,1:T(2,128)}, u32[]{:S(2)}) copy-start(s32[24,2]{0,1:T(2,128)} %param.11) | copy-start | bytes 580
  4.2 16.1 %collective-permute-start.2 = (bf16[12,12,8,128]{3,2,1,0:T(8,128)(2,1)S(1)}, bf16[12,12,8,128]{3,2,1,0:T(8,128)(2,1)S(1)}, u32[]{:S(2)}, u32[]{:S(2)}) collective-permute-start(bf16[12,12,8,128]{3,2,1,0:T(8,128)(2,1)S(1)} %constant_dynamic-slice_fusion.1), channel_id=1, source_target_pairs={{0,2},{2,4},{4,6},{3,1},{5,3},{7,5},{8,10},{10,12},{12,14},{11,9},... | collective-permute-start | bytes 884744 | tf_op jit(solution)/shard_map/ppermute | solution.py:209
  12.8 41.7 %collective-permute-start.12 = (bf16[24,16,8,128]{3,0,2,1:T(8,128)(2,1)}, bf16[24,16,8,128]{3,0,2,1:T(8,128)(2,1)}, u32[]{:S(2)}, u32[]{:S(2)}) collective-permute-start(bf16[24,16,8,128]{3,0,2,1:T(8,128)(2,1)} %get-tuple-element.19), channel_id=1, source_target_pairs={{0,8},{8,0},{16,24},{24,16},{1,9},{9,1},{17,25},{25,17},{2,10},{10... | collective-permute-start | bytes 2359304 | tf_op jit(solution)/shard_map/ppermute | solution.py:255
  20.3 45.4 %copy-start.2 = (bf16[256,128]{1,0:T(8,128)(2,1)S(1)}, bf16[256,128]{1,0:T(8,128)(2,1)}, u32[]{:S(2)}) copy-start(bf16[256,128]{1,0:T(8,128)(2,1)} %constant.101.clone.refs_11_) | copy-start | bytes 196612
  20.4 8.4 %collective-permute-start.5 = (bf16[5,16,8,128]{3,1,2,0:T(8,128)(2,1)S(1)}, bf16[5,16,8,128]{3,1,2,0:T(8,128)(2,1)S(1)}, u32[]{:S(2)}, u32[]{:S(2)}) collective-permute-start(bf16[5,16,8,128]{3,1,2,0:T(8,128)(2,1)S(1)} %pad_maximum_fusion.2), channel_id=1, source_target_pairs={{2,0},{4,2},{6,4},{1,3},{3,5},{5,7},{10,8},{12,10},{14,12},{9,11},... | collective-permute-start | bytes 491528 | tf_op jit(solution)/shard_map/ppermute | solution.py:209
  21.8 6.9 %collective-permute-start.6 = (bf16[3,12,8,128]{3,1,2,0:T(8,128)(2,1)S(1)}, bf16[3,12,8,128]{3,1,2,0:T(8,128)(2,1)S(1)}, u32[]{:S(2)}, u32[]{:S(2)}) collective-permute-start(bf16[3,12,8,128]{3,1,2,0:T(8,128)(2,1)S(1)} %dynamic-slice_maximum_fusion), channel_id=1, source_target_pairs={{0,2},{2,4},{4,6},{3,1},{5,3},{7,5},{8,10},{10,12},{12,14},{11,9},... | collective-permute-start | bytes 221192 | tf_op jit(solution)/shard_map/ppermute | solution.py:209
  26.3 29.5 %collective-permute-start.13 = (bf16[24,16,8,128]{3,0,2,1:T(8,128)(2,1)}, bf16[24,16,8,128]{3,0,2,1:T(8,128)(2,1)}, u32[]{:S(2)}, u32[]{:S(2)}) collective-permute-start(bf16[24,16,8,128]{3,0,2,1:T(8,128)(2,1)} %get-tuple-element.19), channel_id=1, source_target_pairs={{0,16},{8,24},{16,0},{24,8},{1,17},{9,25},{17,1},{25,9},{2,18},{10... | collective-permute-start | bytes 2359304 | tf_op jit(solution)/shard_map/ppermute | solution.py:255
  28.9 24.3 %collective-permute-start.7 = (bf16[196,8,128]{2,1,0:T(8,128)(2,1)S(1)}, bf16[196,8,128]{2,1,0:T(8,128)(2,1)S(1)}, u32[]{:S(2)}, u32[]{:S(2)}) collective-permute-start(bf16[196,8,128]{2,1,0:T(8,128)(2,1)S(1)} %pad_maximum_fusion.1.refs_6_), channel_id=1, source_target_pairs={{0,1},{1,0},{2,3},{3,2},{4,5},{5,4},{6,7},{7,6},{8,9},{9,8},{10,11... | collective-permute-start | bytes 1204232 | tf_op jit(solution)/shard_map/ppermute | solution.py:209
  32.5 17.2 %collective-permute-start = (bf16[12,16,8,128]{3,2,1,0:T(8,128)(2,1)S(1)}, bf16[12,16,8,128]{3,2,1,0:T(8,128)(2,1)S(1)}, u32[]{:S(2)}, u32[]{:S(2)}) collective-permute-start(bf16[12,16,8,128]{3,2,1,0:T(8,128)(2,1)S(1)} %get-tuple-element.21), channel_id=1, source_target_pairs={{0,1},{1,0},{2,3},{3,2},{4,5},{5,4},{6,7},{7,6},{8,9},{9,8},{10,11... | collective-permute-start | bytes 1179656 | tf_op jit(solution)/shard_map/ppermute | solution.py:209
  49.8 15.9 %collective-permute-start.3 = (bf16[12,16,8,128]{3,2,1,0:T(8,128)(2,1)S(1)}, bf16[12,16,8,128]{3,2,1,0:T(8,128)(2,1)S(1)}, u32[]{:S(2)}, u32[]{:S(2)}) collective-permute-start(bf16[12,16,8,128]{3,2,1,0:T(8,128)(2,1)S(1)} %collective-permute-done.refs_1_), channel_id=1, source_target_pairs={{0,2},{2,4},{4,6},{3,1},{5,3},{7,5},{8,10},{10,12},{12,14},{11,9},... | collective-permute-start | bytes 1179656 | tf_op jit(solution)/shard_map/ppermute | solution.py:209
  53.1 12.5 %collective-permute-start.8 = (bf16[196,8,128]{2,1,0:T(8,128)(2,1)S(1)}, bf16[196,8,128]{2,1,0:T(8,128)(2,1)S(1)}, u32[]{:S(2)}, u32[]{:S(2)}) collective-permute-start(bf16[196,8,128]{2,1,0:T(8,128)(2,1)S(1)} %pad_maximum_fusion.1.refs_6_), channel_id=1, source_target_pairs={{0,8},{8,0},{16,24},{24,16},{1,9},{9,1},{17,25},{25,17},{2,10},{10... | collective-permute-start | bytes 1204232 | tf_op jit(solution)/shard_map/ppermute | solution.py:210
  53.2 12.5 %collective-permute-start.9 = (bf16[196,8,128]{2,1,0:T(8,128)(2,1)S(1)}, bf16[196,8,128]{2,1,0:T(8,128)(2,1)S(1)}, u32[]{:S(2)}, u32[]{:S(2)}) collective-permute-start(bf16[196,8,128]{2,1,0:T(8,128)(2,1)S(1)} %collective-permute-done.7.refs_7_), channel_id=1, source_target_pairs={{0,8},{8,0},{16,24},{24,16},{1,9},{9,1},{17,25},{25,17},{2,10},{10... | collective-permute-start | bytes 1204232 | tf_op jit(solution)/shard_map/ppermute | solution.py:210
  54.5 11.2 %collective-permute-start.4 = (bf16[12,12,8,128]{3,2,1,0:T(8,128)(2,1)}, bf16[12,12,8,128]{3,2,1,0:T(8,128)(2,1)}, u32[]{:S(2)}, u32[]{:S(2)}) collective-permute-start(bf16[12,12,8,128]{3,2,1,0:T(8,128)(2,1)} %constant_dynamic-slice_fusion), channel_id=1, source_target_pairs={{2,0},{4,2},{6,4},{1,3},{3,5},{5,7},{10,8},{12,10},{14,12},{9,11},... | collective-permute-start | bytes 884744 | tf_op jit(solution)/shard_map/ppermute | solution.py:209
  55.8 9.9 %copy-start.1 = (bf16[192,256]{1,0:T(8,128)(2,1)S(1)}, bf16[192,256]{1,0:T(8,128)(2,1)}, u32[]{:S(2)}) copy-start(bf16[192,256]{1,0:T(8,128)(2,1)} %constant.100.clone.refs_10_) | copy-start | bytes 294916
  55.8 35.9 %collective-permute-start.14 = (bf16[24,16,8,128]{3,0,2,1:T(8,128)(2,1)}, bf16[24,16,8,128]{3,0,2,1:T(8,128)(2,1)S(1)}, u32[]{:S(2)}, u32[]{:S(2)}) collective-permute-start(bf16[24,16,8,128]{3,0,2,1:T(8,128)(2,1)} %collective-permute-done.13), channel_id=1, source_target_pairs={{0,8},{8,0},{16,24},{24,16},{1,9},{9,1},{17,25},{25,17},{2,10},{10... | collective-permute-start | bytes 2359304 | tf_op jit(solution)/shard_map/ppermute | solution.py:255
  75.4 16.0 %collective-permute-start.11 = (bf16[6,16,8,128]{3,2,1,0:T(8,128)(2,1)S(1)}, bf16[6,16,8,128]{3,2,1,0:T(8,128)(2,1)S(1)}, u32[]{:S(2)}, u32[]{:S(2)}) collective-permute-start(bf16[6,16,8,128]{3,2,1,0:T(8,128)(2,1)S(1)} %get-tuple-element.15), channel_id=1, source_target_pairs={{0,1},{1,0},{2,3},{3,2},{4,5},{5,4},{6,7},{7,6},{8,9},{9,8},{10,11... | collective-permute-start | bytes 589832 | tf_op jit(solution)/shard_map/ppermute | solution.py:209
  85.3 6.1 %collective-permute-start.10 = (bf16[6,16,8,128]{3,2,1,0:T(8,128)(2,1)S(1)}, bf16[6,16,8,128]{3,2,1,0:T(8,128)(2,1)S(1)}, u32[]{:S(2)}, u32[]{:S(2)}) collective-permute-start(bf16[6,16,8,128]{3,2,1,0:T(8,128)(2,1)S(1)} %get-tuple-element.14), channel_id=1, source_target_pairs={{0,1},{1,0},{2,3},{3,2},{4,5},{5,4},{6,7},{7,6},{8,9},{9,8},{10,11... | collective-permute-start | bytes 589832 | tf_op jit(solution)/shard_map/ppermute | solution.py:209
  94.3 3.8 %collective-permute-start.15 = (f32[96,24]{0,1:T(8,128)S(1)}, f32[96,24]{0,1:T(8,128)S(1)}, u32[]{:S(2)}, u32[]{:S(2)}) collective-permute-start(f32[96,24]{0,1:T(8,128)S(1)} %select_select_fusion), channel_id=1, source_target_pairs={{0,1},{1,0},{2,3},{3,2},{4,5},{5,4},{6,7},{7,6},{8,9},{9,8},{10,11... | collective-permute-start | bytes 27656 | tf_op jit(solution)/shard_map/ppermute | solution.py:209
  98.1 3.8 %collective-permute-start.16 = (f32[96,24]{0,1:T(8,128)S(1)}, f32[96,24]{0,1:T(8,128)S(1)}, u32[]{:S(2)}, u32[]{:S(2)}) collective-permute-start(f32[96,24]{0,1:T(8,128)S(1)} %add.64), channel_id=1, source_target_pairs={{0,2},{1,3},{2,0},{3,1},{4,6},{5,7},{6,4},{7,5},{8,10},{9,11},{10,... | collective-permute-start | bytes 27656 | tf_op jit(solution)/shard_map/ppermute | solution.py:209
  101.9 4.6 %collective-permute-start.17 = (f32[96,24]{0,1:T(8,128)S(1)}, f32[96,24]{0,1:T(8,128)S(1)}, u32[]{:S(2)}, u32[]{:S(2)}) collective-permute-start(f32[96,24]{0,1:T(8,128)S(1)} %add.65), channel_id=1, source_target_pairs={{0,4},{1,5},{2,6},{3,7},{4,0},{5,1},{6,2},{7,3},{8,12},{9,13},{10,... | collective-permute-start | bytes 27656 | tf_op jit(solution)/shard_map/ppermute | solution.py:209
  (1 other events, 6.4 us)

commit v4 on v3

--- a/solution.py
+++ b/solution.py
@@ -51,13 +51,14 @@
 
 def march(steps, rows, halo, begin, scalars, *refs):
     pieces = refs[0:6]
-    extras = refs[6:10]
-    left_ref, right_ref, own_ref, send_ref = refs[10:14]
-    pert, snap, scale, gain, fields, split = refs[14:20]
+    near_ref, near_x_ref, other_ref, first_ref, second_ref = refs[6:11]
+    left_ref, right_ref, own_ref, send_ref = refs[11:15]
+    pert, snap, scale, gain, fields, split = refs[15:21]
     total = 2 * rows + 2 * halo
     cy = 8
     far = halo - rows
     par, core = scalars[0], scalars[1]
+    probes = pieces[0].shape[0]
     even = (halo, halo + rows, halo + 2 * rows, 0, halo - rows, halo + 3 * rows)
     odd = (halo + rows, halo, halo - rows, halo + 3 * rows, halo + 2 * rows, 0)
     counts = (rows, rows, rows, far, rows, far)
@@ -66,21 +67,27 @@
 
     @pl.when(pl.program_id(0) == 0)
     def _():
-        for side, order in ((0, (0, 2, 3)), (1, (1, 4, 5))):
-            at = 0
-            for j, kept in zip(order, (near_half, near_half, far_half)):
-                where = pl.ds(pl.multiple_of(starts[j] * cy, 32), counts[j] * cy)
-                flat = (counts[j] * cy, 128)
-                for t in range(kept + 1):
-                    mine = extras[side][at : at + counts[j]].reshape(flat).astype(jnp.float32)
-                    other = extras[side + 2][at : at + counts[j]].reshape(flat).astype(jnp.float32)
-                    at += counts[j]
-                    if t < kept:
-                        snap[2 * t + core, where, :] = mine
-                        snap[2 * t + 1 - core, where, :] = other
-                    else:
-                        scale[where, :] = 2.0 + (3.0 * taps[0]) * (mine + other)
-                        gain[where, :] = taps[1] * (mine + other)
+        sizes = [(near_half + 1) * rows, (near_half + 1) * rows, (far_half + 1) * far]
+        for j in range(6):
+            kept = far_half if j in (3, 5) else near_half
+            where = pl.ds(pl.multiple_of(starts[j] * cy, 32), counts[j] * cy)
+            for t in range(kept + 1):
+                at = t * counts[j]
+                if j == 0:
+                    mine, other = near_ref[t], other_ref[t]
+                else:
+                    mine = near_x_ref[t] if j == 1 else pieces[j][probes + t]
+                    held = first_ref if j < 4 else second_ref
+                    at += sum(sizes[: j - 1]) if j < 4 else sum(sizes[1 : j - 3])
+                    other = held[at : at + counts[j]]
+                mine = mine.reshape(counts[j] * cy, 128).astype(jnp.float32)
+                other = other.reshape(counts[j] * cy, 128).astype(jnp.float32)
+                if t < kept:
+                    snap[2 * t + core, where, :] = mine
+                    snap[2 * t + 1 - core, where, :] = other
+                else:
+                    scale[where, :] = 2.0 + (3.0 * taps[0]) * (mine + other)
+                    gain[where, :] = taps[1] * (mine + other)
 
     for q in range(PACK):
         probe = begin + pl.program_id(0) * PACK + q
@@ -185,7 +192,7 @@
             jax.ShapeDtypeStruct((count, rows, cy, cz), jnp.float32),
             jax.ShapeDtypeStruct((count, rows, cy, cz), jnp.bfloat16),
         ],
-        compiler_params=pltpu.CompilerParams(vmem_limit_bytes=40 << 20),
+        compiler_params=pltpu.CompilerParams(vmem_limit_bytes=20 << 20),
         cost_estimate=pl.CostEstimate(flops=cells * 8000, bytes_accessed=cells * 4, transcendentals=0),
         name="march",
     )(scalars, *pieces, *extras, left, right)
@@ -218,45 +225,44 @@
     high = lax.reduce_precision(courant, 8, 7)
     rate = jnp.where(core == 0, high, courant - high).astype(jnp.bfloat16)[None]
     extra = jnp.concatenate([picked, rate], axis=0)
+    trim = lambda x: jnp.concatenate([x[:far_half], x[near_half:]], axis=0)
+    planes = lambda *xs: jnp.concatenate([x.reshape(-1, cy, cz) for x in xs], axis=0)
     mine = lax.dynamic_slice_in_dim(probe_field, half * par, half, axis=0)
     theirs = lax.dynamic_slice_in_dim(probe_field, half * (1 - par), half, axis=0)
     partner = hop(theirs, swap)
-    side_a = hop(mine, perm_a)
-    side_b = hop(cut(mine, near * (1 - par)), perm_b)
-    extra, side_a, side_b = lax.optimization_barrier((extra, side_a, side_b))
-    extra_a = hop(extra, perm_a)
-    tail = jnp.concatenate([extra[:far_half], extra[near_half:]], axis=0)
-    extra_b = hop(cut(tail, near * (1 - par)), perm_b)
-    planes = lambda x: x.reshape(-1, cy, cz)
-    bundle = jnp.concatenate([planes(extra), planes(extra_a), planes(extra_b)], axis=0)
-    bundle_x = hop(bundle, swap)
-    extras = (bundle, bundle_x, cores(bundle), cores(bundle_x))
-    pieces = (
-        mine,
-        partner,
-        side_a,
-        side_b,
-        hop(partner, perm_b),
-        hop(cut(partner, near * par), perm_a),
+    side_a = hop(jnp.concatenate([mine, extra], axis=0), perm_a)
+    side_b = hop(cut(jnp.concatenate([mine, trim(extra)], axis=0), near * (1 - par)), perm_b)
+    extra_x = hop(lax.optimization_barrier((extra, partner))[0], swap)
+    side_c = hop(jnp.concatenate([partner, extra_x], axis=0), perm_b)
+    side_d = hop(cut(jnp.concatenate([partner, trim(extra_x)], axis=0), near * par), perm_a)
+    pieces = (mine, partner, side_a, side_b, side_c, side_d)
+    extras = (
+        extra,
+        extra_x,
+        cores(extra),
+        cores(planes(extra_x, side_a[half:], side_b[half:])),
+        cores(planes(side_c[half:], side_d[half:])),
     )
     base = (place // 2) * 2 * rows - halo
     mine_bounds = lax.dynamic_slice_in_dim(bounds, half * par, half, axis=0) - base
     scalars = jnp.concatenate([jnp.stack([par, core]), mine_bounds.reshape(-1)]).astype(jnp.int32)
+    basis_later = lax.optimization_barrier((basis_panels, extra_x))[0]
+    crossed = lax.ppermute(basis_later, "probe", [(i, i ^ 2) for i in range(members)])
     first = par == 0
     own, back = [], []
     for begin, count in ((0, half // 2), (half // 2, half - half // 2)):
         kept, sent = propagate(scalars, pieces, extras, begin, count, steps, rows, halo)
         own.append(kept)
         back.append(hop(sent, swap))
-    panels = [basis_panels]
-    span = members // 2
-    while span:
-        pairs = [(i, i ^ span) for i in range(members)]
-        panels = [y for x in panels for y in (x, lax.ppermute(x, "probe", pairs))]
-        span //= 2
-    panels = jnp.concatenate(panels, axis=0)
-    dots = lambda x: lax.dot_general(
-        panels, x, (((1, 2, 3), (1, 2, 3)), ((), ())), preferred_element_type=jnp.float32
+    panels = [basis_later, cores(basis_later)]
+    crossed = lax.optimization_barrier((crossed, own[0]))[0]
+    panels = [jnp.concatenate(panels, axis=0), jnp.concatenate([crossed, cores(crossed)], axis=0)]
+    dots = lambda x: jnp.concatenate(
+        [
+            lax.dot_general(y, x, (((1, 2, 3), (1, 2, 3)), ((), ())), preferred_element_type=jnp.float32)
+            for y in panels
+        ],
+        axis=0,
     )
     own = jnp.concatenate(own, axis=0)
     mine_part = dots(own.astype(jnp.bfloat16))

time: 108 us -> 95.4 us (0.88)
  starting transfers between devices: 32.3 us -> 24.2 us
  other arithmetic: 2.43 us -> 6.57 us
  waiting for transfers between devices: 31 us -> 26.9 us
  local copies, waits for them, and re-layouts: 12.7 us -> 8.98 us
    ppermute x13 -> x11, starting transfers between devices: 29.8 us -> 22 us  [local(): hop = lambda x, pairs: lax.ppermute(x, 'store', pairs)]
    unnamed x20 -> x21, local copies, waits for them, and re-layouts: 7.45 us -> 3.06 us
    ppermute x13 -> x11, waiting for transfers between devices: 31 us -> 26.8 us  [local(): hop = lambda x, pairs: lax.ppermute(x, 'store', pairs)]
    concatenate x2 -> x6, other arithmetic: 0.09 us -> 4.1 us  [the longest x2 1.53 us: local(): jnp.concatenate([x.reshape(-1, cy, cz) for x in xs], axis=0)]
    concatenate x1 -> x4, local copies, waits for them, and re-layouts: 0.15 us -> 2.53 us  [the longest x1 2.19 us: local(): jnp.concatenate(panels, axis=0)]
    dynamic_slice x2 -> x0, local copies, waits for them, and re-layouts: 1.75 us -> none  [local(): cut = lambda x, start: lax.dynamic_slice_in_dim(x, start, far, axis=1)]
  transfers between devices with their start and end apart: 18 -> 17, of which waited for: 8 -> 7; matrix products, arithmetic and copies ran while one was open for 12% -> 14% of each run, Pallas kernels for 18% -> 20%
where the time goes in v4:
time: 95.4 us; the launch traced here: 95.1 us
  waiting for transfers between devices  26.9 us (28%)
  starting transfers between devices  24.2 us (25%)
  Pallas kernels  19.5 us (20%)
  local copies, waits for them, and re-layouts  8.98 us (9%)
  other arithmetic  6.57 us (7%)
  blocking collectives  5.79 us (6%)
  matrix products  2.12 us (2%)
  between operations  1.09 us (1%)
    ppermute x11, waiting for transfers between devices, local(): hop = lambda x, pairs: lax.ppermute(x, 'store', pairs)  26.8 us
    ppermute x11, starting transfers between devices, local(): hop = lambda x, pairs: lax.ppermute(x, 'store', pairs)  22 us
    pallas_call x2, Pallas kernels, propagate(): pl.pallas_call(functools.partial(march, steps, rows, halo, begin), grid_s...  19.5 us
    all_gather x1, blocking collectives, local(): all_snaps = lax.all_gather(snapshots, 'probe', axis=2, tiled=True)  5.79 us
    unnamed x21, local copies, waits for them, and re-layouts  3.06 us
    concatenate x1, local copies, waits for them, and re-layouts, local(): jnp.concatenate(panels, axis=0)  2.19 us
    dot_general x4, matrix products, local(): lax.dot_general(y, x, (((1, 2, 3), (1, 2, 3)), ((), ())), preferred_eleme...  2.12 us
  transfers between devices with their start and end apart: 17, of which 7 were waited for; matrix products, arithmetic and copies ran while one was open for 14% of the time, Pallas kernels for 20%

profile of v4, /device:TPU:0, one launch (start us, length us, event | category | flops | bytes accessed | tf_op | source)
XLA Modules:
  0.0 95.1 jit_solution(13640119417939799038)
XLA Ops:
  0.7 1.2 %constant_dynamic-slice_fusion = (bf16[12,16,8,128]{3,2,1,0:T(8,128)(2,1)S(1)}, bf16[12,16,8,128]{3,2,1,0:T(8,128)(2,1)S(1)}) fusion(bf16[24,16,8,128]{3,2,1,0:T(8,128)(2,1)} %param.10, s32[]{:T(128)S(6)} %select_n.140, s32[]{:T(128)S(6)} %select_n.138), kind=kLoop, calls=%fused_computation.49 | loop fusion | bytes 1572872 | tf_op jit(solution)/shard_map/dynamic_slice | solution.py:231
  1.9 3.0 %collective-permute-start = (bf16[12,16,8,128]{3,2,1,0:T(8,128)(2,1)S(1)}, bf16[12,16,8,128]{3,2,1,0:T(8,128)(2,1)S(1)}, u32[]{:S(2)}, u32[]{:S(2)}) collective-permute-start(bf16[12,16,8,128]{3,2,1,0:T(8,128)(2,1)S(1)} %get-tuple-element.21), channel_id=1, source_target_pairs={{0,1},{1,0},{2,3},{3,2},{4,5},{5,4},{6,7},{7,6},{8,9},{9,8},{10,11... | collective-permute-start | bytes 1179656 | tf_op jit(solution)/shard_map/ppermute | solution.py:216
  5.6 5.8 %all_gather.3 = bf16[8,16,8,128]{3,1,0,2:T(8,128)(2,1)S(1)} all-gather(bf16[8,16,2,128]{3,1,0,2:T(8,128)(2,1)S(1)} %copy.38), channel_id=1, replica_groups=mesh['probe'=4,'store'=8] {'probe'}, dimensions={2}, use_global_device_ids=true | all-gather | bytes 327680 | tf_op jit(solution)/shard_map/all_gather | solution.py:221
  12.2 1.8 %collective-permute-done.refs_1_ = bf16[12,16,8,128]{3,2,1,0:T(8,128)(2,1)S(1)} collective-permute-done((bf16[12,16,8,128]{3,2,1,0:T(8,128)(2,1)S(1)}, bf16[12,16,8,128]{3,2,1,0:T(8,128)(2,1)S(1)}, u32[]{:S(2)}, u32[]{:S(2)}) %collective-permute-start) | collective-permute-done | bytes 393248 | tf_op jit(solution)/shard_map/ppermute | solution.py:216
  14.0 1.7 %collective-permute-start.3 = (bf16[5,16,8,128]{3,2,1,0:T(8,128)(2,1)S(1)}, bf16[5,16,8,128]{3,2,1,0:T(8,128)(2,1)S(1)}, u32[]{:S(2)}, u32[]{:S(2)}) collective-permute-start(bf16[5,16,8,128]{3,2,1,0:T(8,128)(2,1)S(1)} %pad_maximum_fusion.5.refs_6_), channel_id=1, source_target_pairs={{0,1},{1,0},{2,3},{3,2},{4,5},{5,4},{6,7},{7,6},{8,9},{9,8},{10,11... | collective-permute-start | bytes 491528 | tf_op jit(solution)/shard_map/ppermute | solution.py:216
  16.6 3.5 %collective-permute-start.2 = (bf16[15,12,8,128]{3,2,1,0:T(8,128)(2,1)}, bf16[15,12,8,128]{3,2,1,0:T(8,128)(2,1)S(1)}, u32[]{:S(2)}, u32[]{:S(2)}) collective-permute-start(bf16[15,12,8,128]{3,2,1,0:T(8,128)(2,1)} %fusion.7), channel_id=1, source_target_pairs={{0,2},{2,4},{4,6},{3,1},{5,3},{7,5},{8,10},{10,12},{12,14},{11,9},... | collective-permute-start | bytes 1105928 | tf_op jit(solution)/shard_map/ppermute | solution.py:216
  20.2 1.3 %collective-permute-start.1 = (bf16[17,16,8,128]{3,2,1,0:T(8,128)(2,1)S(1)}, bf16[17,16,8,128]{3,2,1,0:T(8,128)(2,1)S(1)}, u32[]{:S(2)}, u32[]{:S(2)}) collective-permute-start(bf16[17,16,8,128]{3,2,1,0:T(8,128)(2,1)S(1)} %pad_maximum_fusion.1), channel_id=1, source_target_pairs={{2,0},{4,2},{6,4},{1,3},{3,5},{5,7},{10,8},{12,10},{14,12},{9,11},... | collective-permute-start | bytes 1671176 | tf_op jit(solution)/shard_map/ppermute | solution.py:216
  22.3 4.6 %collective-permute-start.4 = (bf16[17,16,8,128]{3,2,1,0:T(8,128)(2,1)}, bf16[17,16,8,128]{3,2,1,0:T(8,128)(2,1)S(1)}, u32[]{:S(2)}, u32[]{:S(2)}) collective-permute-start(bf16[17,16,8,128]{3,2,1,0:T(8,128)(2,1)} %pad_maximum_fusion.2), channel_id=1, source_target_pairs={{0,2},{2,4},{4,6},{3,1},{5,3},{7,5},{8,10},{10,12},{12,14},{11,9},... | collective-permute-start | bytes 1671176 | tf_op jit(solution)/shard_map/ppermute | solution.py:216
  26.9 1.7 %constant_dynamic-update-slice_fusion.5 = (bf16[48,16,8,128]{3,0,2,1:T(8,128)(2,1)}, bf16[24,16,8,128]{3,0,2,1:T(8,128)(2,1)}) fusion(bf16[24,16,8,128]{3,2,1,0:T(8,128)(2,1)S(1)} %copy-done.4), kind=kLoop, calls=%fused_computation.38 | loop fusion | bytes 2359296
  29.5 1.3 %collective-permute-start.5 = (bf16[15,12,8,128]{3,2,1,0:T(8,128)(2,1)}, bf16[15,12,8,128]{3,2,1,0:T(8,128)(2,1)S(1)}, u32[]{:S(2)}, u32[]{:S(2)}) collective-permute-start(bf16[15,12,8,128]{3,2,1,0:T(8,128)(2,1)} %fusion.5), channel_id=1, source_target_pairs={{2,0},{4,2},{6,4},{1,3},{3,5},{5,7},{10,8},{12,10},{14,12},{9,11},... | collective-permute-start | bytes 1105928 | tf_op jit(solution)/shard_map/ppermute | solution.py:216
  30.8 1.6 %collective-permute-start.12 = (bf16[24,16,8,128]{3,0,2,1:T(8,128)(2,1)}, bf16[24,16,8,128]{3,0,2,1:T(8,128)(2,1)}, u32[]{:S(2)}, u32[]{:S(2)}) collective-permute-start(bf16[24,16,8,128]{3,0,2,1:T(8,128)(2,1)} %get-tuple-element.20), channel_id=1, source_target_pairs={{0,16},{8,24},{16,0},{24,8},{1,17},{9,25},{17,1},{25,9},{2,18},{10... | collective-permute-start | bytes 2359304 | tf_op jit(solution)/shard_map/ppermute | solution.py:250
  32.4 2.8 %collective-permute-done.1.refs_2_ = bf16[17,16,8,128]{3,2,1,0:T(8,128)(2,1)S(1)} collective-permute-done((bf16[17,16,8,128]{3,2,1,0:T(8,128)(2,1)S(1)}, bf16[17,16,8,128]{3,2,1,0:T(8,128)(2,1)S(1)}, u32[]{:S(2)}, u32[]{:S(2)}) %collective-permute-start.1) | collective-permute-done | bytes 557088 | tf_op jit(solution)/shard_map/ppermute | solution.py:216
  36.3 6.6 %collective-permute-done.5.refs_5_ = bf16[15,12,8,128]{3,2,1,0:T(8,128)(2,1)S(1)} collective-permute-done((bf16[15,12,8,128]{3,2,1,0:T(8,128)(2,1)}, bf16[15,12,8,128]{3,2,1,0:T(8,128)(2,1)S(1)}, u32[]{:S(2)}, u32[]{:S(2)}) %collective-permute-start.5) | collective-permute-done | bytes 368672 | tf_op jit(solution)/shard_map/ppermute | solution.py:216
  44.2 2.2 %constant_dynamic-update-slice_fusion.4 = bf16[48,16,8,128]{3,0,2,1:T(8,128)(2,1)} fusion(bf16[48,16,8,128]{3,0,2,1:T(8,128)(2,1)} %get-tuple-element.19, bf16[24,16,8,128]{3,0,2,1:T(8,128)(2,1)} %collective-permute-done.11), kind=kLoop, calls=%fused_computation.37 | loop fusion | bytes 1572864 | tf_op jit(solution)/shard_map/concatenate | solution.py:259
  46.5 9.8 %march.2 = (f32[6,16,8,128]{3,2,1,0:T(8,128)S(1)}, bf16[6,16,8,128]{3,2,1,0:T(8,128)(2,1)S(1)}) custom-call(s32[26]{0:T(128)S(1)} %pad_add_fusion.scalars, bf16[12,16,8,128]{3,2,1,0:T(8,128)(2,1)S(1)} %get-tuple-element.22.refs_0_, bf16[12,16,8,128]{3,2,1,0:T(8,128)(2,1)S(1)} %collective-permute-done.refs_1_, ...), custom_call_target="tpu_custom_call" | custom-call | flops 4325376000 | bytes 2162688 | tf_op jit(solution)/shard_map/march/pallas_call | solution.py:188
  56.3 1.2 %constant_dynamic-update-slice_fusion.7 = bf16[48,16,8,128]{3,0,2,1:T(8,128)(2,1)S(1)} fusion(bf16[24,16,8,128]{3,0,2,1:T(8,128)(2,1)} %collective-permute-done.12), kind=kLoop, calls=%fused_computation.40 | loop fusion | bytes 1572864
  57.5 9.7 %march.3 = (f32[6,16,8,128]{3,2,1,0:T(8,128)S(1)}, bf16[6,16,8,128]{3,2,1,0:T(8,128)(2,1)S(1)}) custom-call(s32[26]{0:T(128)S(1)} %pad_add_fusion.scalars, bf16[12,16,8,128]{3,2,1,0:T(8,128)(2,1)S(1)} %get-tuple-element.22.refs_0_, bf16[12,16,8,128]{3,2,1,0:T(8,128)(2,1)S(1)} %collective-permute-done.refs_1_, ...), custom_call_target="tpu_custom_call" | custom-call | flops 4325376000 | bytes 2162688 | tf_op jit(solution)/shard_map/march/pallas_call | solution.py:188
  67.4 2.0 %collective-permute-start.9 = (bf16[6,16,8,128]{3,2,1,0:T(8,128)(2,1)S(1)}, bf16[6,16,8,128]{3,2,1,0:T(8,128)(2,1)S(1)}, u32[]{:S(2)}, u32[]{:S(2)}) collective-permute-start(bf16[6,16,8,128]{3,2,1,0:T(8,128)(2,1)S(1)} %get-tuple-element.12), channel_id=1, source_target_pairs={{0,1},{1,0},{2,3},{3,2},{4,5},{5,4},{6,7},{7,6},{8,9},{9,8},{10,11... | collective-permute-start | bytes 589832 | tf_op jit(solution)/shard_map/ppermute | solution.py:216
  69.4 9.4 %collective-permute-done.9 = bf16[6,16,8,128]{3,2,1,0:T(8,128)(2,1)S(1)} collective-permute-done((bf16[6,16,8,128]{3,2,1,0:T(8,128)(2,1)S(1)}, bf16[6,16,8,128]{3,2,1,0:T(8,128)(2,1)S(1)}, u32[]{:S(2)}, u32[]{:S(2)}) %collective-permute-start.9) | collective-permute-done | bytes 196640 | tf_op jit(solution)/shard_map/ppermute | solution.py:216
  82.7 3.4 %collective-permute-done.14 = f32[96,24]{0,1:T(8,128)S(1)} collective-permute-done((f32[96,24]{0,1:T(8,128)S(1)}, f32[96,24]{0,1:T(8,128)S(1)}, u32[]{:S(2)}, u32[]{:S(2)}) %collective-permute-start.14) | collective-permute-done | bytes 9248 | tf_op jit(solution)/shard_map/ppermute | solution.py:216
  86.2 1.6 %collective-permute-start.15 = (f32[96,24]{0,1:T(8,128)S(1)}, f32[96,24]{0,1:T(8,128)S(1)}, u32[]{:S(2)}, u32[]{:S(2)}) collective-permute-start(f32[96,24]{0,1:T(8,128)S(1)} %add.59), channel_id=1, source_target_pairs={{0,2},{1,3},{2,0},{3,1},{4,6},{5,7},{6,4},{7,5},{8,10},{9,11},{10,... | collective-permute-start | bytes 27656 | tf_op jit(solution)/shard_map/ppermute | solution.py:216
  87.7 2.1 %collective-permute-done.15 = f32[96,24]{0,1:T(8,128)S(1)} collective-permute-done((f32[96,24]{0,1:T(8,128)S(1)}, f32[96,24]{0,1:T(8,128)S(1)}, u32[]{:S(2)}, u32[]{:S(2)}) %collective-permute-start.15) | collective-permute-done | bytes 9248 | tf_op jit(solution)/shard_map/ppermute | solution.py:216
  89.9 2.7 %collective-permute-start.16 = (f32[96,24]{0,1:T(8,128)S(1)}, f32[96,24]{0,1:T(8,128)S(1)}, u32[]{:S(2)}, u32[]{:S(2)}) collective-permute-start(f32[96,24]{0,1:T(8,128)S(1)} %add.60), channel_id=1, source_target_pairs={{0,4},{1,5},{2,6},{3,7},{4,0},{5,1},{6,2},{7,3},{8,12},{9,13},{10,... | collective-permute-start | bytes 27656 | tf_op jit(solution)/shard_map/ppermute | solution.py:216
  92.5 1.2 %pad_maximum_fusion = f32[24,16,8,128]{3,2,1,0:T(8,128)} fusion(f32[12,16,8,128]{3,2,1,0:T(8,128)S(1)} %get-tuple-element.17, f32[12,16,8,128]{3,2,1,0:T(8,128)S(1)} %get-tuple-element.16), kind=kLoop, calls=%fused_computation.2 | loop fusion | flops 393216 | bytes 3145728 | tf_op jit(solution)/shard_map/concatenate | solution.py:272
  (85 shorter events, 11.8 us)
Async XLA Ops:
  0.6 4.3 %copy-start = (s32[8]{0:T(128)S(1)}, s32[8]{0:T(128)}, u32[]{:S(2)}) copy-start(s32[8]{0:T(128)} %param.14) | copy-start | bytes 100
  0.6 4.9 %copy-start.6 = (bf16[8,16,2,128]{3,2,1,0:T(2,128)(2,1)S(1)}, bf16[8,16,2,128]{3,2,1,0:T(2,128)(2,1)}, u32[]{:S(2)}) copy-start(bf16[8,16,2,128]{3,2,1,0:T(2,128)(2,1)} %param.13) | copy-start | bytes 196612
  0.7 11.5 %copy-start.5 = (f32[16,8,128]{2,1,0:T(8,128)S(1)}, f32[16,8,128]{2,1,0:T(8,128)}, u32[]{:S(2)}) copy-start(f32[16,8,128]{2,1,0:T(8,128)} %param.12) | copy-start | bytes 196612
  1.9 12.1 %collective-permute-start = (bf16[12,16,8,128]{3,2,1,0:T(8,128)(2,1)S(1)}, bf16[12,16,8,128]{3,2,1,0:T(8,128)(2,1)S(1)}, u32[]{:S(2)}, u32[]{:S(2)}) collective-permute-start(bf16[12,16,8,128]{3,2,1,0:T(8,128)(2,1)S(1)} %get-tuple-element.21), channel_id=1, source_target_pairs={{0,1},{1,0},{2,3},{3,2},{4,5},{5,4},{6,7},{7,6},{8,9},{9,8},{10,11... | collective-permute-start | bytes 1179656 | tf_op jit(solution)/shard_map/ppermute | solution.py:216
  12.2 14.7 %copy-start.4 = (bf16[24,16,8,128]{3,2,1,0:T(8,128)(2,1)S(1)}, bf16[24,16,8,128]{3,2,1,0:T(8,128)(2,1)}, u32[]{:S(2)}) copy-start(bf16[24,16,8,128]{3,2,1,0:T(8,128)(2,1)} %param.15) | copy-start | bytes 2359300
  14.0 7.4 %collective-permute-start.3 = (bf16[5,16,8,128]{3,2,1,0:T(8,128)(2,1)S(1)}, bf16[5,16,8,128]{3,2,1,0:T(8,128)(2,1)S(1)}, u32[]{:S(2)}, u32[]{:S(2)}) collective-permute-start(bf16[5,16,8,128]{3,2,1,0:T(8,128)(2,1)S(1)} %pad_maximum_fusion.5.refs_6_), channel_id=1, source_target_pairs={{0,1},{1,0},{2,3},{3,2},{4,5},{5,4},{6,7},{7,6},{8,9},{9,8},{10,11... | collective-permute-start | bytes 491528 | tf_op jit(solution)/shard_map/ppermute | solution.py:216
  16.6 14.2 %collective-permute-start.2 = (bf16[15,12,8,128]{3,2,1,0:T(8,128)(2,1)}, bf16[15,12,8,128]{3,2,1,0:T(8,128)(2,1)S(1)}, u32[]{:S(2)}, u32[]{:S(2)}) collective-permute-start(bf16[15,12,8,128]{3,2,1,0:T(8,128)(2,1)} %fusion.7), channel_id=1, source_target_pairs={{0,2},{2,4},{4,6},{3,1},{5,3},{7,5},{8,10},{10,12},{12,14},{11,9},... | collective-permute-start | bytes 1105928 | tf_op jit(solution)/shard_map/ppermute | solution.py:216
  20.2 15.0 %collective-permute-start.1 = (bf16[17,16,8,128]{3,2,1,0:T(8,128)(2,1)S(1)}, bf16[17,16,8,128]{3,2,1,0:T(8,128)(2,1)S(1)}, u32[]{:S(2)}, u32[]{:S(2)}) collective-permute-start(bf16[17,16,8,128]{3,2,1,0:T(8,128)(2,1)S(1)} %pad_maximum_fusion.1), channel_id=1, source_target_pairs={{2,0},{4,2},{6,4},{1,3},{3,5},{5,7},{10,8},{12,10},{14,12},{9,11},... | collective-permute-start | bytes 1671176 | tf_op jit(solution)/shard_map/ppermute | solution.py:216
  22.3 20.6 %collective-permute-start.4 = (bf16[17,16,8,128]{3,2,1,0:T(8,128)(2,1)}, bf16[17,16,8,128]{3,2,1,0:T(8,128)(2,1)S(1)}, u32[]{:S(2)}, u32[]{:S(2)}) collective-permute-start(bf16[17,16,8,128]{3,2,1,0:T(8,128)(2,1)} %pad_maximum_fusion.2), channel_id=1, source_target_pairs={{0,2},{2,4},{4,6},{3,1},{5,3},{7,5},{8,10},{10,12},{12,14},{11,9},... | collective-permute-start | bytes 1671176 | tf_op jit(solution)/shard_map/ppermute | solution.py:216
  28.7 7.4 %copy-start.7 = (s32[24,2]{0,1:T(2,128)S(1)}, s32[24,2]{0,1:T(2,128)}, u32[]{:S(2)}) copy-start(s32[24,2]{0,1:T(2,128)} %param.11) | copy-start | bytes 580
  28.7 15.6 %collective-permute-start.11 = (bf16[24,16,8,128]{3,0,2,1:T(8,128)(2,1)}, bf16[24,16,8,128]{3,0,2,1:T(8,128)(2,1)}, u32[]{:S(2)}, u32[]{:S(2)}) collective-permute-start(bf16[24,16,8,128]{3,0,2,1:T(8,128)(2,1)} %get-tuple-element.20), channel_id=1, source_target_pairs={{0,8},{8,0},{16,24},{24,16},{1,9},{9,1},{17,25},{25,17},{2,10},{10... | collective-permute-start | bytes 2359304 | tf_op jit(solution)/shard_map/ppermute | solution.py:217
  29.5 13.4 %collective-permute-start.5 = (bf16[15,12,8,128]{3,2,1,0:T(8,128)(2,1)}, bf16[15,12,8,128]{3,2,1,0:T(8,128)(2,1)S(1)}, u32[]{:S(2)}, u32[]{:S(2)}) collective-permute-start(bf16[15,12,8,128]{3,2,1,0:T(8,128)(2,1)} %fusion.5), channel_id=1, source_target_pairs={{2,0},{4,2},{6,4},{1,3},{3,5},{5,7},{10,8},{12,10},{14,12},{9,11},... | collective-permute-start | bytes 1105928 | tf_op jit(solution)/shard_map/ppermute | solution.py:216
  30.8 25.4 %collective-permute-start.12 = (bf16[24,16,8,128]{3,0,2,1:T(8,128)(2,1)}, bf16[24,16,8,128]{3,0,2,1:T(8,128)(2,1)}, u32[]{:S(2)}, u32[]{:S(2)}) collective-permute-start(bf16[24,16,8,128]{3,0,2,1:T(8,128)(2,1)} %get-tuple-element.20), channel_id=1, source_target_pairs={{0,16},{8,24},{16,0},{24,8},{1,17},{9,25},{17,1},{25,9},{2,18},{10... | collective-permute-start | bytes 2359304 | tf_op jit(solution)/shard_map/ppermute | solution.py:250
  36.0 10.4 %collective-permute-start.7 = (bf16[196,8,128]{2,1,0:T(8,128)(2,1)}, bf16[196,8,128]{2,1,0:T(8,128)(2,1)S(1)}, u32[]{:S(2)}, u32[]{:S(2)}) collective-permute-start(bf16[196,8,128]{2,1,0:T(8,128)(2,1)} %pad_maximum_fusion.3), channel_id=1, source_target_pairs={{0,8},{8,0},{16,24},{24,16},{1,9},{9,1},{17,25},{25,17},{2,10},{10... | collective-permute-start | bytes 1204232 | tf_op jit(solution)/shard_map/ppermute | solution.py:217
  42.9 3.6 %collective-permute-start.6 = (bf16[5,16,8,128]{3,2,1,0:T(8,128)(2,1)S(1)}, bf16[5,16,8,128]{3,2,1,0:T(8,128)(2,1)S(1)}, u32[]{:S(2)}, u32[]{:S(2)}) collective-permute-start(bf16[5,16,8,128]{3,2,1,0:T(8,128)(2,1)S(1)} %pad_maximum_fusion.5.refs_6_), channel_id=1, source_target_pairs={{0,8},{8,0},{16,24},{24,16},{1,9},{9,1},{17,25},{25,17},{2,10},{10... | collective-permute-start | bytes 491528 | tf_op jit(solution)/shard_map/ppermute | solution.py:217
  43.7 2.8 %collective-permute-start.8 = (bf16[116,8,128]{2,1,0:T(8,128)(2,1)}, bf16[116,8,128]{2,1,0:T(8,128)(2,1)}, u32[]{:S(2)}, u32[]{:S(2)}) collective-permute-start(bf16[116,8,128]{2,1,0:T(8,128)(2,1)} %pad_maximum_fusion.4), channel_id=1, source_target_pairs={{0,8},{8,0},{16,24},{24,16},{1,9},{9,1},{17,25},{25,17},{2,10},{10... | collective-permute-start | bytes 712712 | tf_op jit(solution)/shard_map/ppermute | solution.py:217
  44.2 2.2 %copy-start.2 = (bf16[256,128]{1,0:T(8,128)(2,1)S(1)}, bf16[256,128]{1,0:T(8,128)(2,1)}, u32[]{:S(2)}) copy-start(bf16[256,128]{1,0:T(8,128)(2,1)} %constant.82.clone.refs_12_) | copy-start | bytes 196612
  56.2 24.0 %collective-permute-start.13 = (bf16[24,16,8,128]{3,0,2,1:T(8,128)(2,1)}, bf16[24,16,8,128]{3,0,2,1:T(8,128)(2,1)S(1)}, u32[]{:S(2)}, u32[]{:S(2)}) collective-permute-start(bf16[24,16,8,128]{3,0,2,1:T(8,128)(2,1)} %collective-permute-done.12), channel_id=1, source_target_pairs={{0,8},{8,0},{16,24},{24,16},{1,9},{9,1},{17,25},{25,17},{2,10},{10... | collective-permute-start | bytes 2359304 | tf_op jit(solution)/shard_map/ppermute | solution.py:217
  67.3 11.7 %copy-start.3 = (bf16[48,16,8,128]{3,0,2,1:T(8,128)(2,1)S(1)}, bf16[48,16,8,128]{3,0,2,1:T(8,128)(2,1)}, u32[]{:S(2)}) copy-start(bf16[48,16,8,128]{3,0,2,1:T(8,128)(2,1)} %constant_dynamic-update-slice_fusion.4) | copy-start | bytes 4718596
  67.3 11.6 %collective-permute-start.10 = (bf16[6,16,8,128]{3,2,1,0:T(8,128)(2,1)S(1)}, bf16[6,16,8,128]{3,2,1,0:T(8,128)(2,1)S(1)}, u32[]{:S(2)}, u32[]{:S(2)}) collective-permute-start(bf16[6,16,8,128]{3,2,1,0:T(8,128)(2,1)S(1)} %get-tuple-element.13), channel_id=1, source_target_pairs={{0,1},{1,0},{2,3},{3,2},{4,5},{5,4},{6,7},{7,6},{8,9},{9,8},{10,11... | collective-permute-start | bytes 589832 | tf_op jit(solution)/shard_map/ppermute | solution.py:216
  67.4 11.5 %collective-permute-start.9 = (bf16[6,16,8,128]{3,2,1,0:T(8,128)(2,1)S(1)}, bf16[6,16,8,128]{3,2,1,0:T(8,128)(2,1)S(1)}, u32[]{:S(2)}, u32[]{:S(2)}) collective-permute-start(bf16[6,16,8,128]{3,2,1,0:T(8,128)(2,1)S(1)} %get-tuple-element.12), channel_id=1, source_target_pairs={{0,1},{1,0},{2,3},{3,2},{4,5},{5,4},{6,7},{7,6},{8,9},{9,8},{10,11... | collective-permute-start | bytes 589832 | tf_op jit(solution)/shard_map/ppermute | solution.py:216
  82.4 3.8 %collective-permute-start.14 = (f32[96,24]{0,1:T(8,128)S(1)}, f32[96,24]{0,1:T(8,128)S(1)}, u32[]{:S(2)}, u32[]{:S(2)}) collective-permute-start(f32[96,24]{0,1:T(8,128)S(1)} %fusion.10), channel_id=1, source_target_pairs={{0,1},{1,0},{2,3},{3,2},{4,5},{5,4},{6,7},{7,6},{8,9},{9,8},{10,11... | collective-permute-start | bytes 27656 | tf_op jit(solution)/shard_map/ppermute | solution.py:216
  86.2 3.7 %collective-permute-start.15 = (f32[96,24]{0,1:T(8,128)S(1)}, f32[96,24]{0,1:T(8,128)S(1)}, u32[]{:S(2)}, u32[]{:S(2)}) collective-permute-start(f32[96,24]{0,1:T(8,128)S(1)} %add.59), channel_id=1, source_target_pairs={{0,2},{1,3},{2,0},{3,1},{4,6},{5,7},{6,4},{7,5},{8,10},{9,11},{10,... | collective-permute-start | bytes 27656 | tf_op jit(solution)/shard_map/ppermute | solution.py:216
  89.9 4.6 %collective-permute-start.16 = (f32[96,24]{0,1:T(8,128)S(1)}, f32[96,24]{0,1:T(8,128)S(1)}, u32[]{:S(2)}, u32[]{:S(2)}) collective-permute-start(f32[96,24]{0,1:T(8,128)S(1)} %add.60), channel_id=1, source_target_pairs={{0,4},{1,5},{2,6},{3,7},{4,0},{5,1},{6,2},{7,3},{8,12},{9,13},{10,... | collective-permute-start | bytes 27656 | tf_op jit(solution)/shard_map/ppermute | solution.py:216
  (1 other events, 2.2 us)

commit v5 on v4

--- a/solution.py
+++ b/solution.py
@@ -50,15 +50,15 @@
 
 
 def march(steps, rows, halo, begin, scalars, *refs):
-    pieces = refs[0:6]
-    near_ref, near_x_ref, other_ref, first_ref, second_ref = refs[6:11]
-    left_ref, right_ref, own_ref, send_ref = refs[11:15]
-    pert, snap, scale, gain, fields, split = refs[15:21]
+    wide, narrow = refs[0:4], refs[4:6]
+    near_refs = refs[6:8]
+    c_ref, d_ref, near_other, far_other = refs[8:12]
+    left_ref, right_ref, own_ref, send_ref = refs[12:16]
+    pert, snap, scale, gain, fields, split = refs[16:22]
     total = 2 * rows + 2 * halo
     cy = 8
     far = halo - rows
     par, core = scalars[0], scalars[1]
-    probes = pieces[0].shape[0]
     even = (halo, halo + rows, halo + 2 * rows, 0, halo - rows, halo + 3 * rows)
     odd = (halo + rows, halo, halo - rows, halo + 3 * rows, halo + 2 * rows, 0)
     counts = (rows, rows, rows, far, rows, far)
@@ -67,19 +67,28 @@
 
     @pl.when(pl.program_id(0) == 0)
     def _():
-        sizes = [(near_half + 1) * rows, (near_half + 1) * rows, (far_half + 1) * far]
+        near_size, far_size = (near_half + 1) * rows, (far_half + 1) * far
+        c_base = c_ref.shape[0] - near_size - far_size
+        d_base = d_ref.shape[0] - near_size - far_size
+        held = (
+            (d_ref, d_base, near_size + far_size),
+            (c_ref, c_base + near_size, near_size),
+            (c_ref, c_base, 0),
+            (d_ref, d_base + near_size, 2 * near_size + far_size),
+        )
         for j in range(6):
             kept = far_half if j in (3, 5) else near_half
             where = pl.ds(pl.multiple_of(starts[j] * cy, 32), counts[j] * cy)
             for t in range(kept + 1):
                 at = t * counts[j]
-                if j == 0:
-                    mine, other = near_ref[t], other_ref[t]
+                if j < 2:
+                    mine = near_refs[j][t]
+                    at += j * near_size
+                    other = near_other[at : at + counts[j]]
                 else:
-                    mine = near_x_ref[t] if j == 1 else pieces[j][probes + t]
-                    held = first_ref if j < 4 else second_ref
-                    at += sum(sizes[: j - 1]) if j < 4 else sum(sizes[1 : j - 3])
-                    other = held[at : at + counts[j]]
+                    source, first, second = held[j - 2]
+                    mine = source[first + at : first + at + counts[j]]
+                    other = far_other[second + at : second + at + counts[j]]
                 mine = mine.reshape(counts[j] * cy, 128).astype(jnp.float32)
                 other = other.reshape(counts[j] * cy, 128).astype(jnp.float32)
                 if t < kept:
@@ -90,12 +99,16 @@
                     gain[where, :] = taps[1] * (mine + other)
 
     for q in range(PACK):
-        probe = begin + pl.program_id(0) * PACK + q
+        place = pl.program_id(0) * PACK + q
+        probe = begin + place
         low = scalars[2 + 2 * probe]
         high = scalars[3 + 2 * probe]
         for j in range(6):
             where = pl.ds(pl.multiple_of(starts[j] * cy, 32), counts[j] * cy)
-            value = pieces[j][probe].astype(jnp.float32)
+            if j < 4:
+                value = wide[j][probe].astype(jnp.float32)
+            else:
+                value = narrow[j - 4][pl.ds(place * counts[j], counts[j])].astype(jnp.float32)
             plane = lax.broadcasted_iota(jnp.int32, value.shape, 0) + starts[j]
             value = jnp.where((plane >= low) & (plane < high), value, 0.0)
             pert[q, where, :] = value.reshape(counts[j] * cy, 128)
@@ -164,8 +177,8 @@
         advanced(*first, *made)
 
 
-def propagate(scalars, pieces, extras, begin, count, steps, rows, halo):
-    _, _, cy, cz = pieces[0].shape
+def propagate(scalars, operands, begin, count, steps, rows, halo):
+    _, _, cy, cz = operands[0].shape
     left, right = tables(cy, cz)
     left, right = jnp.asarray(left, jnp.bfloat16), jnp.asarray(right, jnp.bfloat16)
     total = 2 * rows + 2 * halo
@@ -173,7 +186,7 @@
     grid_spec = pltpu.PrefetchScalarGridSpec(
         num_scalar_prefetch=1,
         grid=(count // PACK,),
-        in_specs=[whole] * (len(pieces) + len(extras) + 2),
+        in_specs=[whole] * (len(operands) + 2),
         out_specs=[whole, whole],
         scratch_shapes=[
             pltpu.VMEM((PACK, total * cy, cz), jnp.float32),
@@ -193,9 +206,9 @@
             jax.ShapeDtypeStruct((count, rows, cy, cz), jnp.bfloat16),
         ],
         compiler_params=pltpu.CompilerParams(vmem_limit_bytes=20 << 20),
-        cost_estimate=pl.CostEstimate(flops=cells * 8000, bytes_accessed=cells * 4, transcendentals=0),
+        cost_estimate=pl.CostEstimate(flops=cells * 8000 if begin else 0, bytes_accessed=cells * 4 if begin else 0, transcendentals=0),
         name="march",
-    )(scalars, *pieces, *extras, left, right)
+    )(scalars, *operands, left, right)
 
 
 def local(probe_field, bounds, courant, snapshots, snap_times, basis_panels):
@@ -218,45 +231,58 @@
     cut = lambda x, start: lax.dynamic_slice_in_dim(x, start, far, axis=1)
     near = rows - far
 
-    all_snaps = lax.all_gather(snapshots, "probe", axis=2, tiled=True)
-    near_half, far_half = shares(steps, rows, halo)
-    chosen = jnp.minimum(2 * jnp.arange(near_half) + core, steps - 1)
-    picked = jnp.take(all_snaps, jnp.take(snap_times, chosen, mode="clip"), axis=0, mode="clip")
-    high = lax.reduce_precision(courant, 8, 7)
-    rate = jnp.where(core == 0, high, courant - high).astype(jnp.bfloat16)[None]
-    extra = jnp.concatenate([picked, rate], axis=0)
-    trim = lambda x: jnp.concatenate([x[:far_half], x[near_half:]], axis=0)
-    planes = lambda *xs: jnp.concatenate([x.reshape(-1, cy, cz) for x in xs], axis=0)
     mine = lax.dynamic_slice_in_dim(probe_field, half * par, half, axis=0)
     theirs = lax.dynamic_slice_in_dim(probe_field, half * (1 - par), half, axis=0)
     partner = hop(theirs, swap)
-    side_a = hop(jnp.concatenate([mine, extra], axis=0), perm_a)
-    side_b = hop(cut(jnp.concatenate([mine, trim(extra)], axis=0), near * (1 - par)), perm_b)
-    extra_x = hop(lax.optimization_barrier((extra, partner))[0], swap)
-    side_c = hop(jnp.concatenate([partner, extra_x], axis=0), perm_b)
-    side_d = hop(cut(jnp.concatenate([partner, trim(extra_x)], axis=0), near * par), perm_a)
-    pieces = (mine, partner, side_a, side_b, side_c, side_d)
-    extras = (
-        extra,
-        extra_x,
-        cores(extra),
-        cores(planes(extra_x, side_a[half:], side_b[half:])),
-        cores(planes(side_c[half:], side_d[half:])),
-    )
+    side_a = hop(mine, perm_a)
+    side_b = hop(cut(mine, near * (1 - par)), perm_b)
+
+    near_half, far_half = shares(steps, rows, halo)
+
+    def picked(parity):
+        chosen = jnp.minimum(2 * jnp.arange(near_half) + parity, steps - 1)
+        return jnp.take(snapshots, jnp.take(snap_times, chosen, mode="clip"), axis=0, mode="clip")
+
+    joined = picked(core)
+    sent = picked(1 - core)
+    span = 1
+    while span < members:
+        got = lax.ppermute(sent, "probe", [(i, i ^ span) for i in range(members)])
+        upper = (member // span) % 2 == 1
+        joined = jnp.concatenate([jnp.where(upper, got, joined), jnp.where(upper, joined, got)], axis=2)
+        sent = joined
+        span *= 2
+    high = lax.reduce_precision(courant, 8, 7)
+    rate = jnp.where(core == 0, high, courant - high).astype(jnp.bfloat16)[None]
+    extra = jnp.concatenate([joined, rate], axis=0)
+    trim = lambda x: jnp.concatenate([x[:far_half], x[near_half:]], axis=0)
+    planes = lambda *xs: jnp.concatenate([x.reshape(-1, cy, cz) for x in xs], axis=0)
+    extra_x = hop(lax.optimization_barrier((extra, partner, side_a, side_b))[0], swap)
+    part = half // 2
+    far_own, far_x = cut(trim(extra), near * (1 - par)), cut(trim(extra_x), near * par)
+    far_partner = cut(partner, near * par)
+    side_c = [hop(planes(partner[:part], extra_x, far_own), perm_b), hop(planes(partner[part:]), perm_b)]
+    side_d = [hop(planes(far_partner[:part], extra, far_x), perm_a), hop(planes(far_partner[part:]), perm_a)]
+    near_other = cores(planes(extra, extra_x))
+    far_other = cores(planes(side_c[0][part * rows :], side_d[0][part * far :]))
     base = (place // 2) * 2 * rows - halo
     mine_bounds = lax.dynamic_slice_in_dim(bounds, half * par, half, axis=0) - base
     scalars = jnp.concatenate([jnp.stack([par, core]), mine_bounds.reshape(-1)]).astype(jnp.int32)
-    basis_later = lax.optimization_barrier((basis_panels, extra_x))[0]
-    crossed = lax.ppermute(basis_later, "probe", [(i, i ^ 2) for i in range(members)])
+    crossed = lax.ppermute(basis_panels, "probe", [(i, i ^ 2) for i in range(members)])
     first = par == 0
     own, back = [], []
-    for begin, count in ((0, half // 2), (half // 2, half - half // 2)):
-        kept, sent = propagate(scalars, pieces, extras, begin, count, steps, rows, halo)
+    for i in range(2):
+        operands = (mine, partner, side_a, side_b, side_c[i], side_d[i], extra, extra_x)
+        operands += (side_c[0], side_d[0], near_other, far_other)
+        kept, sent = propagate(scalars, operands, i * part, part, steps, rows, halo)
+        scalars = lax.optimization_barrier((scalars, kept))[0]
         own.append(kept)
+        if back:
+            sent = lax.optimization_barrier((sent, back[0]))[0]
         back.append(hop(sent, swap))
-    panels = [basis_later, cores(basis_later)]
-    crossed = lax.optimization_barrier((crossed, own[0]))[0]
-    panels = [jnp.concatenate(panels, axis=0), jnp.concatenate([crossed, cores(crossed)], axis=0)]
+    beside = cores(basis_panels)
+    crossed, beside = lax.optimization_barrier((crossed, beside, own[1]))[:2]
+    panels = [basis_panels, beside, crossed, cores(crossed)]
     dots = lambda x: jnp.concatenate(
         [
             lax.dot_general(y, x, (((1, 2, 3), (1, 2, 3)), ((), ())), preferred_element_type=jnp.float32)

time: 95.4 us -> 110 us (1.15)
  matrix products: 2.12 us -> 12.5 us
  starting transfers between devices: 24.2 us -> 32.1 us
  blocking collectives: 5.79 us -> 0 us
  local copies, waits for them, and re-layouts: 8.98 us -> 13 us
  Pallas kernels: 19.5 us -> 17.9 us
    dot_general x4 -> x8, matrix products: 2.12 us -> 12.5 us  [local(): lax.dot_general(y, x, (((1, 2, 3), (1, 2, 3)), ((), ())), preferred_eleme...]
    ppermute x11 -> x13, starting transfers between devices: 22 us -> 28.6 us  [local(): hop = lambda x, pairs: lax.ppermute(x, 'store', pairs)]
    all_gather x1 -> x0, blocking collectives: 5.79 us -> none  [local(): all_snaps = lax.all_gather(snapshots, 'probe', axis=2, tiled=True)]
    ppermute x11 -> x13, waiting for transfers between devices: 26.8 us -> 23.5 us  [local(): hop = lambda x, pairs: lax.ppermute(x, 'store', pairs)]
    ppermute x1 -> x3, waiting for transfers between devices: 0.01 us -> 2.92 us  [the longest x2 2.92 us: local(): got = lax.ppermute(sent, 'probe', [(i, i ^ span) for i in range(members)])]
    concatenate x5 -> x4, other arithmetic: 2.58 us -> 0.21 us  [the longest x1 0.07 us: local(): extra = jnp.concatenate([joined, rate], axis=0)]
    concatenate x2 -> x0, local copies, waits for them, and re-layouts: 2.35 us -> none  [the longest x1 2.19 us: local(): jnp.concatenate(panels, axis=0)]
    ppermute x1 -> x3, starting transfers between devices: 1.58 us -> 3.18 us  [the longest x2 1.66 us: local(): got = lax.ppermute(sent, 'probe', [(i, i ^ span) for i in range(members)])]
  transfers between devices with their start and end apart: 17 -> 20, of which waited for: 7 -> 7; matrix products, arithmetic and copies ran while one was open for 14% -> 25% of each run, Pallas kernels for 20% -> 16%
where the time goes in v5:
time: 110 us; the launch traced here: 109 us
  starting transfers between devices  32.1 us (29%)
  waiting for transfers between devices  26.4 us (24%)
  Pallas kernels  17.9 us (16%)
  local copies, waits for them, and re-layouts  13 us (12%)
  matrix products  12.5 us (11%)
  other arithmetic  6.33 us (6%)
  between operations  1.16 us (1%)
    ppermute x13, starting transfers between devices, local(): hop = lambda x, pairs: lax.ppermute(x, 'store', pairs)  28.6 us
    ppermute x13, waiting for transfers between devices, local(): hop = lambda x, pairs: lax.ppermute(x, 'store', pairs)  23.5 us
    pallas_call x2, Pallas kernels, propagate(): pl.pallas_call(functools.partial(march, steps, rows, halo, begin), grid_s...  17.9 us
    dot_general x8, matrix products, local(): lax.dot_general(y, x, (((1, 2, 3), (1, 2, 3)), ((), ())), preferred_eleme...  12.5 us
    unnamed x13, local copies, waits for them, and re-layouts  3.48 us
    ppermute x2, waiting for transfers between devices, local(): got = lax.ppermute(sent, 'probe', [(i, i ^ span) for i in range(members)])  2.92 us
  transfers between devices with their start and end apart: 20, of which 7 were waited for; matrix products, arithmetic and copies ran while one was open for 25% of the time, Pallas kernels for 16%

profile of v5, /device:TPU:0, one launch (start us, length us, event | category | flops | bytes accessed | tf_op | source)
XLA Modules:
  0.0 109.3 jit_solution(1589963411895935618)
XLA Ops:
  1.9 3.0 %collective-permute-start = (bf16[12,16,8,128]{3,2,1,0:T(8,128)(2,1)S(1)}, bf16[12,16,8,128]{3,2,1,0:T(8,128)(2,1)S(1)}, u32[]{:S(2)}, u32[]{:S(2)}) collective-permute-start(bf16[12,16,8,128]{3,2,1,0:T(8,128)(2,1)S(1)} %get-tuple-element.26), channel_id=1, source_target_pairs={{0,1},{1,0},{2,3},{3,2},{4,5},{5,4},{6,7},{7,6},{8,9},{9,8},{10,11... | collective-permute-start | bytes 1179656 | tf_op jit(solution)/shard_map/ppermute | solution.py:229
  7.2 4.6 %collective-permute-start.2 = (bf16[12,12,8,128]{3,2,1,0:T(8,128)(2,1)S(1)}, bf16[12,12,8,128]{3,2,1,0:T(8,128)(2,1)S(1)}, u32[]{:S(2)}, u32[]{:S(2)}) collective-permute-start(bf16[12,12,8,128]{3,2,1,0:T(8,128)(2,1)S(1)} %constant_dynamic-slice_fusion.2), channel_id=1, source_target_pairs={{0,2},{2,4},{4,6},{3,1},{5,3},{7,5},{8,10},{10,12},{12,14},{11,9},... | collective-permute-start | bytes 884744 | tf_op jit(solution)/shard_map/ppermute | solution.py:229
  14.6 1.6 %collective-permute-start.4 = (bf16[4,16,4,128]{3,2,1,0:T(4,128)(2,1)S(1)}, bf16[4,16,4,128]{3,2,1,0:T(4,128)(2,1)S(1)}, u32[]{:S(2)}, u32[]{:S(2)}) collective-permute-start(bf16[4,16,4,128]{3,2,1,0:T(4,128)(2,1)S(1)} %pad_maximum_fusion.6), channel_id=1, source_target_pairs={{0,16},{8,24},{16,0},{24,8},{1,17},{9,25},{17,1},{25,9},{2,18},{10... | collective-permute-start | bytes 196616 | tf_op jit(solution)/shard_map/ppermute | solution.py:250
  16.2 2.9 %collective-permute-done.4 = bf16[4,16,4,128]{3,2,1,0:T(4,128)(2,1)S(1)} collective-permute-done((bf16[4,16,4,128]{3,2,1,0:T(4,128)(2,1)S(1)}, bf16[4,16,4,128]{3,2,1,0:T(4,128)(2,1)S(1)}, u32[]{:S(2)}, u32[]{:S(2)}) %collective-permute-start.4) | collective-permute-done | bytes 65568 | tf_op jit(solution)/shard_map/ppermute | solution.py:250
  21.4 3.9 %collective-permute-done.5.refs_7_ = bf16[5,16,8,128]{3,2,1,0:T(8,128)(2,1)S(1)} collective-permute-done((bf16[5,16,8,128]{3,2,1,0:T(8,128)(2,1)S(1)}, bf16[5,16,8,128]{3,2,1,0:T(8,128)(2,1)S(1)}, u32[]{:S(2)}, u32[]{:S(2)}) %collective-permute-start.5) | collective-permute-done | bytes 163872 | tf_op jit(solution)/shard_map/ppermute | solution.py:229
  25.3 3.5 %collective-permute-start.6 = (bf16[212,8,128]{2,1,0:T(8,128)(2,1)S(1)}, bf16[212,8,128]{2,1,0:T(8,128)(2,1)S(1)}, u32[]{:S(2)}, u32[]{:S(2)}) collective-permute-start(bf16[212,8,128]{2,1,0:T(8,128)(2,1)S(1)} %pad_maximum_fusion.2), channel_id=1, source_target_pairs={{0,2},{2,4},{4,6},{3,1},{5,3},{7,5},{8,10},{10,12},{12,14},{11,9},... | collective-permute-start | bytes 1302536 | tf_op jit(solution)/shard_map/ppermute | solution.py:229
  31.0 9.2 %collective-permute-done.7.refs_5_.refs_9_ = bf16[188,8,128]{2,1,0:T(8,128)(2,1)S(1)} collective-permute-done((bf16[188,8,128]{2,1,0:T(8,128)(2,1)S(1)}, bf16[188,8,128]{2,1,0:T(8,128)(2,1)S(1)}, u32[]{:S(2)}, u32[]{:S(2)}) %collective-permute-start.7) | collective-permute-done | bytes 385056 | tf_op jit(solution)/shard_map/ppermute | solution.py:229
  41.1 2.5 %copy.28 = bf16[24,16,8,128]{3,0,2,1:T(8,128)(2,1)} copy(bf16[24,16,8,128]{3,2,1,0:T(8,128)(2,1)} %param.15) | data formatting | bytes 1572864 | tf_op args[5]
  45.4 4.2 %collective-permute-start.10 = (bf16[96,8,128]{2,1,0:T(8,128)(2,1)}, bf16[96,8,128]{2,1,0:T(8,128)(2,1)}, u32[]{:S(2)}, u32[]{:S(2)}) collective-permute-start(bf16[96,8,128]{2,1,0:T(8,128)(2,1)} %bitcast.86), channel_id=1, source_target_pairs={{0,2},{2,4},{4,6},{3,1},{5,3},{7,5},{8,10},{10,12},{12,14},{11,9},... | collective-permute-start | bytes 589832 | tf_op jit(solution)/shard_map/ppermute | solution.py:229
  56.6 8.4 %march.2 = (f32[6,16,8,128]{3,2,1,0:T(8,128)S(1)}, bf16[6,16,8,128]{3,2,1,0:T(8,128)(2,1)S(1)}) custom-call(s32[26]{0:T(128)S(1)} %pad_add_fusion.scalars, bf16[12,16,8,128]{3,2,1,0:T(8,128)(2,1)S(1)} %get-tuple-element.27.refs_0_, bf16[12,16,8,128]{3,2,1,0:T(8,128)(2,1)S(1)} %collective-permute-done.refs_1_, ...), custom_call_target="tpu_custom_call" | custom-call | tf_op jit(solution)/shard_map/march/pallas_call | solution.py:201
  65.2 9.5 %march.3 = (f32[6,16,8,128]{3,2,1,0:T(8,128)S(1)}, bf16[6,16,8,128]{3,2,1,0:T(8,128)(2,1)S(1)}) custom-call(s32[26]{0:T(128)S(1)} %pad_add_fusion.scalars, bf16[12,16,8,128]{3,2,1,0:T(8,128)(2,1)S(1)} %get-tuple-element.27.refs_0_, bf16[12,16,8,128]{3,2,1,0:T(8,128)(2,1)S(1)} %collective-permute-done.refs_1_, ...), custom_call_target="tpu_custom_call" | custom-call | flops 4325376000 | bytes 2162688 | tf_op jit(solution)/shard_map/march/pallas_call | solution.py:201
  74.8 2.1 %collective-permute-start.13 = (bf16[6,16,8,128]{3,2,1,0:T(8,128)(2,1)S(1)}, bf16[6,16,8,128]{3,2,1,0:T(8,128)(2,1)S(1)}, u32[]{:S(2)}, u32[]{:S(2)}) collective-permute-start(bf16[6,16,8,128]{3,2,1,0:T(8,128)(2,1)S(1)} %get-tuple-element.17), channel_id=1, source_target_pairs={{0,1},{1,0},{2,3},{3,2},{4,5},{5,4},{6,7},{7,6},{8,9},{9,8},{10,11... | collective-permute-start | bytes 589832 | tf_op jit(solution)/shard_map/ppermute | solution.py:229
  76.9 5.5 %collective-permute-done.13 = bf16[6,16,8,128]{3,2,1,0:T(8,128)(2,1)S(1)} collective-permute-done((bf16[6,16,8,128]{3,2,1,0:T(8,128)(2,1)S(1)}, bf16[6,16,8,128]{3,2,1,0:T(8,128)(2,1)S(1)}, u32[]{:S(2)}, u32[]{:S(2)}) %collective-permute-start.13) | collective-permute-done | bytes 196640 | tf_op jit(solution)/shard_map/ppermute | solution.py:229
  82.4 1.6 %convolution_bitcast_fusion.1 = f32[24,12]{0,1:T(8,128)S(1)} fusion(bf16[24,16,8,128]{3,0,2,1:T(8,128)(2,1)} %collective-permute-done.14, bf16[12,16,8,128]{3,2,1,0:T(8,128)(2,1)S(1)} %constant_dynamic-update-slice_fusion.2), kind=kOutput, calls=%fused_computation.6 | convolution fusion | flops 9437184 | bytes 1180800 | tf_op jit(solution)/shard_map/dot_general | solution.py:288
  84.2 1.6 %convolution_bitcast_fusion.5 = f32[24,12]{0,1:T(8,128)S(1)} fusion(bf16[24,16,8,128]{3,0,2,1:T(8,128)(2,1)} %collective-permute-done.14, bf16[12,16,8,128]{3,2,1,0:T(8,128)(2,1)S(1)} %get-tuple-element.25), kind=kOutput, calls=%fused_computation.10 | convolution fusion | flops 9437184 | bytes 1180800 | tf_op jit(solution)/shard_map/dot_general | solution.py:288
  85.8 2.0 %convolution_bitcast_fusion.7 = f32[24,12]{0,1:T(8,128)S(1)} fusion(bf16[12,16,8,128]{3,2,1,0:T(8,128)(2,1)S(1)} %get-tuple-element.25, bf16[24,16,8,128]{3,2,1,0:T(8,128)(2,1)} %param.15), kind=kOutput, calls=%fused_computation.12 | convolution fusion | flops 9437184 | bytes 1180800 | tf_op jit(solution)/shard_map/dot_general | solution.py:288
  87.8 2.0 %convolution_bitcast_fusion.3 = f32[24,12]{0,1:T(8,128)S(1)} fusion(bf16[12,16,8,128]{3,2,1,0:T(8,128)(2,1)S(1)} %constant_dynamic-update-slice_fusion.2, bf16[24,16,8,128]{3,2,1,0:T(8,128)(2,1)} %param.15), kind=kOutput, calls=%fused_computation.8 | convolution fusion | flops 9437184 | bytes 1180800 | tf_op jit(solution)/shard_map/dot_general | solution.py:288
  89.8 2.2 %convolution_bitcast_fusion.6 = f32[24,12]{0,1:T(8,128)S(1)} fusion(bf16[24,16,8,128]{3,2,1,0:T(8,128)(2,1)} %collective-permute-done.15, bf16[12,16,8,128]{3,2,1,0:T(8,128)(2,1)S(1)} %get-tuple-element.25), kind=kOutput, calls=%fused_computation.11 | convolution fusion | flops 9437184 | bytes 1180800 | tf_op jit(solution)/shard_map/dot_general | solution.py:288
  92.0 2.2 %convolution_bitcast_fusion.2 = f32[24,12]{0,1:T(8,128)S(1)} fusion(bf16[24,16,8,128]{3,2,1,0:T(8,128)(2,1)} %collective-permute-done.15, bf16[12,16,8,128]{3,2,1,0:T(8,128)(2,1)S(1)} %constant_dynamic-update-slice_fusion.2), kind=kOutput, calls=%fused_computation.7 | convolution fusion | flops 9437184 | bytes 1180800 | tf_op jit(solution)/shard_map/dot_general | solution.py:288
  96.1 1.8 %collective-permute-start.17 = (f32[96,24]{0,1:T(8,128)S(1)}, f32[96,24]{0,1:T(8,128)S(1)}, u32[]{:S(2)}, u32[]{:S(2)}) collective-permute-start(f32[96,24]{0,1:T(8,128)S(1)} %fusion.17), channel_id=1, source_target_pairs={{0,1},{1,0},{2,3},{3,2},{4,5},{5,4},{6,7},{7,6},{8,9},{9,8},{10,11... | collective-permute-start | bytes 27656 | tf_op jit(solution)/shard_map/ppermute | solution.py:229
  97.9 2.0 %collective-permute-done.17 = f32[96,24]{0,1:T(8,128)S(1)} collective-permute-done((f32[96,24]{0,1:T(8,128)S(1)}, f32[96,24]{0,1:T(8,128)S(1)}, u32[]{:S(2)}, u32[]{:S(2)}) %collective-permute-start.17) | collective-permute-done | bytes 9248 | tf_op jit(solution)/shard_map/ppermute | solution.py:229
  99.8 2.6 %collective-permute-start.18 = (f32[96,24]{0,1:T(8,128)S(1)}, f32[96,24]{0,1:T(8,128)S(1)}, u32[]{:S(2)}, u32[]{:S(2)}) collective-permute-start(f32[96,24]{0,1:T(8,128)S(1)} %add.82), channel_id=1, source_target_pairs={{0,2},{1,3},{2,0},{3,1},{4,6},{5,7},{6,4},{7,5},{8,10},{9,11},{10,... | collective-permute-start | bytes 27656 | tf_op jit(solution)/shard_map/ppermute | solution.py:229
  102.5 1.7 %collective-permute-done.18 = f32[96,24]{0,1:T(8,128)S(1)} collective-permute-done((f32[96,24]{0,1:T(8,128)S(1)}, f32[96,24]{0,1:T(8,128)S(1)}, u32[]{:S(2)}, u32[]{:S(2)}) %collective-permute-start.18) | collective-permute-done | bytes 9248 | tf_op jit(solution)/shard_map/ppermute | solution.py:229
  104.1 2.1 %collective-permute-start.19 = (f32[96,24]{0,1:T(8,128)S(1)}, f32[96,24]{0,1:T(8,128)S(1)}, u32[]{:S(2)}, u32[]{:S(2)}) collective-permute-start(f32[96,24]{0,1:T(8,128)S(1)} %add.83), channel_id=1, source_target_pairs={{0,4},{1,5},{2,6},{3,7},{4,0},{5,1},{6,2},{7,3},{8,12},{9,13},{10,... | collective-permute-start | bytes 27656 | tf_op jit(solution)/shard_map/ppermute | solution.py:229
  (91 shorter events, 25.6 us)
Async XLA Ops:
  0.6 11.9 %copy-start = (bf16[8,16,2,128]{3,2,1,0:T(2,128)(2,1)S(1)}, bf16[8,16,2,128]{3,2,1,0:T(2,128)(2,1)}, u32[]{:S(2)}) copy-start(bf16[8,16,2,128]{3,2,1,0:T(2,128)(2,1)} %param.13) | copy-start | bytes 196612
  0.6 11.2 %copy-start.3 = (s32[8]{0:T(128)S(1)}, s32[8]{0:T(128)}, u32[]{:S(2)}) copy-start(s32[8]{0:T(128)} %param.14) | copy-start | bytes 100
  0.7 15.5 %copy-start.4 = (f32[16,8,128]{2,1,0:T(8,128)S(1)}, f32[16,8,128]{2,1,0:T(8,128)}, u32[]{:S(2)}) copy-start(f32[16,8,128]{2,1,0:T(8,128)} %param.12) | copy-start | bytes 196612
  1.9 17.5 %collective-permute-start = (bf16[12,16,8,128]{3,2,1,0:T(8,128)(2,1)S(1)}, bf16[12,16,8,128]{3,2,1,0:T(8,128)(2,1)S(1)}, u32[]{:S(2)}, u32[]{:S(2)}) collective-permute-start(bf16[12,16,8,128]{3,2,1,0:T(8,128)(2,1)S(1)} %get-tuple-element.26), channel_id=1, source_target_pairs={{0,1},{1,0},{2,3},{3,2},{4,5},{5,4},{6,7},{7,6},{8,9},{9,8},{10,11... | collective-permute-start | bytes 1179656 | tf_op jit(solution)/shard_map/ppermute | solution.py:229
  4.9 14.5 %collective-permute-start.1 = (bf16[12,16,8,128]{3,2,1,0:T(8,128)(2,1)S(1)}, bf16[12,16,8,128]{3,2,1,0:T(8,128)(2,1)S(1)}, u32[]{:S(2)}, u32[]{:S(2)}) collective-permute-start(bf16[12,16,8,128]{3,2,1,0:T(8,128)(2,1)S(1)} %get-tuple-element.27.refs_0_), channel_id=1, source_target_pairs={{2,0},{4,2},{6,4},{1,3},{3,5},{5,7},{10,8},{12,10},{14,12},{9,11},... | collective-permute-start | bytes 1179656 | tf_op jit(solution)/shard_map/ppermute | solution.py:229
  7.2 12.2 %collective-permute-start.2 = (bf16[12,12,8,128]{3,2,1,0:T(8,128)(2,1)S(1)}, bf16[12,12,8,128]{3,2,1,0:T(8,128)(2,1)S(1)}, u32[]{:S(2)}, u32[]{:S(2)}) collective-permute-start(bf16[12,12,8,128]{3,2,1,0:T(8,128)(2,1)S(1)} %constant_dynamic-slice_fusion.2), channel_id=1, source_target_pairs={{0,2},{2,4},{4,6},{3,1},{5,3},{7,5},{8,10},{10,12},{12,14},{11,9},... | collective-permute-start | bytes 884744 | tf_op jit(solution)/shard_map/ppermute | solution.py:229
  13.1 1.4 %collective-permute-start.3 = (bf16[4,16,2,128]{3,2,1,0:T(2,128)(2,1)S(1)}, bf16[4,16,2,128]{3,2,1,0:T(2,128)(2,1)S(1)}, u32[]{:S(2)}, u32[]{:S(2)}) collective-permute-start(bf16[4,16,2,128]{3,2,1,0:T(2,128)(2,1)S(1)} %gather_fusion.1), channel_id=1, source_target_pairs={{0,8},{8,0},{16,24},{24,16},{1,9},{9,1},{17,25},{25,17},{2,10},{10... | collective-permute-start | bytes 98312 | tf_op jit(solution)/shard_map/ppermute | solution.py:250
  14.6 4.6 %collective-permute-start.4 = (bf16[4,16,4,128]{3,2,1,0:T(4,128)(2,1)S(1)}, bf16[4,16,4,128]{3,2,1,0:T(4,128)(2,1)S(1)}, u32[]{:S(2)}, u32[]{:S(2)}) collective-permute-start(bf16[4,16,4,128]{3,2,1,0:T(4,128)(2,1)S(1)} %pad_maximum_fusion.6), channel_id=1, source_target_pairs={{0,16},{8,24},{16,0},{24,8},{1,17},{9,25},{17,1},{25,9},{2,18},{10... | collective-permute-start | bytes 196616 | tf_op jit(solution)/shard_map/ppermute | solution.py:250
  19.4 5.9 %collective-permute-start.5 = (bf16[5,16,8,128]{3,2,1,0:T(8,128)(2,1)S(1)}, bf16[5,16,8,128]{3,2,1,0:T(8,128)(2,1)S(1)}, u32[]{:S(2)}, u32[]{:S(2)}) collective-permute-start(bf16[5,16,8,128]{3,2,1,0:T(8,128)(2,1)S(1)} %pad_maximum_fusion.5.refs_6_), channel_id=1, source_target_pairs={{0,1},{1,0},{2,3},{3,2},{4,5},{5,4},{6,7},{7,6},{8,9},{9,8},{10,11... | collective-permute-start | bytes 491528 | tf_op jit(solution)/shard_map/ppermute | solution.py:229
  25.3 14.9 %collective-permute-start.6 = (bf16[212,8,128]{2,1,0:T(8,128)(2,1)S(1)}, bf16[212,8,128]{2,1,0:T(8,128)(2,1)S(1)}, u32[]{:S(2)}, u32[]{:S(2)}) collective-permute-start(bf16[212,8,128]{2,1,0:T(8,128)(2,1)S(1)} %pad_maximum_fusion.2), channel_id=1, source_target_pairs={{0,2},{2,4},{4,6},{3,1},{5,3},{7,5},{8,10},{10,12},{12,14},{11,9},... | collective-permute-start | bytes 1302536 | tf_op jit(solution)/shard_map/ppermute | solution.py:229
  29.0 11.3 %collective-permute-start.7 = (bf16[188,8,128]{2,1,0:T(8,128)(2,1)S(1)}, bf16[188,8,128]{2,1,0:T(8,128)(2,1)S(1)}, u32[]{:S(2)}, u32[]{:S(2)}) collective-permute-start(bf16[188,8,128]{2,1,0:T(8,128)(2,1)S(1)} %pad_maximum_fusion.3), channel_id=1, source_target_pairs={{2,0},{4,2},{6,4},{1,3},{3,5},{5,7},{10,8},{12,10},{14,12},{9,11},... | collective-permute-start | bytes 1155080 | tf_op jit(solution)/shard_map/ppermute | solution.py:229
  31.0 18.6 %collective-permute-start.8 = (bf16[160,8,128]{2,1,0:T(8,128)(2,1)}, bf16[160,8,128]{2,1,0:T(8,128)(2,1)S(1)}, u32[]{:S(2)}, u32[]{:S(2)}) collective-permute-start(bf16[160,8,128]{2,1,0:T(8,128)(2,1)} %pad_maximum_fusion.4), channel_id=1, source_target_pairs={{0,8},{8,0},{16,24},{24,16},{1,9},{9,1},{17,25},{25,17},{2,10},{10... | collective-permute-start | bytes 983048 | tf_op jit(solution)/shard_map/ppermute | solution.py:230
  40.3 15.5 %copy-start.2 = (bf16[256,128]{1,0:T(8,128)(2,1)S(1)}, bf16[256,128]{1,0:T(8,128)(2,1)}, u32[]{:S(2)}) copy-start(bf16[256,128]{1,0:T(8,128)(2,1)} %constant.109.clone.refs_13_) | copy-start | bytes 196612
  41.1 14.6 %collective-permute-start.9 = (bf16[232,8,128]{2,1,0:T(8,128)(2,1)}, bf16[232,8,128]{2,1,0:T(8,128)(2,1)S(1)}, u32[]{:S(2)}, u32[]{:S(2)}) collective-permute-start(bf16[232,8,128]{2,1,0:T(8,128)(2,1)} %pad_maximum_fusion.1), channel_id=1, source_target_pairs={{0,8},{8,0},{16,24},{24,16},{1,9},{9,1},{17,25},{25,17},{2,10},{10... | collective-permute-start | bytes 1425416 | tf_op jit(solution)/shard_map/ppermute | solution.py:230
  43.7 31.0 %collective-permute-start.14 = (bf16[24,16,8,128]{3,0,2,1:T(8,128)(2,1)}, bf16[24,16,8,128]{3,0,2,1:T(8,128)(2,1)}, u32[]{:S(2)}, u32[]{:S(2)}) collective-permute-start(bf16[24,16,8,128]{3,0,2,1:T(8,128)(2,1)} %copy.28), channel_id=1, source_target_pairs={{0,16},{8,24},{16,0},{24,8},{1,17},{9,25},{17,1},{25,9},{2,18},{10... | collective-permute-start | bytes 2359304 | tf_op jit(solution)/shard_map/ppermute | solution.py:271
  45.2 29.5 %collective-permute-start.15 = (bf16[24,16,8,128]{3,2,1,0:T(8,128)(2,1)}, bf16[24,16,8,128]{3,2,1,0:T(8,128)(2,1)}, u32[]{:S(2)}, u32[]{:S(2)}) collective-permute-start(bf16[24,16,8,128]{3,2,1,0:T(8,128)(2,1)} %param.15), channel_id=1, source_target_pairs={{0,8},{8,0},{16,24},{24,16},{1,9},{9,1},{17,25},{25,17},{2,10},{10... | collective-permute-start | bytes 2359304 | tf_op jit(solution)/shard_map/ppermute | solution.py:230
  45.4 19.8 %collective-permute-start.10 = (bf16[96,8,128]{2,1,0:T(8,128)(2,1)}, bf16[96,8,128]{2,1,0:T(8,128)(2,1)}, u32[]{:S(2)}, u32[]{:S(2)}) collective-permute-start(bf16[96,8,128]{2,1,0:T(8,128)(2,1)} %bitcast.86), channel_id=1, source_target_pairs={{0,2},{2,4},{4,6},{3,1},{5,3},{7,5},{8,10},{10,12},{12,14},{11,9},... | collective-permute-start | bytes 589832 | tf_op jit(solution)/shard_map/ppermute | solution.py:229
  49.6 15.6 %collective-permute-start.11 = (bf16[72,8,128]{2,1,0:T(8,128)(2,1)}, bf16[72,8,128]{2,1,0:T(8,128)(2,1)}, u32[]{:S(2)}, u32[]{:S(2)}) collective-permute-start(bf16[72,8,128]{2,1,0:T(8,128)(2,1)} %bitcast.87), channel_id=1, source_target_pairs={{2,0},{4,2},{6,4},{1,3},{3,5},{5,7},{10,8},{12,10},{14,12},{9,11},... | collective-permute-start | bytes 442376 | tf_op jit(solution)/shard_map/ppermute | solution.py:229
  65.1 9.7 %collective-permute-start.12 = (bf16[6,16,8,128]{3,2,1,0:T(8,128)(2,1)S(1)}, bf16[6,16,8,128]{3,2,1,0:T(8,128)(2,1)S(1)}, u32[]{:S(2)}, u32[]{:S(2)}) collective-permute-start(bf16[6,16,8,128]{3,2,1,0:T(8,128)(2,1)S(1)} %get-tuple-element.15), channel_id=1, source_target_pairs={{0,1},{1,0},{2,3},{3,2},{4,5},{5,4},{6,7},{7,6},{8,9},{9,8},{10,11... | collective-permute-start | bytes 589832 | tf_op jit(solution)/shard_map/ppermute | solution.py:229
  74.7 19.6 %collective-permute-start.16 = (bf16[24,16,8,128]{3,0,2,1:T(8,128)(2,1)}, bf16[24,16,8,128]{3,0,2,1:T(8,128)(2,1)S(1)}, u32[]{:S(2)}, u32[]{:S(2)}) collective-permute-start(bf16[24,16,8,128]{3,0,2,1:T(8,128)(2,1)} %collective-permute-done.14), channel_id=1, source_target_pairs={{0,8},{8,0},{16,24},{24,16},{1,9},{9,1},{17,25},{25,17},{2,10},{10... | collective-permute-start | bytes 2359304 | tf_op jit(solution)/shard_map/ppermute | solution.py:230
  74.8 7.6 %collective-permute-start.13 = (bf16[6,16,8,128]{3,2,1,0:T(8,128)(2,1)S(1)}, bf16[6,16,8,128]{3,2,1,0:T(8,128)(2,1)S(1)}, u32[]{:S(2)}, u32[]{:S(2)}) collective-permute-start(bf16[6,16,8,128]{3,2,1,0:T(8,128)(2,1)S(1)} %get-tuple-element.17), channel_id=1, source_target_pairs={{0,1},{1,0},{2,3},{3,2},{4,5},{5,4},{6,7},{7,6},{8,9},{9,8},{10,11... | collective-permute-start | bytes 589832 | tf_op jit(solution)/shard_map/ppermute | solution.py:229
  96.1 3.8 %collective-permute-start.17 = (f32[96,24]{0,1:T(8,128)S(1)}, f32[96,24]{0,1:T(8,128)S(1)}, u32[]{:S(2)}, u32[]{:S(2)}) collective-permute-start(f32[96,24]{0,1:T(8,128)S(1)} %fusion.17), channel_id=1, source_target_pairs={{0,1},{1,0},{2,3},{3,2},{4,5},{5,4},{6,7},{7,6},{8,9},{9,8},{10,11... | collective-permute-start | bytes 27656 | tf_op jit(solution)/shard_map/ppermute | solution.py:229
  99.8 4.3 %collective-permute-start.18 = (f32[96,24]{0,1:T(8,128)S(1)}, f32[96,24]{0,1:T(8,128)S(1)}, u32[]{:S(2)}, u32[]{:S(2)}) collective-permute-start(f32[96,24]{0,1:T(8,128)S(1)} %add.82), channel_id=1, source_target_pairs={{0,2},{1,3},{2,0},{3,1},{4,6},{5,7},{6,4},{7,5},{8,10},{9,11},{10,... | collective-permute-start | bytes 27656 | tf_op jit(solution)/shard_map/ppermute | solution.py:229
  104.1 4.6 %collective-permute-start.19 = (f32[96,24]{0,1:T(8,128)S(1)}, f32[96,24]{0,1:T(8,128)S(1)}, u32[]{:S(2)}, u32[]{:S(2)}) collective-permute-start(f32[96,24]{0,1:T(8,128)S(1)} %add.83), channel_id=1, source_target_pairs={{0,4},{1,5},{2,6},{3,7},{4,0},{5,1},{6,2},{7,3},{8,12},{9,13},{10,... | collective-permute-start | bytes 27656 | tf_op jit(solution)/shard_map/ppermute | solution.py:229
  (1 other events, 0.9 us)

commit v6 on v4

--- a/solution.py
+++ b/solution.py
@@ -49,7 +49,7 @@
     return (steps + 1) // 2, (-(-(halo - rows) // 4) + 1) // 2
 
 
-def march(steps, rows, halo, begin, scalars, *refs):
+def march(steps, rows, halo, begin, bounds_ref, *refs):
     pieces = refs[0:6]
     near_ref, near_x_ref, other_ref, first_ref, second_ref = refs[6:11]
     left_ref, right_ref, own_ref, send_ref = refs[11:15]
@@ -57,7 +57,9 @@
     total = 2 * rows + 2 * halo
     cy = 8
     far = halo - rows
-    par, core = scalars[0], scalars[1]
+    place = lax.axis_index("store")
+    par, core = place % 2, lax.axis_index("probe") % 2
+    base = (place // 2) * 2 * rows - halo
     probes = pieces[0].shape[0]
     even = (halo, halo + rows, halo + 2 * rows, 0, halo - rows, halo + 3 * rows)
     odd = (halo + rows, halo, halo - rows, halo + 3 * rows, halo + 2 * rows, 0)
@@ -91,8 +93,8 @@
 
     for q in range(PACK):
         probe = begin + pl.program_id(0) * PACK + q
-        low = scalars[2 + 2 * probe]
-        high = scalars[3 + 2 * probe]
+        low = bounds_ref[probes * par + probe, 0] - base
+        high = bounds_ref[probes * par + probe, 1] - base
         for j in range(6):
             where = pl.ds(pl.multiple_of(starts[j] * cy, 32), counts[j] * cy)
             value = pieces[j][probe].astype(jnp.float32)
@@ -164,7 +166,7 @@
         advanced(*first, *made)
 
 
-def propagate(scalars, pieces, extras, begin, count, steps, rows, halo):
+def propagate(bounds, pieces, extras, begin, count, steps, rows, halo):
     _, _, cy, cz = pieces[0].shape
     left, right = tables(cy, cz)
     left, right = jnp.asarray(left, jnp.bfloat16), jnp.asarray(right, jnp.bfloat16)
@@ -195,7 +197,7 @@
         compiler_params=pltpu.CompilerParams(vmem_limit_bytes=20 << 20),
         cost_estimate=pl.CostEstimate(flops=cells * 8000, bytes_accessed=cells * 4, transcendentals=0),
         name="march",
-    )(scalars, *pieces, *extras, left, right)
+    )(bounds, *pieces, *extras, left, right)
 
 
 def local(probe_field, bounds, courant, snapshots, snap_times, basis_panels):
@@ -243,15 +245,15 @@
         cores(planes(extra_x, side_a[half:], side_b[half:])),
         cores(planes(side_c[half:], side_d[half:])),
     )
-    base = (place // 2) * 2 * rows - halo
-    mine_bounds = lax.dynamic_slice_in_dim(bounds, half * par, half, axis=0) - base
-    scalars = jnp.concatenate([jnp.stack([par, core]), mine_bounds.reshape(-1)]).astype(jnp.int32)
-    basis_later = lax.optimization_barrier((basis_panels, extra_x))[0]
+    basis_later = basis_panels
     crossed = lax.ppermute(basis_later, "probe", [(i, i ^ 2) for i in range(members)])
     first = par == 0
     own, back = [], []
     for begin, count in ((0, half // 2), (half // 2, half - half // 2)):
-        kept, sent = propagate(scalars, pieces, extras, begin, count, steps, rows, halo)
+        kept, sent = propagate(bounds, pieces, extras, begin, count, steps, rows, halo)
+        bounds = lax.optimization_barrier((bounds, kept))[0]
+        if back:
+            sent = lax.optimization_barrier((sent, back[0]))[0]
         own.append(kept)
         back.append(hop(sent, swap))
     panels = [basis_later, cores(basis_later)]

time: 95.4 us -> 106 us (1.11)
  local copies, waits for them, and re-layouts: 8.98 us -> 16.5 us
  starting transfers between devices: 24.2 us -> 26 us
  waiting for transfers between devices: 26.9 us -> 28.4 us
    unnamed x21 -> x34, local copies, waits for them, and re-layouts: 3.06 us -> 9.95 us
    ppermute x11, starting transfers between devices: 22 us -> 24 us  [local(): hop = lambda x, pairs: lax.ppermute(x, 'store', pairs)]
    ppermute x11, waiting for transfers between devices: 26.8 us -> 28.4 us  [local(): hop = lambda x, pairs: lax.ppermute(x, 'store', pairs)]
  transfers between devices with their start and end apart: 17 -> 17, of which waited for: 7 -> 7; matrix products, arithmetic and copies ran while one was open for 14% -> 12% of each run, Pallas kernels for 20% -> 19%
where the time goes in v6:
time: 106 us; the launch traced here: 105 us
  waiting for transfers between devices  28.4 us (27%)
  starting transfers between devices  26 us (25%)
  Pallas kernels  19.7 us (19%)
  local copies, waits for them, and re-layouts  16.5 us (16%)
  blocking collectives  5.79 us (5%)
  other arithmetic  5.64 us (5%)
  matrix products  2.06 us (2%)
    ppermute x11, waiting for transfers between devices, local(): hop = lambda x, pairs: lax.ppermute(x, 'store', pairs)  28.4 us
    ppermute x11, starting transfers between devices, local(): hop = lambda x, pairs: lax.ppermute(x, 'store', pairs)  24 us
    pallas_call x2, Pallas kernels, propagate(): pl.pallas_call(functools.partial(march, steps, rows, halo, begin), grid_s...  19.7 us
    unnamed x34, local copies, waits for them, and re-layouts  9.95 us
    all_gather x1, blocking collectives, local(): all_snaps = lax.all_gather(snapshots, 'probe', axis=2, tiled=True)  5.79 us
    concatenate x1, local copies, waits for them, and re-layouts, local(): jnp.concatenate(panels, axis=0)  2.15 us
  transfers between devices with their start and end apart: 17, of which 7 were waited for; matrix products, arithmetic and copies ran while one was open for 12% of the time, Pallas kernels for 19%

profile of v6, /device:TPU:0, one launch (start us, length us, event | category | flops | bytes accessed | tf_op | source)
XLA Modules:
  0.0 105.2 jit_solution(2002606432512658106)
XLA Ops:
  0.7 2.0 %constant_dynamic-slice_fusion = (bf16[12,16,8,128]{3,2,1,0:T(8,128)(2,1)}, bf16[12,16,8,128]{3,2,1,0:T(8,128)(2,1)S(1)}) fusion(bf16[24,16,8,128]{3,2,1,0:T(8,128)(2,1)} %param.10, s32[]{:T(128)S(6)} %select_n.134, s32[]{:T(128)S(6)} %select_n.133), kind=kLoop, calls=%fused_computation.49 | loop fusion | bytes 1572872 | tf_op jit(solution)/shard_map/dynamic_slice | solution.py:233
  2.7 2.9 %collective-permute-start = (bf16[12,16,8,128]{3,2,1,0:T(8,128)(2,1)}, bf16[12,16,8,128]{3,2,1,0:T(8,128)(2,1)S(1)}, u32[]{:S(2)}, u32[]{:S(2)}) collective-permute-start(bf16[12,16,8,128]{3,2,1,0:T(8,128)(2,1)} %get-tuple-element.23), channel_id=1, source_target_pairs={{0,1},{1,0},{2,3},{3,2},{4,5},{5,4},{6,7},{7,6},{8,9},{9,8},{10,11... | collective-permute-start | bytes 1179656 | tf_op jit(solution)/shard_map/ppermute | solution.py:218
  6.3 5.8 %all_gather.3 = bf16[8,16,8,128]{3,1,0,2:T(8,128)(2,1)S(1)} all-gather(bf16[8,16,2,128]{3,1,0,2:T(8,128)(2,1)S(1)} %copy.40), channel_id=1, replica_groups=mesh['probe'=4,'store'=8] {'probe'}, dimensions={2}, use_global_device_ids=true | all-gather | bytes 327680 | tf_op jit(solution)/shard_map/all_gather | solution.py:223
  13.0 1.3 %collective-permute-start.1 = (bf16[17,16,8,128]{3,2,1,0:T(8,128)(2,1)S(1)}, bf16[17,16,8,128]{3,2,1,0:T(8,128)(2,1)S(1)}, u32[]{:S(2)}, u32[]{:S(2)}) collective-permute-start(bf16[17,16,8,128]{3,2,1,0:T(8,128)(2,1)S(1)} %pad_maximum_fusion.1), channel_id=1, source_target_pairs={{2,0},{4,2},{6,4},{1,3},{3,5},{5,7},{10,8},{12,10},{14,12},{9,11},... | collective-permute-start | bytes 1671176 | tf_op jit(solution)/shard_map/ppermute | solution.py:218
  14.9 2.2 %collective-permute-start.3 = (bf16[5,16,8,128]{3,2,1,0:T(8,128)(2,1)S(1)}, bf16[5,16,8,128]{3,2,1,0:T(8,128)(2,1)S(1)}, u32[]{:S(2)}, u32[]{:S(2)}) collective-permute-start(bf16[5,16,8,128]{3,2,1,0:T(8,128)(2,1)S(1)} %pad_maximum_fusion.5.refs_6_), channel_id=1, source_target_pairs={{0,1},{1,0},{2,3},{3,2},{4,5},{5,4},{6,7},{7,6},{8,9},{9,8},{10,11... | collective-permute-start | bytes 491528 | tf_op jit(solution)/shard_map/ppermute | solution.py:218
  17.1 1.7 %constant_dynamic-update-slice_fusion.5 = (bf16[48,16,8,128]{3,0,2,1:T(8,128)(2,1)}, bf16[24,16,8,128]{3,0,2,1:T(8,128)(2,1)}) fusion(bf16[24,16,8,128]{3,2,1,0:T(8,128)(2,1)S(1)} %copy-done.10), kind=kLoop, calls=%fused_computation.38 | loop fusion | bytes 2359296
  18.9 2.7 %collective-permute-done.3.refs_7_ = bf16[5,16,8,128]{3,2,1,0:T(8,128)(2,1)S(1)} collective-permute-done((bf16[5,16,8,128]{3,2,1,0:T(8,128)(2,1)S(1)}, bf16[5,16,8,128]{3,2,1,0:T(8,128)(2,1)S(1)}, u32[]{:S(2)}, u32[]{:S(2)}) %collective-permute-start.3) | collective-permute-done | bytes 163872 | tf_op jit(solution)/shard_map/ppermute | solution.py:218
  22.4 3.6 %collective-permute-start.4 = (bf16[17,16,8,128]{3,2,1,0:T(8,128)(2,1)}, bf16[17,16,8,128]{3,2,1,0:T(8,128)(2,1)S(1)}, u32[]{:S(2)}, u32[]{:S(2)}) collective-permute-start(bf16[17,16,8,128]{3,2,1,0:T(8,128)(2,1)} %pad_maximum_fusion.2), channel_id=1, source_target_pairs={{0,2},{2,4},{4,6},{3,1},{5,3},{7,5},{8,10},{10,12},{12,14},{11,9},... | collective-permute-start | bytes 1671176 | tf_op jit(solution)/shard_map/ppermute | solution.py:218
  26.8 3.5 %collective-permute-start.2 = (bf16[15,12,8,128]{3,2,1,0:T(8,128)(2,1)}, bf16[15,12,8,128]{3,2,1,0:T(8,128)(2,1)S(1)}, u32[]{:S(2)}, u32[]{:S(2)}) collective-permute-start(bf16[15,12,8,128]{3,2,1,0:T(8,128)(2,1)} %fusion.7), channel_id=1, source_target_pairs={{0,2},{2,4},{4,6},{3,1},{5,3},{7,5},{8,10},{10,12},{12,14},{11,9},... | collective-permute-start | bytes 1105928 | tf_op jit(solution)/shard_map/ppermute | solution.py:218
  30.4 1.3 %collective-permute-start.5 = (bf16[15,12,8,128]{3,2,1,0:T(8,128)(2,1)S(1)}, bf16[15,12,8,128]{3,2,1,0:T(8,128)(2,1)S(1)}, u32[]{:S(2)}, u32[]{:S(2)}) collective-permute-start(bf16[15,12,8,128]{3,2,1,0:T(8,128)(2,1)S(1)} %fusion.5), channel_id=1, source_target_pairs={{2,0},{4,2},{6,4},{1,3},{3,5},{5,7},{10,8},{12,10},{14,12},{9,11},... | collective-permute-start | bytes 1105928 | tf_op jit(solution)/shard_map/ppermute | solution.py:218
  31.7 13.8 %collective-permute-done.2.refs_3_ = bf16[15,12,8,128]{3,2,1,0:T(8,128)(2,1)S(1)} collective-permute-done((bf16[15,12,8,128]{3,2,1,0:T(8,128)(2,1)}, bf16[15,12,8,128]{3,2,1,0:T(8,128)(2,1)S(1)}, u32[]{:S(2)}, u32[]{:S(2)}) %collective-permute-start.2) | collective-permute-done | bytes 368672 | tf_op jit(solution)/shard_map/ppermute | solution.py:218
  46.2 1.5 %collective-permute-start.12 = (bf16[24,16,8,128]{3,0,2,1:T(8,128)(2,1)}, bf16[24,16,8,128]{3,0,2,1:T(8,128)(2,1)}, u32[]{:S(2)}, u32[]{:S(2)}) collective-permute-start(bf16[24,16,8,128]{3,0,2,1:T(8,128)(2,1)} %get-tuple-element.22), channel_id=1, source_target_pairs={{0,16},{8,24},{16,0},{24,8},{1,17},{9,25},{17,1},{25,9},{2,18},{10... | collective-permute-start | bytes 2359304 | tf_op jit(solution)/shard_map/ppermute | solution.py:249
  49.1 2.2 %constant_dynamic-update-slice_fusion.4 = bf16[48,16,8,128]{3,0,2,1:T(8,128)(2,1)} fusion(bf16[48,16,8,128]{3,0,2,1:T(8,128)(2,1)} %get-tuple-element.21, bf16[24,16,8,128]{3,0,2,1:T(8,128)(2,1)} %collective-permute-done.11), kind=kLoop, calls=%fused_computation.37 | loop fusion | bytes 1572864 | tf_op jit(solution)/shard_map/concatenate | solution.py:261
  54.7 9.9 %march.2 = (f32[6,16,8,128]{3,2,1,0:T(8,128)S(1)}, bf16[6,16,8,128]{3,2,1,0:T(8,128)(2,1)S(1)}) custom-call(s32[24,2]{1,0:T(8,128)S(1)} %copy.42.bounds_ref, bf16[12,16,8,128]{3,2,1,0:T(8,128)(2,1)S(1)} %get-tuple-element.24.refs_0_, bf16[12,16,8,128]{3,2,1,0:T(8,128)(2,1)S(1)} %collective-permute-done.refs_1_, ...), custom_call_target="tpu_custom_call" | custom-call | flops 4325376000 | bytes 2162688 | tf_op jit(solution)/shard_map/march/pallas_call | solution.py:190
  65.3 2.5 %collective-permute-start.9 = (bf16[6,16,8,128]{3,2,1,0:T(8,128)(2,1)}, bf16[6,16,8,128]{3,2,1,0:T(8,128)(2,1)S(1)}, u32[]{:S(2)}, u32[]{:S(2)}) collective-permute-start(bf16[6,16,8,128]{3,2,1,0:T(8,128)(2,1)} %copy-done.4), channel_id=1, source_target_pairs={{0,1},{1,0},{2,3},{3,2},{4,5},{5,4},{6,7},{7,6},{8,9},{9,8},{10,11... | collective-permute-start | bytes 589832 | tf_op jit(solution)/shard_map/ppermute | solution.py:218
  70.5 9.9 %march.3 = (f32[6,16,8,128]{3,2,1,0:T(8,128)S(1)}, bf16[6,16,8,128]{3,2,1,0:T(8,128)(2,1)S(1)}) custom-call(s32[24,2]{1,0:T(8,128)S(1)} %copy.43.bounds_ref, bf16[12,16,8,128]{3,2,1,0:T(8,128)(2,1)S(1)} %get-tuple-element.24.refs_0_, bf16[12,16,8,128]{3,2,1,0:T(8,128)(2,1)S(1)} %collective-permute-done.refs_1_, ...), custom_call_target="tpu_custom_call" | custom-call | flops 4325376000 | bytes 2162688 | tf_op jit(solution)/shard_map/march/pallas_call | solution.py:190
  80.4 1.3 %constant_dynamic-update-slice_fusion.7 = bf16[48,16,8,128]{3,0,2,1:T(8,128)(2,1)S(1)} fusion(bf16[24,16,8,128]{3,0,2,1:T(8,128)(2,1)} %collective-permute-done.12), kind=kLoop, calls=%fused_computation.40 | loop fusion | bytes 1572864
  81.7 1.3 %collective-permute-start.10 = (bf16[6,16,8,128]{3,2,1,0:T(8,128)(2,1)S(1)}, bf16[6,16,8,128]{3,2,1,0:T(8,128)(2,1)S(1)}, u32[]{:S(2)}, u32[]{:S(2)}) collective-permute-start(bf16[6,16,8,128]{3,2,1,0:T(8,128)(2,1)S(1)} %get-tuple-element.16), channel_id=1, source_target_pairs={{0,1},{1,0},{2,3},{3,2},{4,5},{5,4},{6,7},{7,6},{8,9},{9,8},{10,11... | collective-permute-start | bytes 589832 | tf_op jit(solution)/shard_map/ppermute | solution.py:218
  83.1 6.0 %collective-permute-done.10 = bf16[6,16,8,128]{3,2,1,0:T(8,128)(2,1)S(1)} collective-permute-done((bf16[6,16,8,128]{3,2,1,0:T(8,128)(2,1)S(1)}, bf16[6,16,8,128]{3,2,1,0:T(8,128)(2,1)S(1)}, u32[]{:S(2)}, u32[]{:S(2)}) %collective-permute-start.10) | collective-permute-done | bytes 196640 | tf_op jit(solution)/shard_map/ppermute | solution.py:218
  92.6 1.3 %collective-permute-start.14 = (f32[96,24]{0,1:T(8,128)S(1)}, f32[96,24]{0,1:T(8,128)S(1)}, u32[]{:S(2)}, u32[]{:S(2)}) collective-permute-start(f32[96,24]{0,1:T(8,128)S(1)} %fusion.10), channel_id=1, source_target_pairs={{0,1},{1,0},{2,3},{3,2},{4,5},{5,4},{6,7},{7,6},{8,9},{9,8},{10,11... | collective-permute-start | bytes 27656 | tf_op jit(solution)/shard_map/ppermute | solution.py:218
  93.8 2.5 %collective-permute-done.14 = f32[96,24]{0,1:T(8,128)S(1)} collective-permute-done((f32[96,24]{0,1:T(8,128)S(1)}, f32[96,24]{0,1:T(8,128)S(1)}, u32[]{:S(2)}, u32[]{:S(2)}) %collective-permute-start.14) | collective-permute-done | bytes 9248 | tf_op jit(solution)/shard_map/ppermute | solution.py:218
  96.3 1.5 %collective-permute-start.15 = (f32[96,24]{0,1:T(8,128)S(1)}, f32[96,24]{0,1:T(8,128)S(1)}, u32[]{:S(2)}, u32[]{:S(2)}) collective-permute-start(f32[96,24]{0,1:T(8,128)S(1)} %add.56), channel_id=1, source_target_pairs={{0,2},{1,3},{2,0},{3,1},{4,6},{5,7},{6,4},{7,5},{8,10},{9,11},{10,... | collective-permute-start | bytes 27656 | tf_op jit(solution)/shard_map/ppermute | solution.py:218
  97.9 2.2 %collective-permute-done.15 = f32[96,24]{0,1:T(8,128)S(1)} collective-permute-done((f32[96,24]{0,1:T(8,128)S(1)}, f32[96,24]{0,1:T(8,128)S(1)}, u32[]{:S(2)}, u32[]{:S(2)}) %collective-permute-start.15) | collective-permute-done | bytes 9248 | tf_op jit(solution)/shard_map/ppermute | solution.py:218
  100.0 2.6 %collective-permute-start.16 = (f32[96,24]{0,1:T(8,128)S(1)}, f32[96,24]{0,1:T(8,128)S(1)}, u32[]{:S(2)}, u32[]{:S(2)}) collective-permute-start(f32[96,24]{0,1:T(8,128)S(1)} %add.57), channel_id=1, source_target_pairs={{0,4},{1,5},{2,6},{3,7},{4,0},{5,1},{6,2},{7,3},{8,12},{9,13},{10,... | collective-permute-start | bytes 27656 | tf_op jit(solution)/shard_map/ppermute | solution.py:218
  (95 shorter events, 18.9 us)
Async XLA Ops:
  0.6 5.0 %copy-start = (s32[8]{0:T(128)S(1)}, s32[8]{0:T(128)}, u32[]{:S(2)}) copy-start(s32[8]{0:T(128)} %param.14) | copy-start | bytes 100
  0.6 5.6 %copy-start.12 = (bf16[8,16,2,128]{3,2,1,0:T(2,128)(2,1)S(1)}, bf16[8,16,2,128]{3,2,1,0:T(2,128)(2,1)}, u32[]{:S(2)}) copy-start(bf16[8,16,2,128]{3,2,1,0:T(2,128)(2,1)} %param.13) | copy-start | bytes 196612
  0.7 12.2 %copy-start.11 = (f32[16,8,128]{2,1,0:T(8,128)S(1)}, f32[16,8,128]{2,1,0:T(8,128)}, u32[]{:S(2)}) copy-start(f32[16,8,128]{2,1,0:T(8,128)} %param.12) | copy-start | bytes 196612
  2.7 12.3 %collective-permute-start = (bf16[12,16,8,128]{3,2,1,0:T(8,128)(2,1)}, bf16[12,16,8,128]{3,2,1,0:T(8,128)(2,1)S(1)}, u32[]{:S(2)}, u32[]{:S(2)}) collective-permute-start(bf16[12,16,8,128]{3,2,1,0:T(8,128)(2,1)} %get-tuple-element.23), channel_id=1, source_target_pairs={{0,1},{1,0},{2,3},{3,2},{4,5},{5,4},{6,7},{7,6},{8,9},{9,8},{10,11... | collective-permute-start | bytes 1179656 | tf_op jit(solution)/shard_map/ppermute | solution.py:218
  5.6 11.5 %copy-start.10 = (bf16[24,16,8,128]{3,2,1,0:T(8,128)(2,1)S(1)}, bf16[24,16,8,128]{3,2,1,0:T(8,128)(2,1)}, u32[]{:S(2)}) copy-start(bf16[24,16,8,128]{3,2,1,0:T(8,128)(2,1)} %param.15) | copy-start | bytes 2359300
  13.0 32.5 %collective-permute-start.1 = (bf16[17,16,8,128]{3,2,1,0:T(8,128)(2,1)S(1)}, bf16[17,16,8,128]{3,2,1,0:T(8,128)(2,1)S(1)}, u32[]{:S(2)}, u32[]{:S(2)}) collective-permute-start(bf16[17,16,8,128]{3,2,1,0:T(8,128)(2,1)S(1)} %pad_maximum_fusion.1), channel_id=1, source_target_pairs={{2,0},{4,2},{6,4},{1,3},{3,5},{5,7},{10,8},{12,10},{14,12},{9,11},... | collective-permute-start | bytes 1671176 | tf_op jit(solution)/shard_map/ppermute | solution.py:218
  14.9 6.6 %collective-permute-start.3 = (bf16[5,16,8,128]{3,2,1,0:T(8,128)(2,1)S(1)}, bf16[5,16,8,128]{3,2,1,0:T(8,128)(2,1)S(1)}, u32[]{:S(2)}, u32[]{:S(2)}) collective-permute-start(bf16[5,16,8,128]{3,2,1,0:T(8,128)(2,1)S(1)} %pad_maximum_fusion.5.refs_6_), channel_id=1, source_target_pairs={{0,1},{1,0},{2,3},{3,2},{4,5},{5,4},{6,7},{7,6},{8,9},{9,8},{10,11... | collective-permute-start | bytes 491528 | tf_op jit(solution)/shard_map/ppermute | solution.py:218
  18.9 30.3 %collective-permute-start.11 = (bf16[24,16,8,128]{3,0,2,1:T(8,128)(2,1)}, bf16[24,16,8,128]{3,0,2,1:T(8,128)(2,1)}, u32[]{:S(2)}, u32[]{:S(2)}) collective-permute-start(bf16[24,16,8,128]{3,0,2,1:T(8,128)(2,1)} %get-tuple-element.22), channel_id=1, source_target_pairs={{0,8},{8,0},{16,24},{24,16},{1,9},{9,1},{17,25},{25,17},{2,10},{10... | collective-permute-start | bytes 2359304 | tf_op jit(solution)/shard_map/ppermute | solution.py:219
  22.4 25.4 %collective-permute-start.4 = (bf16[17,16,8,128]{3,2,1,0:T(8,128)(2,1)}, bf16[17,16,8,128]{3,2,1,0:T(8,128)(2,1)S(1)}, u32[]{:S(2)}, u32[]{:S(2)}) collective-permute-start(bf16[17,16,8,128]{3,2,1,0:T(8,128)(2,1)} %pad_maximum_fusion.2), channel_id=1, source_target_pairs={{0,2},{2,4},{4,6},{3,1},{5,3},{7,5},{8,10},{10,12},{12,14},{11,9},... | collective-permute-start | bytes 1671176 | tf_op jit(solution)/shard_map/ppermute | solution.py:218
  26.8 18.6 %collective-permute-start.2 = (bf16[15,12,8,128]{3,2,1,0:T(8,128)(2,1)}, bf16[15,12,8,128]{3,2,1,0:T(8,128)(2,1)S(1)}, u32[]{:S(2)}, u32[]{:S(2)}) collective-permute-start(bf16[15,12,8,128]{3,2,1,0:T(8,128)(2,1)} %fusion.7), channel_id=1, source_target_pairs={{0,2},{2,4},{4,6},{3,1},{5,3},{7,5},{8,10},{10,12},{12,14},{11,9},... | collective-permute-start | bytes 1105928 | tf_op jit(solution)/shard_map/ppermute | solution.py:218
  30.3 18.8 %copy-start.13 = (s32[24,2]{0,1:T(2,128)S(1)}, s32[24,2]{0,1:T(2,128)}, u32[]{:S(2)}) copy-start(s32[24,2]{0,1:T(2,128)} %param.11) | copy-start | bytes 580
  30.4 17.4 %collective-permute-start.5 = (bf16[15,12,8,128]{3,2,1,0:T(8,128)(2,1)S(1)}, bf16[15,12,8,128]{3,2,1,0:T(8,128)(2,1)S(1)}, u32[]{:S(2)}, u32[]{:S(2)}) collective-permute-start(bf16[15,12,8,128]{3,2,1,0:T(8,128)(2,1)S(1)} %fusion.5), channel_id=1, source_target_pairs={{2,0},{4,2},{6,4},{1,3},{3,5},{5,7},{10,8},{12,10},{14,12},{9,11},... | collective-permute-start | bytes 1105928 | tf_op jit(solution)/shard_map/ppermute | solution.py:218
  46.2 5.1 %collective-permute-start.7 = (bf16[196,8,128]{2,1,0:T(8,128)(2,1)}, bf16[196,8,128]{2,1,0:T(8,128)(2,1)}, u32[]{:S(2)}, u32[]{:S(2)}) collective-permute-start(bf16[196,8,128]{2,1,0:T(8,128)(2,1)} %pad_maximum_fusion.3), channel_id=1, source_target_pairs={{0,8},{8,0},{16,24},{24,16},{1,9},{9,1},{17,25},{25,17},{2,10},{10... | collective-permute-start | bytes 1204232 | tf_op jit(solution)/shard_map/ppermute | solution.py:219
  46.2 21.6 %collective-permute-start.12 = (bf16[24,16,8,128]{3,0,2,1:T(8,128)(2,1)}, bf16[24,16,8,128]{3,0,2,1:T(8,128)(2,1)}, u32[]{:S(2)}, u32[]{:S(2)}) collective-permute-start(bf16[24,16,8,128]{3,0,2,1:T(8,128)(2,1)} %get-tuple-element.22), channel_id=1, source_target_pairs={{0,16},{8,24},{16,0},{24,8},{1,17},{9,25},{17,1},{25,9},{2,18},{10... | collective-permute-start | bytes 2359304 | tf_op jit(solution)/shard_map/ppermute | solution.py:249
  48.5 2.8 %collective-permute-start.8 = (bf16[116,8,128]{2,1,0:T(8,128)(2,1)}, bf16[116,8,128]{2,1,0:T(8,128)(2,1)S(1)}, u32[]{:S(2)}, u32[]{:S(2)}) collective-permute-start(bf16[116,8,128]{2,1,0:T(8,128)(2,1)} %pad_maximum_fusion.4), channel_id=1, source_target_pairs={{0,8},{8,0},{16,24},{24,16},{1,9},{9,1},{17,25},{25,17},{2,10},{10... | collective-permute-start | bytes 712712 | tf_op jit(solution)/shard_map/ppermute | solution.py:219
  48.8 2.5 %collective-permute-start.6 = (bf16[5,16,8,128]{3,2,1,0:T(8,128)(2,1)S(1)}, bf16[5,16,8,128]{3,2,1,0:T(8,128)(2,1)S(1)}, u32[]{:S(2)}, u32[]{:S(2)}) collective-permute-start(bf16[5,16,8,128]{3,2,1,0:T(8,128)(2,1)S(1)} %pad_maximum_fusion.5.refs_6_), channel_id=1, source_target_pairs={{0,8},{8,0},{16,24},{24,16},{1,9},{9,1},{17,25},{25,17},{2,10},{10... | collective-permute-start | bytes 491528 | tf_op jit(solution)/shard_map/ppermute | solution.py:219
  65.3 16.4 %collective-permute-start.9 = (bf16[6,16,8,128]{3,2,1,0:T(8,128)(2,1)}, bf16[6,16,8,128]{3,2,1,0:T(8,128)(2,1)S(1)}, u32[]{:S(2)}, u32[]{:S(2)}) collective-permute-start(bf16[6,16,8,128]{3,2,1,0:T(8,128)(2,1)} %copy-done.4), channel_id=1, source_target_pairs={{0,1},{1,0},{2,3},{3,2},{4,5},{5,4},{6,7},{7,6},{8,9},{9,8},{10,11... | collective-permute-start | bytes 589832 | tf_op jit(solution)/shard_map/ppermute | solution.py:218
  67.8 22.6 %collective-permute-start.13 = (bf16[24,16,8,128]{3,0,2,1:T(8,128)(2,1)}, bf16[24,16,8,128]{3,0,2,1:T(8,128)(2,1)S(1)}, u32[]{:S(2)}, u32[]{:S(2)}) collective-permute-start(bf16[24,16,8,128]{3,0,2,1:T(8,128)(2,1)} %collective-permute-done.12), channel_id=1, source_target_pairs={{0,8},{8,0},{16,24},{24,16},{1,9},{9,1},{17,25},{25,17},{2,10},{10... | collective-permute-start | bytes 2359304 | tf_op jit(solution)/shard_map/ppermute | solution.py:219
  67.8 0.9 copy-start.3
  80.4 8.8 %copy-start.9 = (bf16[48,16,8,128]{3,0,2,1:T(8,128)(2,1)S(1)}, bf16[48,16,8,128]{3,0,2,1:T(8,128)(2,1)}, u32[]{:S(2)}) copy-start(bf16[48,16,8,128]{3,0,2,1:T(8,128)(2,1)} %constant_dynamic-update-slice_fusion.4) | copy-start | bytes 4718596
  81.7 7.4 %collective-permute-start.10 = (bf16[6,16,8,128]{3,2,1,0:T(8,128)(2,1)S(1)}, bf16[6,16,8,128]{3,2,1,0:T(8,128)(2,1)S(1)}, u32[]{:S(2)}, u32[]{:S(2)}) collective-permute-start(bf16[6,16,8,128]{3,2,1,0:T(8,128)(2,1)S(1)} %get-tuple-element.16), channel_id=1, source_target_pairs={{0,1},{1,0},{2,3},{3,2},{4,5},{5,4},{6,7},{7,6},{8,9},{9,8},{10,11... | collective-permute-start | bytes 589832 | tf_op jit(solution)/shard_map/ppermute | solution.py:218
  92.6 3.8 %collective-permute-start.14 = (f32[96,24]{0,1:T(8,128)S(1)}, f32[96,24]{0,1:T(8,128)S(1)}, u32[]{:S(2)}, u32[]{:S(2)}) collective-permute-start(f32[96,24]{0,1:T(8,128)S(1)} %fusion.10), channel_id=1, source_target_pairs={{0,1},{1,0},{2,3},{3,2},{4,5},{5,4},{6,7},{7,6},{8,9},{9,8},{10,11... | collective-permute-start | bytes 27656 | tf_op jit(solution)/shard_map/ppermute | solution.py:218
  96.3 3.7 %collective-permute-start.15 = (f32[96,24]{0,1:T(8,128)S(1)}, f32[96,24]{0,1:T(8,128)S(1)}, u32[]{:S(2)}, u32[]{:S(2)}) collective-permute-start(f32[96,24]{0,1:T(8,128)S(1)} %add.56), channel_id=1, source_target_pairs={{0,2},{1,3},{2,0},{3,1},{4,6},{5,7},{6,4},{7,5},{8,10},{9,11},{10,... | collective-permute-start | bytes 27656 | tf_op jit(solution)/shard_map/ppermute | solution.py:218
  100.0 4.6 %collective-permute-start.16 = (f32[96,24]{0,1:T(8,128)S(1)}, f32[96,24]{0,1:T(8,128)S(1)}, u32[]{:S(2)}, u32[]{:S(2)}) collective-permute-start(f32[96,24]{0,1:T(8,128)S(1)} %add.57), channel_id=1, source_target_pairs={{0,4},{1,5},{2,6},{3,7},{4,0},{5,1},{6,2},{7,3},{8,12},{9,13},{10,... | collective-permute-start | bytes 27656 | tf_op jit(solution)/shard_map/ppermute | solution.py:218
  (7 other events, 5.8 us)

commit v7 on v5

--- a/solution.py
+++ b/solution.py
@@ -15,26 +15,23 @@
 
 
 def tables(cells_y, cells_z):
-    ratio = [0.0] + [t / taps[1] for t in taps[1:]]
-    left = np.zeros((SPAN, cells_y, SPAN + 8, cells_y), np.float32)
-    for i in range(SPAN):
+    def banded(apart, allowed):
+        out = jnp.zeros(apart.shape, jnp.float32)
         for d in range(1, 5):
-            for y in range(cells_y):
-                left[i, y, i + 4 + d, y] = ratio[d]
-                left[i, y, i + 4 - d, y] = ratio[d]
-                if y + d < cells_y:
-                    left[i, y, i + 4, y + d] = ratio[d]
-                if y - d >= 0:
-                    left[i, y, i + 4, y - d] = ratio[d]
-    right = np.zeros((cells_z, cells_z), np.float32)
-    for z in range(cells_z):
-        for d in range(1, 5):
-            if z + d < cells_z:
-                right[z, z + d] = ratio[d]
-            if z - d >= 0:
-                right[z, z - d] = ratio[d]
-    left = left.reshape(SPAN * cells_y, (SPAN + 8) * cells_y)
-    return left, np.concatenate([right, right], axis=0)
+            out = jnp.where(allowed & (apart == d), taps[d] / taps[1], out)
+        return out
+
+    shape = (SPAN * cells_y, (SPAN + 8) * cells_y)
+    row = lax.broadcasted_iota(jnp.int32, shape, 0)
+    column = lax.broadcasted_iota(jnp.int32, shape, 1)
+    planes = jnp.abs(column // cells_y - 4 - row // cells_y)
+    lines = jnp.abs(column % cells_y - row % cells_y)
+    left = banded(planes, lines == 0) + banded(lines, planes == 0)
+    shape = (2 * cells_z, cells_z)
+    row = lax.broadcasted_iota(jnp.int32, shape, 0) % cells_z
+    apart = jnp.abs(row - lax.broadcasted_iota(jnp.int32, shape, 1))
+    right = banded(apart, apart > 0)
+    return left.astype(jnp.bfloat16), right.astype(jnp.bfloat16)
 
 
 def spans(rows):
@@ -49,16 +46,24 @@
     return (steps + 1) // 2, (-(-(halo - rows) // 4) + 1) // 2
 
 
-def march(steps, rows, halo, begin, scalars, *refs):
+def march(steps, rows, halo, begin, bounds_ref, *refs):
     wide, narrow = refs[0:4], refs[4:6]
+    c_ref, d_ref = narrow
     near_refs = refs[6:8]
-    c_ref, d_ref, near_other, far_other = refs[8:12]
-    left_ref, right_ref, own_ref, send_ref = refs[12:16]
-    pert, snap, scale, gain, fields, split = refs[16:22]
+    near_other, far_other, own_ref, send_ref = refs[8:12]
+    pert, snap, scale, gain, fields, split, left_ref, right_ref, a_buf, b_buf, sems = refs[12:23]
+    count = a_buf.shape[0]
+    fetch = [
+        pltpu.make_async_copy(wide[j].at[pl.ds(begin, count)], buf, sems.at[j - 2])
+        for j, buf in ((2, a_buf), (3, b_buf))
+    ]
     total = 2 * rows + 2 * halo
     cy = 8
     far = halo - rows
-    par, core = scalars[0], scalars[1]
+    place = lax.axis_index("store")
+    par, core = place % 2, lax.axis_index("probe") % 2
+    base = (place // 2) * 2 * rows - halo
+    probes = wide[0].shape[0]
     even = (halo, halo + rows, halo + 2 * rows, 0, halo - rows, halo + 3 * rows)
     odd = (halo + rows, halo, halo - rows, halo + 3 * rows, halo + 2 * rows, 0)
     counts = (rows, rows, rows, far, rows, far)
@@ -67,6 +72,9 @@
 
     @pl.when(pl.program_id(0) == 0)
     def _():
+        for copy in fetch:
+            copy.start()
+        left_ref[...], right_ref[...] = tables(cy, 128)
         near_size, far_size = (near_half + 1) * rows, (far_half + 1) * far
         c_base = c_ref.shape[0] - near_size - far_size
         d_base = d_ref.shape[0] - near_size - far_size
@@ -98,17 +106,21 @@
                     scale[where, :] = 2.0 + (3.0 * taps[0]) * (mine + other)
                     gain[where, :] = taps[1] * (mine + other)
 
+        for copy in fetch:
+            copy.wait()
+
     for q in range(PACK):
-        place = pl.program_id(0) * PACK + q
-        probe = begin + place
-        low = scalars[2 + 2 * probe]
-        high = scalars[3 + 2 * probe]
+        probe = begin + pl.program_id(0) * PACK + q
+        low = bounds_ref[probes * par + probe, 0] - base
+        high = bounds_ref[probes * par + probe, 1] - base
         for j in range(6):
             where = pl.ds(pl.multiple_of(starts[j] * cy, 32), counts[j] * cy)
-            if j < 4:
+            if j < 2:
                 value = wide[j][probe].astype(jnp.float32)
+            elif j < 4:
+                value = (a_buf, b_buf)[j - 2][probe - begin].astype(jnp.float32)
             else:
-                value = narrow[j - 4][pl.ds(place * counts[j], counts[j])].astype(jnp.float32)
+                value = narrow[j - 4][pl.ds(probe * counts[j], counts[j])].astype(jnp.float32)
             plane = lax.broadcasted_iota(jnp.int32, value.shape, 0) + starts[j]
             value = jnp.where((plane >= low) & (plane < high), value, 0.0)
             pert[q, where, :] = value.reshape(counts[j] * cy, 128)
@@ -177,16 +189,14 @@
         advanced(*first, *made)
 
 
-def propagate(scalars, operands, begin, count, steps, rows, halo):
+def propagate(bounds, operands, begin, count, steps, rows, halo):
     _, _, cy, cz = operands[0].shape
-    left, right = tables(cy, cz)
-    left, right = jnp.asarray(left, jnp.bfloat16), jnp.asarray(right, jnp.bfloat16)
     total = 2 * rows + 2 * halo
     whole = pl.BlockSpec(memory_space=pltpu.VMEM)
     grid_spec = pltpu.PrefetchScalarGridSpec(
         num_scalar_prefetch=1,
         grid=(count // PACK,),
-        in_specs=[whole] * (len(operands) + 2),
+        in_specs=[whole] * 2 + [pl.BlockSpec(memory_space=pltpu.HBM)] * 2 + [whole] * (len(operands) - 4),
         out_specs=[whole, whole],
         scratch_shapes=[
             pltpu.VMEM((PACK, total * cy, cz), jnp.float32),
@@ -195,6 +205,11 @@
             pltpu.VMEM((total * cy, cz), jnp.float32),
             pltpu.VMEM((PACK, 2, total * cy, cz), jnp.float32),
             pltpu.VMEM((PACK, 2, total * cy, 2 * cz), jnp.bfloat16),
+            pltpu.VMEM((SPAN * cy, (SPAN + 8) * cy), jnp.bfloat16),
+            pltpu.VMEM((2 * cz, cz), jnp.bfloat16),
+            pltpu.VMEM((count, rows, cy, cz), jnp.bfloat16),
+            pltpu.VMEM((count, halo - rows, cy, cz), jnp.bfloat16),
+            pltpu.SemaphoreType.DMA((2,)),
         ],
     )
     cells = count * total * cy * cz
@@ -205,10 +220,10 @@
             jax.ShapeDtypeStruct((count, rows, cy, cz), jnp.float32),
             jax.ShapeDtypeStruct((count, rows, cy, cz), jnp.bfloat16),
         ],
-        compiler_params=pltpu.CompilerParams(vmem_limit_bytes=20 << 20),
-        cost_estimate=pl.CostEstimate(flops=cells * 8000 if begin else 0, bytes_accessed=cells * 4 if begin else 0, transcendentals=0),
+        compiler_params=pltpu.CompilerParams(vmem_limit_bytes=16 << 20),
+        cost_estimate=pl.CostEstimate(flops=cells * 8000, bytes_accessed=cells * 4, transcendentals=0),
         name="march",
-    )(scalars, *operands, left, right)
+    )(bounds, *operands)
 
 
 def local(probe_field, bounds, courant, snapshots, snap_times, basis_panels):
@@ -231,12 +246,9 @@
     cut = lambda x, start: lax.dynamic_slice_in_dim(x, start, far, axis=1)
     near = rows - far
 
-    mine = lax.dynamic_slice_in_dim(probe_field, half * par, half, axis=0)
-    theirs = lax.dynamic_slice_in_dim(probe_field, half * (1 - par), half, axis=0)
-    partner = hop(theirs, swap)
-    side_a = hop(mine, perm_a)
-    side_b = hop(cut(mine, near * (1 - par)), perm_b)
-
+    after = lambda x, *first: lax.optimization_barrier((x, *first))[0]
+    trim = lambda x: jnp.concatenate([x[:far_half], x[near_half:]], axis=0)
+    planes = lambda *xs: jnp.concatenate([x.reshape(-1, cy, cz) for x in xs], axis=0)
     near_half, far_half = shares(steps, rows, halo)
 
     def picked(parity):
@@ -245,44 +257,42 @@
 
     joined = picked(core)
     sent = picked(1 - core)
+    gots = []
     span = 1
     while span < members:
         got = lax.ppermute(sent, "probe", [(i, i ^ span) for i in range(members)])
         upper = (member // span) % 2 == 1
         joined = jnp.concatenate([jnp.where(upper, got, joined), jnp.where(upper, joined, got)], axis=2)
         sent = joined
+        gots.append(got)
         span *= 2
     high = lax.reduce_precision(courant, 8, 7)
     rate = jnp.where(core == 0, high, courant - high).astype(jnp.bfloat16)[None]
     extra = jnp.concatenate([joined, rate], axis=0)
-    trim = lambda x: jnp.concatenate([x[:far_half], x[near_half:]], axis=0)
-    planes = lambda *xs: jnp.concatenate([x.reshape(-1, cy, cz) for x in xs], axis=0)
-    extra_x = hop(lax.optimization_barrier((extra, partner, side_a, side_b))[0], swap)
-    part = half // 2
+
+    mine = lax.dynamic_slice_in_dim(probe_field, half * par, half, axis=0)
+    theirs = lax.dynamic_slice_in_dim(probe_field, half * (1 - par), half, axis=0)
+    partner = hop(theirs, swap)
+    side_a = hop(after(mine, gots[0]), perm_a)
+    side_b = hop(cut(after(mine, gots[-1]), near * (1 - par)), perm_b)
+    extra_x = hop(after(extra, partner), swap)
     far_own, far_x = cut(trim(extra), near * (1 - par)), cut(trim(extra_x), near * par)
-    far_partner = cut(partner, near * par)
-    side_c = [hop(planes(partner[:part], extra_x, far_own), perm_b), hop(planes(partner[part:]), perm_b)]
-    side_d = [hop(planes(far_partner[:part], extra, far_x), perm_a), hop(planes(far_partner[part:]), perm_a)]
+    side_c = hop(after(planes(partner, extra_x, far_own), side_b), perm_b)
+    side_d = hop(after(planes(cut(partner, near * par), extra, far_x), side_a), perm_a)
     near_other = cores(planes(extra, extra_x))
-    far_other = cores(planes(side_c[0][part * rows :], side_d[0][part * far :]))
-    base = (place // 2) * 2 * rows - halo
-    mine_bounds = lax.dynamic_slice_in_dim(bounds, half * par, half, axis=0) - base
-    scalars = jnp.concatenate([jnp.stack([par, core]), mine_bounds.reshape(-1)]).astype(jnp.int32)
-    crossed = lax.ppermute(basis_panels, "probe", [(i, i ^ 2) for i in range(members)])
+    far_other = cores(planes(side_c[half * rows :], side_d[half * far :]))
+    operands = (mine, partner, side_a, side_b, side_c, side_d, extra, extra_x, near_other, far_other)
+    basis_later = basis_panels
+    crossed = lax.ppermute(basis_later, "probe", [(i, i ^ 2) for i in range(members)])
     first = par == 0
     own, back = [], []
-    for i in range(2):
-        operands = (mine, partner, side_a, side_b, side_c[i], side_d[i], extra, extra_x)
-        operands += (side_c[0], side_d[0], near_other, far_other)
-        kept, sent = propagate(scalars, operands, i * part, part, steps, rows, halo)
-        scalars = lax.optimization_barrier((scalars, kept))[0]
+    for begin, count in ((0, half // 2), (half // 2, half - half // 2)):
+        kept, sent = propagate(bounds, operands, begin, count, steps, rows, halo)
         own.append(kept)
-        if back:
-            sent = lax.optimization_barrier((sent, back[0]))[0]
         back.append(hop(sent, swap))
-    beside = cores(basis_panels)
-    crossed, beside = lax.optimization_barrier((crossed, beside, own[1]))[:2]
-    panels = [basis_panels, beside, crossed, cores(crossed)]
+    panels = [basis_later, cores(basis_later)]
+    crossed = lax.optimization_barrier((crossed, own[0]))[0]
+    panels = [jnp.concatenate(panels, axis=0), jnp.concatenate([crossed, cores(crossed)], axis=0)]
     dots = lambda x: jnp.concatenate(
         [
             lax.dot_general(y, x, (((1, 2, 3), (1, 2, 3)), ((), ())), preferred_element_type=jnp.float32)

time: 110 us -> 100 us (0.909)
  waiting for transfers between devices: 26.4 us -> 39.3 us
  matrix products: 12.5 us -> 2.06 us
  starting transfers between devices: 32.1 us -> 24.5 us
  local copies, waits for them, and re-layouts: 13 us -> 10.7 us
  other arithmetic: 6.33 us -> 4.38 us
    dot_general x8 -> x4, matrix products: 12.5 us -> 2.06 us  [local(): lax.dot_general(y, x, (((1, 2, 3), (1, 2, 3)), ((), ())), preferred_eleme...]
    ppermute x13 -> x11, waiting for transfers between devices: 23.5 us -> 31.5 us  [local(): hop = lambda x, pairs: lax.ppermute(x, 'store', pairs)]
    ppermute x13 -> x11, starting transfers between devices: 28.6 us -> 20.6 us  [local(): hop = lambda x, pairs: lax.ppermute(x, 'store', pairs)]
    ppermute x1, waiting for transfers between devices: 0.01 us -> 6.36 us  [local(): lax.ppermute(basis_later, 'probe', [(i, i ^ 2) for i in range(members)])]
    concatenate x0 -> x2, local copies, waits for them, and re-layouts: none -> 2.36 us  [the longest x1 2.19 us: local(): jnp.concatenate(panels, axis=0)]
    ppermute x2, waiting for transfers between devices: 2.92 us -> 1.38 us  [local(): got = lax.ppermute(sent, 'probe', [(i, i ^ span) for i in range(members)])]
    slice x4 -> x2, local copies, waits for them, and re-layouts: 1.42 us -> 0.03 us  [local(): far_other = cores(planes(side_c[half * rows:], side_d[half * far:]))]
    sub x1 -> x0, local copies, waits for them, and re-layouts: 1.36 us -> none  [local(): lax.dynamic_slice_in_dim(bounds, half * par, half, axis=0) - base]
  transfers between devices with their start and end apart: 20 -> 18, of which waited for: 7 -> 9; matrix products, arithmetic and copies ran while one was open for 25% -> 12% of each run, Pallas kernels for 16% -> 18%
where the time goes in v7:
time: 100 us
  waiting for transfers between devices  39.3 us (39%)
  starting transfers between devices  24.5 us (24%)
  Pallas kernels  18.2 us (18%)
  local copies, waits for them, and re-layouts  10.7 us (11%)
  other arithmetic  4.38 us (4%)
  matrix products  2.06 us (2%)
  between operations  1.09 us (1%)
    ppermute x11, waiting for transfers between devices, local(): hop = lambda x, pairs: lax.ppermute(x, 'store', pairs)  31.5 us
    ppermute x11, starting transfers between devices, local(): hop = lambda x, pairs: lax.ppermute(x, 'store', pairs)  20.6 us
    pallas_call x2, Pallas kernels, propagate(): pl.pallas_call(functools.partial(march, steps, rows, halo, begin), grid_s...  18.2 us
    ppermute x1, waiting for transfers between devices, local(): lax.ppermute(basis_later, 'probe', [(i, i ^ 2) for i in range(members)])  6.36 us
    unnamed x21, local copies, waits for them, and re-layouts  3.13 us
    concatenate x1, local copies, waits for them, and re-layouts, local(): jnp.concatenate(panels, axis=0)  2.19 us
    ppermute x2, starting transfers between devices, local(): got = lax.ppermute(sent, 'probe', [(i, i ^ span) for i in range(members)])  2.1 us
    dot_general x4, matrix products, local(): lax.dot_general(y, x, (((1, 2, 3), (1, 2, 3)), ((), ())), preferred_eleme...  2.06 us
  transfers between devices with their start and end apart: 18, of which 9 were waited for; matrix products, arithmetic and copies ran while one was open for 12% of the time, Pallas kernels for 18%

profile of v7, /device:TPU:0, one launch (start us, length us, event | category | flops | bytes accessed | tf_op | source)
XLA Modules:
  0.0 100.1 jit_solution(6376441505935255849)
XLA Ops:
  0.7 1.3 %gather_fusion = s32[4]{0:T(128)S(1)} fusion(s32[8]{0:T(128)} %param.10, s32[1024]{0:T(1024)S(1)} %pad_clamp_fusion.3), kind=kCustom, calls=%fused_computation | custom fusion | bytes 48 | tf_op jit(solution)/shard_map/jit(_take)/gather | solution.py:256
  4.3 2.6 %collective-permute-start = (bf16[12,16,8,128]{3,2,1,0:T(8,128)(2,1)S(1)}, bf16[12,16,8,128]{3,2,1,0:T(8,128)(2,1)S(1)}, u32[]{:S(2)}, u32[]{:S(2)}) collective-permute-start(bf16[12,16,8,128]{3,2,1,0:T(8,128)(2,1)S(1)} %get-tuple-element.27), channel_id=1, source_target_pairs={{0,1},{1,0},{2,3},{3,2},{4,5},{5,4},{6,7},{7,6},{8,9},{9,8},{10,11... | collective-permute-start | bytes 1179656 | tf_op jit(solution)/shard_map/ppermute | solution.py:244
  8.3 1.6 %collective-permute-start.3 = (bf16[4,16,4,128]{3,2,1,0:T(4,128)(2,1)S(1)}, bf16[4,16,4,128]{3,2,1,0:T(4,128)(2,1)S(1)}, u32[]{:S(2)}, u32[]{:S(2)}) collective-permute-start(bf16[4,16,4,128]{3,2,1,0:T(4,128)(2,1)S(1)} %pad_maximum_fusion.6), channel_id=1, source_target_pairs={{0,16},{8,24},{16,0},{24,8},{1,17},{9,25},{17,1},{25,9},{2,18},{10... | collective-permute-start | bytes 196616 | tf_op jit(solution)/shard_map/ppermute | solution.py:263
  10.0 1.3 %collective-permute-start.2 = (bf16[12,16,8,128]{3,2,1,0:T(8,128)(2,1)S(1)}, bf16[12,16,8,128]{3,2,1,0:T(8,128)(2,1)S(1)}, u32[]{:S(2)}, u32[]{:S(2)}) collective-permute-start(bf16[12,16,8,128]{3,2,1,0:T(8,128)(2,1)S(1)} %get-tuple-element.13.refs_0_), channel_id=1, source_target_pairs={{2,0},{4,2},{6,4},{1,3},{3,5},{5,7},{10,8},{12,10},{14,12},{9,11},... | collective-permute-start | bytes 1179656 | tf_op jit(solution)/shard_map/ppermute | solution.py:244
  11.3 1.4 %collective-permute-done.3 = bf16[4,16,4,128]{3,2,1,0:T(4,128)(2,1)S(1)} collective-permute-done((bf16[4,16,4,128]{3,2,1,0:T(4,128)(2,1)S(1)}, bf16[4,16,4,128]{3,2,1,0:T(4,128)(2,1)S(1)}, u32[]{:S(2)}, u32[]{:S(2)}) %collective-permute-start.3) | collective-permute-done | bytes 65568 | tf_op jit(solution)/shard_map/ppermute | solution.py:263
  12.7 3.5 %collective-permute-start.4 = (bf16[12,12,8,128]{3,2,1,0:T(8,128)(2,1)S(1)}, bf16[12,12,8,128]{3,2,1,0:T(8,128)(2,1)S(1)}, u32[]{:S(2)}, u32[]{:S(2)}) collective-permute-start(bf16[12,12,8,128]{3,2,1,0:T(8,128)(2,1)S(1)} %constant_dynamic-slice_fusion.1), channel_id=1, source_target_pairs={{0,2},{2,4},{4,6},{3,1},{5,3},{7,5},{8,10},{10,12},{12,14},{11,9},... | collective-permute-start | bytes 884744 | tf_op jit(solution)/shard_map/ppermute | solution.py:244
  16.7 1.7 %collective-permute-start.5 = (bf16[5,16,8,128]{3,2,1,0:T(8,128)(2,1)S(1)}, bf16[5,16,8,128]{3,2,1,0:T(8,128)(2,1)S(1)}, u32[]{:S(2)}, u32[]{:S(2)}) collective-permute-start(bf16[5,16,8,128]{3,2,1,0:T(8,128)(2,1)S(1)} %pad_maximum_fusion.5.refs_6_), channel_id=1, source_target_pairs={{0,1},{1,0},{2,3},{3,2},{4,5},{5,4},{6,7},{7,6},{8,9},{9,8},{10,11... | collective-permute-start | bytes 491528 | tf_op jit(solution)/shard_map/ppermute | solution.py:244
  18.5 4.2 %collective-permute-done.5.refs_7_ = bf16[5,16,8,128]{3,2,1,0:T(8,128)(2,1)S(1)} collective-permute-done((bf16[5,16,8,128]{3,2,1,0:T(8,128)(2,1)S(1)}, bf16[5,16,8,128]{3,2,1,0:T(8,128)(2,1)S(1)}, u32[]{:S(2)}, u32[]{:S(2)}) %collective-permute-start.5) | collective-permute-done | bytes 163872 | tf_op jit(solution)/shard_map/ppermute | solution.py:244
  22.8 3.6 %collective-permute-start.6 = (bf16[308,8,128]{2,1,0:T(8,128)(2,1)S(1)}, bf16[308,8,128]{2,1,0:T(8,128)(2,1)S(1)}, u32[]{:S(2)}, u32[]{:S(2)}) collective-permute-start(bf16[308,8,128]{2,1,0:T(8,128)(2,1)S(1)} %pad_maximum_fusion.1), channel_id=1, source_target_pairs={{0,2},{2,4},{4,6},{3,1},{5,3},{7,5},{8,10},{10,12},{12,14},{11,9},... | collective-permute-start | bytes 1892360 | tf_op jit(solution)/shard_map/ppermute | solution.py:244
  26.5 1.3 %collective-permute-start.7 = (bf16[260,8,128]{2,1,0:T(8,128)(2,1)S(1)}, bf16[260,8,128]{2,1,0:T(8,128)(2,1)S(1)}, u32[]{:S(2)}, u32[]{:S(2)}) collective-permute-start(bf16[260,8,128]{2,1,0:T(8,128)(2,1)S(1)} %pad_maximum_fusion.2), channel_id=1, source_target_pairs={{2,0},{4,2},{6,4},{1,3},{3,5},{5,7},{10,8},{12,10},{14,12},{9,11},... | collective-permute-start | bytes 1597448 | tf_op jit(solution)/shard_map/ppermute | solution.py:244
  27.8 1.7 %constant_dynamic-update-slice_fusion.5 = (bf16[48,16,8,128]{3,0,2,1:T(8,128)(2,1)}, bf16[24,16,8,128]{3,0,2,1:T(8,128)(2,1)}) fusion(bf16[24,16,8,128]{3,2,1,0:T(8,128)(2,1)S(1)} %copy-done.5), kind=kLoop, calls=%fused_computation.46 | loop fusion | bytes 2359296
  29.6 11.3 %collective-permute-done.7.refs_5_ = bf16[260,8,128]{2,1,0:T(8,128)(2,1)S(1)} collective-permute-done((bf16[260,8,128]{2,1,0:T(8,128)(2,1)S(1)}, bf16[260,8,128]{2,1,0:T(8,128)(2,1)S(1)}, u32[]{:S(2)}, u32[]{:S(2)}) %collective-permute-start.7) | collective-permute-done | bytes 532512 | tf_op jit(solution)/shard_map/ppermute | solution.py:244
  41.8 1.5 %collective-permute-start.13 = (bf16[24,16,8,128]{3,0,2,1:T(8,128)(2,1)}, bf16[24,16,8,128]{3,0,2,1:T(8,128)(2,1)}, u32[]{:S(2)}, u32[]{:S(2)}) collective-permute-start(bf16[24,16,8,128]{3,0,2,1:T(8,128)(2,1)} %get-tuple-element.26), channel_id=1, source_target_pairs={{0,16},{8,24},{16,0},{24,8},{1,17},{9,25},{17,1},{25,9},{2,18},{10... | collective-permute-start | bytes 2359304 | tf_op jit(solution)/shard_map/ppermute | solution.py:286
  44.4 2.2 %constant_dynamic-update-slice_fusion.4 = bf16[48,16,8,128]{3,0,2,1:T(8,128)(2,1)} fusion(bf16[48,16,8,128]{3,0,2,1:T(8,128)(2,1)} %get-tuple-element.25, bf16[24,16,8,128]{3,0,2,1:T(8,128)(2,1)} %collective-permute-done.12), kind=kLoop, calls=%fused_computation.45 | loop fusion | bytes 1572864 | tf_op jit(solution)/shard_map/concatenate | solution.py:295
  46.6 9.1 %march.2 = (f32[6,16,8,128]{3,2,1,0:T(8,128)S(1)}, bf16[6,16,8,128]{3,2,1,0:T(8,128)(2,1)S(1)}) custom-call(s32[24,2]{1,0:T(8,128)S(1)} %copy.17.bounds_ref, bf16[12,16,8,128]{3,2,1,0:T(8,128)(2,1)S(1)} %get-tuple-element.13.refs_0_, bf16[12,16,8,128]{3,2,1,0:T(8,128)(2,1)S(1)} %collective-permute-done.refs_1_, ...), custom_call_target="tpu_custom_call" | custom-call | flops 4325376000 | bytes 2162688 | tf_op jit(solution)/shard_map/march/pallas_call | solution.py:216
  55.7 6.4 %collective-permute-done.13 = bf16[24,16,8,128]{3,0,2,1:T(8,128)(2,1)} collective-permute-done((bf16[24,16,8,128]{3,0,2,1:T(8,128)(2,1)}, bf16[24,16,8,128]{3,0,2,1:T(8,128)(2,1)}, u32[]{:S(2)}, u32[]{:S(2)}) %collective-permute-start.13) | collective-permute-done | bytes 786464 | tf_op jit(solution)/shard_map/ppermute | solution.py:286
  63.3 9.1 %march.3 = (f32[6,16,8,128]{3,2,1,0:T(8,128)S(1)}, bf16[6,16,8,128]{3,2,1,0:T(8,128)(2,1)S(1)}) custom-call(s32[24,2]{1,0:T(8,128)S(1)} %copy.17.bounds_ref, bf16[12,16,8,128]{3,2,1,0:T(8,128)(2,1)S(1)} %get-tuple-element.13.refs_0_, bf16[12,16,8,128]{3,2,1,0:T(8,128)(2,1)S(1)} %collective-permute-done.refs_1_, ...), custom_call_target="tpu_custom_call" | custom-call | flops 4325376000 | bytes 2162688 | tf_op jit(solution)/shard_map/march/pallas_call | solution.py:216
  72.8 1.7 %collective-permute-start.10 = (bf16[6,16,8,128]{3,2,1,0:T(8,128)(2,1)S(1)}, bf16[6,16,8,128]{3,2,1,0:T(8,128)(2,1)S(1)}, u32[]{:S(2)}, u32[]{:S(2)}) collective-permute-start(bf16[6,16,8,128]{3,2,1,0:T(8,128)(2,1)S(1)} %get-tuple-element.19), channel_id=1, source_target_pairs={{0,1},{1,0},{2,3},{3,2},{4,5},{5,4},{6,7},{7,6},{8,9},{9,8},{10,11... | collective-permute-start | bytes 589832 | tf_op jit(solution)/shard_map/ppermute | solution.py:244
  74.6 9.4 %collective-permute-done.10 = bf16[6,16,8,128]{3,2,1,0:T(8,128)(2,1)S(1)} collective-permute-done((bf16[6,16,8,128]{3,2,1,0:T(8,128)(2,1)S(1)}, bf16[6,16,8,128]{3,2,1,0:T(8,128)(2,1)S(1)}, u32[]{:S(2)}, u32[]{:S(2)}) %collective-permute-start.10) | collective-permute-done | bytes 196640 | tf_op jit(solution)/shard_map/ppermute | solution.py:244
  87.8 3.4 %collective-permute-done.15 = f32[96,24]{0,1:T(8,128)S(1)} collective-permute-done((f32[96,24]{0,1:T(8,128)S(1)}, f32[96,24]{0,1:T(8,128)S(1)}, u32[]{:S(2)}, u32[]{:S(2)}) %collective-permute-start.15) | collective-permute-done | bytes 9248 | tf_op jit(solution)/shard_map/ppermute | solution.py:244
  91.2 1.5 %collective-permute-start.16 = (f32[96,24]{0,1:T(8,128)S(1)}, f32[96,24]{0,1:T(8,128)S(1)}, u32[]{:S(2)}, u32[]{:S(2)}) collective-permute-start(f32[96,24]{0,1:T(8,128)S(1)} %add.75), channel_id=1, source_target_pairs={{0,2},{1,3},{2,0},{3,1},{4,6},{5,7},{6,4},{7,5},{8,10},{9,11},{10,... | collective-permute-start | bytes 27656 | tf_op jit(solution)/shard_map/ppermute | solution.py:244
  92.8 2.2 %collective-permute-done.16 = f32[96,24]{0,1:T(8,128)S(1)} collective-permute-done((f32[96,24]{0,1:T(8,128)S(1)}, f32[96,24]{0,1:T(8,128)S(1)}, u32[]{:S(2)}, u32[]{:S(2)}) %collective-permute-start.16) | collective-permute-done | bytes 9248 | tf_op jit(solution)/shard_map/ppermute | solution.py:244
  94.9 2.6 %collective-permute-start.17 = (f32[96,24]{0,1:T(8,128)S(1)}, f32[96,24]{0,1:T(8,128)S(1)}, u32[]{:S(2)}, u32[]{:S(2)}) collective-permute-start(f32[96,24]{0,1:T(8,128)S(1)} %add.76), channel_id=1, source_target_pairs={{0,4},{1,5},{2,6},{3,7},{4,0},{5,1},{6,2},{7,3},{8,12},{9,13},{10,... | collective-permute-start | bytes 27656 | tf_op jit(solution)/shard_map/ppermute | solution.py:244
  97.6 1.2 %pad_maximum_fusion = f32[24,16,8,128]{3,2,1,0:T(8,128)} fusion(f32[12,16,8,128]{3,2,1,0:T(8,128)S(1)} %get-tuple-element.23, f32[12,16,8,128]{3,2,1,0:T(8,128)S(1)} %get-tuple-element.22), kind=kLoop, calls=%fused_computation.4 | loop fusion | flops 393216 | bytes 3145728 | tf_op jit(solution)/shard_map/concatenate | solution.py:308
  (87 shorter events, 13.1 us)
Async XLA Ops:
  0.6 6.3 %copy-start.3 = (s32[8]{0:T(128)S(1)}, s32[8]{0:T(128)}, u32[]{:S(2)}) copy-start(s32[8]{0:T(128)} %param.10) | copy-start | bytes 100
  0.7 9.2 %copy-start.6 = (f32[16,8,128]{2,1,0:T(8,128)S(1)}, f32[16,8,128]{2,1,0:T(8,128)}, u32[]{:S(2)}) copy-start(f32[16,8,128]{2,1,0:T(8,128)} %param.8) | copy-start | bytes 196612
  2.7 5.6 %collective-permute-start.1 = (bf16[4,16,2,128]{3,2,1,0:T(2,128)(2,1)S(1)}, bf16[4,16,2,128]{3,2,1,0:T(2,128)(2,1)S(1)}, u32[]{:S(2)}, u32[]{:S(2)}) collective-permute-start(bf16[4,16,2,128]{3,2,1,0:T(2,128)(2,1)S(1)} %gather_fusion.1), channel_id=1, source_target_pairs={{0,8},{8,0},{16,24},{24,16},{1,9},{9,1},{17,25},{25,17},{2,10},{10... | collective-permute-start | bytes 98312 | tf_op jit(solution)/shard_map/ppermute | solution.py:263
  4.3 12.3 %collective-permute-start = (bf16[12,16,8,128]{3,2,1,0:T(8,128)(2,1)S(1)}, bf16[12,16,8,128]{3,2,1,0:T(8,128)(2,1)S(1)}, u32[]{:S(2)}, u32[]{:S(2)}) collective-permute-start(bf16[12,16,8,128]{3,2,1,0:T(8,128)(2,1)S(1)} %get-tuple-element.27), channel_id=1, source_target_pairs={{0,1},{1,0},{2,3},{3,2},{4,5},{5,4},{6,7},{7,6},{8,9},{9,8},{10,11... | collective-permute-start | bytes 1179656 | tf_op jit(solution)/shard_map/ppermute | solution.py:244
  8.3 4.3 %collective-permute-start.3 = (bf16[4,16,4,128]{3,2,1,0:T(4,128)(2,1)S(1)}, bf16[4,16,4,128]{3,2,1,0:T(4,128)(2,1)S(1)}, u32[]{:S(2)}, u32[]{:S(2)}) collective-permute-start(bf16[4,16,4,128]{3,2,1,0:T(4,128)(2,1)S(1)} %pad_maximum_fusion.6), channel_id=1, source_target_pairs={{0,16},{8,24},{16,0},{24,8},{1,17},{9,25},{17,1},{25,9},{2,18},{10... | collective-permute-start | bytes 196616 | tf_op jit(solution)/shard_map/ppermute | solution.py:263
  10.0 16.5 %collective-permute-start.2 = (bf16[12,16,8,128]{3,2,1,0:T(8,128)(2,1)S(1)}, bf16[12,16,8,128]{3,2,1,0:T(8,128)(2,1)S(1)}, u32[]{:S(2)}, u32[]{:S(2)}) collective-permute-start(bf16[12,16,8,128]{3,2,1,0:T(8,128)(2,1)S(1)} %get-tuple-element.13.refs_0_), channel_id=1, source_target_pairs={{2,0},{4,2},{6,4},{1,3},{3,5},{5,7},{10,8},{12,10},{14,12},{9,11},... | collective-permute-start | bytes 1179656 | tf_op jit(solution)/shard_map/ppermute | solution.py:244
  12.7 10.1 %collective-permute-start.4 = (bf16[12,12,8,128]{3,2,1,0:T(8,128)(2,1)S(1)}, bf16[12,12,8,128]{3,2,1,0:T(8,128)(2,1)S(1)}, u32[]{:S(2)}, u32[]{:S(2)}) collective-permute-start(bf16[12,12,8,128]{3,2,1,0:T(8,128)(2,1)S(1)} %constant_dynamic-slice_fusion.1), channel_id=1, source_target_pairs={{0,2},{2,4},{4,6},{3,1},{5,3},{7,5},{8,10},{10,12},{12,14},{11,9},... | collective-permute-start | bytes 884744 | tf_op jit(solution)/shard_map/ppermute | solution.py:244
  16.7 6.0 %collective-permute-start.5 = (bf16[5,16,8,128]{3,2,1,0:T(8,128)(2,1)S(1)}, bf16[5,16,8,128]{3,2,1,0:T(8,128)(2,1)S(1)}, u32[]{:S(2)}, u32[]{:S(2)}) collective-permute-start(bf16[5,16,8,128]{3,2,1,0:T(8,128)(2,1)S(1)} %pad_maximum_fusion.5.refs_6_), channel_id=1, source_target_pairs={{0,1},{1,0},{2,3},{3,2},{4,5},{5,4},{6,7},{7,6},{8,9},{9,8},{10,11... | collective-permute-start | bytes 491528 | tf_op jit(solution)/shard_map/ppermute | solution.py:244
  18.5 9.3 %copy-start.5 = (bf16[24,16,8,128]{3,2,1,0:T(8,128)(2,1)S(1)}, bf16[24,16,8,128]{3,2,1,0:T(8,128)(2,1)}, u32[]{:S(2)}) copy-start(bf16[24,16,8,128]{3,2,1,0:T(8,128)(2,1)} %param.11) | copy-start | bytes 2359300
  22.8 3.7 %copy-start.1 = (bf16[12,12,8,128]{3,2,1,0:T(8,128)(2,1)}, bf16[12,12,8,128]{3,2,1,0:T(8,128)(2,1)S(1)}, u32[]{:S(2)}) copy-start(bf16[12,12,8,128]{3,2,1,0:T(8,128)(2,1)S(1)} %collective-permute-done.4.refs_3_) | copy-start | bytes 884740
  22.8 18.1 %collective-permute-start.6 = (bf16[308,8,128]{2,1,0:T(8,128)(2,1)S(1)}, bf16[308,8,128]{2,1,0:T(8,128)(2,1)S(1)}, u32[]{:S(2)}, u32[]{:S(2)}) collective-permute-start(bf16[308,8,128]{2,1,0:T(8,128)(2,1)S(1)} %pad_maximum_fusion.1), channel_id=1, source_target_pairs={{0,2},{2,4},{4,6},{3,1},{5,3},{7,5},{8,10},{10,12},{12,14},{11,9},... | collective-permute-start | bytes 1892360 | tf_op jit(solution)/shard_map/ppermute | solution.py:244
  26.5 14.4 %collective-permute-start.7 = (bf16[260,8,128]{2,1,0:T(8,128)(2,1)S(1)}, bf16[260,8,128]{2,1,0:T(8,128)(2,1)S(1)}, u32[]{:S(2)}, u32[]{:S(2)}) collective-permute-start(bf16[260,8,128]{2,1,0:T(8,128)(2,1)S(1)} %pad_maximum_fusion.2), channel_id=1, source_target_pairs={{2,0},{4,2},{6,4},{1,3},{3,5},{5,7},{10,8},{12,10},{14,12},{9,11},... | collective-permute-start | bytes 1597448 | tf_op jit(solution)/shard_map/ppermute | solution.py:244
  29.6 14.8 %copy-start.7 = (s32[24,2]{0,1:T(2,128)S(1)}, s32[24,2]{0,1:T(2,128)}, u32[]{:S(2)}) copy-start(s32[24,2]{0,1:T(2,128)} %param.7) | copy-start | bytes 580
  29.6 14.8 %collective-permute-start.12 = (bf16[24,16,8,128]{3,0,2,1:T(8,128)(2,1)}, bf16[24,16,8,128]{3,0,2,1:T(8,128)(2,1)}, u32[]{:S(2)}, u32[]{:S(2)}) collective-permute-start(bf16[24,16,8,128]{3,0,2,1:T(8,128)(2,1)} %get-tuple-element.26), channel_id=1, source_target_pairs={{0,8},{8,0},{16,24},{24,16},{1,9},{9,1},{17,25},{25,17},{2,10},{10... | collective-permute-start | bytes 2359304 | tf_op jit(solution)/shard_map/ppermute | solution.py:245
  41.8 4.8 %collective-permute-start.9 = (bf16[232,8,128]{2,1,0:T(8,128)(2,1)}, bf16[232,8,128]{2,1,0:T(8,128)(2,1)S(1)}, u32[]{:S(2)}, u32[]{:S(2)}) collective-permute-start(bf16[232,8,128]{2,1,0:T(8,128)(2,1)} %pad_maximum_fusion.3), channel_id=1, source_target_pairs={{0,8},{8,0},{16,24},{24,16},{1,9},{9,1},{17,25},{25,17},{2,10},{10... | collective-permute-start | bytes 1425416 | tf_op jit(solution)/shard_map/ppermute | solution.py:245
  41.8 20.3 %collective-permute-start.13 = (bf16[24,16,8,128]{3,0,2,1:T(8,128)(2,1)}, bf16[24,16,8,128]{3,0,2,1:T(8,128)(2,1)}, u32[]{:S(2)}, u32[]{:S(2)}) collective-permute-start(bf16[24,16,8,128]{3,0,2,1:T(8,128)(2,1)} %get-tuple-element.26), channel_id=1, source_target_pairs={{0,16},{8,24},{16,0},{24,8},{1,17},{9,25},{17,1},{25,9},{2,18},{10... | collective-permute-start | bytes 2359304 | tf_op jit(solution)/shard_map/ppermute | solution.py:286
  44.1 2.5 %collective-permute-start.8 = (bf16[160,8,128]{2,1,0:T(8,128)(2,1)}, bf16[160,8,128]{2,1,0:T(8,128)(2,1)S(1)}, u32[]{:S(2)}, u32[]{:S(2)}) collective-permute-start(bf16[160,8,128]{2,1,0:T(8,128)(2,1)} %pad_maximum_fusion.4), channel_id=1, source_target_pairs={{0,8},{8,0},{16,24},{24,16},{1,9},{9,1},{17,25},{25,17},{2,10},{10... | collective-permute-start | bytes 983048 | tf_op jit(solution)/shard_map/ppermute | solution.py:245
  62.1 23.3 %collective-permute-start.14 = (bf16[24,16,8,128]{3,0,2,1:T(8,128)(2,1)}, bf16[24,16,8,128]{3,0,2,1:T(8,128)(2,1)S(1)}, u32[]{:S(2)}, u32[]{:S(2)}) collective-permute-start(bf16[24,16,8,128]{3,0,2,1:T(8,128)(2,1)} %collective-permute-done.13), channel_id=1, source_target_pairs={{0,8},{8,0},{16,24},{24,16},{1,9},{9,1},{17,25},{25,17},{2,10},{10... | collective-permute-start | bytes 2359304 | tf_op jit(solution)/shard_map/ppermute | solution.py:245
  72.4 11.7 %copy-start.4 = (bf16[48,16,8,128]{3,0,2,1:T(8,128)(2,1)S(1)}, bf16[48,16,8,128]{3,0,2,1:T(8,128)(2,1)}, u32[]{:S(2)}) copy-start(bf16[48,16,8,128]{3,0,2,1:T(8,128)(2,1)} %constant_dynamic-update-slice_fusion.4) | copy-start | bytes 4718596
  72.4 11.6 %collective-permute-start.11 = (bf16[6,16,8,128]{3,2,1,0:T(8,128)(2,1)S(1)}, bf16[6,16,8,128]{3,2,1,0:T(8,128)(2,1)S(1)}, u32[]{:S(2)}, u32[]{:S(2)}) collective-permute-start(bf16[6,16,8,128]{3,2,1,0:T(8,128)(2,1)S(1)} %get-tuple-element.20), channel_id=1, source_target_pairs={{0,1},{1,0},{2,3},{3,2},{4,5},{5,4},{6,7},{7,6},{8,9},{9,8},{10,11... | collective-permute-start | bytes 589832 | tf_op jit(solution)/shard_map/ppermute | solution.py:244
  72.8 11.2 %collective-permute-start.10 = (bf16[6,16,8,128]{3,2,1,0:T(8,128)(2,1)S(1)}, bf16[6,16,8,128]{3,2,1,0:T(8,128)(2,1)S(1)}, u32[]{:S(2)}, u32[]{:S(2)}) collective-permute-start(bf16[6,16,8,128]{3,2,1,0:T(8,128)(2,1)S(1)} %get-tuple-element.19), channel_id=1, source_target_pairs={{0,1},{1,0},{2,3},{3,2},{4,5},{5,4},{6,7},{7,6},{8,9},{9,8},{10,11... | collective-permute-start | bytes 589832 | tf_op jit(solution)/shard_map/ppermute | solution.py:244
  87.5 3.8 %collective-permute-start.15 = (f32[96,24]{0,1:T(8,128)S(1)}, f32[96,24]{0,1:T(8,128)S(1)}, u32[]{:S(2)}, u32[]{:S(2)}) collective-permute-start(f32[96,24]{0,1:T(8,128)S(1)} %fusion.11), channel_id=1, source_target_pairs={{0,1},{1,0},{2,3},{3,2},{4,5},{5,4},{6,7},{7,6},{8,9},{9,8},{10,11... | collective-permute-start | bytes 27656 | tf_op jit(solution)/shard_map/ppermute | solution.py:244
  91.2 3.7 %collective-permute-start.16 = (f32[96,24]{0,1:T(8,128)S(1)}, f32[96,24]{0,1:T(8,128)S(1)}, u32[]{:S(2)}, u32[]{:S(2)}) collective-permute-start(f32[96,24]{0,1:T(8,128)S(1)} %add.75), channel_id=1, source_target_pairs={{0,2},{1,3},{2,0},{3,1},{4,6},{5,7},{6,4},{7,5},{8,10},{9,11},{10,... | collective-permute-start | bytes 27656 | tf_op jit(solution)/shard_map/ppermute | solution.py:244
  94.9 4.6 %collective-permute-start.17 = (f32[96,24]{0,1:T(8,128)S(1)}, f32[96,24]{0,1:T(8,128)S(1)}, u32[]{:S(2)}, u32[]{:S(2)}) collective-permute-start(f32[96,24]{0,1:T(8,128)S(1)} %add.76), channel_id=1, source_target_pairs={{0,4},{1,5},{2,6},{3,7},{4,0},{5,1},{6,2},{7,3},{8,12},{9,13},{10,... | collective-permute-start | bytes 27656 | tf_op jit(solution)/shard_map/ppermute | solution.py:244
  (2 other events, 3.6 us)

commit v8 on v7

--- a/solution.py
+++ b/solution.py
@@ -291,7 +291,7 @@
         own.append(kept)
         back.append(hop(sent, swap))
     panels = [basis_later, cores(basis_later)]
-    crossed = lax.optimization_barrier((crossed, own[0]))[0]
+    crossed = lax.optimization_barrier((crossed, back[0][0, 0, 0, 0]))[0]
     panels = [jnp.concatenate(panels, axis=0), jnp.concatenate([crossed, cores(crossed)], axis=0)]
     dots = lambda x: jnp.concatenate(
         [

time: 100 us -> 96.4 us (0.964)
  waiting for transfers between devices: 39.3 us -> 33.6 us
  matrix products: 2.06 us -> 4.34 us
  local copies, waits for them, and re-layouts: 10.7 us -> 9.24 us
    ppermute x11, waiting for transfers between devices: 31.5 us -> 27.6 us  [local(): hop = lambda x, pairs: lax.ppermute(x, 'store', pairs)]
    dot_general x4, matrix products: 2.06 us -> 4.34 us  [local(): lax.dot_general(y, x, (((1, 2, 3), (1, 2, 3)), ((), ())), preferred_eleme...]
    ppermute x1, waiting for transfers between devices: 6.36 us -> 4.67 us  [local(): lax.ppermute(basis_later, 'probe', [(i, i ^ 2) for i in range(members)])]
    unnamed x21 -> x20, local copies, waits for them, and re-layouts: 3.13 us -> 1.92 us
  transfers between devices with their start and end apart: 18 -> 18, of which waited for: 9 -> 9; matrix products, arithmetic and copies ran while one was open for 12% -> 12% of each run, Pallas kernels for 18% -> 19%
where the time goes in v8:
time: 96.4 us; the launch traced here: 96 us
  waiting for transfers between devices  33.6 us (35%)
  starting transfers between devices  25.1 us (26%)
  Pallas kernels  18.2 us (19%)
  local copies, waits for them, and re-layouts  9.24 us (10%)
  other arithmetic  4.39 us (5%)
  matrix products  4.34 us (5%)
  between operations  1.08 us (1%)
    ppermute x11, waiting for transfers between devices, local(): hop = lambda x, pairs: lax.ppermute(x, 'store', pairs)  27.6 us
    ppermute x11, starting transfers between devices, local(): hop = lambda x, pairs: lax.ppermute(x, 'store', pairs)  21 us
    pallas_call x2, Pallas kernels, propagate(): pl.pallas_call(functools.partial(march, steps, rows, halo, begin), grid_s...  18.2 us
    ppermute x1, waiting for transfers between devices, local(): lax.ppermute(basis_later, 'probe', [(i, i ^ 2) for i in range(members)])  4.67 us
    dot_general x4, matrix products, local(): lax.dot_general(y, x, (((1, 2, 3), (1, 2, 3)), ((), ())), preferred_eleme...  4.34 us
    concatenate x1, local copies, waits for them, and re-layouts, local(): jnp.concatenate(panels, axis=0)  2.15 us
    ppermute x2, starting transfers between devices, local(): got = lax.ppermute(sent, 'probe', [(i, i ^ span) for i in range(members)])  2.1 us
    gather x2, local copies, waits for them, and re-layouts, picked(): jnp.take(snap_times, chosen, mode='clip')  1.93 us
  transfers between devices with their start and end apart: 18, of which 9 were waited for; matrix products, arithmetic and copies ran while one was open for 12% of the time, Pallas kernels for 19%

profile of v8, /device:TPU:0, one launch (start us, length us, event | category | flops | bytes accessed | tf_op | source)
XLA Modules:
  0.0 96.0 jit_solution(17064380115550150111)
XLA Ops:
  0.7 1.3 %gather_fusion = s32[4]{0:T(128)S(1)} fusion(s32[8]{0:T(128)} %param.10, s32[1024]{0:T(1024)S(1)} %pad_clamp_fusion.3), kind=kCustom, calls=%fused_computation | custom fusion | bytes 48 | tf_op jit(solution)/shard_map/jit(_take)/gather | solution.py:256
  4.3 2.6 %collective-permute-start = (bf16[12,16,8,128]{3,2,1,0:T(8,128)(2,1)S(1)}, bf16[12,16,8,128]{3,2,1,0:T(8,128)(2,1)S(1)}, u32[]{:S(2)}, u32[]{:S(2)}) collective-permute-start(bf16[12,16,8,128]{3,2,1,0:T(8,128)(2,1)S(1)} %get-tuple-element.25), channel_id=1, source_target_pairs={{0,1},{1,0},{2,3},{3,2},{4,5},{5,4},{6,7},{7,6},{8,9},{9,8},{10,11... | collective-permute-start | bytes 1179656 | tf_op jit(solution)/shard_map/ppermute | solution.py:244
  8.3 1.6 %collective-permute-start.3 = (bf16[4,16,4,128]{3,2,1,0:T(4,128)(2,1)S(1)}, bf16[4,16,4,128]{3,2,1,0:T(4,128)(2,1)S(1)}, u32[]{:S(2)}, u32[]{:S(2)}) collective-permute-start(bf16[4,16,4,128]{3,2,1,0:T(4,128)(2,1)S(1)} %pad_maximum_fusion.9), channel_id=1, source_target_pairs={{0,16},{8,24},{16,0},{24,8},{1,17},{9,25},{17,1},{25,9},{2,18},{10... | collective-permute-start | bytes 196616 | tf_op jit(solution)/shard_map/ppermute | solution.py:263
  10.0 1.3 %collective-permute-start.2 = (bf16[12,16,8,128]{3,2,1,0:T(8,128)(2,1)S(1)}, bf16[12,16,8,128]{3,2,1,0:T(8,128)(2,1)S(1)}, u32[]{:S(2)}, u32[]{:S(2)}) collective-permute-start(bf16[12,16,8,128]{3,2,1,0:T(8,128)(2,1)S(1)} %get-tuple-element.12.refs_0_), channel_id=1, source_target_pairs={{2,0},{4,2},{6,4},{1,3},{3,5},{5,7},{10,8},{12,10},{14,12},{9,11},... | collective-permute-start | bytes 1179656 | tf_op jit(solution)/shard_map/ppermute | solution.py:244
  11.3 1.4 %collective-permute-done.3 = bf16[4,16,4,128]{3,2,1,0:T(4,128)(2,1)S(1)} collective-permute-done((bf16[4,16,4,128]{3,2,1,0:T(4,128)(2,1)S(1)}, bf16[4,16,4,128]{3,2,1,0:T(4,128)(2,1)S(1)}, u32[]{:S(2)}, u32[]{:S(2)}) %collective-permute-start.3) | collective-permute-done | bytes 65568 | tf_op jit(solution)/shard_map/ppermute | solution.py:263
  12.7 3.5 %collective-permute-start.4 = (bf16[12,12,8,128]{3,2,1,0:T(8,128)(2,1)S(1)}, bf16[12,12,8,128]{3,2,1,0:T(8,128)(2,1)S(1)}, u32[]{:S(2)}, u32[]{:S(2)}) collective-permute-start(bf16[12,12,8,128]{3,2,1,0:T(8,128)(2,1)S(1)} %constant_dynamic-slice_fusion.1), channel_id=1, source_target_pairs={{0,2},{2,4},{4,6},{3,1},{5,3},{7,5},{8,10},{10,12},{12,14},{11,9},... | collective-permute-start | bytes 884744 | tf_op jit(solution)/shard_map/ppermute | solution.py:244
  16.7 1.7 %collective-permute-start.5 = (bf16[5,16,8,128]{3,2,1,0:T(8,128)(2,1)S(1)}, bf16[5,16,8,128]{3,2,1,0:T(8,128)(2,1)S(1)}, u32[]{:S(2)}, u32[]{:S(2)}) collective-permute-start(bf16[5,16,8,128]{3,2,1,0:T(8,128)(2,1)S(1)} %pad_maximum_fusion.8.refs_6_), channel_id=1, source_target_pairs={{0,1},{1,0},{2,3},{3,2},{4,5},{5,4},{6,7},{7,6},{8,9},{9,8},{10,11... | collective-permute-start | bytes 491528 | tf_op jit(solution)/shard_map/ppermute | solution.py:244
  18.5 4.2 %collective-permute-done.5.refs_7_ = bf16[5,16,8,128]{3,2,1,0:T(8,128)(2,1)S(1)} collective-permute-done((bf16[5,16,8,128]{3,2,1,0:T(8,128)(2,1)S(1)}, bf16[5,16,8,128]{3,2,1,0:T(8,128)(2,1)S(1)}, u32[]{:S(2)}, u32[]{:S(2)}) %collective-permute-start.5) | collective-permute-done | bytes 163872 | tf_op jit(solution)/shard_map/ppermute | solution.py:244
  22.8 3.6 %collective-permute-start.6 = (bf16[308,8,128]{2,1,0:T(8,128)(2,1)S(1)}, bf16[308,8,128]{2,1,0:T(8,128)(2,1)S(1)}, u32[]{:S(2)}, u32[]{:S(2)}) collective-permute-start(bf16[308,8,128]{2,1,0:T(8,128)(2,1)S(1)} %pad_maximum_fusion.4), channel_id=1, source_target_pairs={{0,2},{2,4},{4,6},{3,1},{5,3},{7,5},{8,10},{10,12},{12,14},{11,9},... | collective-permute-start | bytes 1892360 | tf_op jit(solution)/shard_map/ppermute | solution.py:244
  27.8 1.7 %constant_dynamic-update-slice_fusion.5 = (bf16[48,16,8,128]{3,0,2,1:T(8,128)(2,1)}, bf16[24,16,8,128]{3,0,2,1:T(8,128)(2,1)}) fusion(bf16[24,16,8,128]{3,2,1,0:T(8,128)(2,1)S(1)} %copy-done.5), kind=kLoop, calls=%fused_computation.47 | loop fusion | bytes 2359296
  29.6 1.5 %collective-permute-start.13 = (bf16[24,16,8,128]{3,0,2,1:T(8,128)(2,1)}, bf16[24,16,8,128]{3,0,2,1:T(8,128)(2,1)}, u32[]{:S(2)}, u32[]{:S(2)}) collective-permute-start(bf16[24,16,8,128]{3,0,2,1:T(8,128)(2,1)} %get-tuple-element.24), channel_id=1, source_target_pairs={{0,16},{8,24},{16,0},{24,8},{1,17},{9,25},{17,1},{25,9},{2,18},{10... | collective-permute-start | bytes 2359304 | tf_op jit(solution)/shard_map/ppermute | solution.py:286
  31.1 9.8 %collective-permute-done.7.refs_5_ = bf16[260,8,128]{2,1,0:T(8,128)(2,1)S(1)} collective-permute-done((bf16[260,8,128]{2,1,0:T(8,128)(2,1)S(1)}, bf16[260,8,128]{2,1,0:T(8,128)(2,1)S(1)}, u32[]{:S(2)}, u32[]{:S(2)}) %collective-permute-start.7) | collective-permute-done | bytes 532512 | tf_op jit(solution)/shard_map/ppermute | solution.py:244
  43.2 4.7 %collective-permute-done.13 = bf16[24,16,8,128]{3,0,2,1:T(8,128)(2,1)} collective-permute-done((bf16[24,16,8,128]{3,0,2,1:T(8,128)(2,1)}, bf16[24,16,8,128]{3,0,2,1:T(8,128)(2,1)}, u32[]{:S(2)}, u32[]{:S(2)}) %collective-permute-start.13) | collective-permute-done | bytes 786464 | tf_op jit(solution)/shard_map/ppermute | solution.py:286
  47.8 2.2 %constant_dynamic-update-slice_fusion.4 = bf16[48,16,8,128]{3,0,2,1:T(8,128)(2,1)} fusion(bf16[48,16,8,128]{3,0,2,1:T(8,128)(2,1)} %get-tuple-element.23, bf16[24,16,8,128]{3,0,2,1:T(8,128)(2,1)} %collective-permute-done.12), kind=kLoop, calls=%fused_computation.46 | loop fusion | bytes 1572864 | tf_op jit(solution)/shard_map/concatenate | solution.py:295
  50.0 9.1 %march.3 = (f32[6,16,8,128]{3,2,1,0:T(8,128)S(1)}, bf16[6,16,8,128]{3,2,1,0:T(8,128)(2,1)S(1)}) custom-call(s32[24,2]{1,0:T(8,128)S(1)} %copy.17.bounds_ref, bf16[12,16,8,128]{3,2,1,0:T(8,128)(2,1)S(1)} %get-tuple-element.12.refs_0_, bf16[12,16,8,128]{3,2,1,0:T(8,128)(2,1)S(1)} %collective-permute-done.refs_1_, ...), custom_call_target="tpu_custom_call" | custom-call | flops 4325376000 | bytes 2162688 | tf_op jit(solution)/shard_map/march/pallas_call | solution.py:216
  59.1 2.5 %collective-permute-start.11 = (bf16[6,16,8,128]{3,2,1,0:T(8,128)(2,1)S(1)}, bf16[6,16,8,128]{3,2,1,0:T(8,128)(2,1)S(1)}, u32[]{:S(2)}, u32[]{:S(2)}) collective-permute-start(bf16[6,16,8,128]{3,2,1,0:T(8,128)(2,1)S(1)} %get-tuple-element.19), channel_id=1, source_target_pairs={{0,1},{1,0},{2,3},{3,2},{4,5},{5,4},{6,7},{7,6},{8,9},{9,8},{10,11... | collective-permute-start | bytes 589832 | tf_op jit(solution)/shard_map/ppermute | solution.py:244
  61.6 9.1 %march.2 = (f32[6,16,8,128]{3,2,1,0:T(8,128)S(1)}, bf16[6,16,8,128]{3,2,1,0:T(8,128)(2,1)S(1)}) custom-call(s32[24,2]{1,0:T(8,128)S(1)} %copy.17.bounds_ref, bf16[12,16,8,128]{3,2,1,0:T(8,128)(2,1)S(1)} %get-tuple-element.12.refs_0_, bf16[12,16,8,128]{3,2,1,0:T(8,128)(2,1)S(1)} %collective-permute-done.refs_1_, ...), custom_call_target="tpu_custom_call" | custom-call | flops 4325376000 | bytes 2162688 | tf_op jit(solution)/shard_map/march/pallas_call | solution.py:216
  70.8 6.9 %collective-permute-done.10 = bf16[6,16,8,128]{3,2,1,0:T(8,128)(2,1)S(1)} collective-permute-done((bf16[6,16,8,128]{3,2,1,0:T(8,128)(2,1)S(1)}, bf16[6,16,8,128]{3,2,1,0:T(8,128)(2,1)S(1)}, u32[]{:S(2)}, u32[]{:S(2)}) %collective-permute-start.10) | collective-permute-done | bytes 196640 | tf_op jit(solution)/shard_map/ppermute | solution.py:244
  79.1 1.7 %convolution_bitcast_fusion = f32[48,12]{0,1:T(8,128)S(1)} fusion(bf16[24,16,8,128]{3,0,2,1:T(8,128)(2,1)S(1)} %collective-permute-done.14, bf16[24,16,8,128]{3,0,2,1:T(8,128)(2,1)} %collective-permute-done.13, bf16[12,16,8,128]{3,2,1,0:T(8,128)(2,1)S(1)} %constant_dynamic-update-slice_fusion.2), kind=kOutput, calls=%fused_computation.6 | convolution fusion | flops 22020096 | bytes 1968384 | tf_op jit(solution)/shard_map/dot_general | solution.py:298
  80.8 1.7 %convolution_bitcast_fusion.2 = f32[48,12]{0,1:T(8,128)S(1)} fusion(bf16[24,16,8,128]{3,0,2,1:T(8,128)(2,1)S(1)} %collective-permute-done.14, bf16[24,16,8,128]{3,0,2,1:T(8,128)(2,1)} %collective-permute-done.13, bf16[12,16,8,128]{3,2,1,0:T(8,128)(2,1)S(1)} %get-tuple-element.22), kind=kOutput, calls=%fused_computation.8 | convolution fusion | flops 22020096 | bytes 1968384 | tf_op jit(solution)/shard_map/dot_general | solution.py:298
  83.7 3.4 %collective-permute-done.15 = f32[96,24]{0,1:T(8,128)S(1)} collective-permute-done((f32[96,24]{0,1:T(8,128)S(1)}, f32[96,24]{0,1:T(8,128)S(1)}, u32[]{:S(2)}, u32[]{:S(2)}) %collective-permute-start.15) | collective-permute-done | bytes 9248 | tf_op jit(solution)/shard_map/ppermute | solution.py:244
  87.1 1.5 %collective-permute-start.16 = (f32[96,24]{0,1:T(8,128)S(1)}, f32[96,24]{0,1:T(8,128)S(1)}, u32[]{:S(2)}, u32[]{:S(2)}) collective-permute-start(f32[96,24]{0,1:T(8,128)S(1)} %add.75), channel_id=1, source_target_pairs={{0,2},{1,3},{2,0},{3,1},{4,6},{5,7},{6,4},{7,5},{8,10},{9,11},{10,... | collective-permute-start | bytes 27656 | tf_op jit(solution)/shard_map/ppermute | solution.py:244
  88.6 2.2 %collective-permute-done.16 = f32[96,24]{0,1:T(8,128)S(1)} collective-permute-done((f32[96,24]{0,1:T(8,128)S(1)}, f32[96,24]{0,1:T(8,128)S(1)}, u32[]{:S(2)}, u32[]{:S(2)}) %collective-permute-start.16) | collective-permute-done | bytes 9248 | tf_op jit(solution)/shard_map/ppermute | solution.py:244
  90.8 2.6 %collective-permute-start.17 = (f32[96,24]{0,1:T(8,128)S(1)}, f32[96,24]{0,1:T(8,128)S(1)}, u32[]{:S(2)}, u32[]{:S(2)}) collective-permute-start(f32[96,24]{0,1:T(8,128)S(1)} %add.76), channel_id=1, source_target_pairs={{0,4},{1,5},{2,6},{3,7},{4,0},{5,1},{6,2},{7,3},{8,12},{9,13},{10,... | collective-permute-start | bytes 27656 | tf_op jit(solution)/shard_map/ppermute | solution.py:244
  (85 shorter events, 13.3 us)
Async XLA Ops:
  0.6 6.3 %copy-start.3 = (s32[8]{0:T(128)S(1)}, s32[8]{0:T(128)}, u32[]{:S(2)}) copy-start(s32[8]{0:T(128)} %param.10) | copy-start | bytes 100
  0.7 9.2 %copy-start.6 = (f32[16,8,128]{2,1,0:T(8,128)S(1)}, f32[16,8,128]{2,1,0:T(8,128)}, u32[]{:S(2)}) copy-start(f32[16,8,128]{2,1,0:T(8,128)} %param.8) | copy-start | bytes 196612
  2.7 5.6 %collective-permute-start.1 = (bf16[4,16,2,128]{3,2,1,0:T(2,128)(2,1)S(1)}, bf16[4,16,2,128]{3,2,1,0:T(2,128)(2,1)S(1)}, u32[]{:S(2)}, u32[]{:S(2)}) collective-permute-start(bf16[4,16,2,128]{3,2,1,0:T(2,128)(2,1)S(1)} %gather_fusion.1), channel_id=1, source_target_pairs={{0,8},{8,0},{16,24},{24,16},{1,9},{9,1},{17,25},{25,17},{2,10},{10... | collective-permute-start | bytes 98312 | tf_op jit(solution)/shard_map/ppermute | solution.py:263
  4.3 12.3 %collective-permute-start = (bf16[12,16,8,128]{3,2,1,0:T(8,128)(2,1)S(1)}, bf16[12,16,8,128]{3,2,1,0:T(8,128)(2,1)S(1)}, u32[]{:S(2)}, u32[]{:S(2)}) collective-permute-start(bf16[12,16,8,128]{3,2,1,0:T(8,128)(2,1)S(1)} %get-tuple-element.25), channel_id=1, source_target_pairs={{0,1},{1,0},{2,3},{3,2},{4,5},{5,4},{6,7},{7,6},{8,9},{9,8},{10,11... | collective-permute-start | bytes 1179656 | tf_op jit(solution)/shard_map/ppermute | solution.py:244
  8.3 4.3 %collective-permute-start.3 = (bf16[4,16,4,128]{3,2,1,0:T(4,128)(2,1)S(1)}, bf16[4,16,4,128]{3,2,1,0:T(4,128)(2,1)S(1)}, u32[]{:S(2)}, u32[]{:S(2)}) collective-permute-start(bf16[4,16,4,128]{3,2,1,0:T(4,128)(2,1)S(1)} %pad_maximum_fusion.9), channel_id=1, source_target_pairs={{0,16},{8,24},{16,0},{24,8},{1,17},{9,25},{17,1},{25,9},{2,18},{10... | collective-permute-start | bytes 196616 | tf_op jit(solution)/shard_map/ppermute | solution.py:263
  10.0 16.5 %collective-permute-start.2 = (bf16[12,16,8,128]{3,2,1,0:T(8,128)(2,1)S(1)}, bf16[12,16,8,128]{3,2,1,0:T(8,128)(2,1)S(1)}, u32[]{:S(2)}, u32[]{:S(2)}) collective-permute-start(bf16[12,16,8,128]{3,2,1,0:T(8,128)(2,1)S(1)} %get-tuple-element.12.refs_0_), channel_id=1, source_target_pairs={{2,0},{4,2},{6,4},{1,3},{3,5},{5,7},{10,8},{12,10},{14,12},{9,11},... | collective-permute-start | bytes 1179656 | tf_op jit(solution)/shard_map/ppermute | solution.py:244
  12.7 10.1 %collective-permute-start.4 = (bf16[12,12,8,128]{3,2,1,0:T(8,128)(2,1)S(1)}, bf16[12,12,8,128]{3,2,1,0:T(8,128)(2,1)S(1)}, u32[]{:S(2)}, u32[]{:S(2)}) collective-permute-start(bf16[12,12,8,128]{3,2,1,0:T(8,128)(2,1)S(1)} %constant_dynamic-slice_fusion.1), channel_id=1, source_target_pairs={{0,2},{2,4},{4,6},{3,1},{5,3},{7,5},{8,10},{10,12},{12,14},{11,9},... | collective-permute-start | bytes 884744 | tf_op jit(solution)/shard_map/ppermute | solution.py:244
  16.7 6.0 %collective-permute-start.5 = (bf16[5,16,8,128]{3,2,1,0:T(8,128)(2,1)S(1)}, bf16[5,16,8,128]{3,2,1,0:T(8,128)(2,1)S(1)}, u32[]{:S(2)}, u32[]{:S(2)}) collective-permute-start(bf16[5,16,8,128]{3,2,1,0:T(8,128)(2,1)S(1)} %pad_maximum_fusion.8.refs_6_), channel_id=1, source_target_pairs={{0,1},{1,0},{2,3},{3,2},{4,5},{5,4},{6,7},{7,6},{8,9},{9,8},{10,11... | collective-permute-start | bytes 491528 | tf_op jit(solution)/shard_map/ppermute | solution.py:244
  18.5 9.3 %copy-start.5 = (bf16[24,16,8,128]{3,2,1,0:T(8,128)(2,1)S(1)}, bf16[24,16,8,128]{3,2,1,0:T(8,128)(2,1)}, u32[]{:S(2)}) copy-start(bf16[24,16,8,128]{3,2,1,0:T(8,128)(2,1)} %param.11) | copy-start | bytes 2359300
  22.8 18.1 %collective-permute-start.6 = (bf16[308,8,128]{2,1,0:T(8,128)(2,1)S(1)}, bf16[308,8,128]{2,1,0:T(8,128)(2,1)S(1)}, u32[]{:S(2)}, u32[]{:S(2)}) collective-permute-start(bf16[308,8,128]{2,1,0:T(8,128)(2,1)S(1)} %pad_maximum_fusion.4), channel_id=1, source_target_pairs={{0,2},{2,4},{4,6},{3,1},{5,3},{7,5},{8,10},{10,12},{12,14},{11,9},... | collective-permute-start | bytes 1892360 | tf_op jit(solution)/shard_map/ppermute | solution.py:244
  26.5 14.4 %collective-permute-start.7 = (bf16[260,8,128]{2,1,0:T(8,128)(2,1)S(1)}, bf16[260,8,128]{2,1,0:T(8,128)(2,1)S(1)}, u32[]{:S(2)}, u32[]{:S(2)}) collective-permute-start(bf16[260,8,128]{2,1,0:T(8,128)(2,1)S(1)} %pad_maximum_fusion.5), channel_id=1, source_target_pairs={{2,0},{4,2},{6,4},{1,3},{3,5},{5,7},{10,8},{12,10},{14,12},{9,11},... | collective-permute-start | bytes 1597448 | tf_op jit(solution)/shard_map/ppermute | solution.py:244
  29.6 13.5 %copy-start.7 = (s32[24,2]{0,1:T(2,128)S(1)}, s32[24,2]{0,1:T(2,128)}, u32[]{:S(2)}) copy-start(s32[24,2]{0,1:T(2,128)} %param.7) | copy-start | bytes 580
  29.6 18.3 %collective-permute-start.13 = (bf16[24,16,8,128]{3,0,2,1:T(8,128)(2,1)}, bf16[24,16,8,128]{3,0,2,1:T(8,128)(2,1)}, u32[]{:S(2)}, u32[]{:S(2)}) collective-permute-start(bf16[24,16,8,128]{3,0,2,1:T(8,128)(2,1)} %get-tuple-element.24), channel_id=1, source_target_pairs={{0,16},{8,24},{16,0},{24,8},{1,17},{9,25},{17,1},{25,9},{2,18},{10... | collective-permute-start | bytes 2359304 | tf_op jit(solution)/shard_map/ppermute | solution.py:286
  31.1 16.8 %collective-permute-start.12 = (bf16[24,16,8,128]{3,0,2,1:T(8,128)(2,1)}, bf16[24,16,8,128]{3,0,2,1:T(8,128)(2,1)}, u32[]{:S(2)}, u32[]{:S(2)}) collective-permute-start(bf16[24,16,8,128]{3,0,2,1:T(8,128)(2,1)} %get-tuple-element.24), channel_id=1, source_target_pairs={{0,8},{8,0},{16,24},{24,16},{1,9},{9,1},{17,25},{25,17},{2,10},{10... | collective-permute-start | bytes 2359304 | tf_op jit(solution)/shard_map/ppermute | solution.py:245
  41.8 8.2 %collective-permute-start.9 = (bf16[232,8,128]{2,1,0:T(8,128)(2,1)}, bf16[232,8,128]{2,1,0:T(8,128)(2,1)S(1)}, u32[]{:S(2)}, u32[]{:S(2)}) collective-permute-start(bf16[232,8,128]{2,1,0:T(8,128)(2,1)} %pad_maximum_fusion.6), channel_id=1, source_target_pairs={{0,8},{8,0},{16,24},{24,16},{1,9},{9,1},{17,25},{25,17},{2,10},{10... | collective-permute-start | bytes 1425416 | tf_op jit(solution)/shard_map/ppermute | solution.py:245
  42.6 7.4 %collective-permute-start.8 = (bf16[160,8,128]{2,1,0:T(8,128)(2,1)}, bf16[160,8,128]{2,1,0:T(8,128)(2,1)S(1)}, u32[]{:S(2)}, u32[]{:S(2)}) collective-permute-start(bf16[160,8,128]{2,1,0:T(8,128)(2,1)} %pad_maximum_fusion.7), channel_id=1, source_target_pairs={{0,8},{8,0},{16,24},{24,16},{1,9},{9,1},{17,25},{25,17},{2,10},{10... | collective-permute-start | bytes 983048 | tf_op jit(solution)/shard_map/ppermute | solution.py:245
  43.2 6.8 %copy-start.2 = (bf16[12,12,8,128]{3,2,1,0:T(8,128)(2,1)S(1)}, bf16[12,12,8,128]{3,2,1,0:T(8,128)(2,1)}, u32[]{:S(2)}) copy-start(bf16[12,12,8,128]{3,2,1,0:T(8,128)(2,1)} %copy-done.1) | copy-start | bytes 884740
  47.8 31.3 %collective-permute-start.14 = (bf16[24,16,8,128]{3,0,2,1:T(8,128)(2,1)}, bf16[24,16,8,128]{3,0,2,1:T(8,128)(2,1)S(1)}, u32[]{:S(2)}, u32[]{:S(2)}) collective-permute-start(bf16[24,16,8,128]{3,0,2,1:T(8,128)(2,1)} %collective-permute-done.13), channel_id=1, source_target_pairs={{0,8},{8,0},{16,24},{24,16},{1,9},{9,1},{17,25},{25,17},{2,10},{10... | collective-permute-start | bytes 2359304 | tf_op jit(solution)/shard_map/ppermute | solution.py:245
  59.1 18.7 %collective-permute-start.11 = (bf16[6,16,8,128]{3,2,1,0:T(8,128)(2,1)S(1)}, bf16[6,16,8,128]{3,2,1,0:T(8,128)(2,1)S(1)}, u32[]{:S(2)}, u32[]{:S(2)}) collective-permute-start(bf16[6,16,8,128]{3,2,1,0:T(8,128)(2,1)S(1)} %get-tuple-element.19), channel_id=1, source_target_pairs={{0,1},{1,0},{2,3},{3,2},{4,5},{5,4},{6,7},{7,6},{8,9},{9,8},{10,11... | collective-permute-start | bytes 589832 | tf_op jit(solution)/shard_map/ppermute | solution.py:244
  70.7 7.2 %copy-start.4 = (bf16[48,16,8,128]{3,0,2,1:T(8,128)(2,1)S(1)}, bf16[48,16,8,128]{3,0,2,1:T(8,128)(2,1)}, u32[]{:S(2)}) copy-start(bf16[48,16,8,128]{3,0,2,1:T(8,128)(2,1)} %constant_dynamic-update-slice_fusion.4) | copy-start | bytes 4718596
  70.7 7.1 %collective-permute-start.10 = (bf16[6,16,8,128]{3,2,1,0:T(8,128)(2,1)S(1)}, bf16[6,16,8,128]{3,2,1,0:T(8,128)(2,1)S(1)}, u32[]{:S(2)}, u32[]{:S(2)}) collective-permute-start(bf16[6,16,8,128]{3,2,1,0:T(8,128)(2,1)S(1)} %get-tuple-element.18), channel_id=1, source_target_pairs={{0,1},{1,0},{2,3},{3,2},{4,5},{5,4},{6,7},{7,6},{8,9},{9,8},{10,11... | collective-permute-start | bytes 589832 | tf_op jit(solution)/shard_map/ppermute | solution.py:244
  83.3 3.8 %collective-permute-start.15 = (f32[96,24]{0,1:T(8,128)S(1)}, f32[96,24]{0,1:T(8,128)S(1)}, u32[]{:S(2)}, u32[]{:S(2)}) collective-permute-start(f32[96,24]{0,1:T(8,128)S(1)} %fusion.11), channel_id=1, source_target_pairs={{0,1},{1,0},{2,3},{3,2},{4,5},{5,4},{6,7},{7,6},{8,9},{9,8},{10,11... | collective-permute-start | bytes 27656 | tf_op jit(solution)/shard_map/ppermute | solution.py:244
  87.1 3.7 %collective-permute-start.16 = (f32[96,24]{0,1:T(8,128)S(1)}, f32[96,24]{0,1:T(8,128)S(1)}, u32[]{:S(2)}, u32[]{:S(2)}) collective-permute-start(f32[96,24]{0,1:T(8,128)S(1)} %add.75), channel_id=1, source_target_pairs={{0,2},{1,3},{2,0},{3,1},{4,6},{5,7},{6,4},{7,5},{8,10},{9,11},{10,... | collective-permute-start | bytes 27656 | tf_op jit(solution)/shard_map/ppermute | solution.py:244
  90.8 4.6 %collective-permute-start.17 = (f32[96,24]{0,1:T(8,128)S(1)}, f32[96,24]{0,1:T(8,128)S(1)}, u32[]{:S(2)}, u32[]{:S(2)}) collective-permute-start(f32[96,24]{0,1:T(8,128)S(1)} %add.76), channel_id=1, source_target_pairs={{0,4},{1,5},{2,6},{3,7},{4,0},{5,1},{6,2},{7,3},{8,12},{9,13},{10,... | collective-permute-start | bytes 27656 | tf_op jit(solution)/shard_map/ppermute | solution.py:244
  (2 other events, 5.1 us)

commit v9 on v8

--- a/solution.py
+++ b/solution.py
@@ -50,8 +50,9 @@
     wide, narrow = refs[0:4], refs[4:6]
     c_ref, d_ref = narrow
     near_refs = refs[6:8]
-    near_other, far_other, own_ref, send_ref = refs[8:12]
-    pert, snap, scale, gain, fields, split, left_ref, right_ref, a_buf, b_buf, sems = refs[12:23]
+    near_others = refs[8:10]
+    far_other, own_ref, send_ref = refs[10:13]
+    pert, snap, scale, gain, fields, split, left_ref, right_ref, a_buf, b_buf, sems = refs[13:24]
     count = a_buf.shape[0]
     fetch = [
         pltpu.make_async_copy(wide[j].at[pl.ds(begin, count)], buf, sems.at[j - 2])
@@ -90,9 +91,7 @@
             for t in range(kept + 1):
                 at = t * counts[j]
                 if j < 2:
-                    mine = near_refs[j][t]
-                    at += j * near_size
-                    other = near_other[at : at + counts[j]]
+                    mine, other = near_refs[j][t], near_others[j][t]
                 else:
                     source, first, second = held[j - 2]
                     mine = source[first + at : first + at + counts[j]]
@@ -221,7 +220,7 @@
             jax.ShapeDtypeStruct((count, rows, cy, cz), jnp.bfloat16),
         ],
         compiler_params=pltpu.CompilerParams(vmem_limit_bytes=16 << 20),
-        cost_estimate=pl.CostEstimate(flops=cells * 8000, bytes_accessed=cells * 4, transcendentals=0),
+        cost_estimate=pl.CostEstimate(flops=cells * 8000 if begin else 0, bytes_accessed=cells * 4 if begin else 0, transcendentals=0),
         name="march",
     )(bounds, *operands)
 
@@ -277,25 +276,22 @@
     side_b = hop(cut(after(mine, gots[-1]), near * (1 - par)), perm_b)
     extra_x = hop(after(extra, partner), swap)
     far_own, far_x = cut(trim(extra), near * (1 - par)), cut(trim(extra_x), near * par)
-    side_c = hop(after(planes(partner, extra_x, far_own), side_b), perm_b)
+    turned = jnp.transpose(after(basis_panels, extra), (1, 2, 0, 3))
+    crossed = lax.ppermute(turned, "probe", [(i, i ^ 2) for i in range(members)])
+    side_c = hop(after(planes(partner, extra_x, far_own), side_b, turned), perm_b)
     side_d = hop(after(planes(cut(partner, near * par), extra, far_x), side_a), perm_a)
-    near_other = cores(planes(extra, extra_x))
-    far_other = cores(planes(side_c[half * rows :], side_d[half * far :]))
-    operands = (mine, partner, side_a, side_b, side_c, side_d, extra, extra_x, near_other, far_other)
-    basis_later = basis_panels
-    crossed = lax.ppermute(basis_later, "probe", [(i, i ^ 2) for i in range(members)])
+    far_other = cores(after(planes(side_c[half * rows :], side_d[half * far :]), crossed))
+    operands = (mine, partner, side_a, side_b, side_c, side_d, extra, extra_x, cores(extra), cores(extra_x), far_other)
     first = par == 0
     own, back = [], []
     for begin, count in ((0, half // 2), (half // 2, half - half // 2)):
         kept, sent = propagate(bounds, operands, begin, count, steps, rows, halo)
         own.append(kept)
         back.append(hop(sent, swap))
-    panels = [basis_later, cores(basis_later)]
-    crossed = lax.optimization_barrier((crossed, back[0][0, 0, 0, 0]))[0]
-    panels = [jnp.concatenate(panels, axis=0), jnp.concatenate([crossed, cores(crossed)], axis=0)]
+    panels = [turned, cores(turned), crossed, cores(crossed)]
     dots = lambda x: jnp.concatenate(
         [
-            lax.dot_general(y, x, (((1, 2, 3), (1, 2, 3)), ((), ())), preferred_element_type=jnp.float32)
+            lax.dot_general(y, x, (((0, 1, 3), (1, 2, 3)), ((), ())), preferred_element_type=jnp.float32)
             for y in panels
         ],
         axis=0,

time: 96.4 us -> 91.1 us (0.945)
  waiting for transfers between devices: 33.6 us -> 27 us
  local copies, waits for them, and re-layouts: 9.24 us -> 6.94 us
  starting transfers between devices: 25.1 us -> 27.2 us
  Pallas kernels: 18.2 us -> 20.1 us
    ppermute x1, waiting for transfers between devices: 4.67 us -> 0.01 us  [local(): lax.ppermute(turned, 'probe', [(i, i ^ 2) for i in range(members)])]
    ppermute x11, waiting for transfers between devices: 27.6 us -> 24.9 us  [local(): hop = lambda x, pairs: lax.ppermute(x, 'store', pairs)]
    concatenate x1 -> x0, local copies, waits for them, and re-layouts: 2.15 us -> none  [local(): jnp.concatenate(panels, axis=0)]
    pallas_call x2, Pallas kernels: 18.2 us -> 20.1 us  [propagate(): pl.pallas_call(functools.partial(march, steps, rows, halo, begin), grid_s...]
    ppermute x11, starting transfers between devices: 21 us -> 22.5 us  [local(): hop = lambda x, pairs: lax.ppermute(x, 'store', pairs)]
    dot_general x4 -> x8, matrix products: 4.34 us -> 4.88 us  [local(): lax.dot_general(y, x, (((0, 1, 3), (1, 2, 3)), ((), ())), preferred_eleme...]
  transfers between devices with their start and end apart: 18 -> 19, of which waited for: 9 -> 10; matrix products, arithmetic and copies ran while one was open for 12% -> 11% of each run, Pallas kernels for 19% -> 22%
where the time goes in v9:
time: 91.1 us; the launch traced here: 90.8 us
  starting transfers between devices  27.2 us (30%)
  waiting for transfers between devices  27 us (30%)
  Pallas kernels  20.1 us (22%)
  local copies, waits for them, and re-layouts  6.94 us (8%)
  matrix products  4.88 us (5%)
  other arithmetic  3.62 us (4%)
  between operations  1.1 us (1%)
    ppermute x11, waiting for transfers between devices, local(): hop = lambda x, pairs: lax.ppermute(x, 'store', pairs)  24.9 us
    ppermute x11, starting transfers between devices, local(): hop = lambda x, pairs: lax.ppermute(x, 'store', pairs)  22.5 us
    pallas_call x2, Pallas kernels, propagate(): pl.pallas_call(functools.partial(march, steps, rows, halo, begin), grid_s...  20.1 us
    dot_general x8, matrix products, local(): lax.dot_general(y, x, (((0, 1, 3), (1, 2, 3)), ((), ())), preferred_eleme...  4.88 us
    ppermute x2, starting transfers between devices, local(): got = lax.ppermute(sent, 'probe', [(i, i ^ span) for i in range(members)])  2.1 us
    gather x2, local copies, waits for them, and re-layouts, picked(): jnp.take(snap_times, chosen, mode='clip')  1.93 us
  transfers between devices with their start and end apart: 19, of which 10 were waited for; matrix products, arithmetic and copies ran while one was open for 11% of the time, Pallas kernels for 22%

profile of v9, /device:TPU:0, one launch (start us, length us, event | category | flops | bytes accessed | tf_op | source)
XLA Modules:
  0.0 90.8 jit_solution(10250456262981937377)
XLA Ops:
  0.7 1.3 %gather_fusion = s32[4]{0:T(128)S(1)} fusion(s32[8]{0:T(128)} %param.10, s32[1024]{0:T(1024)S(1)} %pad_clamp_fusion.3), kind=kCustom, calls=%fused_computation | custom fusion | bytes 48 | tf_op jit(solution)/shard_map/jit(_take)/gather | solution.py:255
  3.2 1.2 %constant_dynamic-slice_fusion.2 = (bf16[12,16,8,128]{3,2,1,0:T(8,128)(2,1)S(1)}, bf16[12,16,8,128]{3,2,1,0:T(8,128)(2,1)S(1)}) fusion(bf16[24,16,8,128]{3,2,1,0:T(8,128)(2,1)} %param.6, s32[]{:T(128)S(6)} %select_n.166, s32[]{:T(128)S(6)} %select_n.165), kind=kLoop, calls=%fused_computation.65 | loop fusion | bytes 1572872 | tf_op jit(solution)/shard_map/dynamic_slice | solution.py:273
  4.4 2.6 %collective-permute-start = (bf16[12,16,8,128]{3,2,1,0:T(8,128)(2,1)S(1)}, bf16[12,16,8,128]{3,2,1,0:T(8,128)(2,1)S(1)}, u32[]{:S(2)}, u32[]{:S(2)}) collective-permute-start(bf16[12,16,8,128]{3,2,1,0:T(8,128)(2,1)S(1)} %get-tuple-element.30), channel_id=1, source_target_pairs={{0,1},{1,0},{2,3},{3,2},{4,5},{5,4},{6,7},{7,6},{8,9},{9,8},{10,11... | collective-permute-start | bytes 1179656 | tf_op jit(solution)/shard_map/ppermute | solution.py:243
  8.3 1.6 %collective-permute-start.3 = (bf16[4,16,4,128]{3,2,1,0:T(4,128)(2,1)S(1)}, bf16[4,16,4,128]{3,2,1,0:T(4,128)(2,1)S(1)}, u32[]{:S(2)}, u32[]{:S(2)}) collective-permute-start(bf16[4,16,4,128]{3,2,1,0:T(4,128)(2,1)S(1)} %pad_maximum_fusion.5), channel_id=1, source_target_pairs={{0,16},{8,24},{16,0},{24,8},{1,17},{9,25},{17,1},{25,9},{2,18},{10... | collective-permute-start | bytes 196616 | tf_op jit(solution)/shard_map/ppermute | solution.py:262
  10.0 1.3 %collective-permute-start.2 = (bf16[12,16,8,128]{3,2,1,0:T(8,128)(2,1)S(1)}, bf16[12,16,8,128]{3,2,1,0:T(8,128)(2,1)S(1)}, u32[]{:S(2)}, u32[]{:S(2)}) collective-permute-start(bf16[12,16,8,128]{3,2,1,0:T(8,128)(2,1)S(1)} %get-tuple-element.14.refs_0_), channel_id=1, source_target_pairs={{2,0},{4,2},{6,4},{1,3},{3,5},{5,7},{10,8},{12,10},{14,12},{9,11},... | collective-permute-start | bytes 1179656 | tf_op jit(solution)/shard_map/ppermute | solution.py:243
  11.3 1.4 %collective-permute-done.3 = bf16[4,16,4,128]{3,2,1,0:T(4,128)(2,1)S(1)} collective-permute-done((bf16[4,16,4,128]{3,2,1,0:T(4,128)(2,1)S(1)}, bf16[4,16,4,128]{3,2,1,0:T(4,128)(2,1)S(1)}, u32[]{:S(2)}, u32[]{:S(2)}) %collective-permute-start.3) | collective-permute-done | bytes 65568 | tf_op jit(solution)/shard_map/ppermute | solution.py:262
  12.7 3.5 %collective-permute-start.4 = (bf16[12,12,8,128]{3,2,1,0:T(8,128)(2,1)S(1)}, bf16[12,12,8,128]{3,2,1,0:T(8,128)(2,1)S(1)}, u32[]{:S(2)}, u32[]{:S(2)}) collective-permute-start(bf16[12,12,8,128]{3,2,1,0:T(8,128)(2,1)S(1)} %constant_dynamic-slice_fusion.1), channel_id=1, source_target_pairs={{0,2},{2,4},{4,6},{3,1},{5,3},{7,5},{8,10},{10,12},{12,14},{11,9},... | collective-permute-start | bytes 884744 | tf_op jit(solution)/shard_map/ppermute | solution.py:243
  16.7 1.7 %collective-permute-start.5 = (bf16[5,16,8,128]{3,2,1,0:T(8,128)(2,1)S(1)}, bf16[5,16,8,128]{3,2,1,0:T(8,128)(2,1)S(1)}, u32[]{:S(2)}, u32[]{:S(2)}) collective-permute-start(bf16[5,16,8,128]{3,2,1,0:T(8,128)(2,1)S(1)} %pad_maximum_fusion.4.refs_6_), channel_id=1, source_target_pairs={{0,1},{1,0},{2,3},{3,2},{4,5},{5,4},{6,7},{7,6},{8,9},{9,8},{10,11... | collective-permute-start | bytes 491528 | tf_op jit(solution)/shard_map/ppermute | solution.py:243
  19.0 1.6 %collective-permute-start.10 = (bf16[16,8,24,128]{3,2,1,0:T(8,128)(2,1)S(1)}, bf16[16,8,24,128]{3,2,1,0:T(8,128)(2,1)S(1)}, u32[]{:S(2)}, u32[]{:S(2)}) collective-permute-start(bf16[16,8,24,128]{3,2,1,0:T(8,128)(2,1)S(1)} %bitcast.77), channel_id=1, source_target_pairs={{0,16},{8,24},{16,0},{24,8},{1,17},{9,25},{17,1},{25,9},{2,18},{10... | collective-permute-start | bytes 2359304 | tf_op jit(solution)/shard_map/ppermute | solution.py:280
  20.6 2.1 %collective-permute-done.5.refs_7_ = bf16[5,16,8,128]{3,2,1,0:T(8,128)(2,1)S(1)} collective-permute-done((bf16[5,16,8,128]{3,2,1,0:T(8,128)(2,1)S(1)}, bf16[5,16,8,128]{3,2,1,0:T(8,128)(2,1)S(1)}, u32[]{:S(2)}, u32[]{:S(2)}) %collective-permute-start.5) | collective-permute-done | bytes 163872 | tf_op jit(solution)/shard_map/ppermute | solution.py:243
  22.8 3.6 %collective-permute-start.6 = (bf16[308,8,128]{2,1,0:T(8,128)(2,1)S(1)}, bf16[308,8,128]{2,1,0:T(8,128)(2,1)S(1)}, u32[]{:S(2)}, u32[]{:S(2)}) collective-permute-start(bf16[308,8,128]{2,1,0:T(8,128)(2,1)S(1)} %pad_maximum_fusion.1), channel_id=1, source_target_pairs={{0,2},{2,4},{4,6},{3,1},{5,3},{7,5},{8,10},{10,12},{12,14},{11,9},... | collective-permute-start | bytes 1892360 | tf_op jit(solution)/shard_map/ppermute | solution.py:243
  26.5 1.5 %collective-permute-start.7 = (bf16[260,8,128]{2,1,0:T(8,128)(2,1)S(1)}, bf16[260,8,128]{2,1,0:T(8,128)(2,1)S(1)}, u32[]{:S(2)}, u32[]{:S(2)}) collective-permute-start(bf16[260,8,128]{2,1,0:T(8,128)(2,1)S(1)} %pad_maximum_fusion.2), channel_id=1, source_target_pairs={{2,0},{4,2},{6,4},{1,3},{3,5},{5,7},{10,8},{12,10},{14,12},{9,11},... | collective-permute-start | bytes 1597448 | tf_op jit(solution)/shard_map/ppermute | solution.py:243
  28.0 12.9 %collective-permute-done.7.refs_5_ = bf16[260,8,128]{2,1,0:T(8,128)(2,1)S(1)} collective-permute-done((bf16[260,8,128]{2,1,0:T(8,128)(2,1)S(1)}, bf16[260,8,128]{2,1,0:T(8,128)(2,1)S(1)}, u32[]{:S(2)}, u32[]{:S(2)}) %collective-permute-start.7) | collective-permute-done | bytes 532512 | tf_op jit(solution)/shard_map/ppermute | solution.py:243
  44.5 10.0 %march.3 = (f32[6,16,8,128]{3,2,1,0:T(8,128)S(1)}, bf16[6,16,8,128]{3,2,1,0:T(8,128)(2,1)S(1)}) custom-call(s32[24,2]{1,0:T(8,128)S(1)} %copy.20.bounds_ref, bf16[12,16,8,128]{3,2,1,0:T(8,128)(2,1)S(1)} %get-tuple-element.14.refs_0_, bf16[12,16,8,128]{3,2,1,0:T(8,128)(2,1)S(1)} %collective-permute-done.refs_1_, ...), custom_call_target="tpu_custom_call" | custom-call | flops 4325376000 | bytes 2162688 | tf_op jit(solution)/shard_map/march/pallas_call | solution.py:215
  54.9 10.0 %march.2 = (f32[6,16,8,128]{3,2,1,0:T(8,128)S(1)}, bf16[6,16,8,128]{3,2,1,0:T(8,128)(2,1)S(1)}) custom-call(s32[24,2]{1,0:T(8,128)S(1)} %copy.20.bounds_ref, bf16[12,16,8,128]{3,2,1,0:T(8,128)(2,1)S(1)} %get-tuple-element.14.refs_0_, bf16[12,16,8,128]{3,2,1,0:T(8,128)(2,1)S(1)} %collective-permute-done.refs_1_, ...), custom_call_target="tpu_custom_call" | custom-call | tf_op jit(solution)/shard_map/march/pallas_call | solution.py:215
  64.9 1.8 %collective-permute-start.12 = (bf16[6,16,8,128]{3,2,1,0:T(8,128)(2,1)S(1)}, bf16[6,16,8,128]{3,2,1,0:T(8,128)(2,1)S(1)}, u32[]{:S(2)}, u32[]{:S(2)}) collective-permute-start(bf16[6,16,8,128]{3,2,1,0:T(8,128)(2,1)S(1)} %get-tuple-element.22), channel_id=1, source_target_pairs={{0,1},{1,0},{2,3},{3,2},{4,5},{5,4},{6,7},{7,6},{8,9},{9,8},{10,11... | collective-permute-start | bytes 589832 | tf_op jit(solution)/shard_map/ppermute | solution.py:243
  66.8 5.0 %collective-permute-done.12 = bf16[6,16,8,128]{3,2,1,0:T(8,128)(2,1)S(1)} collective-permute-done((bf16[6,16,8,128]{3,2,1,0:T(8,128)(2,1)S(1)}, bf16[6,16,8,128]{3,2,1,0:T(8,128)(2,1)S(1)}, u32[]{:S(2)}, u32[]{:S(2)}) %collective-permute-start.12) | collective-permute-done | bytes 196640 | tf_op jit(solution)/shard_map/ppermute | solution.py:243
  75.2 1.1 %convolution_bitcast_fusion.7 = f32[24,12]{0,1:T(8,128)S(1)} fusion(bf16[12,16,8,128]{3,2,1,0:T(8,128)(2,1)S(1)} %get-tuple-element.29, bf16[24,16,8,128]{3,2,1,0:T(8,128)(2,1)S(1)} %copy-done.5), kind=kOutput, calls=%fused_computation.12 | convolution fusion | flops 9437184 | bytes 1180800 | tf_op jit(solution)/shard_map/dot_general | solution.py:294
  78.1 1.8 %collective-permute-start.16 = (f32[96,24]{0,1:T(8,128)S(1)}, f32[96,24]{0,1:T(8,128)S(1)}, u32[]{:S(2)}, u32[]{:S(2)}) collective-permute-start(f32[96,24]{0,1:T(8,128)S(1)} %fusion.15), channel_id=1, source_target_pairs={{0,1},{1,0},{2,3},{3,2},{4,5},{5,4},{6,7},{7,6},{8,9},{9,8},{10,11... | collective-permute-start | bytes 27656 | tf_op jit(solution)/shard_map/ppermute | solution.py:243
  79.9 2.0 %collective-permute-done.16 = f32[96,24]{0,1:T(8,128)S(1)} collective-permute-done((f32[96,24]{0,1:T(8,128)S(1)}, f32[96,24]{0,1:T(8,128)S(1)}, u32[]{:S(2)}, u32[]{:S(2)}) %collective-permute-start.16) | collective-permute-done | bytes 9248 | tf_op jit(solution)/shard_map/ppermute | solution.py:243
  81.9 1.7 %collective-permute-start.17 = (f32[96,24]{0,1:T(8,128)S(1)}, f32[96,24]{0,1:T(8,128)S(1)}, u32[]{:S(2)}, u32[]{:S(2)}) collective-permute-start(f32[96,24]{0,1:T(8,128)S(1)} %add.75), channel_id=1, source_target_pairs={{0,2},{1,3},{2,0},{3,1},{4,6},{5,7},{6,4},{7,5},{8,10},{9,11},{10,... | collective-permute-start | bytes 27656 | tf_op jit(solution)/shard_map/ppermute | solution.py:243
  83.6 2.0 %collective-permute-done.17 = f32[96,24]{0,1:T(8,128)S(1)} collective-permute-done((f32[96,24]{0,1:T(8,128)S(1)}, f32[96,24]{0,1:T(8,128)S(1)}, u32[]{:S(2)}, u32[]{:S(2)}) %collective-permute-start.17) | collective-permute-done | bytes 9248 | tf_op jit(solution)/shard_map/ppermute | solution.py:243
  85.6 2.7 %collective-permute-start.18 = (f32[96,24]{0,1:T(8,128)S(1)}, f32[96,24]{0,1:T(8,128)S(1)}, u32[]{:S(2)}, u32[]{:S(2)}) collective-permute-start(f32[96,24]{0,1:T(8,128)S(1)} %add.76), channel_id=1, source_target_pairs={{0,4},{1,5},{2,6},{3,7},{4,0},{5,1},{6,2},{7,3},{8,12},{9,13},{10,... | collective-permute-start | bytes 27656 | tf_op jit(solution)/shard_map/ppermute | solution.py:243
  88.3 1.2 %pad_maximum_fusion = f32[24,16,8,128]{3,2,1,0:T(8,128)} fusion(f32[12,16,8,128]{3,2,1,0:T(8,128)S(1)} %get-tuple-element.28, f32[12,16,8,128]{3,2,1,0:T(8,128)S(1)} %get-tuple-element.27), kind=kLoop, calls=%fused_computation.4 | loop fusion | flops 393216 | bytes 3145728 | tf_op jit(solution)/shard_map/concatenate | solution.py:304
  (92 shorter events, 14.2 us)
Async XLA Ops:
  0.7 9.3 %copy-start.7 = (f32[16,8,128]{2,1,0:T(8,128)S(1)}, f32[16,8,128]{2,1,0:T(8,128)}, u32[]{:S(2)}) copy-start(f32[16,8,128]{2,1,0:T(8,128)} %param.8) | copy-start | bytes 196612
  2.7 5.6 %collective-permute-start.1 = (bf16[4,16,2,128]{3,2,1,0:T(2,128)(2,1)S(1)}, bf16[4,16,2,128]{3,2,1,0:T(2,128)(2,1)S(1)}, u32[]{:S(2)}, u32[]{:S(2)}) collective-permute-start(bf16[4,16,2,128]{3,2,1,0:T(2,128)(2,1)S(1)} %gather_fusion.1), channel_id=1, source_target_pairs={{0,8},{8,0},{16,24},{24,16},{1,9},{9,1},{17,25},{25,17},{2,10},{10... | collective-permute-start | bytes 98312 | tf_op jit(solution)/shard_map/ppermute | solution.py:262
  4.3 14.1 %copy-start.4 = (bf16[24,16,8,128]{3,2,1,0:T(8,128)(2,1)S(1)}, bf16[24,16,8,128]{3,2,1,0:T(8,128)(2,1)}, u32[]{:S(2)}) copy-start(bf16[24,16,8,128]{3,2,1,0:T(8,128)(2,1)} %param.11) | copy-start | bytes 2359300
  4.4 12.3 %collective-permute-start = (bf16[12,16,8,128]{3,2,1,0:T(8,128)(2,1)S(1)}, bf16[12,16,8,128]{3,2,1,0:T(8,128)(2,1)S(1)}, u32[]{:S(2)}, u32[]{:S(2)}) collective-permute-start(bf16[12,16,8,128]{3,2,1,0:T(8,128)(2,1)S(1)} %get-tuple-element.30), channel_id=1, source_target_pairs={{0,1},{1,0},{2,3},{3,2},{4,5},{5,4},{6,7},{7,6},{8,9},{9,8},{10,11... | collective-permute-start | bytes 1179656 | tf_op jit(solution)/shard_map/ppermute | solution.py:243
  8.3 4.3 %collective-permute-start.3 = (bf16[4,16,4,128]{3,2,1,0:T(4,128)(2,1)S(1)}, bf16[4,16,4,128]{3,2,1,0:T(4,128)(2,1)S(1)}, u32[]{:S(2)}, u32[]{:S(2)}) collective-permute-start(bf16[4,16,4,128]{3,2,1,0:T(4,128)(2,1)S(1)} %pad_maximum_fusion.5), channel_id=1, source_target_pairs={{0,16},{8,24},{16,0},{24,8},{1,17},{9,25},{17,1},{25,9},{2,18},{10... | collective-permute-start | bytes 196616 | tf_op jit(solution)/shard_map/ppermute | solution.py:262
  10.0 16.5 %collective-permute-start.2 = (bf16[12,16,8,128]{3,2,1,0:T(8,128)(2,1)S(1)}, bf16[12,16,8,128]{3,2,1,0:T(8,128)(2,1)S(1)}, u32[]{:S(2)}, u32[]{:S(2)}) collective-permute-start(bf16[12,16,8,128]{3,2,1,0:T(8,128)(2,1)S(1)} %get-tuple-element.14.refs_0_), channel_id=1, source_target_pairs={{2,0},{4,2},{6,4},{1,3},{3,5},{5,7},{10,8},{12,10},{14,12},{9,11},... | collective-permute-start | bytes 1179656 | tf_op jit(solution)/shard_map/ppermute | solution.py:243
  12.7 10.1 %collective-permute-start.4 = (bf16[12,12,8,128]{3,2,1,0:T(8,128)(2,1)S(1)}, bf16[12,12,8,128]{3,2,1,0:T(8,128)(2,1)S(1)}, u32[]{:S(2)}, u32[]{:S(2)}) collective-permute-start(bf16[12,12,8,128]{3,2,1,0:T(8,128)(2,1)S(1)} %constant_dynamic-slice_fusion.1), channel_id=1, source_target_pairs={{0,2},{2,4},{4,6},{3,1},{5,3},{7,5},{8,10},{10,12},{12,14},{11,9},... | collective-permute-start | bytes 884744 | tf_op jit(solution)/shard_map/ppermute | solution.py:243
  16.7 6.0 %collective-permute-start.5 = (bf16[5,16,8,128]{3,2,1,0:T(8,128)(2,1)S(1)}, bf16[5,16,8,128]{3,2,1,0:T(8,128)(2,1)S(1)}, u32[]{:S(2)}, u32[]{:S(2)}) collective-permute-start(bf16[5,16,8,128]{3,2,1,0:T(8,128)(2,1)S(1)} %pad_maximum_fusion.4.refs_6_), channel_id=1, source_target_pairs={{0,1},{1,0},{2,3},{3,2},{4,5},{5,4},{6,7},{7,6},{8,9},{9,8},{10,11... | collective-permute-start | bytes 491528 | tf_op jit(solution)/shard_map/ppermute | solution.py:243
  19.0 23.7 %copy-start.6 = (bf16[24,16,8,128]{3,0,2,1:T(8,128)(2,1)}, bf16[24,16,8,128]{3,0,2,1:T(8,128)(2,1)S(1)}, u32[]{:S(2)}) copy-start(bf16[24,16,8,128]{3,0,2,1:T(8,128)(2,1)S(1)} %copy.57) | copy-start | bytes 2359300
  19.0 22.8 %collective-permute-start.10 = (bf16[16,8,24,128]{3,2,1,0:T(8,128)(2,1)S(1)}, bf16[16,8,24,128]{3,2,1,0:T(8,128)(2,1)S(1)}, u32[]{:S(2)}, u32[]{:S(2)}) collective-permute-start(bf16[16,8,24,128]{3,2,1,0:T(8,128)(2,1)S(1)} %bitcast.77), channel_id=1, source_target_pairs={{0,16},{8,24},{16,0},{24,8},{1,17},{9,25},{17,1},{25,9},{2,18},{10... | collective-permute-start | bytes 2359304 | tf_op jit(solution)/shard_map/ppermute | solution.py:280
  22.8 18.1 %collective-permute-start.6 = (bf16[308,8,128]{2,1,0:T(8,128)(2,1)S(1)}, bf16[308,8,128]{2,1,0:T(8,128)(2,1)S(1)}, u32[]{:S(2)}, u32[]{:S(2)}) collective-permute-start(bf16[308,8,128]{2,1,0:T(8,128)(2,1)S(1)} %pad_maximum_fusion.1), channel_id=1, source_target_pairs={{0,2},{2,4},{4,6},{3,1},{5,3},{7,5},{8,10},{10,12},{12,14},{11,9},... | collective-permute-start | bytes 1892360 | tf_op jit(solution)/shard_map/ppermute | solution.py:243
  26.4 16.8 %copy-start.8 = (s32[24,2]{0,1:T(2,128)S(1)}, s32[24,2]{0,1:T(2,128)}, u32[]{:S(2)}) copy-start(s32[24,2]{0,1:T(2,128)} %param.7) | copy-start | bytes 580
  26.5 14.4 %collective-permute-start.7 = (bf16[260,8,128]{2,1,0:T(8,128)(2,1)S(1)}, bf16[260,8,128]{2,1,0:T(8,128)(2,1)S(1)}, u32[]{:S(2)}, u32[]{:S(2)}) collective-permute-start(bf16[260,8,128]{2,1,0:T(8,128)(2,1)S(1)} %pad_maximum_fusion.2), channel_id=1, source_target_pairs={{2,0},{4,2},{6,4},{1,3},{3,5},{5,7},{10,8},{12,10},{14,12},{9,11},... | collective-permute-start | bytes 1597448 | tf_op jit(solution)/shard_map/ppermute | solution.py:243
  41.8 2.6 %collective-permute-start.11 = (bf16[232,8,128]{2,1,0:T(8,128)(2,1)}, bf16[232,8,128]{2,1,0:T(8,128)(2,1)S(1)}, u32[]{:S(2)}, u32[]{:S(2)}) collective-permute-start(bf16[232,8,128]{2,1,0:T(8,128)(2,1)} %pad_maximum_fusion.3), channel_id=1, source_target_pairs={{0,8},{8,0},{16,24},{24,16},{1,9},{9,1},{17,25},{25,17},{2,10},{10... | collective-permute-start | bytes 1425416 | tf_op jit(solution)/shard_map/ppermute | solution.py:244
  42.7 1.5 %collective-permute-start.8 = (bf16[5,16,8,128]{3,2,1,0:T(8,128)(2,1)S(1)}, bf16[5,16,8,128]{3,2,1,0:T(8,128)(2,1)}, u32[]{:S(2)}, u32[]{:S(2)}) collective-permute-start(bf16[5,16,8,128]{3,2,1,0:T(8,128)(2,1)S(1)} %pad_maximum_fusion.4.refs_6_), channel_id=1, source_target_pairs={{0,8},{8,0},{16,24},{24,16},{1,9},{9,1},{17,25},{25,17},{2,10},{10... | collective-permute-start | bytes 491528 | tf_op jit(solution)/shard_map/ppermute | solution.py:244
  42.7 1.8 %collective-permute-start.9 = (bf16[5,16,8,128]{3,2,1,0:T(8,128)(2,1)S(1)}, bf16[5,16,8,128]{3,2,1,0:T(8,128)(2,1)}, u32[]{:S(2)}, u32[]{:S(2)}) collective-permute-start(bf16[5,16,8,128]{3,2,1,0:T(8,128)(2,1)S(1)} %collective-permute-done.5.refs_7_), channel_id=1, source_target_pairs={{0,8},{8,0},{16,24},{24,16},{1,9},{9,1},{17,25},{25,17},{2,10},{10... | collective-permute-start | bytes 491528 | tf_op jit(solution)/shard_map/ppermute | solution.py:244
  43.3 29.3 %collective-permute-start.14 = (bf16[16,8,24,128]{3,2,1,0:T(8,128)(2,1)}, bf16[16,8,24,128]{3,2,1,0:T(8,128)(2,1)S(1)}, u32[]{:S(2)}, u32[]{:S(2)}) collective-permute-start(bf16[16,8,24,128]{3,2,1,0:T(8,128)(2,1)} %bitcast.78), channel_id=1, source_target_pairs={{0,8},{8,0},{16,24},{24,16},{1,9},{9,1},{17,25},{25,17},{2,10},{10... | collective-permute-start | bytes 2359304 | tf_op jit(solution)/shard_map/ppermute | solution.py:244
  43.3 33.0 %collective-permute-start.15 = (bf16[16,8,24,128]{3,2,1,0:T(8,128)(2,1)}, bf16[16,8,24,128]{3,2,1,0:T(8,128)(2,1)S(1)}, u32[]{:S(2)}, u32[]{:S(2)}) collective-permute-start(bf16[16,8,24,128]{3,2,1,0:T(8,128)(2,1)} %copy-done.2), channel_id=1, source_target_pairs={{0,8},{8,0},{16,24},{24,16},{1,9},{9,1},{17,25},{25,17},{2,10},{10... | collective-permute-start | bytes 2359304 | tf_op jit(solution)/shard_map/ppermute | solution.py:244
  54.5 17.3 %collective-permute-start.13 = (bf16[6,16,8,128]{3,2,1,0:T(8,128)(2,1)S(1)}, bf16[6,16,8,128]{3,2,1,0:T(8,128)(2,1)S(1)}, u32[]{:S(2)}, u32[]{:S(2)}) collective-permute-start(bf16[6,16,8,128]{3,2,1,0:T(8,128)(2,1)S(1)} %get-tuple-element.23), channel_id=1, source_target_pairs={{0,1},{1,0},{2,3},{3,2},{4,5},{5,4},{6,7},{7,6},{8,9},{9,8},{10,11... | collective-permute-start | bytes 589832 | tf_op jit(solution)/shard_map/ppermute | solution.py:243
  64.9 7.0 %copy-start.3 = (bf16[16,8,24,128]{3,2,1,0:T(8,128)(2,1)S(1)}, bf16[16,8,24,128]{3,2,1,0:T(8,128)(2,1)}, u32[]{:S(2)}) copy-start(bf16[16,8,24,128]{3,2,1,0:T(8,128)(2,1)} %copy-done.2) | copy-start | bytes 2359300
  64.9 6.9 %collective-permute-start.12 = (bf16[6,16,8,128]{3,2,1,0:T(8,128)(2,1)S(1)}, bf16[6,16,8,128]{3,2,1,0:T(8,128)(2,1)S(1)}, u32[]{:S(2)}, u32[]{:S(2)}) collective-permute-start(bf16[6,16,8,128]{3,2,1,0:T(8,128)(2,1)S(1)} %get-tuple-element.22), channel_id=1, source_target_pairs={{0,1},{1,0},{2,3},{3,2},{4,5},{5,4},{6,7},{7,6},{8,9},{9,8},{10,11... | collective-permute-start | bytes 589832 | tf_op jit(solution)/shard_map/ppermute | solution.py:243
  78.1 3.8 %collective-permute-start.16 = (f32[96,24]{0,1:T(8,128)S(1)}, f32[96,24]{0,1:T(8,128)S(1)}, u32[]{:S(2)}, u32[]{:S(2)}) collective-permute-start(f32[96,24]{0,1:T(8,128)S(1)} %fusion.15), channel_id=1, source_target_pairs={{0,1},{1,0},{2,3},{3,2},{4,5},{5,4},{6,7},{7,6},{8,9},{9,8},{10,11... | collective-permute-start | bytes 27656 | tf_op jit(solution)/shard_map/ppermute | solution.py:243
  81.9 3.7 %collective-permute-start.17 = (f32[96,24]{0,1:T(8,128)S(1)}, f32[96,24]{0,1:T(8,128)S(1)}, u32[]{:S(2)}, u32[]{:S(2)}) collective-permute-start(f32[96,24]{0,1:T(8,128)S(1)} %add.75), channel_id=1, source_target_pairs={{0,2},{1,3},{2,0},{3,1},{4,6},{5,7},{6,4},{7,5},{8,10},{9,11},{10,... | collective-permute-start | bytes 27656 | tf_op jit(solution)/shard_map/ppermute | solution.py:243
  85.6 4.6 %collective-permute-start.18 = (f32[96,24]{0,1:T(8,128)S(1)}, f32[96,24]{0,1:T(8,128)S(1)}, u32[]{:S(2)}, u32[]{:S(2)}) collective-permute-start(f32[96,24]{0,1:T(8,128)S(1)} %add.76), channel_id=1, source_target_pairs={{0,4},{1,5},{2,6},{3,7},{4,0},{5,1},{6,2},{7,3},{8,12},{9,13},{10,... | collective-permute-start | bytes 27656 | tf_op jit(solution)/shard_map/ppermute | solution.py:243
  (4 other events, 9.7 us)

commit v10 on v9

--- a/solution.py
+++ b/solution.py
@@ -250,12 +250,15 @@
     planes = lambda *xs: jnp.concatenate([x.reshape(-1, cy, cz) for x in xs], axis=0)
     near_half, far_half = shares(steps, rows, halo)
 
-    def picked(parity):
-        chosen = jnp.minimum(2 * jnp.arange(near_half) + parity, steps - 1)
-        return jnp.take(snapshots, jnp.take(snap_times, chosen, mode="clip"), axis=0, mode="clip")
-
-    joined = picked(core)
-    sent = picked(1 - core)
+    mine = lax.dynamic_slice_in_dim(probe_field, half * par, half, axis=0)
+    theirs = lax.dynamic_slice_in_dim(probe_field, half * (1 - par), half, axis=0)
+    partner = hop(theirs, swap)
+
+    pairs = jnp.pad(snap_times, (0, steps % 2))
+    evens, odds = pairs[0::2], pairs[1::2]
+    order = jnp.concatenate([jnp.where(core == 0, evens, odds), jnp.where(core == 0, odds, evens)])
+    ordered = jnp.take(after(snapshots, theirs), order, axis=0, mode="clip")
+    joined, sent = ordered[:near_half], ordered[near_half:]
     gots = []
     span = 1
     while span < members:
@@ -269,49 +272,38 @@
     rate = jnp.where(core == 0, high, courant - high).astype(jnp.bfloat16)[None]
     extra = jnp.concatenate([joined, rate], axis=0)
 
-    mine = lax.dynamic_slice_in_dim(probe_field, half * par, half, axis=0)
-    theirs = lax.dynamic_slice_in_dim(probe_field, half * (1 - par), half, axis=0)
-    partner = hop(theirs, swap)
     side_a = hop(after(mine, gots[0]), perm_a)
     side_b = hop(cut(after(mine, gots[-1]), near * (1 - par)), perm_b)
     extra_x = hop(after(extra, partner), swap)
     far_own, far_x = cut(trim(extra), near * (1 - par)), cut(trim(extra_x), near * par)
     turned = jnp.transpose(after(basis_panels, extra), (1, 2, 0, 3))
     crossed = lax.ppermute(turned, "probe", [(i, i ^ 2) for i in range(members)])
-    side_c = hop(after(planes(partner, extra_x, far_own), side_b, turned), perm_b)
+    message, turned = lax.optimization_barrier((planes(partner, extra_x, far_own), turned, side_b))[:2]
+    side_c = hop(message, perm_b)
     side_d = hop(after(planes(cut(partner, near * par), extra, far_x), side_a), perm_a)
     far_other = cores(after(planes(side_c[half * rows :], side_d[half * far :]), crossed))
     operands = (mine, partner, side_a, side_b, side_c, side_d, extra, extra_x, cores(extra), cores(extra_x), far_other)
     first = par == 0
     own, back = [], []
-    for begin, count in ((0, half // 2), (half // 2, half - half // 2)):
+    early = half * 2 // 3 // PACK * PACK
+    for begin, count in ((0, early), (early, half - early)):
         kept, sent = propagate(bounds, operands, begin, count, steps, rows, halo)
         own.append(kept)
         back.append(hop(sent, swap))
     panels = [turned, cores(turned), crossed, cores(crossed)]
-    dots = lambda x: jnp.concatenate(
-        [
-            lax.dot_general(y, x, (((0, 1, 3), (1, 2, 3)), ((), ())), preferred_element_type=jnp.float32)
-            for y in panels
-        ],
-        axis=0,
+    own = jnp.concatenate(own, axis=0)
+    back = jnp.concatenate(back, axis=0)
+    in_order = lambda x, y: jnp.concatenate([jnp.where(first, x, y), jnp.where(first, y, x)], axis=0)
+    low = in_order(own.astype(jnp.bfloat16), back)
+    parts = [
+        lax.dot_general(x, low, (((0, 1, 3), (1, 2, 3)), ((), ())), preferred_element_type=jnp.float32)
+        for x in panels
+    ]
+    rows_of = lambda q: functools.reduce(
+        lambda kept, j: jnp.where(member == j, parts[q ^ j], kept), range(1, members), parts[q]
     )
-    own = jnp.concatenate(own, axis=0)
-    mine_part = dots(own.astype(jnp.bfloat16))
-    back = jnp.concatenate(back, axis=0)
-    back_part = dots(back)
-    back = back.astype(jnp.float32)
-    response = jnp.concatenate([jnp.where(first, own, back), jnp.where(first, back, own)], axis=0)
-    product = jnp.concatenate(
-        [jnp.where(first, mine_part, back_part), jnp.where(first, back_part, mine_part)], axis=1
-    )
-    product = product.reshape(members, -1, probes_here)
-    span = 1
-    while span < members:
-        swapped = product.reshape(-1, 2, span, *product.shape[1:])[:, ::-1].reshape(product.shape)
-        product = jnp.where((member // span) % 2 == 1, swapped, product)
-        span *= 2
-    product = product.reshape(-1, probes_here)
+    product = jnp.concatenate([rows_of(q) for q in range(members)], axis=0)
+    response = in_order(own, back.astype(jnp.float32))
     span = 1
     while span < devices:
         product = product + hop(product, [(i, i ^ span) for i in range(devices)])

time: 91.1 us -> 89.4 us (0.981)
  local copies, waits for them, and re-layouts: 6.94 us -> 5.24 us
    gather x4 -> x1, local copies, waits for them, and re-layouts: 3.18 us -> 0.68 us  [local(): ordered = jnp.take(after(snapshots, theirs), order, axis=0, mode='clip')]
    slice x0 -> x3, local copies, waits for them, and re-layouts: none -> 1.54 us  [the longest x2 1.52 us: local(): evens, odds = (pairs[0::2], pairs[1::2])]
    ppermute x5, waiting for transfers between devices: 0.66 us -> 1.73 us  [local(): lax.ppermute(x, 'probe', [(i, i ^ 1) for i in range(members)])]
    dot_general x8 -> x4, matrix products: 4.88 us -> 4.61 us  [local(): lax.dot_general(x, low, (((0, 1, 3), (1, 2, 3)), ((), ())), preferred_ele...]
  transfers between devices with their start and end apart: 19 -> 19, of which waited for: 10 -> 10; matrix products, arithmetic and copies ran while one was open for 11% -> 8% of each run, Pallas kernels for 22% -> 22%
where the time goes in v10:
time: 89.4 us; the launch traced here: 89 us
  waiting for transfers between devices  27.6 us (31%)
  starting transfers between devices  27.1 us (30%)
  Pallas kernels  19.7 us (22%)
  local copies, waits for them, and re-layouts  5.24 us (6%)
  matrix products  4.61 us (5%)
  other arithmetic  3.77 us (4%)
  between operations  1.04 us (1%)
    ppermute x11, waiting for transfers between devices, local(): hop = lambda x, pairs: lax.ppermute(x, 'store', pairs)  24.4 us
    ppermute x11, starting transfers between devices, local(): hop = lambda x, pairs: lax.ppermute(x, 'store', pairs)  22.3 us
    pallas_call x2, Pallas kernels, propagate(): pl.pallas_call(functools.partial(march, steps, rows, halo, begin), grid_s...  19.7 us
    dot_general x4, matrix products, local(): lax.dot_general(x, low, (((0, 1, 3), (1, 2, 3)), ((), ())), preferred_ele...  4.61 us
    ppermute x2, starting transfers between devices, local(): got = lax.ppermute(sent, 'probe', [(i, i ^ span) for i in range(members)])  2.1 us
  transfers between devices with their start and end apart: 19, of which 10 were waited for; matrix products, arithmetic and copies ran while one was open for 8% of the time, Pallas kernels for 22%

profile of v10, /device:TPU:0, one launch (start us, length us, event | category | flops | bytes accessed | tf_op | source)
XLA Modules:
  0.0 89.0 jit_solution(3638262290414930767)
XLA Ops:
  4.8 2.6 %collective-permute-start = (bf16[12,16,8,128]{3,2,1,0:T(8,128)(2,1)S(1)}, bf16[12,16,8,128]{3,2,1,0:T(8,128)(2,1)S(1)}, u32[]{:S(2)}, u32[]{:S(2)}) collective-permute-start(bf16[12,16,8,128]{3,2,1,0:T(8,128)(2,1)S(1)} %get-tuple-element.32), channel_id=1, source_target_pairs={{0,1},{1,0},{2,3},{3,2},{4,5},{5,4},{6,7},{7,6},{8,9},{9,8},{10,11... | collective-permute-start | bytes 1179656 | tf_op jit(solution)/shard_map/ppermute | solution.py:243
  7.5 1.6 %collective-permute-start.3 = (bf16[4,16,4,128]{3,2,1,0:T(4,128)(2,1)S(1)}, bf16[4,16,4,128]{3,2,1,0:T(4,128)(2,1)S(1)}, u32[]{:S(2)}, u32[]{:S(2)}) collective-permute-start(bf16[4,16,4,128]{3,2,1,0:T(4,128)(2,1)S(1)} %pad_maximum_fusion.6), channel_id=1, source_target_pairs={{0,16},{8,24},{16,0},{24,8},{1,17},{9,25},{17,1},{25,9},{2,18},{10... | collective-permute-start | bytes 196616 | tf_op jit(solution)/shard_map/ppermute | solution.py:265
  9.2 1.3 %collective-permute-start.2 = (bf16[12,16,8,128]{3,2,1,0:T(8,128)(2,1)S(1)}, bf16[12,16,8,128]{3,2,1,0:T(8,128)(2,1)S(1)}, u32[]{:S(2)}, u32[]{:S(2)}) collective-permute-start(bf16[12,16,8,128]{3,2,1,0:T(8,128)(2,1)S(1)} %get-tuple-element.17.refs_0_), channel_id=1, source_target_pairs={{2,0},{4,2},{6,4},{1,3},{3,5},{5,7},{10,8},{12,10},{14,12},{9,11},... | collective-permute-start | bytes 1179656 | tf_op jit(solution)/shard_map/ppermute | solution.py:243
  10.5 1.4 %collective-permute-done.3 = bf16[4,16,4,128]{3,2,1,0:T(4,128)(2,1)S(1)} collective-permute-done((bf16[4,16,4,128]{3,2,1,0:T(4,128)(2,1)S(1)}, bf16[4,16,4,128]{3,2,1,0:T(4,128)(2,1)S(1)}, u32[]{:S(2)}, u32[]{:S(2)}) %collective-permute-start.3) | collective-permute-done | bytes 65568 | tf_op jit(solution)/shard_map/ppermute | solution.py:265
  11.9 3.5 %collective-permute-start.4 = (bf16[12,12,8,128]{3,2,1,0:T(8,128)(2,1)S(1)}, bf16[12,12,8,128]{3,2,1,0:T(8,128)(2,1)S(1)}, u32[]{:S(2)}, u32[]{:S(2)}) collective-permute-start(bf16[12,12,8,128]{3,2,1,0:T(8,128)(2,1)S(1)} %constant_dynamic-slice_fusion.1), channel_id=1, source_target_pairs={{0,2},{2,4},{4,6},{3,1},{5,3},{7,5},{8,10},{10,12},{12,14},{11,9},... | collective-permute-start | bytes 884744 | tf_op jit(solution)/shard_map/ppermute | solution.py:243
  15.6 1.5 %collective-permute-done.refs_1_ = bf16[12,16,8,128]{3,2,1,0:T(8,128)(2,1)S(1)} collective-permute-done((bf16[12,16,8,128]{3,2,1,0:T(8,128)(2,1)S(1)}, bf16[12,16,8,128]{3,2,1,0:T(8,128)(2,1)S(1)}, u32[]{:S(2)}, u32[]{:S(2)}) %collective-permute-start) | collective-permute-done | bytes 393248 | tf_op jit(solution)/shard_map/ppermute | solution.py:243
  17.1 1.8 %collective-permute-start.5 = (bf16[5,16,8,128]{3,2,1,0:T(8,128)(2,1)S(1)}, bf16[5,16,8,128]{3,2,1,0:T(8,128)(2,1)S(1)}, u32[]{:S(2)}, u32[]{:S(2)}) collective-permute-start(bf16[5,16,8,128]{3,2,1,0:T(8,128)(2,1)S(1)} %pad_maximum_fusion.5.refs_6_), channel_id=1, source_target_pairs={{0,1},{1,0},{2,3},{3,2},{4,5},{5,4},{6,7},{7,6},{8,9},{9,8},{10,11... | collective-permute-start | bytes 491528 | tf_op jit(solution)/shard_map/ppermute | solution.py:243
  19.4 1.6 %collective-permute-start.10 = (bf16[16,8,24,128]{3,2,1,0:T(8,128)(2,1)S(1)}, bf16[16,8,24,128]{3,2,1,0:T(8,128)(2,1)}, u32[]{:S(2)}, u32[]{:S(2)}) collective-permute-start(bf16[16,8,24,128]{3,2,1,0:T(8,128)(2,1)S(1)} %bitcast.35), channel_id=1, source_target_pairs={{0,16},{8,24},{16,0},{24,8},{1,17},{9,25},{17,1},{25,9},{2,18},{10... | collective-permute-start | bytes 2359304 | tf_op jit(solution)/shard_map/ppermute | solution.py:280
  21.0 2.0 %collective-permute-done.5.refs_7_ = bf16[5,16,8,128]{3,2,1,0:T(8,128)(2,1)S(1)} collective-permute-done((bf16[5,16,8,128]{3,2,1,0:T(8,128)(2,1)S(1)}, bf16[5,16,8,128]{3,2,1,0:T(8,128)(2,1)S(1)}, u32[]{:S(2)}, u32[]{:S(2)}) %collective-permute-start.5) | collective-permute-done | bytes 163872 | tf_op jit(solution)/shard_map/ppermute | solution.py:243
  23.1 3.6 %collective-permute-start.6 = (bf16[308,8,128]{2,1,0:T(8,128)(2,1)S(1)}, bf16[308,8,128]{2,1,0:T(8,128)(2,1)S(1)}, u32[]{:S(2)}, u32[]{:S(2)}) collective-permute-start(bf16[308,8,128]{2,1,0:T(8,128)(2,1)S(1)} %pad_maximum_fusion.2), channel_id=1, source_target_pairs={{0,2},{2,4},{4,6},{3,1},{5,3},{7,5},{8,10},{10,12},{12,14},{11,9},... | collective-permute-start | bytes 1892360 | tf_op jit(solution)/shard_map/ppermute | solution.py:243
  26.9 1.5 %collective-permute-start.7 = (bf16[260,8,128]{2,1,0:T(8,128)(2,1)S(1)}, bf16[260,8,128]{2,1,0:T(8,128)(2,1)S(1)}, u32[]{:S(2)}, u32[]{:S(2)}) collective-permute-start(bf16[260,8,128]{2,1,0:T(8,128)(2,1)S(1)} %pad_maximum_fusion.3), channel_id=1, source_target_pairs={{2,0},{4,2},{6,4},{1,3},{3,5},{5,7},{10,8},{12,10},{14,12},{9,11},... | collective-permute-start | bytes 1597448 | tf_op jit(solution)/shard_map/ppermute | solution.py:243
  28.4 12.9 %collective-permute-done.7.refs_5_ = bf16[260,8,128]{2,1,0:T(8,128)(2,1)S(1)} collective-permute-done((bf16[260,8,128]{2,1,0:T(8,128)(2,1)S(1)}, bf16[260,8,128]{2,1,0:T(8,128)(2,1)S(1)}, u32[]{:S(2)}, u32[]{:S(2)}) %collective-permute-start.7) | collective-permute-done | bytes 532512 | tf_op jit(solution)/shard_map/ppermute | solution.py:243
  43.4 1.3 %collective-permute-done.8.refs_8_ = bf16[5,16,8,128]{3,2,1,0:T(8,128)(2,1)} collective-permute-done((bf16[5,16,8,128]{3,2,1,0:T(8,128)(2,1)S(1)}, bf16[5,16,8,128]{3,2,1,0:T(8,128)(2,1)}, u32[]{:S(2)}, u32[]{:S(2)}) %collective-permute-start.8) | collective-permute-done | bytes 163872 | tf_op jit(solution)/shard_map/ppermute | solution.py:244
  45.1 12.3 %march.2 = (f32[8,16,8,128]{3,2,1,0:T(8,128)S(1)}, bf16[8,16,8,128]{3,2,1,0:T(8,128)(2,1)S(1)}) custom-call(s32[24,2]{1,0:T(8,128)S(1)} %copy.9.bounds_ref, bf16[12,16,8,128]{3,2,1,0:T(8,128)(2,1)S(1)} %get-tuple-element.17.refs_0_, bf16[12,16,8,128]{3,2,1,0:T(8,128)(2,1)S(1)} %collective-permute-done.refs_1_, ...), custom_call_target="tpu_custom_call" | custom-call | tf_op jit(solution)/shard_map/march/pallas_call | solution.py:215
  57.6 7.4 %march.3 = (f32[4,16,8,128]{3,2,1,0:T(8,128)S(1)}, bf16[4,16,8,128]{3,2,1,0:T(8,128)(2,1)S(1)}) custom-call(s32[24,2]{1,0:T(8,128)S(1)} %copy.9.bounds_ref, bf16[12,16,8,128]{3,2,1,0:T(8,128)(2,1)S(1)} %get-tuple-element.17.refs_0_, bf16[12,16,8,128]{3,2,1,0:T(8,128)(2,1)S(1)} %collective-permute-done.refs_1_, ...), custom_call_target="tpu_custom_call" | custom-call | flops 2883584000 | bytes 1441792 | tf_op jit(solution)/shard_map/march/pallas_call | solution.py:215
  65.1 1.9 %collective-permute-start.13 = (bf16[4,16,8,128]{3,2,1,0:T(8,128)(2,1)S(1)}, bf16[4,16,8,128]{3,2,1,0:T(8,128)(2,1)S(1)}, u32[]{:S(2)}, u32[]{:S(2)}) collective-permute-start(bf16[4,16,8,128]{3,2,1,0:T(8,128)(2,1)S(1)} %get-tuple-element.26), channel_id=1, source_target_pairs={{0,1},{1,0},{2,3},{3,2},{4,5},{5,4},{6,7},{7,6},{8,9},{9,8},{10,11... | collective-permute-start | bytes 393224 | tf_op jit(solution)/shard_map/ppermute | solution.py:243
  67.1 3.4 %collective-permute-done.13 = bf16[4,16,8,128]{3,2,1,0:T(8,128)(2,1)S(1)} collective-permute-done((bf16[4,16,8,128]{3,2,1,0:T(8,128)(2,1)S(1)}, bf16[4,16,8,128]{3,2,1,0:T(8,128)(2,1)S(1)}, u32[]{:S(2)}, u32[]{:S(2)}) %collective-permute-start.13) | collective-permute-done | bytes 131104 | tf_op jit(solution)/shard_map/ppermute | solution.py:243
  72.5 2.0 %convolution_bitcast_fusion.2 = f32[24,24]{0,1:T(8,128)S(1)} fusion(bf16[16,8,24,128]{3,2,1,0:T(8,128)(2,1)} %collective-permute-done.10, bf16[24,16,8,128]{3,2,1,0:T(8,128)(2,1)S(1)} %pad_maximum_fusion.1), kind=kOutput, calls=%fused_computation.4 | convolution fusion | flops 18874368 | bytes 1575168 | tf_op jit(solution)/shard_map/dot_general | solution.py:299
  76.4 1.7 %collective-permute-start.16 = (f32[96,24]{0,1:T(8,128)S(1)}, f32[96,24]{0,1:T(8,128)S(1)}, u32[]{:S(2)}, u32[]{:S(2)}) collective-permute-start(f32[96,24]{0,1:T(8,128)S(1)} %pad_maximum_fusion.7), channel_id=1, source_target_pairs={{0,1},{1,0},{2,3},{3,2},{4,5},{5,4},{6,7},{7,6},{8,9},{9,8},{10,11... | collective-permute-start | bytes 27656 | tf_op jit(solution)/shard_map/ppermute | solution.py:243
  78.1 2.0 %collective-permute-done.16 = f32[96,24]{0,1:T(8,128)S(1)} collective-permute-done((f32[96,24]{0,1:T(8,128)S(1)}, f32[96,24]{0,1:T(8,128)S(1)}, u32[]{:S(2)}, u32[]{:S(2)}) %collective-permute-start.16) | collective-permute-done | bytes 9248 | tf_op jit(solution)/shard_map/ppermute | solution.py:243
  80.1 1.6 %collective-permute-start.17 = (f32[96,24]{0,1:T(8,128)S(1)}, f32[96,24]{0,1:T(8,128)S(1)}, u32[]{:S(2)}, u32[]{:S(2)}) collective-permute-start(f32[96,24]{0,1:T(8,128)S(1)} %add.43), channel_id=1, source_target_pairs={{0,2},{1,3},{2,0},{3,1},{4,6},{5,7},{6,4},{7,5},{8,10},{9,11},{10,... | collective-permute-start | bytes 27656 | tf_op jit(solution)/shard_map/ppermute | solution.py:243
  81.9 1.9 %collective-permute-done.17 = f32[96,24]{0,1:T(8,128)S(1)} collective-permute-done((f32[96,24]{0,1:T(8,128)S(1)}, f32[96,24]{0,1:T(8,128)S(1)}, u32[]{:S(2)}, u32[]{:S(2)}) %collective-permute-start.17) | collective-permute-done | bytes 9248 | tf_op jit(solution)/shard_map/ppermute | solution.py:243
  83.8 2.6 %collective-permute-start.18 = (f32[96,24]{0,1:T(8,128)S(1)}, f32[96,24]{0,1:T(8,128)S(1)}, u32[]{:S(2)}, u32[]{:S(2)}) collective-permute-start(f32[96,24]{0,1:T(8,128)S(1)} %add.44), channel_id=1, source_target_pairs={{0,4},{1,5},{2,6},{3,7},{4,0},{5,1},{6,2},{7,3},{8,12},{9,13},{10,... | collective-permute-start | bytes 27656 | tf_op jit(solution)/shard_map/ppermute | solution.py:243
  86.4 1.3 %pad_maximum_fusion = f32[24,16,8,128]{3,2,1,0:T(8,128)} fusion(f32[12,16,8,128]{3,2,1,0:T(8,128)S(1)} %get-tuple-element.31, f32[12,16,8,128]{3,2,1,0:T(8,128)S(1)} %get-tuple-element.30), kind=kLoop, calls=%fused_computation.1 | loop fusion | flops 393216 | bytes 3145728 | tf_op jit(solution)/shard_map/concatenate | solution.py:296
  (70 shorter events, 13.4 us)
Async XLA Ops:
  0.6 2.9 %copy-start = (bf16[8,16,2,128]{3,2,1,0:T(2,128)(2,1)S(1)}, bf16[8,16,2,128]{3,2,1,0:T(2,128)(2,1)}, u32[]{:S(2)}) copy-start(bf16[8,16,2,128]{3,2,1,0:T(2,128)(2,1)} %param.9) | copy-start | bytes 196612
  0.6 8.4 %copy-start.4 = (f32[16,8,128]{2,1,0:T(8,128)S(1)}, f32[16,8,128]{2,1,0:T(8,128)}, u32[]{:S(2)}) copy-start(f32[16,8,128]{2,1,0:T(8,128)} %param.8) | copy-start | bytes 196612
  2.2 16.7 %copy-start.1 = (bf16[24,16,8,128]{3,2,1,0:T(8,128)(2,1)S(1)}, bf16[24,16,8,128]{3,2,1,0:T(8,128)(2,1)}, u32[]{:S(2)}) copy-start(bf16[24,16,8,128]{3,2,1,0:T(8,128)(2,1)} %param.11) | copy-start | bytes 2359300
  4.3 3.1 %collective-permute-start.1 = (bf16[4,16,2,128]{3,2,1,0:T(2,128)(2,1)S(1)}, bf16[4,16,2,128]{3,2,1,0:T(2,128)(2,1)S(1)}, u32[]{:S(2)}, u32[]{:S(2)}) collective-permute-start(bf16[4,16,2,128]{3,2,1,0:T(2,128)(2,1)S(1)} %slice.38), channel_id=1, source_target_pairs={{0,8},{8,0},{16,24},{24,16},{1,9},{9,1},{17,25},{25,17},{2,10},{10... | collective-permute-start | bytes 98312 | tf_op jit(solution)/shard_map/ppermute | solution.py:265
  4.8 12.3 %collective-permute-start = (bf16[12,16,8,128]{3,2,1,0:T(8,128)(2,1)S(1)}, bf16[12,16,8,128]{3,2,1,0:T(8,128)(2,1)S(1)}, u32[]{:S(2)}, u32[]{:S(2)}) collective-permute-start(bf16[12,16,8,128]{3,2,1,0:T(8,128)(2,1)S(1)} %get-tuple-element.32), channel_id=1, source_target_pairs={{0,1},{1,0},{2,3},{3,2},{4,5},{5,4},{6,7},{7,6},{8,9},{9,8},{10,11... | collective-permute-start | bytes 1179656 | tf_op jit(solution)/shard_map/ppermute | solution.py:243
  7.5 4.3 %collective-permute-start.3 = (bf16[4,16,4,128]{3,2,1,0:T(4,128)(2,1)S(1)}, bf16[4,16,4,128]{3,2,1,0:T(4,128)(2,1)S(1)}, u32[]{:S(2)}, u32[]{:S(2)}) collective-permute-start(bf16[4,16,4,128]{3,2,1,0:T(4,128)(2,1)S(1)} %pad_maximum_fusion.6), channel_id=1, source_target_pairs={{0,16},{8,24},{16,0},{24,8},{1,17},{9,25},{17,1},{25,9},{2,18},{10... | collective-permute-start | bytes 196616 | tf_op jit(solution)/shard_map/ppermute | solution.py:265
  9.2 17.7 %collective-permute-start.2 = (bf16[12,16,8,128]{3,2,1,0:T(8,128)(2,1)S(1)}, bf16[12,16,8,128]{3,2,1,0:T(8,128)(2,1)S(1)}, u32[]{:S(2)}, u32[]{:S(2)}) collective-permute-start(bf16[12,16,8,128]{3,2,1,0:T(8,128)(2,1)S(1)} %get-tuple-element.17.refs_0_), channel_id=1, source_target_pairs={{2,0},{4,2},{6,4},{1,3},{3,5},{5,7},{10,8},{12,10},{14,12},{9,11},... | collective-permute-start | bytes 1179656 | tf_op jit(solution)/shard_map/ppermute | solution.py:243
  11.9 11.3 %collective-permute-start.4 = (bf16[12,12,8,128]{3,2,1,0:T(8,128)(2,1)S(1)}, bf16[12,12,8,128]{3,2,1,0:T(8,128)(2,1)S(1)}, u32[]{:S(2)}, u32[]{:S(2)}) collective-permute-start(bf16[12,12,8,128]{3,2,1,0:T(8,128)(2,1)S(1)} %constant_dynamic-slice_fusion.1), channel_id=1, source_target_pairs={{0,2},{2,4},{4,6},{3,1},{5,3},{7,5},{8,10},{10,12},{12,14},{11,9},... | collective-permute-start | bytes 884744 | tf_op jit(solution)/shard_map/ppermute | solution.py:243
  17.1 6.0 %collective-permute-start.5 = (bf16[5,16,8,128]{3,2,1,0:T(8,128)(2,1)S(1)}, bf16[5,16,8,128]{3,2,1,0:T(8,128)(2,1)S(1)}, u32[]{:S(2)}, u32[]{:S(2)}) collective-permute-start(bf16[5,16,8,128]{3,2,1,0:T(8,128)(2,1)S(1)} %pad_maximum_fusion.5.refs_6_), channel_id=1, source_target_pairs={{0,1},{1,0},{2,3},{3,2},{4,5},{5,4},{6,7},{7,6},{8,9},{9,8},{10,11... | collective-permute-start | bytes 491528 | tf_op jit(solution)/shard_map/ppermute | solution.py:243
  19.4 22.8 %copy-start.2 = (bf16[24,16,8,128]{3,0,2,1:T(8,128)(2,1)}, bf16[24,16,8,128]{3,0,2,1:T(8,128)(2,1)S(1)}, u32[]{:S(2)}) copy-start(bf16[24,16,8,128]{3,0,2,1:T(8,128)(2,1)S(1)} %copy.30) | copy-start | bytes 2359300
  19.4 22.8 %collective-permute-start.10 = (bf16[16,8,24,128]{3,2,1,0:T(8,128)(2,1)S(1)}, bf16[16,8,24,128]{3,2,1,0:T(8,128)(2,1)}, u32[]{:S(2)}, u32[]{:S(2)}) collective-permute-start(bf16[16,8,24,128]{3,2,1,0:T(8,128)(2,1)S(1)} %bitcast.35), channel_id=1, source_target_pairs={{0,16},{8,24},{16,0},{24,8},{1,17},{9,25},{17,1},{25,9},{2,18},{10... | collective-permute-start | bytes 2359304 | tf_op jit(solution)/shard_map/ppermute | solution.py:280
  23.1 18.2 %collective-permute-start.6 = (bf16[308,8,128]{2,1,0:T(8,128)(2,1)S(1)}, bf16[308,8,128]{2,1,0:T(8,128)(2,1)S(1)}, u32[]{:S(2)}, u32[]{:S(2)}) collective-permute-start(bf16[308,8,128]{2,1,0:T(8,128)(2,1)S(1)} %pad_maximum_fusion.2), channel_id=1, source_target_pairs={{0,2},{2,4},{4,6},{3,1},{5,3},{7,5},{8,10},{10,12},{12,14},{11,9},... | collective-permute-start | bytes 1892360 | tf_op jit(solution)/shard_map/ppermute | solution.py:243
  26.7 16.0 %copy-start.5 = (s32[24,2]{0,1:T(2,128)S(1)}, s32[24,2]{0,1:T(2,128)}, u32[]{:S(2)}) copy-start(s32[24,2]{0,1:T(2,128)} %param.7) | copy-start | bytes 580
  26.9 14.4 %collective-permute-start.7 = (bf16[260,8,128]{2,1,0:T(8,128)(2,1)S(1)}, bf16[260,8,128]{2,1,0:T(8,128)(2,1)S(1)}, u32[]{:S(2)}, u32[]{:S(2)}) collective-permute-start(bf16[260,8,128]{2,1,0:T(8,128)(2,1)S(1)} %pad_maximum_fusion.3), channel_id=1, source_target_pairs={{2,0},{4,2},{6,4},{1,3},{3,5},{5,7},{10,8},{12,10},{14,12},{9,11},... | collective-permute-start | bytes 1597448 | tf_op jit(solution)/shard_map/ppermute | solution.py:243
  42.2 2.9 %collective-permute-start.11 = (bf16[232,8,128]{2,1,0:T(8,128)(2,1)}, bf16[232,8,128]{2,1,0:T(8,128)(2,1)S(1)}, u32[]{:S(2)}, u32[]{:S(2)}) collective-permute-start(bf16[232,8,128]{2,1,0:T(8,128)(2,1)} %pad_maximum_fusion.4), channel_id=1, source_target_pairs={{0,8},{8,0},{16,24},{24,16},{1,9},{9,1},{17,25},{25,17},{2,10},{10... | collective-permute-start | bytes 1425416 | tf_op jit(solution)/shard_map/ppermute | solution.py:244
  42.2 2.4 %collective-permute-start.8 = (bf16[5,16,8,128]{3,2,1,0:T(8,128)(2,1)S(1)}, bf16[5,16,8,128]{3,2,1,0:T(8,128)(2,1)}, u32[]{:S(2)}, u32[]{:S(2)}) collective-permute-start(bf16[5,16,8,128]{3,2,1,0:T(8,128)(2,1)S(1)} %pad_maximum_fusion.5.refs_6_), channel_id=1, source_target_pairs={{0,8},{8,0},{16,24},{24,16},{1,9},{9,1},{17,25},{25,17},{2,10},{10... | collective-permute-start | bytes 491528 | tf_op jit(solution)/shard_map/ppermute | solution.py:244
  42.7 2.4 %collective-permute-start.9 = (bf16[5,16,8,128]{3,2,1,0:T(8,128)(2,1)S(1)}, bf16[5,16,8,128]{3,2,1,0:T(8,128)(2,1)}, u32[]{:S(2)}, u32[]{:S(2)}) collective-permute-start(bf16[5,16,8,128]{3,2,1,0:T(8,128)(2,1)S(1)} %collective-permute-done.5.refs_7_), channel_id=1, source_target_pairs={{0,8},{8,0},{16,24},{24,16},{1,9},{9,1},{17,25},{25,17},{2,10},{10... | collective-permute-start | bytes 491528 | tf_op jit(solution)/shard_map/ppermute | solution.py:244
  42.8 31.7 %collective-permute-start.15 = (bf16[16,8,24,128]{3,2,1,0:T(8,128)(2,1)}, bf16[16,8,24,128]{3,2,1,0:T(8,128)(2,1)S(1)}, u32[]{:S(2)}, u32[]{:S(2)}) collective-permute-start(bf16[16,8,24,128]{3,2,1,0:T(8,128)(2,1)} %bitcast.36), channel_id=1, source_target_pairs={{0,8},{8,0},{16,24},{24,16},{1,9},{9,1},{17,25},{25,17},{2,10},{10... | collective-permute-start | bytes 2359304 | tf_op jit(solution)/shard_map/ppermute | solution.py:244
  43.3 32.1 %collective-permute-start.14 = (bf16[16,8,24,128]{3,2,1,0:T(8,128)(2,1)}, bf16[16,8,24,128]{3,2,1,0:T(8,128)(2,1)S(1)}, u32[]{:S(2)}, u32[]{:S(2)}) collective-permute-start(bf16[16,8,24,128]{3,2,1,0:T(8,128)(2,1)} %collective-permute-done.10), channel_id=1, source_target_pairs={{0,8},{8,0},{16,24},{24,16},{1,9},{9,1},{17,25},{25,17},{2,10},{10... | collective-permute-start | bytes 2359304 | tf_op jit(solution)/shard_map/ppermute | solution.py:244
  57.4 9.7 %collective-permute-start.12 = (bf16[8,16,8,128]{3,2,1,0:T(8,128)(2,1)S(1)}, bf16[8,16,8,128]{3,2,1,0:T(8,128)(2,1)S(1)}, u32[]{:S(2)}, u32[]{:S(2)}) collective-permute-start(bf16[8,16,8,128]{3,2,1,0:T(8,128)(2,1)S(1)} %get-tuple-element.25), channel_id=1, source_target_pairs={{0,1},{1,0},{2,3},{3,2},{4,5},{5,4},{6,7},{7,6},{8,9},{9,8},{10,11... | collective-permute-start | bytes 786440 | tf_op jit(solution)/shard_map/ppermute | solution.py:243
  65.1 5.5 %collective-permute-start.13 = (bf16[4,16,8,128]{3,2,1,0:T(8,128)(2,1)S(1)}, bf16[4,16,8,128]{3,2,1,0:T(8,128)(2,1)S(1)}, u32[]{:S(2)}, u32[]{:S(2)}) collective-permute-start(bf16[4,16,8,128]{3,2,1,0:T(8,128)(2,1)S(1)} %get-tuple-element.26), channel_id=1, source_target_pairs={{0,1},{1,0},{2,3},{3,2},{4,5},{5,4},{6,7},{7,6},{8,9},{9,8},{10,11... | collective-permute-start | bytes 393224 | tf_op jit(solution)/shard_map/ppermute | solution.py:243
  76.4 3.7 %collective-permute-start.16 = (f32[96,24]{0,1:T(8,128)S(1)}, f32[96,24]{0,1:T(8,128)S(1)}, u32[]{:S(2)}, u32[]{:S(2)}) collective-permute-start(f32[96,24]{0,1:T(8,128)S(1)} %pad_maximum_fusion.7), channel_id=1, source_target_pairs={{0,1},{1,0},{2,3},{3,2},{4,5},{5,4},{6,7},{7,6},{8,9},{9,8},{10,11... | collective-permute-start | bytes 27656 | tf_op jit(solution)/shard_map/ppermute | solution.py:243
  80.1 3.7 %collective-permute-start.17 = (f32[96,24]{0,1:T(8,128)S(1)}, f32[96,24]{0,1:T(8,128)S(1)}, u32[]{:S(2)}, u32[]{:S(2)}) collective-permute-start(f32[96,24]{0,1:T(8,128)S(1)} %add.43), channel_id=1, source_target_pairs={{0,2},{1,3},{2,0},{3,1},{4,6},{5,7},{6,4},{7,5},{8,10},{9,11},{10,... | collective-permute-start | bytes 27656 | tf_op jit(solution)/shard_map/ppermute | solution.py:243
  83.8 4.6 %collective-permute-start.18 = (f32[96,24]{0,1:T(8,128)S(1)}, f32[96,24]{0,1:T(8,128)S(1)}, u32[]{:S(2)}, u32[]{:S(2)}) collective-permute-start(f32[96,24]{0,1:T(8,128)S(1)} %add.44), channel_id=1, source_target_pairs={{0,4},{1,5},{2,6},{3,7},{4,0},{5,1},{6,2},{7,3},{8,12},{9,13},{10,... | collective-permute-start | bytes 27656 | tf_op jit(solution)/shard_map/ppermute | solution.py:243
  (1 other events, 1.1 us)

commit v11 on v10

--- a/solution.py
+++ b/solution.py
@@ -49,15 +49,14 @@
 def march(steps, rows, halo, begin, bounds_ref, *refs):
     wide, narrow = refs[0:4], refs[4:6]
     c_ref, d_ref = narrow
-    near_refs = refs[6:8]
-    near_others = refs[8:10]
-    far_other, own_ref, send_ref = refs[10:13]
-    pert, snap, scale, gain, fields, split, left_ref, right_ref, a_buf, b_buf, sems = refs[13:24]
-    count = a_buf.shape[0]
-    fetch = [
-        pltpu.make_async_copy(wide[j].at[pl.ds(begin, count)], buf, sems.at[j - 2])
-        for j, buf in ((2, a_buf), (3, b_buf))
-    ]
+    if begin:
+        shared, (own_ref, send_ref) = refs[6:11], refs[11:13]
+        pert, fields, split = refs[13:16]
+    else:
+        near_refs, near_any, far_other = refs[6:8], refs[8:10], refs[10]
+        (own_ref, send_ref), shared = refs[11:13], refs[13:18]
+        pert, fields, split, near_buf, sems = refs[18:23]
+    snap, scale, gain, left_ref, right_ref = shared
     total = 2 * rows + 2 * halo
     cy = 8
     far = halo - rows
@@ -71,8 +70,11 @@
     starts = [e + par * (o - e) for e, o in zip(even, odd)]
     near_half, far_half = shares(steps, rows, halo)
 
-    @pl.when(pl.program_id(0) == 0)
+    @pl.when((pl.program_id(0) == 0) & (begin == 0))
     def _():
+        if begin:
+            return
+        fetch = [pltpu.make_async_copy(near_any[j], near_buf.at[j], sems.at[j]) for j in range(2)]
         for copy in fetch:
             copy.start()
         left_ref[...], right_ref[...] = tables(cy, 128)
@@ -85,13 +87,15 @@
             (c_ref, c_base, 0),
             (d_ref, d_base + near_size, 2 * near_size + far_size),
         )
-        for j in range(6):
+        for j in (2, 3, 4, 5, 0, 1):
             kept = far_half if j in (3, 5) else near_half
+            if j < 2:
+                fetch[j].wait()
             where = pl.ds(pl.multiple_of(starts[j] * cy, 32), counts[j] * cy)
             for t in range(kept + 1):
                 at = t * counts[j]
                 if j < 2:
-                    mine, other = near_refs[j][t], near_others[j][t]
+                    mine, other = near_refs[j][t], near_buf[j, t]
                 else:
                     source, first, second = held[j - 2]
                     mine = source[first + at : first + at + counts[j]]
@@ -105,19 +109,14 @@
                     scale[where, :] = 2.0 + (3.0 * taps[0]) * (mine + other)
                     gain[where, :] = taps[1] * (mine + other)
 
-        for copy in fetch:
-            copy.wait()
-
     for q in range(PACK):
         probe = begin + pl.program_id(0) * PACK + q
         low = bounds_ref[probes * par + probe, 0] - base
         high = bounds_ref[probes * par + probe, 1] - base
         for j in range(6):
             where = pl.ds(pl.multiple_of(starts[j] * cy, 32), counts[j] * cy)
-            if j < 2:
+            if j < 4:
                 value = wide[j][probe].astype(jnp.float32)
-            elif j < 4:
-                value = (a_buf, b_buf)[j - 2][probe - begin].astype(jnp.float32)
             else:
                 value = narrow[j - 4][pl.ds(probe * counts[j], counts[j])].astype(jnp.float32)
             plane = lax.broadcasted_iota(jnp.int32, value.shape, 0) + starts[j]
@@ -192,35 +191,38 @@
     _, _, cy, cz = operands[0].shape
     total = 2 * rows + 2 * halo
     whole = pl.BlockSpec(memory_space=pltpu.VMEM)
-    grid_spec = pltpu.PrefetchScalarGridSpec(
-        num_scalar_prefetch=1,
-        grid=(count // PACK,),
-        in_specs=[whole] * 2 + [pl.BlockSpec(memory_space=pltpu.HBM)] * 2 + [whole] * (len(operands) - 4),
-        out_specs=[whole, whole],
-        scratch_shapes=[
-            pltpu.VMEM((PACK, total * cy, cz), jnp.float32),
-            pltpu.VMEM((steps + steps % 2, total * cy, cz), jnp.float32),
-            pltpu.VMEM((total * cy, cz), jnp.float32),
-            pltpu.VMEM((total * cy, cz), jnp.float32),
-            pltpu.VMEM((PACK, 2, total * cy, cz), jnp.float32),
-            pltpu.VMEM((PACK, 2, total * cy, 2 * cz), jnp.bfloat16),
-            pltpu.VMEM((SPAN * cy, (SPAN + 8) * cy), jnp.bfloat16),
-            pltpu.VMEM((2 * cz, cz), jnp.bfloat16),
-            pltpu.VMEM((count, rows, cy, cz), jnp.bfloat16),
-            pltpu.VMEM((count, halo - rows, cy, cz), jnp.bfloat16),
-            pltpu.SemaphoreType.DMA((2,)),
-        ],
-    )
+    specs = [whole] * len(operands)
+    outs = [((count, rows, cy, cz), jnp.float32), ((count, rows, cy, cz), jnp.bfloat16)]
+    scratch = [
+        pltpu.VMEM((PACK, total * cy, cz), jnp.float32),
+        pltpu.VMEM((PACK, 2, total * cy, cz), jnp.float32),
+        pltpu.VMEM((PACK, 2, total * cy, 2 * cz), jnp.bfloat16),
+    ]
+    if not begin:
+        specs[8:10] = [pl.BlockSpec(memory_space=pl.ANY)] * 2
+        outs += [
+            ((steps + steps % 2, total * cy, cz), jnp.float32),
+            ((total * cy, cz), jnp.float32),
+            ((total * cy, cz), jnp.float32),
+            ((SPAN * cy, (SPAN + 8) * cy), jnp.bfloat16),
+            ((2 * cz, cz), jnp.bfloat16),
+        ]
+        scratch += [pltpu.VMEM((2, *operands[8].shape), jnp.bfloat16), pltpu.SemaphoreType.DMA((2,))]
     cells = count * total * cy * cz
     return pl.pallas_call(
         functools.partial(march, steps, rows, halo, begin),
-        grid_spec=grid_spec,
-        out_shape=[
-            jax.ShapeDtypeStruct((count, rows, cy, cz), jnp.float32),
-            jax.ShapeDtypeStruct((count, rows, cy, cz), jnp.bfloat16),
-        ],
+        grid_spec=pltpu.PrefetchScalarGridSpec(
+            num_scalar_prefetch=1,
+            grid=(count // PACK,),
+            in_specs=specs,
+            out_specs=[whole] * len(outs),
+            scratch_shapes=scratch,
+        ),
+        out_shape=[jax.ShapeDtypeStruct(*x) for x in outs],
         compiler_params=pltpu.CompilerParams(vmem_limit_bytes=16 << 20),
-        cost_estimate=pl.CostEstimate(flops=cells * 8000 if begin else 0, bytes_accessed=cells * 4 if begin else 0, transcendentals=0),
+        cost_estimate=pl.CostEstimate(
+            flops=cells * 8000 if begin else 0, bytes_accessed=cells * 4 if begin else 0, transcendentals=0
+        ),
         name="march",
     )(bounds, *operands)
 
@@ -254,9 +256,9 @@
     theirs = lax.dynamic_slice_in_dim(probe_field, half * (1 - par), half, axis=0)
     partner = hop(theirs, swap)
 
-    pairs = jnp.pad(snap_times, (0, steps % 2))
-    evens, odds = pairs[0::2], pairs[1::2]
-    order = jnp.concatenate([jnp.where(core == 0, evens, odds), jnp.where(core == 0, odds, evens)])
+    slot = jnp.arange(2 * near_half)
+    turn = 2 * (slot % near_half) + jnp.where(slot < near_half, core, 1 - core)
+    order = jnp.sum(jnp.where(turn[:, None] == jnp.arange(steps), snap_times, 0), axis=1)
     ordered = jnp.take(after(snapshots, theirs), order, axis=0, mode="clip")
     joined, sent = ordered[:near_half], ordered[near_half:]
     gots = []
@@ -287,7 +289,8 @@
     own, back = [], []
     early = half * 2 // 3 // PACK * PACK
     for begin, count in ((0, early), (early, half - early)):
-        kept, sent = propagate(bounds, operands, begin, count, steps, rows, halo)
+        kept, sent, *shared = propagate(bounds, operands, begin, count, steps, rows, halo)
+        operands = (*operands[:6], *shared)
         own.append(kept)
         back.append(hop(sent, swap))
     panels = [turned, cores(turned), crossed, cores(crossed)]

time: 89.4 us -> 88.1 us (0.985)
  local copies, waits for them, and re-layouts: 5.24 us -> 3.73 us
    slice x2 -> x0, local copies, waits for them, and re-layouts: 1.52 us -> none  [local(): evens, odds = (pairs[0::2], pairs[1::2])]
  transfers between devices with their start and end apart: 19 -> 19, of which waited for: 10 -> 10; matrix products, arithmetic and copies ran while one was open for 8% -> 8% of each run, Pallas kernels for 22% -> 23%
where the time goes in v11:
time: 88.1 us; the launch traced here: 87.8 us
  waiting for transfers between devices  27.5 us (31%)
  starting transfers between devices  27.1 us (31%)
  Pallas kernels  19.9 us (23%)
  matrix products  4.61 us (5%)
  other arithmetic  3.85 us (4%)
  local copies, waits for them, and re-layouts  3.73 us (4%)
  between operations  1.07 us (1%)
    ppermute x11, waiting for transfers between devices, local(): hop = lambda x, pairs: lax.ppermute(x, 'store', pairs)  24.4 us
    ppermute x11, starting transfers between devices, local(): hop = lambda x, pairs: lax.ppermute(x, 'store', pairs)  22.3 us
    pallas_call x2, Pallas kernels, propagate(): pl.pallas_call(functools.partial(march, steps, rows, halo, begin), grid_s...  19.9 us
    dot_general x4, matrix products, local(): lax.dot_general(x, low, (((0, 1, 3), (1, 2, 3)), ((), ())), preferred_ele...  4.61 us
    ppermute x2, starting transfers between devices, local(): got = lax.ppermute(sent, 'probe', [(i, i ^ span) for i in range(members)])  2.1 us
  transfers between devices with their start and end apart: 19, of which 10 were waited for; matrix products, arithmetic and copies ran while one was open for 8% of the time, Pallas kernels for 23%

profile of v11, /device:TPU:0, one launch (start us, length us, event | category | flops | bytes accessed | tf_op | source)
XLA Modules:
  0.0 87.8 jit_solution(3297205067658119074)
XLA Ops:
  3.4 2.6 %collective-permute-start = (bf16[12,16,8,128]{3,2,1,0:T(8,128)(2,1)S(1)}, bf16[12,16,8,128]{3,2,1,0:T(8,128)(2,1)S(1)}, u32[]{:S(2)}, u32[]{:S(2)}) collective-permute-start(bf16[12,16,8,128]{3,2,1,0:T(8,128)(2,1)S(1)} %get-tuple-element.42), channel_id=1, source_target_pairs={{0,1},{1,0},{2,3},{3,2},{4,5},{5,4},{6,7},{7,6},{8,9},{9,8},{10,11... | collective-permute-start | bytes 1179656 | tf_op jit(solution)/shard_map/ppermute | solution.py:245
  6.1 1.6 %collective-permute-start.3 = (bf16[4,16,4,128]{3,2,1,0:T(4,128)(2,1)S(1)}, bf16[4,16,4,128]{3,2,1,0:T(4,128)(2,1)S(1)}, u32[]{:S(2)}, u32[]{:S(2)}) collective-permute-start(bf16[4,16,4,128]{3,2,1,0:T(4,128)(2,1)S(1)} %pad_maximum_fusion.6), channel_id=1, source_target_pairs={{0,16},{8,24},{16,0},{24,8},{1,17},{9,25},{17,1},{25,9},{2,18},{10... | collective-permute-start | bytes 196616 | tf_op jit(solution)/shard_map/ppermute | solution.py:267
  7.8 1.3 %collective-permute-start.2 = (bf16[12,16,8,128]{3,2,1,0:T(8,128)(2,1)S(1)}, bf16[12,16,8,128]{3,2,1,0:T(8,128)(2,1)S(1)}, u32[]{:S(2)}, u32[]{:S(2)}) collective-permute-start(bf16[12,16,8,128]{3,2,1,0:T(8,128)(2,1)S(1)} %get-tuple-element.22.refs_0_), channel_id=1, source_target_pairs={{2,0},{4,2},{6,4},{1,3},{3,5},{5,7},{10,8},{12,10},{14,12},{9,11},... | collective-permute-start | bytes 1179656 | tf_op jit(solution)/shard_map/ppermute | solution.py:245
  9.1 1.4 %collective-permute-done.3 = bf16[4,16,4,128]{3,2,1,0:T(4,128)(2,1)S(1)} collective-permute-done((bf16[4,16,4,128]{3,2,1,0:T(4,128)(2,1)S(1)}, bf16[4,16,4,128]{3,2,1,0:T(4,128)(2,1)S(1)}, u32[]{:S(2)}, u32[]{:S(2)}) %collective-permute-start.3) | collective-permute-done | bytes 65568 | tf_op jit(solution)/shard_map/ppermute | solution.py:267
  10.5 3.5 %collective-permute-start.4 = (bf16[12,12,8,128]{3,2,1,0:T(8,128)(2,1)S(1)}, bf16[12,12,8,128]{3,2,1,0:T(8,128)(2,1)S(1)}, u32[]{:S(2)}, u32[]{:S(2)}) collective-permute-start(bf16[12,12,8,128]{3,2,1,0:T(8,128)(2,1)S(1)} %constant_dynamic-slice_fusion.1), channel_id=1, source_target_pairs={{0,2},{2,4},{4,6},{3,1},{5,3},{7,5},{8,10},{10,12},{12,14},{11,9},... | collective-permute-start | bytes 884744 | tf_op jit(solution)/shard_map/ppermute | solution.py:245
  14.2 1.5 %collective-permute-done.refs_1_ = bf16[12,16,8,128]{3,2,1,0:T(8,128)(2,1)S(1)} collective-permute-done((bf16[12,16,8,128]{3,2,1,0:T(8,128)(2,1)S(1)}, bf16[12,16,8,128]{3,2,1,0:T(8,128)(2,1)S(1)}, u32[]{:S(2)}, u32[]{:S(2)}) %collective-permute-start) | collective-permute-done | bytes 393248 | tf_op jit(solution)/shard_map/ppermute | solution.py:245
  15.7 1.8 %collective-permute-start.5 = (bf16[5,16,8,128]{3,2,1,0:T(8,128)(2,1)S(1)}, bf16[5,16,8,128]{3,2,1,0:T(8,128)(2,1)S(1)}, u32[]{:S(2)}, u32[]{:S(2)}) collective-permute-start(bf16[5,16,8,128]{3,2,1,0:T(8,128)(2,1)S(1)} %pad_maximum_fusion.5.refs_6_), channel_id=1, source_target_pairs={{0,1},{1,0},{2,3},{3,2},{4,5},{5,4},{6,7},{7,6},{8,9},{9,8},{10,11... | collective-permute-start | bytes 491528 | tf_op jit(solution)/shard_map/ppermute | solution.py:245
  18.0 1.6 %collective-permute-start.10 = (bf16[16,8,24,128]{3,2,1,0:T(8,128)(2,1)S(1)}, bf16[16,8,24,128]{3,2,1,0:T(8,128)(2,1)}, u32[]{:S(2)}, u32[]{:S(2)}) collective-permute-start(bf16[16,8,24,128]{3,2,1,0:T(8,128)(2,1)S(1)} %bitcast.35), channel_id=1, source_target_pairs={{0,16},{8,24},{16,0},{24,8},{1,17},{9,25},{17,1},{25,9},{2,18},{10... | collective-permute-start | bytes 2359304 | tf_op jit(solution)/shard_map/ppermute | solution.py:282
  19.6 2.0 %collective-permute-done.5.refs_7_ = bf16[5,16,8,128]{3,2,1,0:T(8,128)(2,1)S(1)} collective-permute-done((bf16[5,16,8,128]{3,2,1,0:T(8,128)(2,1)S(1)}, bf16[5,16,8,128]{3,2,1,0:T(8,128)(2,1)S(1)}, u32[]{:S(2)}, u32[]{:S(2)}) %collective-permute-start.5) | collective-permute-done | bytes 163872 | tf_op jit(solution)/shard_map/ppermute | solution.py:245
  21.7 3.6 %collective-permute-start.6 = (bf16[308,8,128]{2,1,0:T(8,128)(2,1)S(1)}, bf16[308,8,128]{2,1,0:T(8,128)(2,1)S(1)}, u32[]{:S(2)}, u32[]{:S(2)}) collective-permute-start(bf16[308,8,128]{2,1,0:T(8,128)(2,1)S(1)} %pad_maximum_fusion.2), channel_id=1, source_target_pairs={{0,2},{2,4},{4,6},{3,1},{5,3},{7,5},{8,10},{10,12},{12,14},{11,9},... | collective-permute-start | bytes 1892360 | tf_op jit(solution)/shard_map/ppermute | solution.py:245
  25.5 1.5 %collective-permute-start.7 = (bf16[260,8,128]{2,1,0:T(8,128)(2,1)S(1)}, bf16[260,8,128]{2,1,0:T(8,128)(2,1)S(1)}, u32[]{:S(2)}, u32[]{:S(2)}) collective-permute-start(bf16[260,8,128]{2,1,0:T(8,128)(2,1)S(1)} %pad_maximum_fusion.3), channel_id=1, source_target_pairs={{2,0},{4,2},{6,4},{1,3},{3,5},{5,7},{10,8},{12,10},{14,12},{9,11},... | collective-permute-start | bytes 1597448 | tf_op jit(solution)/shard_map/ppermute | solution.py:245
  27.0 12.9 %collective-permute-done.7.refs_5_ = bf16[260,8,128]{2,1,0:T(8,128)(2,1)S(1)} collective-permute-done((bf16[260,8,128]{2,1,0:T(8,128)(2,1)S(1)}, bf16[260,8,128]{2,1,0:T(8,128)(2,1)S(1)}, u32[]{:S(2)}, u32[]{:S(2)}) %collective-permute-start.7) | collective-permute-done | bytes 532512 | tf_op jit(solution)/shard_map/ppermute | solution.py:245
  42.0 1.3 %collective-permute-done.8.refs_8_ = bf16[5,16,8,128]{3,2,1,0:T(8,128)(2,1)} collective-permute-done((bf16[5,16,8,128]{3,2,1,0:T(8,128)(2,1)S(1)}, bf16[5,16,8,128]{3,2,1,0:T(8,128)(2,1)}, u32[]{:S(2)}, u32[]{:S(2)}) %collective-permute-start.8) | collective-permute-done | bytes 163872 | tf_op jit(solution)/shard_map/ppermute | solution.py:246
  43.7 13.4 %march.2 = (f32[8,16,8,128]{3,2,1,0:T(8,128)S(1)}, bf16[8,16,8,128]{3,2,1,0:T(8,128)(2,1)S(1)}, f32[8,704,128]{2,1,0:T(8,128)S(1)}, f32[704,128]{1,0:T(8,128)S(1...) custom-call(s32[24,2]{1,0:T(8,128)S(1)} %copy.16.bounds_ref, ...), custom_call_target="tpu_custom_call" | custom-call | tf_op jit(solution)/shard_map/march/pallas_call | solution.py:212
  57.3 6.6 %march.3 = (f32[4,16,8,128]{3,2,1,0:T(8,128)S(1)}, bf16[4,16,8,128]{3,2,1,0:T(8,128)(2,1)S(1)}) custom-call(s32[24,2]{1,0:T(8,128)S(1)} %copy.16.bounds_ref, bf16[12,16,8,128]{3,2,1,0:T(8,128)(2,1)S(1)} %get-tuple-element.22.refs_0_, bf16[12,16,8,128]{3,2,1,0:T(8,128)(2,1)S(1)} %collective-permute-done.refs_1_, ...), custom_call_target="tpu_custom_call" | custom-call | flops 2883584000 | bytes 1441792 | tf_op jit(solution)/shard_map/march/pallas_call | solution.py:212
  63.9 1.9 %collective-permute-start.13 = (bf16[4,16,8,128]{3,2,1,0:T(8,128)(2,1)S(1)}, bf16[4,16,8,128]{3,2,1,0:T(8,128)(2,1)S(1)}, u32[]{:S(2)}, u32[]{:S(2)}) collective-permute-start(bf16[4,16,8,128]{3,2,1,0:T(8,128)(2,1)S(1)} %get-tuple-element.36), channel_id=1, source_target_pairs={{0,1},{1,0},{2,3},{3,2},{4,5},{5,4},{6,7},{7,6},{8,9},{9,8},{10,11... | collective-permute-start | bytes 393224 | tf_op jit(solution)/shard_map/ppermute | solution.py:245
  65.9 3.4 %collective-permute-done.13 = bf16[4,16,8,128]{3,2,1,0:T(8,128)(2,1)S(1)} collective-permute-done((bf16[4,16,8,128]{3,2,1,0:T(8,128)(2,1)S(1)}, bf16[4,16,8,128]{3,2,1,0:T(8,128)(2,1)S(1)}, u32[]{:S(2)}, u32[]{:S(2)}) %collective-permute-start.13) | collective-permute-done | bytes 131104 | tf_op jit(solution)/shard_map/ppermute | solution.py:245
  71.4 2.0 %convolution_bitcast_fusion.2 = f32[24,24]{0,1:T(8,128)S(1)} fusion(bf16[16,8,24,128]{3,2,1,0:T(8,128)(2,1)} %collective-permute-done.10, bf16[24,16,8,128]{3,2,1,0:T(8,128)(2,1)S(1)} %pad_maximum_fusion.1), kind=kOutput, calls=%fused_computation.4 | convolution fusion | flops 18874368 | bytes 1575168 | tf_op jit(solution)/shard_map/dot_general | solution.py:302
  75.2 1.7 %collective-permute-start.16 = (f32[96,24]{0,1:T(8,128)S(1)}, f32[96,24]{0,1:T(8,128)S(1)}, u32[]{:S(2)}, u32[]{:S(2)}) collective-permute-start(f32[96,24]{0,1:T(8,128)S(1)} %pad_maximum_fusion.7), channel_id=1, source_target_pairs={{0,1},{1,0},{2,3},{3,2},{4,5},{5,4},{6,7},{7,6},{8,9},{9,8},{10,11... | collective-permute-start | bytes 27656 | tf_op jit(solution)/shard_map/ppermute | solution.py:245
  77.0 2.0 %collective-permute-done.16 = f32[96,24]{0,1:T(8,128)S(1)} collective-permute-done((f32[96,24]{0,1:T(8,128)S(1)}, f32[96,24]{0,1:T(8,128)S(1)}, u32[]{:S(2)}, u32[]{:S(2)}) %collective-permute-start.16) | collective-permute-done | bytes 9248 | tf_op jit(solution)/shard_map/ppermute | solution.py:245
  78.9 1.6 %collective-permute-start.17 = (f32[96,24]{0,1:T(8,128)S(1)}, f32[96,24]{0,1:T(8,128)S(1)}, u32[]{:S(2)}, u32[]{:S(2)}) collective-permute-start(f32[96,24]{0,1:T(8,128)S(1)} %add.62), channel_id=1, source_target_pairs={{0,2},{1,3},{2,0},{3,1},{4,6},{5,7},{6,4},{7,5},{8,10},{9,11},{10,... | collective-permute-start | bytes 27656 | tf_op jit(solution)/shard_map/ppermute | solution.py:245
  80.7 1.9 %collective-permute-done.17 = f32[96,24]{0,1:T(8,128)S(1)} collective-permute-done((f32[96,24]{0,1:T(8,128)S(1)}, f32[96,24]{0,1:T(8,128)S(1)}, u32[]{:S(2)}, u32[]{:S(2)}) %collective-permute-start.17) | collective-permute-done | bytes 9248 | tf_op jit(solution)/shard_map/ppermute | solution.py:245
  82.6 2.6 %collective-permute-start.18 = (f32[96,24]{0,1:T(8,128)S(1)}, f32[96,24]{0,1:T(8,128)S(1)}, u32[]{:S(2)}, u32[]{:S(2)}) collective-permute-start(f32[96,24]{0,1:T(8,128)S(1)} %add.63), channel_id=1, source_target_pairs={{0,4},{1,5},{2,6},{3,7},{4,0},{5,1},{6,2},{7,3},{8,12},{9,13},{10,... | collective-permute-start | bytes 27656 | tf_op jit(solution)/shard_map/ppermute | solution.py:245
  85.2 1.3 %pad_maximum_fusion = f32[24,16,8,128]{3,2,1,0:T(8,128)} fusion(f32[12,16,8,128]{3,2,1,0:T(8,128)S(1)} %get-tuple-element.41, f32[12,16,8,128]{3,2,1,0:T(8,128)S(1)} %get-tuple-element.40), kind=kLoop, calls=%fused_computation.1 | loop fusion | flops 393216 | bytes 3145728 | tf_op jit(solution)/shard_map/concatenate | solution.py:299
  (70 shorter events, 11.9 us)
Async XLA Ops:
  0.6 1.5 %copy-start = (bf16[8,16,2,128]{3,2,1,0:T(2,128)(2,1)S(1)}, bf16[8,16,2,128]{3,2,1,0:T(2,128)(2,1)}, u32[]{:S(2)}) copy-start(bf16[8,16,2,128]{3,2,1,0:T(2,128)(2,1)} %param.9) | copy-start | bytes 196612
  0.7 7.1 %copy-start.4 = (f32[16,8,128]{2,1,0:T(8,128)S(1)}, f32[16,8,128]{2,1,0:T(8,128)}, u32[]{:S(2)}) copy-start(f32[16,8,128]{2,1,0:T(8,128)} %param.8) | copy-start | bytes 196612
  0.7 16.8 %copy-start.1 = (bf16[24,16,8,128]{3,2,1,0:T(8,128)(2,1)S(1)}, bf16[24,16,8,128]{3,2,1,0:T(8,128)(2,1)}, u32[]{:S(2)}) copy-start(bf16[24,16,8,128]{3,2,1,0:T(8,128)(2,1)} %param.11) | copy-start | bytes 2359300
  2.9 3.1 %collective-permute-start.1 = (bf16[4,16,2,128]{3,2,1,0:T(2,128)(2,1)S(1)}, bf16[4,16,2,128]{3,2,1,0:T(2,128)(2,1)S(1)}, u32[]{:S(2)}, u32[]{:S(2)}) collective-permute-start(bf16[4,16,2,128]{3,2,1,0:T(2,128)(2,1)S(1)} %slice.30), channel_id=1, source_target_pairs={{0,8},{8,0},{16,24},{24,16},{1,9},{9,1},{17,25},{25,17},{2,10},{10... | collective-permute-start | bytes 98312 | tf_op jit(solution)/shard_map/ppermute | solution.py:267
  3.4 12.3 %collective-permute-start = (bf16[12,16,8,128]{3,2,1,0:T(8,128)(2,1)S(1)}, bf16[12,16,8,128]{3,2,1,0:T(8,128)(2,1)S(1)}, u32[]{:S(2)}, u32[]{:S(2)}) collective-permute-start(bf16[12,16,8,128]{3,2,1,0:T(8,128)(2,1)S(1)} %get-tuple-element.42), channel_id=1, source_target_pairs={{0,1},{1,0},{2,3},{3,2},{4,5},{5,4},{6,7},{7,6},{8,9},{9,8},{10,11... | collective-permute-start | bytes 1179656 | tf_op jit(solution)/shard_map/ppermute | solution.py:245
  6.1 4.3 %collective-permute-start.3 = (bf16[4,16,4,128]{3,2,1,0:T(4,128)(2,1)S(1)}, bf16[4,16,4,128]{3,2,1,0:T(4,128)(2,1)S(1)}, u32[]{:S(2)}, u32[]{:S(2)}) collective-permute-start(bf16[4,16,4,128]{3,2,1,0:T(4,128)(2,1)S(1)} %pad_maximum_fusion.6), channel_id=1, source_target_pairs={{0,16},{8,24},{16,0},{24,8},{1,17},{9,25},{17,1},{25,9},{2,18},{10... | collective-permute-start | bytes 196616 | tf_op jit(solution)/shard_map/ppermute | solution.py:267
  7.8 17.7 %collective-permute-start.2 = (bf16[12,16,8,128]{3,2,1,0:T(8,128)(2,1)S(1)}, bf16[12,16,8,128]{3,2,1,0:T(8,128)(2,1)S(1)}, u32[]{:S(2)}, u32[]{:S(2)}) collective-permute-start(bf16[12,16,8,128]{3,2,1,0:T(8,128)(2,1)S(1)} %get-tuple-element.22.refs_0_), channel_id=1, source_target_pairs={{2,0},{4,2},{6,4},{1,3},{3,5},{5,7},{10,8},{12,10},{14,12},{9,11},... | collective-permute-start | bytes 1179656 | tf_op jit(solution)/shard_map/ppermute | solution.py:245
  10.5 11.3 %collective-permute-start.4 = (bf16[12,12,8,128]{3,2,1,0:T(8,128)(2,1)S(1)}, bf16[12,12,8,128]{3,2,1,0:T(8,128)(2,1)S(1)}, u32[]{:S(2)}, u32[]{:S(2)}) collective-permute-start(bf16[12,12,8,128]{3,2,1,0:T(8,128)(2,1)S(1)} %constant_dynamic-slice_fusion.1), channel_id=1, source_target_pairs={{0,2},{2,4},{4,6},{3,1},{5,3},{7,5},{8,10},{10,12},{12,14},{11,9},... | collective-permute-start | bytes 884744 | tf_op jit(solution)/shard_map/ppermute | solution.py:245
  15.7 6.0 %collective-permute-start.5 = (bf16[5,16,8,128]{3,2,1,0:T(8,128)(2,1)S(1)}, bf16[5,16,8,128]{3,2,1,0:T(8,128)(2,1)S(1)}, u32[]{:S(2)}, u32[]{:S(2)}) collective-permute-start(bf16[5,16,8,128]{3,2,1,0:T(8,128)(2,1)S(1)} %pad_maximum_fusion.5.refs_6_), channel_id=1, source_target_pairs={{0,1},{1,0},{2,3},{3,2},{4,5},{5,4},{6,7},{7,6},{8,9},{9,8},{10,11... | collective-permute-start | bytes 491528 | tf_op jit(solution)/shard_map/ppermute | solution.py:245
  18.0 22.8 %copy-start.2 = (bf16[24,16,8,128]{3,0,2,1:T(8,128)(2,1)}, bf16[24,16,8,128]{3,0,2,1:T(8,128)(2,1)S(1)}, u32[]{:S(2)}) copy-start(bf16[24,16,8,128]{3,0,2,1:T(8,128)(2,1)S(1)} %copy.37) | copy-start | bytes 2359300
  18.0 22.7 %collective-permute-start.10 = (bf16[16,8,24,128]{3,2,1,0:T(8,128)(2,1)S(1)}, bf16[16,8,24,128]{3,2,1,0:T(8,128)(2,1)}, u32[]{:S(2)}, u32[]{:S(2)}) collective-permute-start(bf16[16,8,24,128]{3,2,1,0:T(8,128)(2,1)S(1)} %bitcast.35), channel_id=1, source_target_pairs={{0,16},{8,24},{16,0},{24,8},{1,17},{9,25},{17,1},{25,9},{2,18},{10... | collective-permute-start | bytes 2359304 | tf_op jit(solution)/shard_map/ppermute | solution.py:282
  21.7 18.2 %collective-permute-start.6 = (bf16[308,8,128]{2,1,0:T(8,128)(2,1)S(1)}, bf16[308,8,128]{2,1,0:T(8,128)(2,1)S(1)}, u32[]{:S(2)}, u32[]{:S(2)}) collective-permute-start(bf16[308,8,128]{2,1,0:T(8,128)(2,1)S(1)} %pad_maximum_fusion.2), channel_id=1, source_target_pairs={{0,2},{2,4},{4,6},{3,1},{5,3},{7,5},{8,10},{10,12},{12,14},{11,9},... | collective-permute-start | bytes 1892360 | tf_op jit(solution)/shard_map/ppermute | solution.py:245
  25.4 16.0 %copy-start.5 = (s32[24,2]{0,1:T(2,128)S(1)}, s32[24,2]{0,1:T(2,128)}, u32[]{:S(2)}) copy-start(s32[24,2]{0,1:T(2,128)} %param.7) | copy-start | bytes 580
  25.5 14.4 %collective-permute-start.7 = (bf16[260,8,128]{2,1,0:T(8,128)(2,1)S(1)}, bf16[260,8,128]{2,1,0:T(8,128)(2,1)S(1)}, u32[]{:S(2)}, u32[]{:S(2)}) collective-permute-start(bf16[260,8,128]{2,1,0:T(8,128)(2,1)S(1)} %pad_maximum_fusion.3), channel_id=1, source_target_pairs={{2,0},{4,2},{6,4},{1,3},{3,5},{5,7},{10,8},{12,10},{14,12},{9,11},... | collective-permute-start | bytes 1597448 | tf_op jit(solution)/shard_map/ppermute | solution.py:245
  40.8 2.9 %collective-permute-start.11 = (bf16[232,8,128]{2,1,0:T(8,128)(2,1)}, bf16[232,8,128]{2,1,0:T(8,128)(2,1)S(1)}, u32[]{:S(2)}, u32[]{:S(2)}) collective-permute-start(bf16[232,8,128]{2,1,0:T(8,128)(2,1)} %pad_maximum_fusion.4), channel_id=1, source_target_pairs={{0,8},{8,0},{16,24},{24,16},{1,9},{9,1},{17,25},{25,17},{2,10},{10... | collective-permute-start | bytes 1425416 | tf_op jit(solution)/shard_map/ppermute | solution.py:246
  40.8 2.4 %collective-permute-start.8 = (bf16[5,16,8,128]{3,2,1,0:T(8,128)(2,1)S(1)}, bf16[5,16,8,128]{3,2,1,0:T(8,128)(2,1)}, u32[]{:S(2)}, u32[]{:S(2)}) collective-permute-start(bf16[5,16,8,128]{3,2,1,0:T(8,128)(2,1)S(1)} %pad_maximum_fusion.5.refs_6_), channel_id=1, source_target_pairs={{0,8},{8,0},{16,24},{24,16},{1,9},{9,1},{17,25},{25,17},{2,10},{10... | collective-permute-start | bytes 491528 | tf_op jit(solution)/shard_map/ppermute | solution.py:246
  41.3 2.4 %collective-permute-start.9 = (bf16[5,16,8,128]{3,2,1,0:T(8,128)(2,1)S(1)}, bf16[5,16,8,128]{3,2,1,0:T(8,128)(2,1)}, u32[]{:S(2)}, u32[]{:S(2)}) collective-permute-start(bf16[5,16,8,128]{3,2,1,0:T(8,128)(2,1)S(1)} %collective-permute-done.5.refs_7_), channel_id=1, source_target_pairs={{0,8},{8,0},{16,24},{24,16},{1,9},{9,1},{17,25},{25,17},{2,10},{10... | collective-permute-start | bytes 491528 | tf_op jit(solution)/shard_map/ppermute | solution.py:246
  41.5 31.9 %collective-permute-start.15 = (bf16[16,8,24,128]{3,2,1,0:T(8,128)(2,1)}, bf16[16,8,24,128]{3,2,1,0:T(8,128)(2,1)S(1)}, u32[]{:S(2)}, u32[]{:S(2)}) collective-permute-start(bf16[16,8,24,128]{3,2,1,0:T(8,128)(2,1)} %bitcast.36), channel_id=1, source_target_pairs={{0,8},{8,0},{16,24},{24,16},{1,9},{9,1},{17,25},{25,17},{2,10},{10... | collective-permute-start | bytes 2359304 | tf_op jit(solution)/shard_map/ppermute | solution.py:246
  41.9 32.3 %collective-permute-start.14 = (bf16[16,8,24,128]{3,2,1,0:T(8,128)(2,1)}, bf16[16,8,24,128]{3,2,1,0:T(8,128)(2,1)S(1)}, u32[]{:S(2)}, u32[]{:S(2)}) collective-permute-start(bf16[16,8,24,128]{3,2,1,0:T(8,128)(2,1)} %collective-permute-done.10), channel_id=1, source_target_pairs={{0,8},{8,0},{16,24},{24,16},{1,9},{9,1},{17,25},{25,17},{2,10},{10... | collective-permute-start | bytes 2359304 | tf_op jit(solution)/shard_map/ppermute | solution.py:246
  57.1 8.8 %collective-permute-start.12 = (bf16[8,16,8,128]{3,2,1,0:T(8,128)(2,1)S(1)}, bf16[8,16,8,128]{3,2,1,0:T(8,128)(2,1)S(1)}, u32[]{:S(2)}, u32[]{:S(2)}) collective-permute-start(bf16[8,16,8,128]{3,2,1,0:T(8,128)(2,1)S(1)} %get-tuple-element.35), channel_id=1, source_target_pairs={{0,1},{1,0},{2,3},{3,2},{4,5},{5,4},{6,7},{7,6},{8,9},{9,8},{10,11... | collective-permute-start | bytes 786440 | tf_op jit(solution)/shard_map/ppermute | solution.py:245
  63.9 5.5 %collective-permute-start.13 = (bf16[4,16,8,128]{3,2,1,0:T(8,128)(2,1)S(1)}, bf16[4,16,8,128]{3,2,1,0:T(8,128)(2,1)S(1)}, u32[]{:S(2)}, u32[]{:S(2)}) collective-permute-start(bf16[4,16,8,128]{3,2,1,0:T(8,128)(2,1)S(1)} %get-tuple-element.36), channel_id=1, source_target_pairs={{0,1},{1,0},{2,3},{3,2},{4,5},{5,4},{6,7},{7,6},{8,9},{9,8},{10,11... | collective-permute-start | bytes 393224 | tf_op jit(solution)/shard_map/ppermute | solution.py:245
  75.2 3.7 %collective-permute-start.16 = (f32[96,24]{0,1:T(8,128)S(1)}, f32[96,24]{0,1:T(8,128)S(1)}, u32[]{:S(2)}, u32[]{:S(2)}) collective-permute-start(f32[96,24]{0,1:T(8,128)S(1)} %pad_maximum_fusion.7), channel_id=1, source_target_pairs={{0,1},{1,0},{2,3},{3,2},{4,5},{5,4},{6,7},{7,6},{8,9},{9,8},{10,11... | collective-permute-start | bytes 27656 | tf_op jit(solution)/shard_map/ppermute | solution.py:245
  78.9 3.7 %collective-permute-start.17 = (f32[96,24]{0,1:T(8,128)S(1)}, f32[96,24]{0,1:T(8,128)S(1)}, u32[]{:S(2)}, u32[]{:S(2)}) collective-permute-start(f32[96,24]{0,1:T(8,128)S(1)} %add.62), channel_id=1, source_target_pairs={{0,2},{1,3},{2,0},{3,1},{4,6},{5,7},{6,4},{7,5},{8,10},{9,11},{10,... | collective-permute-start | bytes 27656 | tf_op jit(solution)/shard_map/ppermute | solution.py:245
  82.6 4.6 %collective-permute-start.18 = (f32[96,24]{0,1:T(8,128)S(1)}, f32[96,24]{0,1:T(8,128)S(1)}, u32[]{:S(2)}, u32[]{:S(2)}) collective-permute-start(f32[96,24]{0,1:T(8,128)S(1)} %add.63), channel_id=1, source_target_pairs={{0,4},{1,5},{2,6},{3,7},{4,0},{5,1},{6,2},{7,3},{8,12},{9,13},{10,... | collective-permute-start | bytes 27656 | tf_op jit(solution)/shard_map/ppermute | solution.py:245
  (2 other events, 2.5 us)

commit v12 on v10

--- a/solution.py
+++ b/solution.py
@@ -254,9 +254,9 @@
     theirs = lax.dynamic_slice_in_dim(probe_field, half * (1 - par), half, axis=0)
     partner = hop(theirs, swap)
 
-    pairs = jnp.pad(snap_times, (0, steps % 2))
-    evens, odds = pairs[0::2], pairs[1::2]
-    order = jnp.concatenate([jnp.where(core == 0, evens, odds), jnp.where(core == 0, odds, evens)])
+    slot = jnp.arange(2 * near_half)
+    turn = 2 * (slot % near_half) + jnp.where(slot < near_half, core, 1 - core)
+    order = jnp.sum(jnp.where(turn[:, None] == jnp.arange(steps), snap_times, 0), axis=1)
     ordered = jnp.take(after(snapshots, theirs), order, axis=0, mode="clip")
     joined, sent = ordered[:near_half], ordered[near_half:]
     gots = []
@@ -274,7 +274,7 @@
 
     side_a = hop(after(mine, gots[0]), perm_a)
     side_b = hop(cut(after(mine, gots[-1]), near * (1 - par)), perm_b)
-    extra_x = hop(after(extra, partner), swap)
+    extra_x = hop(extra, swap)
     far_own, far_x = cut(trim(extra), near * (1 - par)), cut(trim(extra_x), near * par)
     turned = jnp.transpose(after(basis_panels, extra), (1, 2, 0, 3))
     crossed = lax.ppermute(turned, "probe", [(i, i ^ 2) for i in range(members)])

time: 89.4 us -> 86.9 us (0.972)
  matrix products: 4.61 us -> 3.43 us
  local copies, waits for them, and re-layouts: 5.24 us -> 4.1 us
    slice x2 -> x0, local copies, waits for them, and re-layouts: 1.52 us -> none  [local(): evens, odds = (pairs[0::2], pairs[1::2])]
    ppermute x11, waiting for transfers between devices: 24.4 us -> 25.8 us  [local(): hop = lambda x, pairs: lax.ppermute(x, 'store', pairs)]
    dot_general x4, matrix products: 4.61 us -> 3.43 us  [local(): lax.dot_general(x, low, (((0, 1, 3), (1, 2, 3)), ((), ())), preferred_ele...]
  transfers between devices with their start and end apart: 19 -> 19, of which waited for: 10 -> 10; matrix products, arithmetic and copies ran while one was open for 8% -> 7% of each run, Pallas kernels for 22% -> 23%
where the time goes in v12:
time: 86.9 us; the launch traced here: 86.6 us
  waiting for transfers between devices  28.1 us (32%)
  starting transfers between devices  26.3 us (30%)
  Pallas kernels  19.7 us (23%)
  local copies, waits for them, and re-layouts  4.1 us (5%)
  other arithmetic  3.89 us (4%)
  matrix products  3.43 us (4%)
  between operations  1.09 us (1%)
    ppermute x11, waiting for transfers between devices, local(): hop = lambda x, pairs: lax.ppermute(x, 'store', pairs)  25.8 us
    ppermute x11, starting transfers between devices, local(): hop = lambda x, pairs: lax.ppermute(x, 'store', pairs)  22.3 us
    pallas_call x2, Pallas kernels, propagate(): pl.pallas_call(functools.partial(march, steps, rows, halo, begin), grid_s...  19.7 us
    dot_general x4, matrix products, local(): lax.dot_general(x, low, (((0, 1, 3), (1, 2, 3)), ((), ())), preferred_ele...  3.43 us
    ppermute x2, starting transfers between devices, local(): got = lax.ppermute(sent, 'probe', [(i, i ^ span) for i in range(members)])  2.1 us
  transfers between devices with their start and end apart: 19, of which 10 were waited for; matrix products, arithmetic and copies ran while one was open for 7% of the time, Pallas kernels for 23%

profile of v12, /device:TPU:0, one launch (start us, length us, event | category | flops | bytes accessed | tf_op | source)
XLA Modules:
  0.0 86.6 jit_solution(3674516359555780254)
XLA Ops:
  0.7 1.3 %constant_dynamic-slice_fusion.2 = (bf16[12,16,8,128]{3,2,1,0:T(8,128)(2,1)S(1)}, bf16[12,16,8,128]{3,2,1,0:T(8,128)(2,1)S(1)}) fusion(bf16[24,16,8,128]{3,2,1,0:T(8,128)(2,1)} %param.6, s32[]{:T(128)S(6)} %select_n.171, s32[]{:T(128)S(6)} %select_n.170), kind=kLoop, calls=%fused_computation.53 | loop fusion | bytes 1572872 | tf_op jit(solution)/shard_map/dynamic_slice | solution.py:254
  3.4 2.6 %collective-permute-start = (bf16[12,16,8,128]{3,2,1,0:T(8,128)(2,1)S(1)}, bf16[12,16,8,128]{3,2,1,0:T(8,128)(2,1)S(1)}, u32[]{:S(2)}, u32[]{:S(2)}) collective-permute-start(bf16[12,16,8,128]{3,2,1,0:T(8,128)(2,1)S(1)} %get-tuple-element.30), channel_id=1, source_target_pairs={{0,1},{1,0},{2,3},{3,2},{4,5},{5,4},{6,7},{7,6},{8,9},{9,8},{10,11... | collective-permute-start | bytes 1179656 | tf_op jit(solution)/shard_map/ppermute | solution.py:243
  6.1 1.6 %collective-permute-start.3 = (bf16[4,16,4,128]{3,2,1,0:T(4,128)(2,1)S(1)}, bf16[4,16,4,128]{3,2,1,0:T(4,128)(2,1)S(1)}, u32[]{:S(2)}, u32[]{:S(2)}) collective-permute-start(bf16[4,16,4,128]{3,2,1,0:T(4,128)(2,1)S(1)} %pad_maximum_fusion.6), channel_id=1, source_target_pairs={{0,16},{8,24},{16,0},{24,8},{1,17},{9,25},{17,1},{25,9},{2,18},{10... | collective-permute-start | bytes 196616 | tf_op jit(solution)/shard_map/ppermute | solution.py:265
  7.8 1.3 %collective-permute-start.2 = (bf16[12,16,8,128]{3,2,1,0:T(8,128)(2,1)S(1)}, bf16[12,16,8,128]{3,2,1,0:T(8,128)(2,1)S(1)}, u32[]{:S(2)}, u32[]{:S(2)}) collective-permute-start(bf16[12,16,8,128]{3,2,1,0:T(8,128)(2,1)S(1)} %get-tuple-element.16.refs_0_), channel_id=1, source_target_pairs={{2,0},{4,2},{6,4},{1,3},{3,5},{5,7},{10,8},{12,10},{14,12},{9,11},... | collective-permute-start | bytes 1179656 | tf_op jit(solution)/shard_map/ppermute | solution.py:243
  9.1 1.4 %collective-permute-done.3 = bf16[4,16,4,128]{3,2,1,0:T(4,128)(2,1)S(1)} collective-permute-done((bf16[4,16,4,128]{3,2,1,0:T(4,128)(2,1)S(1)}, bf16[4,16,4,128]{3,2,1,0:T(4,128)(2,1)S(1)}, u32[]{:S(2)}, u32[]{:S(2)}) %collective-permute-start.3) | collective-permute-done | bytes 65568 | tf_op jit(solution)/shard_map/ppermute | solution.py:265
  10.7 2.0 %collective-permute-start.5 = (bf16[5,16,8,128]{3,2,1,0:T(8,128)(2,1)S(1)}, bf16[5,16,8,128]{3,2,1,0:T(8,128)(2,1)S(1)}, u32[]{:S(2)}, u32[]{:S(2)}) collective-permute-start(bf16[5,16,8,128]{3,2,1,0:T(8,128)(2,1)S(1)} %pad_maximum_fusion.5.refs_6_), channel_id=1, source_target_pairs={{0,1},{1,0},{2,3},{3,2},{4,5},{5,4},{6,7},{7,6},{8,9},{9,8},{10,11... | collective-permute-start | bytes 491528 | tf_op jit(solution)/shard_map/ppermute | solution.py:243
  12.7 3.5 %collective-permute-start.4 = (bf16[12,12,8,128]{3,2,1,0:T(8,128)(2,1)S(1)}, bf16[12,12,8,128]{3,2,1,0:T(8,128)(2,1)S(1)}, u32[]{:S(2)}, u32[]{:S(2)}) collective-permute-start(bf16[12,12,8,128]{3,2,1,0:T(8,128)(2,1)S(1)} %constant_dynamic-slice_fusion.1), channel_id=1, source_target_pairs={{0,2},{2,4},{4,6},{3,1},{5,3},{7,5},{8,10},{10,12},{12,14},{11,9},... | collective-permute-start | bytes 884744 | tf_op jit(solution)/shard_map/ppermute | solution.py:243
  17.6 1.7 %collective-permute-done.5.refs_7_ = bf16[5,16,8,128]{3,2,1,0:T(8,128)(2,1)S(1)} collective-permute-done((bf16[5,16,8,128]{3,2,1,0:T(8,128)(2,1)S(1)}, bf16[5,16,8,128]{3,2,1,0:T(8,128)(2,1)S(1)}, u32[]{:S(2)}, u32[]{:S(2)}) %collective-permute-start.5) | collective-permute-done | bytes 163872 | tf_op jit(solution)/shard_map/ppermute | solution.py:243
  19.4 2.6 %collective-permute-done.4.refs_3_ = bf16[12,12,8,128]{3,2,1,0:T(8,128)(2,1)S(1)} collective-permute-done((bf16[12,12,8,128]{3,2,1,0:T(8,128)(2,1)S(1)}, bf16[12,12,8,128]{3,2,1,0:T(8,128)(2,1)S(1)}, u32[]{:S(2)}, u32[]{:S(2)}) %collective-permute-start.4) | collective-permute-done | bytes 294944 | tf_op jit(solution)/shard_map/ppermute | solution.py:243
  21.9 4.4 %collective-permute-start.6 = (bf16[308,8,128]{2,1,0:T(8,128)(2,1)S(1)}, bf16[308,8,128]{2,1,0:T(8,128)(2,1)S(1)}, u32[]{:S(2)}, u32[]{:S(2)}) collective-permute-start(bf16[308,8,128]{2,1,0:T(8,128)(2,1)S(1)} %pad_maximum_fusion.2), channel_id=1, source_target_pairs={{0,2},{2,4},{4,6},{3,1},{5,3},{7,5},{8,10},{10,12},{12,14},{11,9},... | collective-permute-start | bytes 1892360 | tf_op jit(solution)/shard_map/ppermute | solution.py:243
  26.5 1.5 %collective-permute-start.7 = (bf16[260,8,128]{2,1,0:T(8,128)(2,1)S(1)}, bf16[260,8,128]{2,1,0:T(8,128)(2,1)S(1)}, u32[]{:S(2)}, u32[]{:S(2)}) collective-permute-start(bf16[260,8,128]{2,1,0:T(8,128)(2,1)S(1)} %pad_maximum_fusion.3), channel_id=1, source_target_pairs={{2,0},{4,2},{6,4},{1,3},{3,5},{5,7},{10,8},{12,10},{14,12},{9,11},... | collective-permute-start | bytes 1597448 | tf_op jit(solution)/shard_map/ppermute | solution.py:243
  28.0 12.5 %collective-permute-done.7.refs_5_ = bf16[260,8,128]{2,1,0:T(8,128)(2,1)S(1)} collective-permute-done((bf16[260,8,128]{2,1,0:T(8,128)(2,1)S(1)}, bf16[260,8,128]{2,1,0:T(8,128)(2,1)S(1)}, u32[]{:S(2)}, u32[]{:S(2)}) %collective-permute-start.7) | collective-permute-done | bytes 532512 | tf_op jit(solution)/shard_map/ppermute | solution.py:243
  43.9 12.3 %march.2 = (f32[8,16,8,128]{3,2,1,0:T(8,128)S(1)}, bf16[8,16,8,128]{3,2,1,0:T(8,128)(2,1)S(1)}) custom-call(s32[24,2]{1,0:T(8,128)S(1)} %copy.16.bounds_ref, bf16[12,16,8,128]{3,2,1,0:T(8,128)(2,1)S(1)} %get-tuple-element.16.refs_0_, bf16[12,16,8,128]{3,2,1,0:T(8,128)(2,1)S(1)} %collective-permute-done.refs_1_, ...), custom_call_target="tpu_custom_call" | custom-call | tf_op jit(solution)/shard_map/march/pallas_call | solution.py:215
  56.3 7.4 %march.3 = (f32[4,16,8,128]{3,2,1,0:T(8,128)S(1)}, bf16[4,16,8,128]{3,2,1,0:T(8,128)(2,1)S(1)}) custom-call(s32[24,2]{1,0:T(8,128)S(1)} %copy.16.bounds_ref, bf16[12,16,8,128]{3,2,1,0:T(8,128)(2,1)S(1)} %get-tuple-element.16.refs_0_, bf16[12,16,8,128]{3,2,1,0:T(8,128)(2,1)S(1)} %collective-permute-done.refs_1_, ...), custom_call_target="tpu_custom_call" | custom-call | flops 2883584000 | bytes 1441792 | tf_op jit(solution)/shard_map/march/pallas_call | solution.py:215
  63.7 2.1 %collective-permute-start.13 = (bf16[4,16,8,128]{3,2,1,0:T(8,128)(2,1)S(1)}, bf16[4,16,8,128]{3,2,1,0:T(8,128)(2,1)S(1)}, u32[]{:S(2)}, u32[]{:S(2)}) collective-permute-start(bf16[4,16,8,128]{3,2,1,0:T(8,128)(2,1)S(1)} %get-tuple-element.24), channel_id=1, source_target_pairs={{0,1},{1,0},{2,3},{3,2},{4,5},{5,4},{6,7},{7,6},{8,9},{9,8},{10,11... | collective-permute-start | bytes 393224 | tf_op jit(solution)/shard_map/ppermute | solution.py:243
  65.9 3.4 %collective-permute-done.13 = bf16[4,16,8,128]{3,2,1,0:T(8,128)(2,1)S(1)} collective-permute-done((bf16[4,16,8,128]{3,2,1,0:T(8,128)(2,1)S(1)}, bf16[4,16,8,128]{3,2,1,0:T(8,128)(2,1)S(1)}, u32[]{:S(2)}, u32[]{:S(2)}) %collective-permute-start.13) | collective-permute-done | bytes 131104 | tf_op jit(solution)/shard_map/ppermute | solution.py:243
  69.5 1.0 %copy-done.3 = bf16[24,16,8,128]{3,0,2,1:T(8,128)(2,1)S(1)} copy-done((bf16[24,16,8,128]{3,0,2,1:T(8,128)(2,1)S(1)}, bf16[24,16,8,128]{3,0,2,1:T(8,128)(2,1)}, u32[]{:S(2)}) %copy-start.3) | copy-done | bytes 786456
  74.0 1.7 %collective-permute-start.16 = (f32[96,24]{0,1:T(8,128)S(1)}, f32[96,24]{0,1:T(8,128)S(1)}, u32[]{:S(2)}, u32[]{:S(2)}) collective-permute-start(f32[96,24]{0,1:T(8,128)S(1)} %pad_maximum_fusion.7), channel_id=1, source_target_pairs={{0,1},{1,0},{2,3},{3,2},{4,5},{5,4},{6,7},{7,6},{8,9},{9,8},{10,11... | collective-permute-start | bytes 27656 | tf_op jit(solution)/shard_map/ppermute | solution.py:243
  75.7 2.0 %collective-permute-done.16 = f32[96,24]{0,1:T(8,128)S(1)} collective-permute-done((f32[96,24]{0,1:T(8,128)S(1)}, f32[96,24]{0,1:T(8,128)S(1)}, u32[]{:S(2)}, u32[]{:S(2)}) %collective-permute-start.16) | collective-permute-done | bytes 9248 | tf_op jit(solution)/shard_map/ppermute | solution.py:243
  77.7 1.5 %collective-permute-start.17 = (f32[96,24]{0,1:T(8,128)S(1)}, f32[96,24]{0,1:T(8,128)S(1)}, u32[]{:S(2)}, u32[]{:S(2)}) collective-permute-start(f32[96,24]{0,1:T(8,128)S(1)} %add.62), channel_id=1, source_target_pairs={{0,2},{1,3},{2,0},{3,1},{4,6},{5,7},{6,4},{7,5},{8,10},{9,11},{10,... | collective-permute-start | bytes 27656 | tf_op jit(solution)/shard_map/ppermute | solution.py:243
  79.4 2.0 %collective-permute-done.17 = f32[96,24]{0,1:T(8,128)S(1)} collective-permute-done((f32[96,24]{0,1:T(8,128)S(1)}, f32[96,24]{0,1:T(8,128)S(1)}, u32[]{:S(2)}, u32[]{:S(2)}) %collective-permute-start.17) | collective-permute-done | bytes 9248 | tf_op jit(solution)/shard_map/ppermute | solution.py:243
  81.4 1.7 %collective-permute-start.18 = (f32[96,24]{0,1:T(8,128)S(1)}, f32[96,24]{0,1:T(8,128)S(1)}, u32[]{:S(2)}, u32[]{:S(2)}) collective-permute-start(f32[96,24]{0,1:T(8,128)S(1)} %add.63), channel_id=1, source_target_pairs={{0,4},{1,5},{2,6},{3,7},{4,0},{5,1},{6,2},{7,3},{8,12},{9,13},{10,... | collective-permute-start | bytes 27656 | tf_op jit(solution)/shard_map/ppermute | solution.py:243
  83.1 1.3 %pad_maximum_fusion = f32[24,16,8,128]{3,2,1,0:T(8,128)} fusion(f32[12,16,8,128]{3,2,1,0:T(8,128)S(1)} %get-tuple-element.29, f32[12,16,8,128]{3,2,1,0:T(8,128)S(1)} %get-tuple-element.28), kind=kLoop, calls=%fused_computation.1 | loop fusion | flops 393216 | bytes 3145728 | tf_op jit(solution)/shard_map/concatenate | solution.py:296
  84.4 1.6 %collective-permute-done.18 = f32[96,24]{0,1:T(8,128)S(1)} collective-permute-done((f32[96,24]{0,1:T(8,128)S(1)}, f32[96,24]{0,1:T(8,128)S(1)}, u32[]{:S(2)}, u32[]{:S(2)}) %collective-permute-start.18) | collective-permute-done | bytes 9248 | tf_op jit(solution)/shard_map/ppermute | solution.py:243
  (74 shorter events, 11.3 us)
Async XLA Ops:
  0.7 7.1 %copy-start.4 = (f32[16,8,128]{2,1,0:T(8,128)S(1)}, f32[16,8,128]{2,1,0:T(8,128)}, u32[]{:S(2)}) copy-start(f32[16,8,128]{2,1,0:T(8,128)} %param.8) | copy-start | bytes 196612
  0.7 15.6 %copy-start.1 = (bf16[24,16,8,128]{3,2,1,0:T(8,128)(2,1)S(1)}, bf16[24,16,8,128]{3,2,1,0:T(8,128)(2,1)}, u32[]{:S(2)}) copy-start(bf16[24,16,8,128]{3,2,1,0:T(8,128)(2,1)} %param.11) | copy-start | bytes 2359300
  2.9 3.1 %collective-permute-start.1 = (bf16[4,16,2,128]{3,2,1,0:T(2,128)(2,1)S(1)}, bf16[4,16,2,128]{3,2,1,0:T(2,128)(2,1)S(1)}, u32[]{:S(2)}, u32[]{:S(2)}) collective-permute-start(bf16[4,16,2,128]{3,2,1,0:T(2,128)(2,1)S(1)} %slice.30), channel_id=1, source_target_pairs={{0,8},{8,0},{16,24},{24,16},{1,9},{9,1},{17,25},{25,17},{2,10},{10... | collective-permute-start | bytes 98312 | tf_op jit(solution)/shard_map/ppermute | solution.py:265
  3.4 15.8 %collective-permute-start = (bf16[12,16,8,128]{3,2,1,0:T(8,128)(2,1)S(1)}, bf16[12,16,8,128]{3,2,1,0:T(8,128)(2,1)S(1)}, u32[]{:S(2)}, u32[]{:S(2)}) collective-permute-start(bf16[12,16,8,128]{3,2,1,0:T(8,128)(2,1)S(1)} %get-tuple-element.30), channel_id=1, source_target_pairs={{0,1},{1,0},{2,3},{3,2},{4,5},{5,4},{6,7},{7,6},{8,9},{9,8},{10,11... | collective-permute-start | bytes 1179656 | tf_op jit(solution)/shard_map/ppermute | solution.py:243
  6.1 4.3 %collective-permute-start.3 = (bf16[4,16,4,128]{3,2,1,0:T(4,128)(2,1)S(1)}, bf16[4,16,4,128]{3,2,1,0:T(4,128)(2,1)S(1)}, u32[]{:S(2)}, u32[]{:S(2)}) collective-permute-start(bf16[4,16,4,128]{3,2,1,0:T(4,128)(2,1)S(1)} %pad_maximum_fusion.6), channel_id=1, source_target_pairs={{0,16},{8,24},{16,0},{24,8},{1,17},{9,25},{17,1},{25,9},{2,18},{10... | collective-permute-start | bytes 196616 | tf_op jit(solution)/shard_map/ppermute | solution.py:265
  7.8 18.7 %collective-permute-start.2 = (bf16[12,16,8,128]{3,2,1,0:T(8,128)(2,1)S(1)}, bf16[12,16,8,128]{3,2,1,0:T(8,128)(2,1)S(1)}, u32[]{:S(2)}, u32[]{:S(2)}) collective-permute-start(bf16[12,16,8,128]{3,2,1,0:T(8,128)(2,1)S(1)} %get-tuple-element.16.refs_0_), channel_id=1, source_target_pairs={{2,0},{4,2},{6,4},{1,3},{3,5},{5,7},{10,8},{12,10},{14,12},{9,11},... | collective-permute-start | bytes 1179656 | tf_op jit(solution)/shard_map/ppermute | solution.py:243
  10.7 8.6 %collective-permute-start.5 = (bf16[5,16,8,128]{3,2,1,0:T(8,128)(2,1)S(1)}, bf16[5,16,8,128]{3,2,1,0:T(8,128)(2,1)S(1)}, u32[]{:S(2)}, u32[]{:S(2)}) collective-permute-start(bf16[5,16,8,128]{3,2,1,0:T(8,128)(2,1)S(1)} %pad_maximum_fusion.5.refs_6_), channel_id=1, source_target_pairs={{0,1},{1,0},{2,3},{3,2},{4,5},{5,4},{6,7},{7,6},{8,9},{9,8},{10,11... | collective-permute-start | bytes 491528 | tf_op jit(solution)/shard_map/ppermute | solution.py:243
  12.7 9.2 %collective-permute-start.4 = (bf16[12,12,8,128]{3,2,1,0:T(8,128)(2,1)S(1)}, bf16[12,12,8,128]{3,2,1,0:T(8,128)(2,1)S(1)}, u32[]{:S(2)}, u32[]{:S(2)}) collective-permute-start(bf16[12,12,8,128]{3,2,1,0:T(8,128)(2,1)S(1)} %constant_dynamic-slice_fusion.1), channel_id=1, source_target_pairs={{0,2},{2,4},{4,6},{3,1},{5,3},{7,5},{8,10},{10,12},{12,14},{11,9},... | collective-permute-start | bytes 884744 | tf_op jit(solution)/shard_map/ppermute | solution.py:243
  16.8 24.6 %copy-start.2 = (bf16[24,16,8,128]{3,0,2,1:T(8,128)(2,1)}, bf16[24,16,8,128]{3,0,2,1:T(8,128)(2,1)S(1)}, u32[]{:S(2)}) copy-start(bf16[24,16,8,128]{3,0,2,1:T(8,128)(2,1)S(1)} %copy.37) | copy-start | bytes 2359300
  16.8 24.6 %collective-permute-start.10 = (bf16[16,8,24,128]{3,2,1,0:T(8,128)(2,1)S(1)}, bf16[16,8,24,128]{3,2,1,0:T(8,128)(2,1)S(1)}, u32[]{:S(2)}, u32[]{:S(2)}) collective-permute-start(bf16[16,8,24,128]{3,2,1,0:T(8,128)(2,1)S(1)} %bitcast.35), channel_id=1, source_target_pairs={{0,16},{8,24},{16,0},{24,8},{1,17},{9,25},{17,1},{25,9},{2,18},{10... | collective-permute-start | bytes 2359304 | tf_op jit(solution)/shard_map/ppermute | solution.py:280
  21.9 18.6 %collective-permute-start.6 = (bf16[308,8,128]{2,1,0:T(8,128)(2,1)S(1)}, bf16[308,8,128]{2,1,0:T(8,128)(2,1)S(1)}, u32[]{:S(2)}, u32[]{:S(2)}) collective-permute-start(bf16[308,8,128]{2,1,0:T(8,128)(2,1)S(1)} %pad_maximum_fusion.2), channel_id=1, source_target_pairs={{0,2},{2,4},{4,6},{3,1},{5,3},{7,5},{8,10},{10,12},{12,14},{11,9},... | collective-permute-start | bytes 1892360 | tf_op jit(solution)/shard_map/ppermute | solution.py:243
  26.4 15.9 %copy-start.5 = (s32[24,2]{0,1:T(2,128)S(1)}, s32[24,2]{0,1:T(2,128)}, u32[]{:S(2)}) copy-start(s32[24,2]{0,1:T(2,128)} %param.7) | copy-start | bytes 580
  26.5 14.0 %collective-permute-start.7 = (bf16[260,8,128]{2,1,0:T(8,128)(2,1)S(1)}, bf16[260,8,128]{2,1,0:T(8,128)(2,1)S(1)}, u32[]{:S(2)}, u32[]{:S(2)}) collective-permute-start(bf16[260,8,128]{2,1,0:T(8,128)(2,1)S(1)} %pad_maximum_fusion.3), channel_id=1, source_target_pairs={{2,0},{4,2},{6,4},{1,3},{3,5},{5,7},{10,8},{12,10},{14,12},{9,11},... | collective-permute-start | bytes 1597448 | tf_op jit(solution)/shard_map/ppermute | solution.py:243
  41.4 2.4 %collective-permute-start.11 = (bf16[232,8,128]{2,1,0:T(8,128)(2,1)}, bf16[232,8,128]{2,1,0:T(8,128)(2,1)S(1)}, u32[]{:S(2)}, u32[]{:S(2)}) collective-permute-start(bf16[232,8,128]{2,1,0:T(8,128)(2,1)} %pad_maximum_fusion.4), channel_id=1, source_target_pairs={{0,8},{8,0},{16,24},{24,16},{1,9},{9,1},{17,25},{25,17},{2,10},{10... | collective-permute-start | bytes 1425416 | tf_op jit(solution)/shard_map/ppermute | solution.py:244
  41.4 2.2 %collective-permute-start.8 = (bf16[5,16,8,128]{3,2,1,0:T(8,128)(2,1)S(1)}, bf16[5,16,8,128]{3,2,1,0:T(8,128)(2,1)}, u32[]{:S(2)}, u32[]{:S(2)}) collective-permute-start(bf16[5,16,8,128]{3,2,1,0:T(8,128)(2,1)S(1)} %pad_maximum_fusion.5.refs_6_), channel_id=1, source_target_pairs={{0,8},{8,0},{16,24},{24,16},{1,9},{9,1},{17,25},{25,17},{2,10},{10... | collective-permute-start | bytes 491528 | tf_op jit(solution)/shard_map/ppermute | solution.py:244
  42.3 1.6 %collective-permute-start.9 = (bf16[5,16,8,128]{3,2,1,0:T(8,128)(2,1)S(1)}, bf16[5,16,8,128]{3,2,1,0:T(8,128)(2,1)}, u32[]{:S(2)}, u32[]{:S(2)}) collective-permute-start(bf16[5,16,8,128]{3,2,1,0:T(8,128)(2,1)S(1)} %collective-permute-done.5.refs_7_), channel_id=1, source_target_pairs={{0,8},{8,0},{16,24},{24,16},{1,9},{9,1},{17,25},{25,17},{2,10},{10... | collective-permute-start | bytes 491528 | tf_op jit(solution)/shard_map/ppermute | solution.py:244
  42.4 29.8 %collective-permute-start.15 = (bf16[16,8,24,128]{3,2,1,0:T(8,128)(2,1)}, bf16[16,8,24,128]{3,2,1,0:T(8,128)(2,1)S(1)}, u32[]{:S(2)}, u32[]{:S(2)}) collective-permute-start(bf16[16,8,24,128]{3,2,1,0:T(8,128)(2,1)} %bitcast.36), channel_id=1, source_target_pairs={{0,8},{8,0},{16,24},{24,16},{1,9},{9,1},{17,25},{25,17},{2,10},{10... | collective-permute-start | bytes 2359304 | tf_op jit(solution)/shard_map/ppermute | solution.py:244
  42.9 30.1 %collective-permute-start.14 = (bf16[16,8,24,128]{3,2,1,0:T(8,128)(2,1)}, bf16[16,8,24,128]{3,2,1,0:T(8,128)(2,1)S(1)}, u32[]{:S(2)}, u32[]{:S(2)}) collective-permute-start(bf16[16,8,24,128]{3,2,1,0:T(8,128)(2,1)} %copy-done.6), channel_id=1, source_target_pairs={{0,8},{8,0},{16,24},{24,16},{1,9},{9,1},{17,25},{25,17},{2,10},{10... | collective-permute-start | bytes 2359304 | tf_op jit(solution)/shard_map/ppermute | solution.py:244
  56.2 9.7 %collective-permute-start.12 = (bf16[8,16,8,128]{3,2,1,0:T(8,128)(2,1)S(1)}, bf16[8,16,8,128]{3,2,1,0:T(8,128)(2,1)S(1)}, u32[]{:S(2)}, u32[]{:S(2)}) collective-permute-start(bf16[8,16,8,128]{3,2,1,0:T(8,128)(2,1)S(1)} %get-tuple-element.23), channel_id=1, source_target_pairs={{0,1},{1,0},{2,3},{3,2},{4,5},{5,4},{6,7},{7,6},{8,9},{9,8},{10,11... | collective-permute-start | bytes 786440 | tf_op jit(solution)/shard_map/ppermute | solution.py:243
  63.7 5.6 %collective-permute-start.13 = (bf16[4,16,8,128]{3,2,1,0:T(8,128)(2,1)S(1)}, bf16[4,16,8,128]{3,2,1,0:T(8,128)(2,1)S(1)}, u32[]{:S(2)}, u32[]{:S(2)}) collective-permute-start(bf16[4,16,8,128]{3,2,1,0:T(8,128)(2,1)S(1)} %get-tuple-element.24), channel_id=1, source_target_pairs={{0,1},{1,0},{2,3},{3,2},{4,5},{5,4},{6,7},{7,6},{8,9},{9,8},{10,11... | collective-permute-start | bytes 393224 | tf_op jit(solution)/shard_map/ppermute | solution.py:243
  69.4 1.9 %copy-start.7 = (bf16[16,8,24,128]{3,2,1,0:T(8,128)(2,1)S(1)}, bf16[16,8,24,128]{3,2,1,0:T(8,128)(2,1)}, u32[]{:S(2)}) copy-start(bf16[16,8,24,128]{3,2,1,0:T(8,128)(2,1)} %copy-done.6) | copy-start | bytes 2359300
  74.0 3.7 %collective-permute-start.16 = (f32[96,24]{0,1:T(8,128)S(1)}, f32[96,24]{0,1:T(8,128)S(1)}, u32[]{:S(2)}, u32[]{:S(2)}) collective-permute-start(f32[96,24]{0,1:T(8,128)S(1)} %pad_maximum_fusion.7), channel_id=1, source_target_pairs={{0,1},{1,0},{2,3},{3,2},{4,5},{5,4},{6,7},{7,6},{8,9},{9,8},{10,11... | collective-permute-start | bytes 27656 | tf_op jit(solution)/shard_map/ppermute | solution.py:243
  77.7 3.7 %collective-permute-start.17 = (f32[96,24]{0,1:T(8,128)S(1)}, f32[96,24]{0,1:T(8,128)S(1)}, u32[]{:S(2)}, u32[]{:S(2)}) collective-permute-start(f32[96,24]{0,1:T(8,128)S(1)} %add.62), channel_id=1, source_target_pairs={{0,2},{1,3},{2,0},{3,1},{4,6},{5,7},{6,4},{7,5},{8,10},{9,11},{10,... | collective-permute-start | bytes 27656 | tf_op jit(solution)/shard_map/ppermute | solution.py:243
  81.4 4.6 %collective-permute-start.18 = (f32[96,24]{0,1:T(8,128)S(1)}, f32[96,24]{0,1:T(8,128)S(1)}, u32[]{:S(2)}, u32[]{:S(2)}) collective-permute-start(f32[96,24]{0,1:T(8,128)S(1)} %add.63), channel_id=1, source_target_pairs={{0,4},{1,5},{2,6},{3,7},{4,0},{5,1},{6,2},{7,3},{8,12},{9,13},{10,... | collective-permute-start | bytes 27656 | tf_op jit(solution)/shard_map/ppermute | solution.py:243
  (4 other events, 4.9 us)

commit v13 on v12

--- a/solution.py
+++ b/solution.py
@@ -10,7 +10,7 @@
 
 taps = (-205.0 / 72.0, 8.0 / 5.0, -1.0 / 5.0, 8.0 / 315.0, -1.0 / 560.0)
 SPAN = 24
-PACK = 2
+PACK = 4
 AHEAD = 1
 
 

time: 86.9 us -> 86.6 us (level)
  no operation moved by 1% of the time
where the time goes in v13:
time: 86.6 us; the launch traced here: 86.3 us
  waiting for transfers between devices  28.2 us (33%)
  starting transfers between devices  26.1 us (30%)
  Pallas kernels  19.5 us (23%)
  local copies, waits for them, and re-layouts  4.1 us (5%)
  other arithmetic  3.89 us (4%)
  matrix products  3.43 us (4%)
  between operations  1.09 us (1%)
    ppermute x11, waiting for transfers between devices, local(): hop = lambda x, pairs: lax.ppermute(x, 'store', pairs)  25.9 us
    ppermute x11, starting transfers between devices, local(): hop = lambda x, pairs: lax.ppermute(x, 'store', pairs)  22.2 us
    pallas_call x2, Pallas kernels, propagate(): pl.pallas_call(functools.partial(march, steps, rows, halo, begin), grid_s...  19.5 us
    dot_general x4, matrix products, local(): lax.dot_general(x, low, (((0, 1, 3), (1, 2, 3)), ((), ())), preferred_ele...  3.43 us
    ppermute x2, starting transfers between devices, local(): got = lax.ppermute(sent, 'probe', [(i, i ^ span) for i in range(members)])  2.1 us
  transfers between devices with their start and end apart: 19, of which 10 were waited for; matrix products, arithmetic and copies ran while one was open for 7% of the time, Pallas kernels for 23%

profile of v13, /device:TPU:0, one launch (start us, length us, event | category | flops | bytes accessed | tf_op | source)
XLA Modules:
  0.0 86.3 jit_solution(13564296428681525484)
XLA Ops:
  0.7 1.3 %constant_dynamic-slice_fusion.2 = (bf16[12,16,8,128]{3,2,1,0:T(8,128)(2,1)S(1)}, bf16[12,16,8,128]{3,2,1,0:T(8,128)(2,1)S(1)}) fusion(bf16[24,16,8,128]{3,2,1,0:T(8,128)(2,1)} %param.6, s32[]{:T(128)S(6)} %select_n.171, s32[]{:T(128)S(6)} %select_n.170), kind=kLoop, calls=%fused_computation.53 | loop fusion | bytes 1572872 | tf_op jit(solution)/shard_map/dynamic_slice | solution.py:254
  3.4 2.6 %collective-permute-start = (bf16[12,16,8,128]{3,2,1,0:T(8,128)(2,1)S(1)}, bf16[12,16,8,128]{3,2,1,0:T(8,128)(2,1)S(1)}, u32[]{:S(2)}, u32[]{:S(2)}) collective-permute-start(bf16[12,16,8,128]{3,2,1,0:T(8,128)(2,1)S(1)} %get-tuple-element.30), channel_id=1, source_target_pairs={{0,1},{1,0},{2,3},{3,2},{4,5},{5,4},{6,7},{7,6},{8,9},{9,8},{10,11... | collective-permute-start | bytes 1179656 | tf_op jit(solution)/shard_map/ppermute | solution.py:243
  6.1 1.6 %collective-permute-start.3 = (bf16[4,16,4,128]{3,2,1,0:T(4,128)(2,1)S(1)}, bf16[4,16,4,128]{3,2,1,0:T(4,128)(2,1)S(1)}, u32[]{:S(2)}, u32[]{:S(2)}) collective-permute-start(bf16[4,16,4,128]{3,2,1,0:T(4,128)(2,1)S(1)} %pad_maximum_fusion.6), channel_id=1, source_target_pairs={{0,16},{8,24},{16,0},{24,8},{1,17},{9,25},{17,1},{25,9},{2,18},{10... | collective-permute-start | bytes 196616 | tf_op jit(solution)/shard_map/ppermute | solution.py:265
  7.8 1.3 %collective-permute-start.2 = (bf16[12,16,8,128]{3,2,1,0:T(8,128)(2,1)S(1)}, bf16[12,16,8,128]{3,2,1,0:T(8,128)(2,1)S(1)}, u32[]{:S(2)}, u32[]{:S(2)}) collective-permute-start(bf16[12,16,8,128]{3,2,1,0:T(8,128)(2,1)S(1)} %get-tuple-element.16.refs_0_), channel_id=1, source_target_pairs={{2,0},{4,2},{6,4},{1,3},{3,5},{5,7},{10,8},{12,10},{14,12},{9,11},... | collective-permute-start | bytes 1179656 | tf_op jit(solution)/shard_map/ppermute | solution.py:243
  9.1 1.4 %collective-permute-done.3 = bf16[4,16,4,128]{3,2,1,0:T(4,128)(2,1)S(1)} collective-permute-done((bf16[4,16,4,128]{3,2,1,0:T(4,128)(2,1)S(1)}, bf16[4,16,4,128]{3,2,1,0:T(4,128)(2,1)S(1)}, u32[]{:S(2)}, u32[]{:S(2)}) %collective-permute-start.3) | collective-permute-done | bytes 65568 | tf_op jit(solution)/shard_map/ppermute | solution.py:265
  10.7 2.0 %collective-permute-start.5 = (bf16[5,16,8,128]{3,2,1,0:T(8,128)(2,1)S(1)}, bf16[5,16,8,128]{3,2,1,0:T(8,128)(2,1)S(1)}, u32[]{:S(2)}, u32[]{:S(2)}) collective-permute-start(bf16[5,16,8,128]{3,2,1,0:T(8,128)(2,1)S(1)} %pad_maximum_fusion.5.refs_6_), channel_id=1, source_target_pairs={{0,1},{1,0},{2,3},{3,2},{4,5},{5,4},{6,7},{7,6},{8,9},{9,8},{10,11... | collective-permute-start | bytes 491528 | tf_op jit(solution)/shard_map/ppermute | solution.py:243
  12.7 3.5 %collective-permute-start.4 = (bf16[12,12,8,128]{3,2,1,0:T(8,128)(2,1)S(1)}, bf16[12,12,8,128]{3,2,1,0:T(8,128)(2,1)S(1)}, u32[]{:S(2)}, u32[]{:S(2)}) collective-permute-start(bf16[12,12,8,128]{3,2,1,0:T(8,128)(2,1)S(1)} %constant_dynamic-slice_fusion.1), channel_id=1, source_target_pairs={{0,2},{2,4},{4,6},{3,1},{5,3},{7,5},{8,10},{10,12},{12,14},{11,9},... | collective-permute-start | bytes 884744 | tf_op jit(solution)/shard_map/ppermute | solution.py:243
  17.6 1.7 %collective-permute-done.5.refs_7_ = bf16[5,16,8,128]{3,2,1,0:T(8,128)(2,1)S(1)} collective-permute-done((bf16[5,16,8,128]{3,2,1,0:T(8,128)(2,1)S(1)}, bf16[5,16,8,128]{3,2,1,0:T(8,128)(2,1)S(1)}, u32[]{:S(2)}, u32[]{:S(2)}) %collective-permute-start.5) | collective-permute-done | bytes 163872 | tf_op jit(solution)/shard_map/ppermute | solution.py:243
  19.4 2.6 %collective-permute-done.4.refs_3_ = bf16[12,12,8,128]{3,2,1,0:T(8,128)(2,1)S(1)} collective-permute-done((bf16[12,12,8,128]{3,2,1,0:T(8,128)(2,1)S(1)}, bf16[12,12,8,128]{3,2,1,0:T(8,128)(2,1)S(1)}, u32[]{:S(2)}, u32[]{:S(2)}) %collective-permute-start.4) | collective-permute-done | bytes 294944 | tf_op jit(solution)/shard_map/ppermute | solution.py:243
  21.9 4.4 %collective-permute-start.6 = (bf16[308,8,128]{2,1,0:T(8,128)(2,1)S(1)}, bf16[308,8,128]{2,1,0:T(8,128)(2,1)S(1)}, u32[]{:S(2)}, u32[]{:S(2)}) collective-permute-start(bf16[308,8,128]{2,1,0:T(8,128)(2,1)S(1)} %pad_maximum_fusion.2), channel_id=1, source_target_pairs={{0,2},{2,4},{4,6},{3,1},{5,3},{7,5},{8,10},{10,12},{12,14},{11,9},... | collective-permute-start | bytes 1892360 | tf_op jit(solution)/shard_map/ppermute | solution.py:243
  26.5 1.3 %collective-permute-start.7 = (bf16[260,8,128]{2,1,0:T(8,128)(2,1)S(1)}, bf16[260,8,128]{2,1,0:T(8,128)(2,1)S(1)}, u32[]{:S(2)}, u32[]{:S(2)}) collective-permute-start(bf16[260,8,128]{2,1,0:T(8,128)(2,1)S(1)} %pad_maximum_fusion.3), channel_id=1, source_target_pairs={{2,0},{4,2},{6,4},{1,3},{3,5},{5,7},{10,8},{12,10},{14,12},{9,11},... | collective-permute-start | bytes 1597448 | tf_op jit(solution)/shard_map/ppermute | solution.py:243
  27.8 12.7 %collective-permute-done.7.refs_5_ = bf16[260,8,128]{2,1,0:T(8,128)(2,1)S(1)} collective-permute-done((bf16[260,8,128]{2,1,0:T(8,128)(2,1)S(1)}, bf16[260,8,128]{2,1,0:T(8,128)(2,1)S(1)}, u32[]{:S(2)}, u32[]{:S(2)}) %collective-permute-start.7) | collective-permute-done | bytes 532512 | tf_op jit(solution)/shard_map/ppermute | solution.py:243
  43.9 12.0 %march.2 = (f32[8,16,8,128]{3,2,1,0:T(8,128)S(1)}, bf16[8,16,8,128]{3,2,1,0:T(8,128)(2,1)S(1)}) custom-call(s32[24,2]{1,0:T(8,128)S(1)} %copy.16.bounds_ref, bf16[12,16,8,128]{3,2,1,0:T(8,128)(2,1)S(1)} %get-tuple-element.16.refs_0_, bf16[12,16,8,128]{3,2,1,0:T(8,128)(2,1)S(1)} %collective-permute-done.refs_1_, ...), custom_call_target="tpu_custom_call" | custom-call | tf_op jit(solution)/shard_map/march/pallas_call | solution.py:215
  56.0 7.4 %march.3 = (f32[4,16,8,128]{3,2,1,0:T(8,128)S(1)}, bf16[4,16,8,128]{3,2,1,0:T(8,128)(2,1)S(1)}) custom-call(s32[24,2]{1,0:T(8,128)S(1)} %copy.16.bounds_ref, bf16[12,16,8,128]{3,2,1,0:T(8,128)(2,1)S(1)} %get-tuple-element.16.refs_0_, bf16[12,16,8,128]{3,2,1,0:T(8,128)(2,1)S(1)} %collective-permute-done.refs_1_, ...), custom_call_target="tpu_custom_call" | custom-call | flops 2883584000 | bytes 1441792 | tf_op jit(solution)/shard_map/march/pallas_call | solution.py:215
  63.4 2.1 %collective-permute-start.13 = (bf16[4,16,8,128]{3,2,1,0:T(8,128)(2,1)S(1)}, bf16[4,16,8,128]{3,2,1,0:T(8,128)(2,1)S(1)}, u32[]{:S(2)}, u32[]{:S(2)}) collective-permute-start(bf16[4,16,8,128]{3,2,1,0:T(8,128)(2,1)S(1)} %get-tuple-element.24), channel_id=1, source_target_pairs={{0,1},{1,0},{2,3},{3,2},{4,5},{5,4},{6,7},{7,6},{8,9},{9,8},{10,11... | collective-permute-start | bytes 393224 | tf_op jit(solution)/shard_map/ppermute | solution.py:243
  65.6 3.4 %collective-permute-done.13 = bf16[4,16,8,128]{3,2,1,0:T(8,128)(2,1)S(1)} collective-permute-done((bf16[4,16,8,128]{3,2,1,0:T(8,128)(2,1)S(1)}, bf16[4,16,8,128]{3,2,1,0:T(8,128)(2,1)S(1)}, u32[]{:S(2)}, u32[]{:S(2)}) %collective-permute-start.13) | collective-permute-done | bytes 131104 | tf_op jit(solution)/shard_map/ppermute | solution.py:243
  69.2 1.0 %copy-done.3 = bf16[24,16,8,128]{3,0,2,1:T(8,128)(2,1)S(1)} copy-done((bf16[24,16,8,128]{3,0,2,1:T(8,128)(2,1)S(1)}, bf16[24,16,8,128]{3,0,2,1:T(8,128)(2,1)}, u32[]{:S(2)}) %copy-start.3) | copy-done | bytes 786456
  73.7 1.7 %collective-permute-start.16 = (f32[96,24]{0,1:T(8,128)S(1)}, f32[96,24]{0,1:T(8,128)S(1)}, u32[]{:S(2)}, u32[]{:S(2)}) collective-permute-start(f32[96,24]{0,1:T(8,128)S(1)} %pad_maximum_fusion.7), channel_id=1, source_target_pairs={{0,1},{1,0},{2,3},{3,2},{4,5},{5,4},{6,7},{7,6},{8,9},{9,8},{10,11... | collective-permute-start | bytes 27656 | tf_op jit(solution)/shard_map/ppermute | solution.py:243
  75.4 2.0 %collective-permute-done.16 = f32[96,24]{0,1:T(8,128)S(1)} collective-permute-done((f32[96,24]{0,1:T(8,128)S(1)}, f32[96,24]{0,1:T(8,128)S(1)}, u32[]{:S(2)}, u32[]{:S(2)}) %collective-permute-start.16) | collective-permute-done | bytes 9248 | tf_op jit(solution)/shard_map/ppermute | solution.py:243
  77.4 1.5 %collective-permute-start.17 = (f32[96,24]{0,1:T(8,128)S(1)}, f32[96,24]{0,1:T(8,128)S(1)}, u32[]{:S(2)}, u32[]{:S(2)}) collective-permute-start(f32[96,24]{0,1:T(8,128)S(1)} %add.62), channel_id=1, source_target_pairs={{0,2},{1,3},{2,0},{3,1},{4,6},{5,7},{6,4},{7,5},{8,10},{9,11},{10,... | collective-permute-start | bytes 27656 | tf_op jit(solution)/shard_map/ppermute | solution.py:243
  79.1 2.0 %collective-permute-done.17 = f32[96,24]{0,1:T(8,128)S(1)} collective-permute-done((f32[96,24]{0,1:T(8,128)S(1)}, f32[96,24]{0,1:T(8,128)S(1)}, u32[]{:S(2)}, u32[]{:S(2)}) %collective-permute-start.17) | collective-permute-done | bytes 9248 | tf_op jit(solution)/shard_map/ppermute | solution.py:243
  81.1 1.7 %collective-permute-start.18 = (f32[96,24]{0,1:T(8,128)S(1)}, f32[96,24]{0,1:T(8,128)S(1)}, u32[]{:S(2)}, u32[]{:S(2)}) collective-permute-start(f32[96,24]{0,1:T(8,128)S(1)} %add.63), channel_id=1, source_target_pairs={{0,4},{1,5},{2,6},{3,7},{4,0},{5,1},{6,2},{7,3},{8,12},{9,13},{10,... | collective-permute-start | bytes 27656 | tf_op jit(solution)/shard_map/ppermute | solution.py:243
  82.8 1.3 %pad_maximum_fusion = f32[24,16,8,128]{3,2,1,0:T(8,128)} fusion(f32[12,16,8,128]{3,2,1,0:T(8,128)S(1)} %get-tuple-element.29, f32[12,16,8,128]{3,2,1,0:T(8,128)S(1)} %get-tuple-element.28), kind=kLoop, calls=%fused_computation.1 | loop fusion | flops 393216 | bytes 3145728 | tf_op jit(solution)/shard_map/concatenate | solution.py:296
  84.1 1.6 %collective-permute-done.18 = f32[96,24]{0,1:T(8,128)S(1)} collective-permute-done((f32[96,24]{0,1:T(8,128)S(1)}, f32[96,24]{0,1:T(8,128)S(1)}, u32[]{:S(2)}, u32[]{:S(2)}) %collective-permute-start.18) | collective-permute-done | bytes 9248 | tf_op jit(solution)/shard_map/ppermute | solution.py:243
  (74 shorter events, 11.3 us)
Async XLA Ops:
  0.7 7.1 %copy-start.4 = (f32[16,8,128]{2,1,0:T(8,128)S(1)}, f32[16,8,128]{2,1,0:T(8,128)}, u32[]{:S(2)}) copy-start(f32[16,8,128]{2,1,0:T(8,128)} %param.8) | copy-start | bytes 196612
  0.7 15.6 %copy-start.1 = (bf16[24,16,8,128]{3,2,1,0:T(8,128)(2,1)S(1)}, bf16[24,16,8,128]{3,2,1,0:T(8,128)(2,1)}, u32[]{:S(2)}) copy-start(bf16[24,16,8,128]{3,2,1,0:T(8,128)(2,1)} %param.11) | copy-start | bytes 2359300
  2.9 3.1 %collective-permute-start.1 = (bf16[4,16,2,128]{3,2,1,0:T(2,128)(2,1)S(1)}, bf16[4,16,2,128]{3,2,1,0:T(2,128)(2,1)S(1)}, u32[]{:S(2)}, u32[]{:S(2)}) collective-permute-start(bf16[4,16,2,128]{3,2,1,0:T(2,128)(2,1)S(1)} %slice.30), channel_id=1, source_target_pairs={{0,8},{8,0},{16,24},{24,16},{1,9},{9,1},{17,25},{25,17},{2,10},{10... | collective-permute-start | bytes 98312 | tf_op jit(solution)/shard_map/ppermute | solution.py:265
  3.4 15.8 %collective-permute-start = (bf16[12,16,8,128]{3,2,1,0:T(8,128)(2,1)S(1)}, bf16[12,16,8,128]{3,2,1,0:T(8,128)(2,1)S(1)}, u32[]{:S(2)}, u32[]{:S(2)}) collective-permute-start(bf16[12,16,8,128]{3,2,1,0:T(8,128)(2,1)S(1)} %get-tuple-element.30), channel_id=1, source_target_pairs={{0,1},{1,0},{2,3},{3,2},{4,5},{5,4},{6,7},{7,6},{8,9},{9,8},{10,11... | collective-permute-start | bytes 1179656 | tf_op jit(solution)/shard_map/ppermute | solution.py:243
  6.1 4.3 %collective-permute-start.3 = (bf16[4,16,4,128]{3,2,1,0:T(4,128)(2,1)S(1)}, bf16[4,16,4,128]{3,2,1,0:T(4,128)(2,1)S(1)}, u32[]{:S(2)}, u32[]{:S(2)}) collective-permute-start(bf16[4,16,4,128]{3,2,1,0:T(4,128)(2,1)S(1)} %pad_maximum_fusion.6), channel_id=1, source_target_pairs={{0,16},{8,24},{16,0},{24,8},{1,17},{9,25},{17,1},{25,9},{2,18},{10... | collective-permute-start | bytes 196616 | tf_op jit(solution)/shard_map/ppermute | solution.py:265
  7.8 18.7 %collective-permute-start.2 = (bf16[12,16,8,128]{3,2,1,0:T(8,128)(2,1)S(1)}, bf16[12,16,8,128]{3,2,1,0:T(8,128)(2,1)S(1)}, u32[]{:S(2)}, u32[]{:S(2)}) collective-permute-start(bf16[12,16,8,128]{3,2,1,0:T(8,128)(2,1)S(1)} %get-tuple-element.16.refs_0_), channel_id=1, source_target_pairs={{2,0},{4,2},{6,4},{1,3},{3,5},{5,7},{10,8},{12,10},{14,12},{9,11},... | collective-permute-start | bytes 1179656 | tf_op jit(solution)/shard_map/ppermute | solution.py:243
  10.7 8.6 %collective-permute-start.5 = (bf16[5,16,8,128]{3,2,1,0:T(8,128)(2,1)S(1)}, bf16[5,16,8,128]{3,2,1,0:T(8,128)(2,1)S(1)}, u32[]{:S(2)}, u32[]{:S(2)}) collective-permute-start(bf16[5,16,8,128]{3,2,1,0:T(8,128)(2,1)S(1)} %pad_maximum_fusion.5.refs_6_), channel_id=1, source_target_pairs={{0,1},{1,0},{2,3},{3,2},{4,5},{5,4},{6,7},{7,6},{8,9},{9,8},{10,11... | collective-permute-start | bytes 491528 | tf_op jit(solution)/shard_map/ppermute | solution.py:243
  12.7 9.2 %collective-permute-start.4 = (bf16[12,12,8,128]{3,2,1,0:T(8,128)(2,1)S(1)}, bf16[12,12,8,128]{3,2,1,0:T(8,128)(2,1)S(1)}, u32[]{:S(2)}, u32[]{:S(2)}) collective-permute-start(bf16[12,12,8,128]{3,2,1,0:T(8,128)(2,1)S(1)} %constant_dynamic-slice_fusion.1), channel_id=1, source_target_pairs={{0,2},{2,4},{4,6},{3,1},{5,3},{7,5},{8,10},{10,12},{12,14},{11,9},... | collective-permute-start | bytes 884744 | tf_op jit(solution)/shard_map/ppermute | solution.py:243
  16.8 24.6 %copy-start.2 = (bf16[24,16,8,128]{3,0,2,1:T(8,128)(2,1)}, bf16[24,16,8,128]{3,0,2,1:T(8,128)(2,1)S(1)}, u32[]{:S(2)}) copy-start(bf16[24,16,8,128]{3,0,2,1:T(8,128)(2,1)S(1)} %copy.37) | copy-start | bytes 2359300
  16.8 24.6 %collective-permute-start.10 = (bf16[16,8,24,128]{3,2,1,0:T(8,128)(2,1)S(1)}, bf16[16,8,24,128]{3,2,1,0:T(8,128)(2,1)S(1)}, u32[]{:S(2)}, u32[]{:S(2)}) collective-permute-start(bf16[16,8,24,128]{3,2,1,0:T(8,128)(2,1)S(1)} %bitcast.35), channel_id=1, source_target_pairs={{0,16},{8,24},{16,0},{24,8},{1,17},{9,25},{17,1},{25,9},{2,18},{10... | collective-permute-start | bytes 2359304 | tf_op jit(solution)/shard_map/ppermute | solution.py:280
  21.9 18.6 %collective-permute-start.6 = (bf16[308,8,128]{2,1,0:T(8,128)(2,1)S(1)}, bf16[308,8,128]{2,1,0:T(8,128)(2,1)S(1)}, u32[]{:S(2)}, u32[]{:S(2)}) collective-permute-start(bf16[308,8,128]{2,1,0:T(8,128)(2,1)S(1)} %pad_maximum_fusion.2), channel_id=1, source_target_pairs={{0,2},{2,4},{4,6},{3,1},{5,3},{7,5},{8,10},{10,12},{12,14},{11,9},... | collective-permute-start | bytes 1892360 | tf_op jit(solution)/shard_map/ppermute | solution.py:243
  26.4 15.9 %copy-start.5 = (s32[24,2]{0,1:T(2,128)S(1)}, s32[24,2]{0,1:T(2,128)}, u32[]{:S(2)}) copy-start(s32[24,2]{0,1:T(2,128)} %param.7) | copy-start | bytes 580
  26.5 14.0 %collective-permute-start.7 = (bf16[260,8,128]{2,1,0:T(8,128)(2,1)S(1)}, bf16[260,8,128]{2,1,0:T(8,128)(2,1)S(1)}, u32[]{:S(2)}, u32[]{:S(2)}) collective-permute-start(bf16[260,8,128]{2,1,0:T(8,128)(2,1)S(1)} %pad_maximum_fusion.3), channel_id=1, source_target_pairs={{2,0},{4,2},{6,4},{1,3},{3,5},{5,7},{10,8},{12,10},{14,12},{9,11},... | collective-permute-start | bytes 1597448 | tf_op jit(solution)/shard_map/ppermute | solution.py:243
  41.4 2.4 %collective-permute-start.11 = (bf16[232,8,128]{2,1,0:T(8,128)(2,1)}, bf16[232,8,128]{2,1,0:T(8,128)(2,1)S(1)}, u32[]{:S(2)}, u32[]{:S(2)}) collective-permute-start(bf16[232,8,128]{2,1,0:T(8,128)(2,1)} %pad_maximum_fusion.4), channel_id=1, source_target_pairs={{0,8},{8,0},{16,24},{24,16},{1,9},{9,1},{17,25},{25,17},{2,10},{10... | collective-permute-start | bytes 1425416 | tf_op jit(solution)/shard_map/ppermute | solution.py:244
  41.4 2.2 %collective-permute-start.8 = (bf16[5,16,8,128]{3,2,1,0:T(8,128)(2,1)S(1)}, bf16[5,16,8,128]{3,2,1,0:T(8,128)(2,1)}, u32[]{:S(2)}, u32[]{:S(2)}) collective-permute-start(bf16[5,16,8,128]{3,2,1,0:T(8,128)(2,1)S(1)} %pad_maximum_fusion.5.refs_6_), channel_id=1, source_target_pairs={{0,8},{8,0},{16,24},{24,16},{1,9},{9,1},{17,25},{25,17},{2,10},{10... | collective-permute-start | bytes 491528 | tf_op jit(solution)/shard_map/ppermute | solution.py:244
  42.3 1.6 %collective-permute-start.9 = (bf16[5,16,8,128]{3,2,1,0:T(8,128)(2,1)S(1)}, bf16[5,16,8,128]{3,2,1,0:T(8,128)(2,1)}, u32[]{:S(2)}, u32[]{:S(2)}) collective-permute-start(bf16[5,16,8,128]{3,2,1,0:T(8,128)(2,1)S(1)} %collective-permute-done.5.refs_7_), channel_id=1, source_target_pairs={{0,8},{8,0},{16,24},{24,16},{1,9},{9,1},{17,25},{25,17},{2,10},{10... | collective-permute-start | bytes 491528 | tf_op jit(solution)/shard_map/ppermute | solution.py:244
  42.4 29.5 %collective-permute-start.15 = (bf16[16,8,24,128]{3,2,1,0:T(8,128)(2,1)}, bf16[16,8,24,128]{3,2,1,0:T(8,128)(2,1)S(1)}, u32[]{:S(2)}, u32[]{:S(2)}) collective-permute-start(bf16[16,8,24,128]{3,2,1,0:T(8,128)(2,1)} %bitcast.36), channel_id=1, source_target_pairs={{0,8},{8,0},{16,24},{24,16},{1,9},{9,1},{17,25},{25,17},{2,10},{10... | collective-permute-start | bytes 2359304 | tf_op jit(solution)/shard_map/ppermute | solution.py:244
  42.9 29.8 %collective-permute-start.14 = (bf16[16,8,24,128]{3,2,1,0:T(8,128)(2,1)}, bf16[16,8,24,128]{3,2,1,0:T(8,128)(2,1)S(1)}, u32[]{:S(2)}, u32[]{:S(2)}) collective-permute-start(bf16[16,8,24,128]{3,2,1,0:T(8,128)(2,1)} %copy-done.6), channel_id=1, source_target_pairs={{0,8},{8,0},{16,24},{24,16},{1,9},{9,1},{17,25},{25,17},{2,10},{10... | collective-permute-start | bytes 2359304 | tf_op jit(solution)/shard_map/ppermute | solution.py:244
  55.9 9.6 %collective-permute-start.12 = (bf16[8,16,8,128]{3,2,1,0:T(8,128)(2,1)S(1)}, bf16[8,16,8,128]{3,2,1,0:T(8,128)(2,1)S(1)}, u32[]{:S(2)}, u32[]{:S(2)}) collective-permute-start(bf16[8,16,8,128]{3,2,1,0:T(8,128)(2,1)S(1)} %get-tuple-element.23), channel_id=1, source_target_pairs={{0,1},{1,0},{2,3},{3,2},{4,5},{5,4},{6,7},{7,6},{8,9},{9,8},{10,11... | collective-permute-start | bytes 786440 | tf_op jit(solution)/shard_map/ppermute | solution.py:243
  63.4 5.6 %collective-permute-start.13 = (bf16[4,16,8,128]{3,2,1,0:T(8,128)(2,1)S(1)}, bf16[4,16,8,128]{3,2,1,0:T(8,128)(2,1)S(1)}, u32[]{:S(2)}, u32[]{:S(2)}) collective-permute-start(bf16[4,16,8,128]{3,2,1,0:T(8,128)(2,1)S(1)} %get-tuple-element.24), channel_id=1, source_target_pairs={{0,1},{1,0},{2,3},{3,2},{4,5},{5,4},{6,7},{7,6},{8,9},{9,8},{10,11... | collective-permute-start | bytes 393224 | tf_op jit(solution)/shard_map/ppermute | solution.py:243
  69.1 1.9 %copy-start.7 = (bf16[16,8,24,128]{3,2,1,0:T(8,128)(2,1)S(1)}, bf16[16,8,24,128]{3,2,1,0:T(8,128)(2,1)}, u32[]{:S(2)}) copy-start(bf16[16,8,24,128]{3,2,1,0:T(8,128)(2,1)} %copy-done.6) | copy-start | bytes 2359300
  73.7 3.7 %collective-permute-start.16 = (f32[96,24]{0,1:T(8,128)S(1)}, f32[96,24]{0,1:T(8,128)S(1)}, u32[]{:S(2)}, u32[]{:S(2)}) collective-permute-start(f32[96,24]{0,1:T(8,128)S(1)} %pad_maximum_fusion.7), channel_id=1, source_target_pairs={{0,1},{1,0},{2,3},{3,2},{4,5},{5,4},{6,7},{7,6},{8,9},{9,8},{10,11... | collective-permute-start | bytes 27656 | tf_op jit(solution)/shard_map/ppermute | solution.py:243
  77.4 3.7 %collective-permute-start.17 = (f32[96,24]{0,1:T(8,128)S(1)}, f32[96,24]{0,1:T(8,128)S(1)}, u32[]{:S(2)}, u32[]{:S(2)}) collective-permute-start(f32[96,24]{0,1:T(8,128)S(1)} %add.62), channel_id=1, source_target_pairs={{0,2},{1,3},{2,0},{3,1},{4,6},{5,7},{6,4},{7,5},{8,10},{9,11},{10,... | collective-permute-start | bytes 27656 | tf_op jit(solution)/shard_map/ppermute | solution.py:243
  81.1 4.6 %collective-permute-start.18 = (f32[96,24]{0,1:T(8,128)S(1)}, f32[96,24]{0,1:T(8,128)S(1)}, u32[]{:S(2)}, u32[]{:S(2)}) collective-permute-start(f32[96,24]{0,1:T(8,128)S(1)} %add.63), channel_id=1, source_target_pairs={{0,4},{1,5},{2,6},{3,7},{4,0},{5,1},{6,2},{7,3},{8,12},{9,13},{10,... | collective-permute-start | bytes 27656 | tf_op jit(solution)/shard_map/ppermute | solution.py:243
  (4 other events, 4.9 us)

commit v14 on v13

--- a/solution.py
+++ b/solution.py
@@ -280,9 +280,10 @@
     crossed = lax.ppermute(turned, "probe", [(i, i ^ 2) for i in range(members)])
     message, turned = lax.optimization_barrier((planes(partner, extra_x, far_own), turned, side_b))[:2]
     side_c = hop(message, perm_b)
-    side_d = hop(after(planes(cut(partner, near * par), extra, far_x), side_a), perm_a)
+    beside = [cores(extra), cores(extra_x)]
+    side_d = hop(after(planes(cut(partner, near * par), extra, far_x), side_a, *beside), perm_a)
     far_other = cores(after(planes(side_c[half * rows :], side_d[half * far :]), crossed))
-    operands = (mine, partner, side_a, side_b, side_c, side_d, extra, extra_x, cores(extra), cores(extra_x), far_other)
+    operands = (mine, partner, side_a, side_b, side_c, side_d, extra, extra_x, *beside, far_other)
     first = par == 0
     own, back = [], []
     early = half * 2 // 3 // PACK * PACK

time: 86.6 us -> 90.9 us (1.050)
  local copies, waits for them, and re-layouts: 4.1 us -> 6.36 us
  waiting for transfers between devices: 28.2 us -> 30.3 us
  Pallas kernels: 19.5 us -> 17.5 us
  matrix products: 3.43 us -> 4.61 us
    pallas_call x2, Pallas kernels: 19.5 us -> 17.5 us  [propagate(): pl.pallas_call(functools.partial(march, steps, rows, halo, begin), grid_s...]
    ppermute x11, waiting for transfers between devices: 25.9 us -> 27.6 us  [local(): hop = lambda x, pairs: lax.ppermute(x, 'store', pairs)]
    unnamed x21 -> x27, local copies, waits for them, and re-layouts: 1.5 us -> 2.99 us
    dot_general x4, matrix products: 3.43 us -> 4.61 us  [local(): lax.dot_general(x, low, (((0, 1, 3), (1, 2, 3)), ((), ())), preferred_ele...]
    ppermute x1, starting transfers between devices: 0.76 us -> 1.79 us  [local(): lax.ppermute(turned, 'probe', [(i, i ^ 2) for i in range(members)])]
  transfers between devices with their start and end apart: 19 -> 19, of which waited for: 10 -> 9; matrix products, arithmetic and copies ran while one was open for 7% -> 8% of each run, Pallas kernels for 23% -> 19%
where the time goes in v14:
time: 90.9 us; the launch traced here: 90.5 us
  waiting for transfers between devices  30.3 us (33%)
  starting transfers between devices  26.7 us (29%)
  Pallas kernels  17.5 us (19%)
  local copies, waits for them, and re-layouts  6.36 us (7%)
  matrix products  4.61 us (5%)
  other arithmetic  3.86 us (4%)
  between operations  1.13 us (1%)
    ppermute x11, waiting for transfers between devices, local(): hop = lambda x, pairs: lax.ppermute(x, 'store', pairs)  27.6 us
    ppermute x11, starting transfers between devices, local(): hop = lambda x, pairs: lax.ppermute(x, 'store', pairs)  22.1 us
    pallas_call x2, Pallas kernels, propagate(): pl.pallas_call(functools.partial(march, steps, rows, halo, begin), grid_s...  17.5 us
    dot_general x4, matrix products, local(): lax.dot_general(x, low, (((0, 1, 3), (1, 2, 3)), ((), ())), preferred_ele...  4.61 us
    unnamed x27, local copies, waits for them, and re-layouts  2.99 us
    ppermute x2, starting transfers between devices, local(): got = lax.ppermute(sent, 'probe', [(i, i ^ span) for i in range(members)])  2.1 us
    dynamic_slice x1, local copies, waits for them, and re-layouts, local(): lax.dynamic_slice_in_dim(probe_field, half * (1 - par), half, axis=0)  2.03 us
  transfers between devices with their start and end apart: 19, of which 9 were waited for; matrix products, arithmetic and copies ran while one was open for 8% of the time, Pallas kernels for 19%

profile of v14, /device:TPU:0, one launch (start us, length us, event | category | flops | bytes accessed | tf_op | source)
XLA Modules:
  0.0 90.5 jit_solution(18429904604304745424)
XLA Ops:
  0.7 2.0 %constant_dynamic-slice_fusion.2 = (bf16[12,16,8,128]{3,2,1,0:T(8,128)(2,1)}, bf16[12,16,8,128]{3,2,1,0:T(8,128)(2,1)S(1)}) fusion(bf16[24,16,8,128]{3,2,1,0:T(8,128)(2,1)} %param.6, s32[]{:T(128)S(6)} %select_n.171, s32[]{:T(128)S(6)} %select_n.170), kind=kLoop, calls=%fused_computation.53 | loop fusion | bytes 1572872 | tf_op jit(solution)/shard_map/dynamic_slice | solution.py:254
  4.2 2.6 %collective-permute-start = (bf16[12,16,8,128]{3,2,1,0:T(8,128)(2,1)}, bf16[12,16,8,128]{3,2,1,0:T(8,128)(2,1)S(1)}, u32[]{:S(2)}, u32[]{:S(2)}) collective-permute-start(bf16[12,16,8,128]{3,2,1,0:T(8,128)(2,1)} %get-tuple-element.30), channel_id=1, source_target_pairs={{0,1},{1,0},{2,3},{3,2},{4,5},{5,4},{6,7},{7,6},{8,9},{9,8},{10,11... | collective-permute-start | bytes 1179656 | tf_op jit(solution)/shard_map/ppermute | solution.py:243
  6.9 1.6 %collective-permute-start.3 = (bf16[4,16,4,128]{3,2,1,0:T(4,128)(2,1)S(1)}, bf16[4,16,4,128]{3,2,1,0:T(4,128)(2,1)S(1)}, u32[]{:S(2)}, u32[]{:S(2)}) collective-permute-start(bf16[4,16,4,128]{3,2,1,0:T(4,128)(2,1)S(1)} %pad_maximum_fusion.6), channel_id=1, source_target_pairs={{0,16},{8,24},{16,0},{24,8},{1,17},{9,25},{17,1},{25,9},{2,18},{10... | collective-permute-start | bytes 196616 | tf_op jit(solution)/shard_map/ppermute | solution.py:265
  9.8 1.4 %collective-permute-done.3 = bf16[4,16,4,128]{3,2,1,0:T(4,128)(2,1)S(1)} collective-permute-done((bf16[4,16,4,128]{3,2,1,0:T(4,128)(2,1)S(1)}, bf16[4,16,4,128]{3,2,1,0:T(4,128)(2,1)S(1)}, u32[]{:S(2)}, u32[]{:S(2)}) %collective-permute-start.3) | collective-permute-done | bytes 65568 | tf_op jit(solution)/shard_map/ppermute | solution.py:265
  11.4 2.0 %collective-permute-start.5 = (bf16[5,16,8,128]{3,2,1,0:T(8,128)(2,1)S(1)}, bf16[5,16,8,128]{3,2,1,0:T(8,128)(2,1)S(1)}, u32[]{:S(2)}, u32[]{:S(2)}) collective-permute-start(bf16[5,16,8,128]{3,2,1,0:T(8,128)(2,1)S(1)} %pad_maximum_fusion.5.refs_6_), channel_id=1, source_target_pairs={{0,1},{1,0},{2,3},{3,2},{4,5},{5,4},{6,7},{7,6},{8,9},{9,8},{10,11... | collective-permute-start | bytes 491528 | tf_op jit(solution)/shard_map/ppermute | solution.py:243
  13.5 3.5 %collective-permute-start.4 = (bf16[12,12,8,128]{3,2,1,0:T(8,128)(2,1)S(1)}, bf16[12,12,8,128]{3,2,1,0:T(8,128)(2,1)S(1)}, u32[]{:S(2)}, u32[]{:S(2)}) collective-permute-start(bf16[12,12,8,128]{3,2,1,0:T(8,128)(2,1)S(1)} %constant_dynamic-slice_fusion.1), channel_id=1, source_target_pairs={{0,2},{2,4},{4,6},{3,1},{5,3},{7,5},{8,10},{10,12},{12,14},{11,9},... | collective-permute-start | bytes 884744 | tf_op jit(solution)/shard_map/ppermute | solution.py:243
  17.6 2.6 %collective-permute-done.5.refs_7_ = bf16[5,16,8,128]{3,2,1,0:T(8,128)(2,1)S(1)} collective-permute-done((bf16[5,16,8,128]{3,2,1,0:T(8,128)(2,1)S(1)}, bf16[5,16,8,128]{3,2,1,0:T(8,128)(2,1)S(1)}, u32[]{:S(2)}, u32[]{:S(2)}) %collective-permute-start.5) | collective-permute-done | bytes 163872 | tf_op jit(solution)/shard_map/ppermute | solution.py:243
  20.2 1.8 %collective-permute-start.10 = (bf16[16,8,24,128]{3,2,1,0:T(8,128)(2,1)S(1)}, bf16[16,8,24,128]{3,2,1,0:T(8,128)(2,1)}, u32[]{:S(2)}, u32[]{:S(2)}) collective-permute-start(bf16[16,8,24,128]{3,2,1,0:T(8,128)(2,1)S(1)} %bitcast.35), channel_id=1, source_target_pairs={{0,16},{8,24},{16,0},{24,8},{1,17},{9,25},{17,1},{25,9},{2,18},{10... | collective-permute-start | bytes 2359304 | tf_op jit(solution)/shard_map/ppermute | solution.py:280
  22.2 1.7 %collective-permute-done.4.refs_3_ = bf16[12,12,8,128]{3,2,1,0:T(8,128)(2,1)S(1)} collective-permute-done((bf16[12,12,8,128]{3,2,1,0:T(8,128)(2,1)S(1)}, bf16[12,12,8,128]{3,2,1,0:T(8,128)(2,1)S(1)}, u32[]{:S(2)}, u32[]{:S(2)}) %collective-permute-start.4) | collective-permute-done | bytes 294944 | tf_op jit(solution)/shard_map/ppermute | solution.py:243
  23.9 4.4 %collective-permute-start.6 = (bf16[308,8,128]{2,1,0:T(8,128)(2,1)S(1)}, bf16[308,8,128]{2,1,0:T(8,128)(2,1)S(1)}, u32[]{:S(2)}, u32[]{:S(2)}) collective-permute-start(bf16[308,8,128]{2,1,0:T(8,128)(2,1)S(1)} %pad_maximum_fusion.2), channel_id=1, source_target_pairs={{0,2},{2,4},{4,6},{3,1},{5,3},{7,5},{8,10},{10,12},{12,14},{11,9},... | collective-permute-start | bytes 1892360 | tf_op jit(solution)/shard_map/ppermute | solution.py:243
  29.8 14.1 %collective-permute-done.9.refs_5_ = bf16[260,8,128]{2,1,0:T(8,128)(2,1)S(1)} collective-permute-done((bf16[260,8,128]{2,1,0:T(8,128)(2,1)S(1)}, bf16[260,8,128]{2,1,0:T(8,128)(2,1)S(1)}, u32[]{:S(2)}, u32[]{:S(2)}) %collective-permute-start.9) | collective-permute-done | bytes 532512 | tf_op jit(solution)/shard_map/ppermute | solution.py:243
  45.6 1.4 %collective-permute-done.11.refs_10_ = bf16[232,8,128]{2,1,0:T(8,128)(2,1)S(1)} collective-permute-done((bf16[232,8,128]{2,1,0:T(8,128)(2,1)}, bf16[232,8,128]{2,1,0:T(8,128)(2,1)S(1)}, u32[]{:S(2)}, u32[]{:S(2)}) %collective-permute-start.11) | collective-permute-done | bytes 475168 | tf_op jit(solution)/shard_map/ppermute | solution.py:244
  48.8 11.1 %march.2 = (f32[8,16,8,128]{3,2,1,0:T(8,128)S(1)}, bf16[8,16,8,128]{3,2,1,0:T(8,128)(2,1)S(1)}) custom-call(s32[24,2]{1,0:T(8,128)S(1)} %copy.16.bounds_ref, bf16[12,16,8,128]{3,2,1,0:T(8,128)(2,1)S(1)} %get-tuple-element.16.refs_0_, bf16[12,16,8,128]{3,2,1,0:T(8,128)(2,1)S(1)} %collective-permute-done.refs_1_, ...), custom_call_target="tpu_custom_call" | custom-call | tf_op jit(solution)/shard_map/march/pallas_call | solution.py:215
  59.9 6.5 %march.3 = (f32[4,16,8,128]{3,2,1,0:T(8,128)S(1)}, bf16[4,16,8,128]{3,2,1,0:T(8,128)(2,1)S(1)}) custom-call(s32[24,2]{1,0:T(8,128)S(1)} %copy.16.bounds_ref, bf16[12,16,8,128]{3,2,1,0:T(8,128)(2,1)S(1)} %get-tuple-element.16.refs_0_, bf16[12,16,8,128]{3,2,1,0:T(8,128)(2,1)S(1)} %collective-permute-done.refs_1_, ...), custom_call_target="tpu_custom_call" | custom-call | flops 2883584000 | bytes 1441792 | tf_op jit(solution)/shard_map/march/pallas_call | solution.py:215
  66.4 2.1 %collective-permute-start.13 = (bf16[4,16,8,128]{3,2,1,0:T(8,128)(2,1)S(1)}, bf16[4,16,8,128]{3,2,1,0:T(8,128)(2,1)S(1)}, u32[]{:S(2)}, u32[]{:S(2)}) collective-permute-start(bf16[4,16,8,128]{3,2,1,0:T(8,128)(2,1)S(1)} %get-tuple-element.24), channel_id=1, source_target_pairs={{0,1},{1,0},{2,3},{3,2},{4,5},{5,4},{6,7},{7,6},{8,9},{9,8},{10,11... | collective-permute-start | bytes 393224 | tf_op jit(solution)/shard_map/ppermute | solution.py:243
  68.6 3.4 %collective-permute-done.13 = bf16[4,16,8,128]{3,2,1,0:T(8,128)(2,1)S(1)} collective-permute-done((bf16[4,16,8,128]{3,2,1,0:T(8,128)(2,1)S(1)}, bf16[4,16,8,128]{3,2,1,0:T(8,128)(2,1)S(1)}, u32[]{:S(2)}, u32[]{:S(2)}) %collective-permute-start.13) | collective-permute-done | bytes 131104 | tf_op jit(solution)/shard_map/ppermute | solution.py:243
  74.0 2.0 %convolution_bitcast_fusion.2 = f32[24,24]{0,1:T(8,128)S(1)} fusion(bf16[16,8,24,128]{3,2,1,0:T(8,128)(2,1)} %collective-permute-done.10, bf16[24,16,8,128]{3,2,1,0:T(8,128)(2,1)S(1)} %pad_maximum_fusion.1), kind=kOutput, calls=%fused_computation.4 | convolution fusion | flops 18874368 | bytes 1575168 | tf_op jit(solution)/shard_map/dot_general | solution.py:300
  77.9 1.7 %collective-permute-start.16 = (f32[96,24]{0,1:T(8,128)S(1)}, f32[96,24]{0,1:T(8,128)S(1)}, u32[]{:S(2)}, u32[]{:S(2)}) collective-permute-start(f32[96,24]{0,1:T(8,128)S(1)} %pad_maximum_fusion.7), channel_id=1, source_target_pairs={{0,1},{1,0},{2,3},{3,2},{4,5},{5,4},{6,7},{7,6},{8,9},{9,8},{10,11... | collective-permute-start | bytes 27656 | tf_op jit(solution)/shard_map/ppermute | solution.py:243
  79.6 2.0 %collective-permute-done.16 = f32[96,24]{0,1:T(8,128)S(1)} collective-permute-done((f32[96,24]{0,1:T(8,128)S(1)}, f32[96,24]{0,1:T(8,128)S(1)}, u32[]{:S(2)}, u32[]{:S(2)}) %collective-permute-start.16) | collective-permute-done | bytes 9248 | tf_op jit(solution)/shard_map/ppermute | solution.py:243
  81.6 1.5 %collective-permute-start.17 = (f32[96,24]{0,1:T(8,128)S(1)}, f32[96,24]{0,1:T(8,128)S(1)}, u32[]{:S(2)}, u32[]{:S(2)}) collective-permute-start(f32[96,24]{0,1:T(8,128)S(1)} %add.62), channel_id=1, source_target_pairs={{0,2},{1,3},{2,0},{3,1},{4,6},{5,7},{6,4},{7,5},{8,10},{9,11},{10,... | collective-permute-start | bytes 27656 | tf_op jit(solution)/shard_map/ppermute | solution.py:243
  83.3 2.0 %collective-permute-done.17 = f32[96,24]{0,1:T(8,128)S(1)} collective-permute-done((f32[96,24]{0,1:T(8,128)S(1)}, f32[96,24]{0,1:T(8,128)S(1)}, u32[]{:S(2)}, u32[]{:S(2)}) %collective-permute-start.17) | collective-permute-done | bytes 9248 | tf_op jit(solution)/shard_map/ppermute | solution.py:243
  85.3 1.6 %collective-permute-start.18 = (f32[96,24]{0,1:T(8,128)S(1)}, f32[96,24]{0,1:T(8,128)S(1)}, u32[]{:S(2)}, u32[]{:S(2)}) collective-permute-start(f32[96,24]{0,1:T(8,128)S(1)} %add.63), channel_id=1, source_target_pairs={{0,4},{1,5},{2,6},{3,7},{4,0},{5,1},{6,2},{7,3},{8,12},{9,13},{10,... | collective-permute-start | bytes 27656 | tf_op jit(solution)/shard_map/ppermute | solution.py:243
  86.9 1.3 %pad_maximum_fusion = f32[24,16,8,128]{3,2,1,0:T(8,128)} fusion(f32[12,16,8,128]{3,2,1,0:T(8,128)S(1)} %get-tuple-element.29, f32[12,16,8,128]{3,2,1,0:T(8,128)S(1)} %get-tuple-element.28), kind=kLoop, calls=%fused_computation.1 | loop fusion | flops 393216 | bytes 3145728 | tf_op jit(solution)/shard_map/concatenate | solution.py:297
  88.2 1.7 %collective-permute-done.18 = f32[96,24]{0,1:T(8,128)S(1)} collective-permute-done((f32[96,24]{0,1:T(8,128)S(1)}, f32[96,24]{0,1:T(8,128)S(1)}, u32[]{:S(2)}, u32[]{:S(2)}) %collective-permute-start.18) | collective-permute-done | bytes 9248 | tf_op jit(solution)/shard_map/ppermute | solution.py:243
  (80 shorter events, 13.4 us)
Async XLA Ops:
  0.7 16.3 %copy-start.6 = (bf16[24,16,8,128]{3,2,1,0:T(8,128)(2,1)S(1)}, bf16[24,16,8,128]{3,2,1,0:T(8,128)(2,1)}, u32[]{:S(2)}) copy-start(bf16[24,16,8,128]{3,2,1,0:T(8,128)(2,1)} %param.11) | copy-start | bytes 2359300
  3.7 3.1 %collective-permute-start.1 = (bf16[4,16,2,128]{3,2,1,0:T(2,128)(2,1)S(1)}, bf16[4,16,2,128]{3,2,1,0:T(2,128)(2,1)S(1)}, u32[]{:S(2)}, u32[]{:S(2)}) collective-permute-start(bf16[4,16,2,128]{3,2,1,0:T(2,128)(2,1)S(1)} %slice.30), channel_id=1, source_target_pairs={{0,8},{8,0},{16,24},{24,16},{1,9},{9,1},{17,25},{25,17},{2,10},{10... | collective-permute-start | bytes 98312 | tf_op jit(solution)/shard_map/ppermute | solution.py:265
  4.2 17.8 %collective-permute-start = (bf16[12,16,8,128]{3,2,1,0:T(8,128)(2,1)}, bf16[12,16,8,128]{3,2,1,0:T(8,128)(2,1)S(1)}, u32[]{:S(2)}, u32[]{:S(2)}) collective-permute-start(bf16[12,16,8,128]{3,2,1,0:T(8,128)(2,1)} %get-tuple-element.30), channel_id=1, source_target_pairs={{0,1},{1,0},{2,3},{3,2},{4,5},{5,4},{6,7},{7,6},{8,9},{9,8},{10,11... | collective-permute-start | bytes 1179656 | tf_op jit(solution)/shard_map/ppermute | solution.py:243
  6.9 4.3 %collective-permute-start.3 = (bf16[4,16,4,128]{3,2,1,0:T(4,128)(2,1)S(1)}, bf16[4,16,4,128]{3,2,1,0:T(4,128)(2,1)S(1)}, u32[]{:S(2)}, u32[]{:S(2)}) collective-permute-start(bf16[4,16,4,128]{3,2,1,0:T(4,128)(2,1)S(1)} %pad_maximum_fusion.6), channel_id=1, source_target_pairs={{0,16},{8,24},{16,0},{24,8},{1,17},{9,25},{17,1},{25,9},{2,18},{10... | collective-permute-start | bytes 196616 | tf_op jit(solution)/shard_map/ppermute | solution.py:265
  8.5 19.9 %collective-permute-start.2 = (bf16[12,16,8,128]{3,2,1,0:T(8,128)(2,1)S(1)}, bf16[12,16,8,128]{3,2,1,0:T(8,128)(2,1)S(1)}, u32[]{:S(2)}, u32[]{:S(2)}) collective-permute-start(bf16[12,16,8,128]{3,2,1,0:T(8,128)(2,1)S(1)} %get-tuple-element.16.refs_0_), channel_id=1, source_target_pairs={{2,0},{4,2},{6,4},{1,3},{3,5},{5,7},{10,8},{12,10},{14,12},{9,11},... | collective-permute-start | bytes 1179656 | tf_op jit(solution)/shard_map/ppermute | solution.py:243
  11.4 8.8 %collective-permute-start.5 = (bf16[5,16,8,128]{3,2,1,0:T(8,128)(2,1)S(1)}, bf16[5,16,8,128]{3,2,1,0:T(8,128)(2,1)S(1)}, u32[]{:S(2)}, u32[]{:S(2)}) collective-permute-start(bf16[5,16,8,128]{3,2,1,0:T(8,128)(2,1)S(1)} %pad_maximum_fusion.5.refs_6_), channel_id=1, source_target_pairs={{0,1},{1,0},{2,3},{3,2},{4,5},{5,4},{6,7},{7,6},{8,9},{9,8},{10,11... | collective-permute-start | bytes 491528 | tf_op jit(solution)/shard_map/ppermute | solution.py:243
  13.5 15.0 %collective-permute-start.7 = (bf16[5,16,8,128]{3,2,1,0:T(8,128)(2,1)S(1)}, bf16[5,16,8,128]{3,2,1,0:T(8,128)(2,1)S(1)}, u32[]{:S(2)}, u32[]{:S(2)}) collective-permute-start(bf16[5,16,8,128]{3,2,1,0:T(8,128)(2,1)S(1)} %pad_maximum_fusion.5.refs_6_), channel_id=1, source_target_pairs={{0,8},{8,0},{16,24},{24,16},{1,9},{9,1},{17,25},{25,17},{2,10},{10... | collective-permute-start | bytes 491528 | tf_op jit(solution)/shard_map/ppermute | solution.py:244
  13.5 10.4 %collective-permute-start.4 = (bf16[12,12,8,128]{3,2,1,0:T(8,128)(2,1)S(1)}, bf16[12,12,8,128]{3,2,1,0:T(8,128)(2,1)S(1)}, u32[]{:S(2)}, u32[]{:S(2)}) collective-permute-start(bf16[12,12,8,128]{3,2,1,0:T(8,128)(2,1)S(1)} %constant_dynamic-slice_fusion.1), channel_id=1, source_target_pairs={{0,2},{2,4},{4,6},{3,1},{5,3},{7,5},{8,10},{10,12},{12,14},{11,9},... | collective-permute-start | bytes 884744 | tf_op jit(solution)/shard_map/ppermute | solution.py:243
  17.5 27.3 %copy-start.7 = (bf16[24,16,8,128]{3,0,2,1:T(8,128)(2,1)}, bf16[24,16,8,128]{3,0,2,1:T(8,128)(2,1)S(1)}, u32[]{:S(2)}) copy-start(bf16[24,16,8,128]{3,0,2,1:T(8,128)(2,1)S(1)} %copy.37) | copy-start | bytes 2359300
  20.2 24.6 %collective-permute-start.10 = (bf16[16,8,24,128]{3,2,1,0:T(8,128)(2,1)S(1)}, bf16[16,8,24,128]{3,2,1,0:T(8,128)(2,1)}, u32[]{:S(2)}, u32[]{:S(2)}) collective-permute-start(bf16[16,8,24,128]{3,2,1,0:T(8,128)(2,1)S(1)} %bitcast.35), channel_id=1, source_target_pairs={{0,16},{8,24},{16,0},{24,8},{1,17},{9,25},{17,1},{25,9},{2,18},{10... | collective-permute-start | bytes 2359304 | tf_op jit(solution)/shard_map/ppermute | solution.py:280
  22.0 6.4 %collective-permute-start.8 = (bf16[5,16,8,128]{3,2,1,0:T(8,128)(2,1)S(1)}, bf16[5,16,8,128]{3,2,1,0:T(8,128)(2,1)S(1)}, u32[]{:S(2)}, u32[]{:S(2)}) collective-permute-start(bf16[5,16,8,128]{3,2,1,0:T(8,128)(2,1)S(1)} %collective-permute-done.5.refs_7_), channel_id=1, source_target_pairs={{0,8},{8,0},{16,24},{24,16},{1,9},{9,1},{17,25},{25,17},{2,10},{10... | collective-permute-start | bytes 491528 | tf_op jit(solution)/shard_map/ppermute | solution.py:244
  23.9 20.1 %collective-permute-start.6 = (bf16[308,8,128]{2,1,0:T(8,128)(2,1)S(1)}, bf16[308,8,128]{2,1,0:T(8,128)(2,1)S(1)}, u32[]{:S(2)}, u32[]{:S(2)}) collective-permute-start(bf16[308,8,128]{2,1,0:T(8,128)(2,1)S(1)} %pad_maximum_fusion.2), channel_id=1, source_target_pairs={{0,2},{2,4},{4,6},{3,1},{5,3},{7,5},{8,10},{10,12},{12,14},{11,9},... | collective-permute-start | bytes 1892360 | tf_op jit(solution)/shard_map/ppermute | solution.py:243
  28.3 16.6 %copy-start.10 = (s32[24,2]{0,1:T(2,128)S(1)}, s32[24,2]{0,1:T(2,128)}, u32[]{:S(2)}) copy-start(s32[24,2]{0,1:T(2,128)} %param.7) | copy-start | bytes 580
  28.4 16.4 %copy-start.1 = (bf16[5,16,8,128]{3,2,1,0:T(8,128)(2,1)}, bf16[5,16,8,128]{3,2,1,0:T(8,128)(2,1)S(1)}, u32[]{:S(2)}) copy-start(bf16[5,16,8,128]{3,2,1,0:T(8,128)(2,1)S(1)} %collective-permute-done.7.refs_8_) | copy-start | bytes 491524
  28.4 16.4 %copy-start.4 = (bf16[5,16,8,128]{3,2,1,0:T(8,128)(2,1)}, bf16[5,16,8,128]{3,2,1,0:T(8,128)(2,1)S(1)}, u32[]{:S(2)}) copy-start(bf16[5,16,8,128]{3,2,1,0:T(8,128)(2,1)S(1)} %collective-permute-done.8.refs_9_) | copy-start | bytes 491524
  28.5 15.4 %collective-permute-start.9 = (bf16[260,8,128]{2,1,0:T(8,128)(2,1)S(1)}, bf16[260,8,128]{2,1,0:T(8,128)(2,1)S(1)}, u32[]{:S(2)}, u32[]{:S(2)}) collective-permute-start(bf16[260,8,128]{2,1,0:T(8,128)(2,1)S(1)} %pad_maximum_fusion.3), channel_id=1, source_target_pairs={{2,0},{4,2},{6,4},{1,3},{3,5},{5,7},{10,8},{12,10},{14,12},{9,11},... | collective-permute-start | bytes 1597448 | tf_op jit(solution)/shard_map/ppermute | solution.py:243
  44.8 2.1 %collective-permute-start.11 = (bf16[232,8,128]{2,1,0:T(8,128)(2,1)}, bf16[232,8,128]{2,1,0:T(8,128)(2,1)S(1)}, u32[]{:S(2)}, u32[]{:S(2)}) collective-permute-start(bf16[232,8,128]{2,1,0:T(8,128)(2,1)} %pad_maximum_fusion.4), channel_id=1, source_target_pairs={{0,8},{8,0},{16,24},{24,16},{1,9},{9,1},{17,25},{25,17},{2,10},{10... | collective-permute-start | bytes 1425416 | tf_op jit(solution)/shard_map/ppermute | solution.py:244
  45.0 31.0 %collective-permute-start.15 = (bf16[16,8,24,128]{3,2,1,0:T(8,128)(2,1)}, bf16[16,8,24,128]{3,2,1,0:T(8,128)(2,1)S(1)}, u32[]{:S(2)}, u32[]{:S(2)}) collective-permute-start(bf16[16,8,24,128]{3,2,1,0:T(8,128)(2,1)} %bitcast.36), channel_id=1, source_target_pairs={{0,8},{8,0},{16,24},{24,16},{1,9},{9,1},{17,25},{25,17},{2,10},{10... | collective-permute-start | bytes 2359304 | tf_op jit(solution)/shard_map/ppermute | solution.py:244
  45.5 31.4 %collective-permute-start.14 = (bf16[16,8,24,128]{3,2,1,0:T(8,128)(2,1)}, bf16[16,8,24,128]{3,2,1,0:T(8,128)(2,1)S(1)}, u32[]{:S(2)}, u32[]{:S(2)}) collective-permute-start(bf16[16,8,24,128]{3,2,1,0:T(8,128)(2,1)} %collective-permute-done.10), channel_id=1, source_target_pairs={{0,8},{8,0},{16,24},{24,16},{1,9},{9,1},{17,25},{25,17},{2,10},{10... | collective-permute-start | bytes 2359304 | tf_op jit(solution)/shard_map/ppermute | solution.py:244
  59.9 8.7 %collective-permute-start.12 = (bf16[8,16,8,128]{3,2,1,0:T(8,128)(2,1)S(1)}, bf16[8,16,8,128]{3,2,1,0:T(8,128)(2,1)S(1)}, u32[]{:S(2)}, u32[]{:S(2)}) collective-permute-start(bf16[8,16,8,128]{3,2,1,0:T(8,128)(2,1)S(1)} %get-tuple-element.23), channel_id=1, source_target_pairs={{0,1},{1,0},{2,3},{3,2},{4,5},{5,4},{6,7},{7,6},{8,9},{9,8},{10,11... | collective-permute-start | bytes 786440 | tf_op jit(solution)/shard_map/ppermute | solution.py:243
  66.4 5.6 %collective-permute-start.13 = (bf16[4,16,8,128]{3,2,1,0:T(8,128)(2,1)S(1)}, bf16[4,16,8,128]{3,2,1,0:T(8,128)(2,1)S(1)}, u32[]{:S(2)}, u32[]{:S(2)}) collective-permute-start(bf16[4,16,8,128]{3,2,1,0:T(8,128)(2,1)S(1)} %get-tuple-element.24), channel_id=1, source_target_pairs={{0,1},{1,0},{2,3},{3,2},{4,5},{5,4},{6,7},{7,6},{8,9},{9,8},{10,11... | collective-permute-start | bytes 393224 | tf_op jit(solution)/shard_map/ppermute | solution.py:243
  77.9 3.7 %collective-permute-start.16 = (f32[96,24]{0,1:T(8,128)S(1)}, f32[96,24]{0,1:T(8,128)S(1)}, u32[]{:S(2)}, u32[]{:S(2)}) collective-permute-start(f32[96,24]{0,1:T(8,128)S(1)} %pad_maximum_fusion.7), channel_id=1, source_target_pairs={{0,1},{1,0},{2,3},{3,2},{4,5},{5,4},{6,7},{7,6},{8,9},{9,8},{10,11... | collective-permute-start | bytes 27656 | tf_op jit(solution)/shard_map/ppermute | solution.py:243
  81.6 3.7 %collective-permute-start.17 = (f32[96,24]{0,1:T(8,128)S(1)}, f32[96,24]{0,1:T(8,128)S(1)}, u32[]{:S(2)}, u32[]{:S(2)}) collective-permute-start(f32[96,24]{0,1:T(8,128)S(1)} %add.62), channel_id=1, source_target_pairs={{0,2},{1,3},{2,0},{3,1},{4,6},{5,7},{6,4},{7,5},{8,10},{9,11},{10,... | collective-permute-start | bytes 27656 | tf_op jit(solution)/shard_map/ppermute | solution.py:243
  85.3 4.6 %collective-permute-start.18 = (f32[96,24]{0,1:T(8,128)S(1)}, f32[96,24]{0,1:T(8,128)S(1)}, u32[]{:S(2)}, u32[]{:S(2)}) collective-permute-start(f32[96,24]{0,1:T(8,128)S(1)} %add.63), channel_id=1, source_target_pairs={{0,4},{1,5},{2,6},{3,7},{4,0},{5,1},{6,2},{7,3},{8,12},{9,13},{10,... | collective-permute-start | bytes 27656 | tf_op jit(solution)/shard_map/ppermute | solution.py:243
  (7 other events, 26.3 us)
